TPU v7x, 32 devices: a whole 2x2x4 slice. The times are simulated.
32 devices in a mesh: req: 4 (over y, core), mp: 8 (over z, x).
Axes of the slice: x: 2, y: 2, z: 4, core: 2. Of those that a mesh axis runs over, the one named last changes fastest.
Arguments:
- latents: bfloat16 [8, 4, 192, 2240], P('req', None, 'mp'), may hold values from -6 to 6
- w_qkv: bfloat16 [2240, 3360], P('mp'), may hold values from -0.125 to 0.125
- state_in: float32 [8, 10, 112, 112], P('req', None, 'mp'), may hold values from -384 to 384
- ksum_in: float32 [8, 10, 112], P('req'), may hold values from 64 to 1024
- frames_live: int32 [8], P('req'), may hold values from 1 to 4
- new_place: int32 [80], replicated, may hold values from 0 to 79, as said below
Outputs:
- attended: bfloat16 [8, 4, 192, 1120], P('req', None, 'mp')
- moved_state: float32 [80, 112, 112], P('req', 'mp')
- moved_ksum: float32 [80, 112], P('req')
Inputs may be any that keep to these rules, and one draw needn't show every extreme that they name: new_place is a permutation; pair g of owner g // 20 goes to owner new_place[g] // 20; every owner receives 20 pairs, and from one owner at most 6 pairs go to one new owner, exactly 6 to some.
All inputs are finite; a program needn't handle non-finite values.
Results may differ from a plain program's by a relative error of at most 0.0075.
Values may be sent and summed in bfloat16 or wider, within the bound.
No kernel may reach another device: no remote copies, remote signals or barrier semaphores. Data moves between devices by JAX's collectives and lax.ppermute only.
A program may use at most 128 MiB of HBM per device.

v0:
```python
import jax
import jax.numpy as jnp
from jax import lax
from jax.sharding import PartitionSpec as P


def feature_map(values):
    return jax.nn.elu(values) + 1.0


def project_rows(shard_piece, flat_rows):
    return jnp.dot(flat_rows, shard_piece, preferred_element_type=jnp.float32)


def combine_states(kv_part, ks_part, state_in, ksum_in):
    share_rows = state_in.shape[2]
    share_start = lax.axis_index("mp") * share_rows
    kv_full, ks_full = (
        lax.psum(kv_part.astype(jnp.bfloat16), "mp").astype(jnp.float32),
        lax.psum(ks_part.astype(jnp.bfloat16), "mp").astype(jnp.float32),
    )
    old_full = lax.all_gather(state_in, "mp", axis=2, tiled=True)
    state_full = old_full + kv_full
    state_share = lax.dynamic_slice_in_dim(state_full, share_start, share_rows, 2)
    ksum_full = ksum_in + ks_full
    return (state_share, state_full, ksum_full)


def hand_over(state_share, ksum_full, new_place):
    owner_count = lax.axis_size("req")
    owner_index = lax.axis_index("req")
    stream_count, head_count, share_rows, head_size = state_share.shape
    unit_count = stream_count * head_count
    capacity = (unit_count - 2) // owner_count + 2
    targets = (new_place // unit_count).reshape(owner_count, unit_count)
    matching = targets[:, :, None] == targets[:, None, :]
    earlier = lax.broadcasted_iota(
        jnp.int32, (1, unit_count, unit_count), 2
    ) < lax.broadcasted_iota(jnp.int32, (1, unit_count, unit_count), 1)
    ranks = jnp.sum(jnp.logical_and(matching, earlier).astype(jnp.int32), axis=2)
    my_targets = lax.dynamic_index_in_dim(targets, owner_index, 0, keepdims=False)
    my_ranks = lax.dynamic_index_in_dim(ranks, owner_index, 0, keepdims=False)
    slot_index = my_targets * capacity + my_ranks
    unit_states = state_share.reshape(unit_count, share_rows, head_size)
    unit_ksums = ksum_full.reshape(unit_count, head_size)
    send_state = (
        jnp.zeros((owner_count * capacity, share_rows, head_size), jnp.float32)
        .at[slot_index]
        .set(unit_states)
    )
    send_ksum = (
        jnp.zeros((owner_count * capacity, head_size), jnp.float32).at[slot_index].set(unit_ksums)
    )
    got_state, got_ksum = (
        lax.all_to_all(send_state, "req", split_axis=0, concat_axis=0, tiled=True),
        lax.all_to_all(send_ksum, "req", split_axis=0, concat_axis=0, tiled=True),
    )
    pair_count = new_place.shape[0]
    inverse = (
        jnp.zeros((pair_count,), jnp.int32)
        .at[new_place]
        .set(jnp.arange(pair_count, dtype=jnp.int32))
    )
    arrivals = lax.dynamic_slice_in_dim(inverse, owner_index * unit_count, unit_count)
    positions = arrivals // unit_count * capacity + ranks.reshape(-1)[arrivals]
    return (got_state[positions], got_ksum[positions])


def body(latents, w_qkv, state_in, ksum_in, frames_live, new_place):
    stream_count, frame_count, spatial_count, model_width = latents.shape
    head_count = ksum_in.shape[1]
    head_size = ksum_in.shape[2]
    inner_width = head_count * head_size
    flat_rows = latents.reshape(-1, model_width)
    frame_index = lax.broadcasted_iota(jnp.int32, (stream_count, frame_count), 1)
    live_frames = (frame_index < frames_live[:, None]).astype(jnp.float32)
    live_mask = jnp.repeat(live_frames, spatial_count, axis=1)

    def split_heads(block_rows):
        return block_rows.reshape(stream_count, frame_count * spatial_count, head_count, head_size)

    projected = project_rows(lax.all_gather(w_qkv, "mp", axis=0, tiled=True), flat_rows).astype(
        jnp.bfloat16
    )
    query_part = projected[:, :inner_width]
    keyed = (
        feature_map(split_heads(projected[:, inner_width : 2 * inner_width]).astype(jnp.float32))
        * live_mask[:, :, None, None]
    )
    values = split_heads(projected[:, 2 * inner_width :]).astype(jnp.float32)
    kv_part = jnp.einsum("sthi,sthj->shij", keyed, values, precision=lax.Precision.HIGHEST)
    ks_part = jnp.sum(keyed, axis=1)
    state_share, state_full, ksum_full = combine_states(kv_part, ks_part, state_in, ksum_in)
    moved_state, moved_ksum = hand_over(state_share, ksum_full, new_place)
    state_full, ksum_full, moved_state, moved_ksum = (
        state_full,
        ksum_full,
        moved_state,
        moved_ksum,
    )
    queried = feature_map(split_heads(query_part).astype(jnp.float32))
    numerator = jnp.einsum("sthi,shij->sthj", queried, state_full, precision=lax.Precision.HIGHEST)
    denominator = jnp.einsum("sthi,shi->sth", queried, ksum_full, precision=lax.Precision.HIGHEST)
    attended = numerator / denominator[:, :, :, None] * live_mask[:, :, None, None]
    attended = attended.astype(jnp.bfloat16).reshape(
        stream_count, frame_count, spatial_count, inner_width
    )
    return (attended, moved_state, moved_ksum)


def solution(mesh):
    placed = (
        P("req", None, "mp", None),
        P("mp", None),
        P("req", None, "mp", None),
        P("req", None, None),
        P("req"),
        P(),
    )
    return jax.shard_map(
        body,
        mesh=mesh,
        in_specs=placed,
        out_specs=(P("req", None, "mp", None), P("req", "mp", None), P("req", None)),
        check_vma=False,
    )
```

profile of v0, /device:TPU:0, one launch (start us, length us, event | category | flops | bytes accessed | tf_op | source)
XLA Modules:
  0.0 343.2 jit_solution(1984746884072966899)
XLA Ops:
  7.2 0.0 copy-start
  7.2 0.0 all-gather.2.cloned.1.call-start
  7.3 0.7 all-gather.2.cloned.1.call-update
  7.9 0.0 all-reduce.2.cloned.1.call-start
  8.0 0.1 reshape.83
  8.1 0.0 copy-done.5
  8.1 0.1 compare_convert_fusion
  8.2 0.1 broadcast_in_dim.27
  8.3 0.1 mul.36
  8.3 0.1 copy.75
  8.4 0.5 convert_reduce_fusion
  8.9 0.1 copy.77
  9.0 0.1 reshape.85
  9.1 0.1 copy.61
  9.2 0.8 scatter_custom_fusion.1
  10.0 0.1 compare_select_fusion.5
  10.1 0.7 gather_fusion
  10.8 0.2 add_reduce_fusion
  11.0 0.1 compare_select_fusion.4
  11.1 41.8 %all_gather.6 = f32[2,10,112,112]{3,0,1,2:T(2,128)} all-gather(f32[2,10,14,112]{3,0,1,2:T(2,128)S(1)} %copy.61), channel_id=1, replica_groups=mesh['req'=4,'mp'=8] {'mp'}, dimensions={2}, use_global_device_ids=true | all-gather | bytes 1128960 | tf_op jit(solution)/shard_map/all_gather | solution.py:22
  52.9 178.4 %all-gather.2.cloned.1.call-done = bf16[2240,3360]{1,0:T(8,128)(2,1)} async-done(((bf16[280,3360]{1,0:T(8,128)(2,1)}), bf16[2240,3360]{1,0:T(8,128)(2,1)}) %all-gather.2.cloned.1.call-update) | async-done | bytes 15052816 | tf_op jit(solution)/shard_map/all_gather | solution.py:82
  231.2 8.8 %convolution_convert_fusion = bf16[192,3360]{1,0:T(8,128)(2,1)S(1)} fusion(bf16[192,2240]{1,0:T(8,128)(2,1)S(1)} %bitcast.26, bf16[2240,3360]{1,0:T(8,128)(2,1)} %all-gather.2.cloned.1.call-done), kind=kOutput, calls=%fused_computation.6 | convolution fusion | flops 2890782720 | bytes 17203200 | tf_op jit(solution)/shard_map/dot_general | solution.py:12
  240.0 1.3 slice_convert_fusion
  241.3 1.8 reshape.143
  243.1 2.1 reshape.144
  245.2 3.5 %convolution_convert_fusion.1 = bf16[2,10,112,112]{3,2,1,0:T(8,128)(2,1)} fusion(bf16[2,96,10,112]{3,2,1,0:T(8,128)(2,1)} %reshape.143, f32[2,96,10,112]{3,2,1,0:T(8,128)S(1)} %reshape.144, f32[2,96]{1,0:T(2,128)S(1)} %mul.36), kind=kOutput, calls=%fused_computation.14 | convolution fusion | flops 290339840 | bytes 1792768 | tf_op jit(solution)/shard_map/sthi,sthj->shij/dot_general | solution.py:91
  248.7 0.0 all-reduce.2.cloned.1.call-update
  248.7 0.6 fusion.12
  249.3 0.0 copy-start.3
  249.3 2.0 reshape.145
  251.3 18.9 %psum.15 = bf16[2,10,112]{2,1,0:T(8,128)(2,1)S(1)} all-reduce(bf16[2,10,112]{2,1,0:T(8,128)(2,1)S(1)} %fusion.12), channel_id=1, replica_groups=mesh['req'=4,'mp'=8] {'mp'}, use_global_device_ids=true, to_apply=%region_2.3 | all-reduce | flops 2240 | bytes 8960 | tf_op jit(solution)/shard_map/psum | solution.py:20
  270.3 0.0 copy-done.3
  270.3 0.6 scatter_custom_fusion.2
  270.9 0.6 all_to_all.12
  271.6 3.3 all-to-all-start.1
  274.8 3.4 fusion.9
  278.2 0.4 all-to-all-done.1
  278.6 1.2 gather_fusion.2
  279.8 40.5 %all-reduce.2.cloned.1.call-done = bf16[2,10,112,112]{3,2,1,0:T(8,128)(2,1)} async-done(((bf16[2,10,112,112]{3,2,1,0:T(8,128)(2,1)}), bf16[2,10,112,112]{3,2,1,0:T(8,128)(2,1)}) %all-reduce.2.cloned.1.call-update) | async-done | bytes 501776 | tf_op jit(solution)/shard_map/psum | solution.py:19
  320.3 1.2 copy_add_fusion
  321.5 0.7 broadcast_in_dim.28
  322.1 4.3 %scatter_fusion = f32[24,14,112]{2,1,0:T(8,128)} fusion(f32[24,14,112]{2,1,0:T(8,128)} %broadcast_in_dim.28, s32[20]{0:T(128)S(1)} %fusion.17, f32[20,14,112]{2,1,0:T(8,128)S(1)} %bitcast.27), kind=kCustom, calls=%fused_computation.3 | custom fusion | bytes 376400 | tf_op jit(solution)/shard_map/scatter | solution.py:49
  326.4 3.5 %all-to-all-start = ((f32[24,14,112]{2,1,0:T(8,128)}), f32[24,14,112]{2,1,0:T(8,128)S(1)}, u32[]{:S(2)}, u32[]{:S(2)}) async-start(f32[24,14,112]{2,1,0:T(8,128)} %scatter_fusion), calls=%async_computation | async-start | bytes 393216 | tf_op jit(solution)/shard_map/all_to_all | solution.py:55
  330.0 3.1 fusion.2
  333.1 0.2 copy.74
  333.4 1.4 reshape.82
  334.8 0.3 all-to-all-done
  335.1 1.2 gather_fusion.1
  (19 shorter events, 0.1 us)
Async XLA Ops:
  7.2 224.1 %copy-start = (bf16[2,4,24,2240]{3,2,1,0:T(8,128)(2,1)S(1)}, bf16[2,4,24,2240]{3,2,1,0:T(8,128)(2,1)}, u32[]{:S(2)}) copy-start(bf16[2,4,24,2240]{3,2,1,0:T(8,128)(2,1)} %param.6) | copy-start | bytes 2580484
  7.2 0.8 copy-start.4
  7.2 0.9 copy-start.5
  7.2 1.9 copy-start.2
  7.2 224.0 %all-gather.2.cloned.1.call-start = ((), (), s32[]{:S(2)}) async-start(), calls=%async_computation.2 | async-start | bytes 17418240 | tf_op jit(solution)/shard_map/all_gather | solution.py:82
  7.9 312.3 %all-reduce.2.cloned.1.call-start = ((), (), s32[]{:S(2)}) async-start(), calls=%async_computation.3 | async-start | bytes 1146880 | tf_op jit(solution)/shard_map/psum | solution.py:19
  249.3 21.0 %copy-start.3 = (f32[2,10,112]{2,0,1:T(2,128)S(1)}, f32[2,10,112]{2,0,1:T(2,128)}, u32[]{:S(2)}) copy-start(f32[2,10,112]{2,0,1:T(2,128)} %param.9) | copy-start | bytes 26884
  251.3 68.9 %copy-start.1 = (f32[2,10,112,112]{3,0,1,2:T(2,128)S(1)}, f32[2,10,112,112]{3,0,1,2:T(2,128)}, u32[]{:S(2)}) copy-start(f32[2,10,112,112]{3,0,1,2:T(2,128)} %all_gather.6) | copy-start | bytes 3010564
  271.6 7.1 %all-to-all-start.1 = ((f32[4,6,112]{2,1,0:T(8,128)}), f32[4,6,112]{2,1,0:T(8,128)S(1)}, u32[]{:S(2)}, u32[]{:S(2)}) async-start(f32[4,6,112]{2,1,0:T(8,128)} %all_to_all.12), calls=%async_computation.1 | async-start | bytes 32768 | tf_op jit(solution)/shard_map/all_to_all | solution.py:56
  326.4 8.6 %all-to-all-start = ((f32[24,14,112]{2,1,0:T(8,128)}), f32[24,14,112]{2,1,0:T(8,128)S(1)}, u32[]{:S(2)}, u32[]{:S(2)}) async-start(f32[24,14,112]{2,1,0:T(8,128)} %scatter_fusion), calls=%async_computation | async-start | bytes 393216 | tf_op jit(solution)/shard_map/all_to_all | solution.py:55
Sparse Core Ops, SparseCore 0:
  10.2 220.9 all-gather.1
  248.8 71.3 all-reduce.1
where the time goes:
time: 344 us; the launch traced here: 343 us
  waiting for transfers between devices  220 us (64%)
  blocking collectives  60.7 us (18%)
  matrix products  18.8 us (5%)
  local copies, waits for them, and re-layouts  18.3 us (5%)
  between operations  14.3 us (4%)
  starting transfers between devices  6.87 us (2%)
  other arithmetic  4.02 us (1%)
    all_gather x1, waiting for transfers between devices, body(): lax.all_gather(w_qkv, 'mp', axis=0, tiled=True)  178 us
    all_gather x1, blocking collectives, combine_states(): old_full = lax.all_gather(state_in, 'mp', axis=2, tiled=True)  41.8 us
    psum x1, waiting for transfers between devices, combine_states(): lax.psum(kv_part.astype(jnp.bfloat16), 'mp').astype(jnp.float32)  40.5 us
    psum x1, blocking collectives, combine_states(): lax.psum(ks_part.astype(jnp.bfloat16), 'mp').astype(jnp.float32)  18.9 us
    dot_general x1, matrix products, project_rows(): return jnp.dot(flat_rows, shard_piece, preferred_element_type=jnp.float32)  8.77 us
  transfers between devices with their start and end apart: 4, of which 4 were waited for; matrix products, arithmetic and copies ran while one was open for 5% of the time, Pallas kernels for 0%

commit v1 on v0

v1 whole, which is shorter than its diff:
```python
import functools

import jax
import jax.numpy as jnp
from jax import lax
from jax.experimental import pallas as pl
from jax.experimental.pallas import tpu as pltpu
from jax.sharding import Mesh
from jax.sharding import PartitionSpec as P

F32 = jnp.float32
BF16 = jnp.bfloat16
LANES = 128
VMEM = pl.BlockSpec(memory_space=pltpu.VMEM)
SMEM = pl.BlockSpec(memory_space=pltpu.SMEM)
SWAP = [(0, 1), (1, 0)]


def phi(u):
    return jnp.where(u > 0.0, u + 1.0, jnp.exp(jnp.minimum(u, 0.0)))


def whole_call(kernel, out_shape, smem_first, count, flops, moved):
    specs = [SMEM] * smem_first + [VMEM] * (count - smem_first)
    return pl.pallas_call(
        kernel,
        out_shape=out_shape,
        in_specs=specs,
        out_specs=jax.tree.map(lambda _: VMEM, out_shape),
        cost_estimate=pl.CostEstimate(flops=flops, bytes_accessed=moved, transcendentals=0),
        compiler_params=pltpu.CompilerParams(vmem_limit_bytes=56 * 1024 * 1024),
    )


def kv_kernel(streams, heads, size, rows, acc_ref, live_ref, group_ref, plain_ref, *outs):
    q_ref, chunks = outs[0], outs[1:]
    width = heads * size
    tokens = acc_ref.shape[0] // streams
    q_ref[...] = acc_ref[:, 2 * width :].astype(BF16)
    keys = acc_ref[:, :width].astype(BF16).astype(F32)
    keyed = (phi(keys) * live_ref[:, :1]).astype(BF16)
    values = acc_ref[:, width : 2 * width].astype(BF16)
    grouped = jnp.dot(keyed, group_ref[...], preferred_element_type=F32).astype(BF16)
    plain = jnp.dot(keyed, plain_ref[...], preferred_element_type=F32)
    spread = jnp.dot(values, plain_ref[...], preferred_element_type=F32)
    lane = lax.broadcasted_iota(jnp.int32, spread.shape, 1) % LANES
    spread = jnp.where(lane == size, 1.0, spread).astype(BF16)
    row = lax.broadcasted_iota(jnp.int32, (LANES, LANES), 0) % rows
    for s in range(streams):
        span = slice(s * tokens, (s + 1) * tokens)
        sums = jnp.sum(plain[span], axis=0, keepdims=True)
        for h in range(heads):
            cols = slice(h * LANES, (h + 1) * LANES)
            outer = lax.dot_general(
                grouped[span, cols],
                spread[span, cols],
                (((0,), (0,)), ((), ())),
                preferred_element_type=F32,
            )
            outer = jnp.where(row == rows - 1, sums[:, cols], outer).astype(BF16)
            for r, chunk in enumerate(chunks):
                chunk[s * heads + h] = outer[r * rows : (r + 1) * rows]


def read_kernel(streams, heads, size, y_ref, own_ref, other_ref, live_ref, group_ref, *refs):
    pieces, out_ref = refs[:-1], refs[-1]
    tokens = own_ref.shape[0] // streams
    first = y_ref[0] == 0
    own, other = own_ref[...], other_ref[...]
    halves = (jnp.where(first, own, other), jnp.where(first, other, own))
    for half, raw in enumerate(halves):
        queried = phi(raw.astype(F32)).astype(BF16)
        grouped = jnp.dot(queried, group_ref[...], preferred_element_type=F32).astype(BF16)
        for s in range(streams):
            span = slice(s * tokens, (s + 1) * tokens)
            live = live_ref[span, :1]
            for h in range(heads):
                pair = s * 2 * heads + half * heads + h
                state = jnp.concatenate([piece[pair] for piece in pieces], axis=0)
                top = jnp.dot(
                    grouped[span, h * LANES : (h + 1) * LANES],
                    state,
                    preferred_element_type=F32,
                )
                result = top[:, :size] / top[:, size : size + 1] * live
                col = (half * heads + h) * size
                out_ref[span, col : col + size] = result.astype(BF16)


def pick_kernel(share, size, rows, place_ref, all_ref, state_ref, ksum_ref):
    for u in range(state_ref.shape[0]):
        block = all_ref[place_ref[u]].astype(F32)
        state_ref[u] = block[:share, :size]
        ksum_ref[u : u + 1] = block[rows - 1 :, :size]


def body(n, latents, w_qkv, state_in, ksum_in, frames_live, new_place):
    streams, frames, spatial, model = latents.shape
    heads_all, size = ksum_in.shape[1:]
    heads = heads_all // 2
    share = state_in.shape[2]
    members = size // share
    rows = LANES // members
    width = heads * size
    depth = w_qkv.shape[0]
    units = streams * heads_all
    o, y, c = lax.axis_index("o"), lax.axis_index("y"), lax.axis_index("c")
    z, x = lax.axis_index("z"), lax.axis_index("x")
    m = z * 2 + x
    owners = lax.axis_size("o") * 4
    me = (o * 2 + y) * 2 + c

    def flat(cc, zz, xx):
        return (cc * n + zz) * 2 + xx

    def swap(axis, v):
        return lax.ppermute(v, axis, SWAP)

    def hop(k, v):
        pairs = [(i, i + 1) for i in range(k - 1, n - 1)]
        pairs += [(n + i, n + i - 1) for i in range(n - k, 0, -1)]
        return lax.ppermute(v, ("c", "z"), pairs)

    def across(k, v):
        pairs = [(flat(0, i, a), flat(0, i, 1 - a)) for i in range(k, n) for a in range(2)]
        pairs += [(flat(1, i, a), flat(1, i, 1 - a)) for i in range(0, n - k) for a in range(2)]
        return lax.ppermute(v, ("c", "z", "x"), pairs)

    def xor(k, v):
        return lax.ppermute(v, ("z", "x"), [(i, i ^ k) for i in range(members)])

    wq, wk, wv = (w_qkv[:, j * 2 * width : (j + 1) * 2 * width] for j in range(3))
    low = jnp.concatenate([v[:, :width] for v in (wk, wv, wq)], axis=1)
    high = jnp.concatenate([v[:, width:] for v in (wk, wv, wq)], axis=1)
    mine = jnp.where(y == 0, low, high)
    half = -(-depth // 16) * 8
    piece = jnp.where(c == 0, mine[:half], mine[depth - half :])

    Z = [None] * n
    X = [None] * n
    with jax.named_scope("z1"):
        Z[1] = hop(1, mine)
    with jax.named_scope("x0"):
        X[0] = swap("x", piece)
    own_tokens = latents.reshape(-1, model)
    with jax.named_scope("tok"):
        other_tokens = swap("y", own_tokens)
    live_own = (
        lax.broadcasted_iota(jnp.int32, (streams, frames), 1) < frames_live[:, None]
    ).astype(F32)
    live_other = swap("y", live_own)
    live = jnp.concatenate([live_own, live_other], axis=0)
    live = jnp.repeat(live.reshape(-1, 1), spatial, axis=0)
    live = jnp.broadcast_to(live, (live.shape[0], LANES))

    tokens = jnp.concatenate([own_tokens, other_tokens], axis=0)
    blocks = tokens.reshape(tokens.shape[0], members, depth).transpose(1, 0, 2)

    for k in range(1, n):
        if k > 1:
            with jax.named_scope(f"z{k}"):
                Z[k] = hop(k, Z[k - 1])
        with jax.named_scope(f"x{k}"):
            X[k] = across(k, Z[k])

    def block(line, col):
        return lax.dynamic_index_in_dim(blocks, (line % n) * 2 + col, 0, keepdims=False)

    def mul(a, b):
        return jnp.dot(a, b, preferred_element_type=F32)

    acc = mul(block(z, x), mine)
    there = block(z, 1 - x)
    rest = jnp.where(
        lax.broadcasted_iota(jnp.int32, (1, half), 1) < 2 * half - depth, 0, there[:, depth - half :]
    )
    x0_other = swap("c", X[0])
    lead, tail = jnp.where(c == 0, X[0], x0_other), jnp.where(c == 0, x0_other, X[0])
    acc = acc + mul(there[:, :half], lead) + mul(rest, tail)
    for k in range(1, n):
        near, far = z - k + 2 * k * c, z + k - 2 * k * c
        acc = acc + mul(block(near, x), Z[k]) + mul(block(far, x), swap("c", Z[k]))
        acc = acc + mul(block(near, 1 - x), X[k]) + mul(block(far, 1 - x), swap("c", X[k]))

    src = lax.broadcasted_iota(jnp.int32, (width, heads * LANES), 0)
    dst = lax.broadcasted_iota(jnp.int32, (width, heads * LANES), 1)
    same = (src // size) == (dst // LANES)
    spot, lane = src % size, dst % LANES
    plain = (same & (spot == lane)).astype(BF16)
    group = (
        same & (lane % rows < share) & (spot == ((lane // rows) ^ m) * share + lane % rows)
    ).astype(BF16)

    pairs = 2 * streams * heads
    chunk = jax.ShapeDtypeStruct((pairs, rows, LANES), BF16)
    q, *parts = whole_call(
        functools.partial(kv_kernel, 2 * streams, heads, size, rows),
        [jax.ShapeDtypeStruct((acc.shape[0], width), BF16)] + [chunk] * members,
        0,
        4,
        2_000_000_000,
        8_000_000,
    )(acc, live, group, plain)

    count = own_tokens.shape[0]
    with jax.named_scope("qy"):
        q_other = swap("y", q[count:])
    total = parts[0].astype(F32)
    for k in range(members - 1, 0, -1):
        with jax.named_scope(f"rs{k}"):
            total = total + xor(k, parts[k]).astype(F32)
    keep, give = total[: pairs // 2], total[pairs // 2 :]
    with jax.named_scope("sy"):
        got = swap("y", give.astype(BF16)).astype(F32)
    keep = keep.reshape(streams, 1, heads, rows, LANES)
    got = got.reshape(streams, 1, heads, rows, LANES)
    joined = jnp.where(
        y == 0, jnp.concatenate([keep, got], axis=1), jnp.concatenate([got, keep], axis=1)
    ).reshape(units, rows, LANES)

    old = state_in.reshape(units, share, size)
    ks = ksum_in.reshape(units, size)
    ks_rows = lax.dynamic_slice_in_dim(ks, m * share, share, 1)[:, :, None]
    old = jnp.concatenate(
        [old, ks_rows, jnp.zeros((units, share, LANES - size - 1), F32)], axis=2
    )
    ks_line = jnp.pad(ks, ((0, 0), (0, LANES - size)))[:, None]
    fill = jnp.zeros((units, rows - 1 - share, LANES), F32)
    old = jnp.concatenate([old, fill, ks_line], axis=1)
    new = (joined + old).astype(BF16)

    gathered = [new]
    for k in range(1, members):
        with jax.named_scope(f"ag{k}"):
            gathered.append(xor(k, new))

    every = new[None]
    bit = 1
    while bit < owners:
        step = [(i, i ^ bit) for i in range(owners)]
        with jax.named_scope(f"mv{bit}"):
            every = jnp.concatenate([every, lax.ppermute(every, ("o", "y", "c"), step)], axis=0)
        bit *= 2
    every = every.reshape(owners * units, rows, LANES)
    inverse = (
        jnp.zeros((owners * units,), jnp.int32)
        .at[new_place]
        .set(jnp.arange(owners * units, dtype=jnp.int32))
    )
    arrivals = lax.dynamic_slice_in_dim(inverse, me * units, units)
    place = ((arrivals // units) ^ me) * units + arrivals % units
    moved_state, moved_ksum = whole_call(
        functools.partial(pick_kernel, share, size, rows),
        [
            jax.ShapeDtypeStruct((units, share, size), F32),
            jax.ShapeDtypeStruct((units, size), F32),
        ],
        1,
        2,
        1_000_000,
        800_000,
    )(place, every)

    attended = whole_call(
        functools.partial(read_kernel, streams, heads, size),
        jax.ShapeDtypeStruct((count, 2 * width), BF16),
        1,
        5 + members,
        1_500_000_000,
        3_000_000,
    )(y.reshape(1).astype(jnp.int32), q[:count], q_other, live[:count], group, *gathered)
    return (
        attended.reshape(streams, frames, spatial, 2 * width),
        moved_state,
        moved_ksum,
    )


def solution(mesh):
    owners, members = mesh.shape["req"], mesh.shape["mp"]
    split = Mesh(
        mesh.devices.reshape(owners // 4, 2, 2, members // 2, 2), ("o", "y", "c", "z", "x")
    )
    req, mp = ("o", "y", "c"), ("z", "x")
    return jax.shard_map(
        functools.partial(body, members // 2),
        mesh=split,
        in_specs=(
            P(req, None, mp, None),
            P(mp, None),
            P(req, None, mp, None),
            P(req, None, None),
            P(req),
            P(),
        ),
        out_specs=(P(req, None, mp, None), P(req, mp, None), P(req, None)),
        check_vma=False,
    )
```

time: 344 us -> 202 us (0.59)
  waiting for transfers between devices: 220 us -> 9.93 us
  starting transfers between devices: 6.87 us -> 67.6 us
  blocking collectives: 60.7 us -> 0 us
  local copies, waits for them, and re-layouts: 18.3 us -> 67.8 us
  between operations: 14.3 us -> 1.37 us
  other arithmetic: 4.02 us -> 15.3 us
  Pallas kernels: 0 us -> 10.2 us
  matrix products: 18.8 us -> 26.8 us
    all_gather x1 -> x0, waiting for transfers between devices: 178 us -> none  [body(): lax.all_gather(w_qkv, 'mp', axis=0, tiled=True)]
    ppermute x0 -> x34, starting transfers between devices: none -> 67.6 us  [the longest x12 31.1 us: swap(): return lax.ppermute(v, axis, SWAP)]
    another operation x0 -> x15, local copies, waits for them, and re-layouts: none -> 46.2 us
    all_gather x1 -> x0, blocking collectives: 41.8 us -> none  [combine_states(): old_full = lax.all_gather(state_in, 'mp', axis=2, tiled=True)]
    psum x1 -> x0, waiting for transfers between devices: 40.5 us -> none  [combine_states(): lax.psum(kv_part.astype(jnp.bfloat16), 'mp').astype(jnp.float32)]
    psum x1 -> x0, blocking collectives: 18.9 us -> none  [combine_states(): lax.psum(ks_part.astype(jnp.bfloat16), 'mp').astype(jnp.float32)]
    pallas_call x0 -> x3, Pallas kernels: none -> 10.2 us  [the longest x1 5.19 us: body(): whole_call(functools.partial(kv_kernel, 2 * streams, heads, size, rows),...]
    ppermute x0 -> x34, waiting for transfers between devices: none -> 9.93 us  [the longest x14 9.72 us: xor(): return lax.ppermute(v, ('z', 'x'), [(i, i ^ k) for i in range(members)])]
  transfers between devices with their start and end apart: 4 -> 34, of which waited for: 4 -> 6; matrix products, arithmetic and copies ran while one was open for 5% -> 53% of each run, Pallas kernels for 0% -> 2%
where the time goes in v1:
time: 202 us; the launch traced here: 199 us
  local copies, waits for them, and re-layouts  67.8 us (34%)
  starting transfers between devices  67.6 us (33%)
  matrix products  26.8 us (13%)
  other arithmetic  15.3 us (8%)
  Pallas kernels  10.2 us (5%)
  waiting for transfers between devices  9.93 us (5%)
    another operation x15, local copies, waits for them, and re-layouts  46.2 us
    ppermute x12, starting transfers between devices, swap(): return lax.ppermute(v, axis, SWAP)  31.1 us
    dot_general x15, matrix products, mul(): return jnp.dot(a, b, preferred_element_type=F32)  26.8 us
    ppermute x14, starting transfers between devices, xor(): return lax.ppermute(v, ('z', 'x'), [(i, i ^ k) for i in range(members)])  24.1 us
    ppermute x14, waiting for transfers between devices, xor(): return lax.ppermute(v, ('z', 'x'), [(i, i ^ k) for i in range(members)])  9.72 us
    ppermute x3, starting transfers between devices, hop(): return lax.ppermute(v, ('c', 'z'), pairs)  7.01 us
    concatenate x3, local copies, waits for them, and re-layouts, body(): tokens = jnp.concatenate([own_tokens, other_tokens], axis=0)  5.41 us
    pallas_call x1, Pallas kernels, body(): whole_call(functools.partial(kv_kernel, 2 * streams, heads, size, rows),...  5.19 us
  transfers between devices with their start and end apart: 34, of which 6 were waited for; matrix products, arithmetic and copies ran while one was open for 53% of the time, Pallas kernels for 2%

profile of v1, /device:TPU:0, one launch (start us, length us, event | category | flops | bytes accessed | tf_op | source)
XLA Modules:
  0.0 199.0 jit_solution(17639259525670437315)
XLA Ops:
  0.6 3.1 %collective-permute-start = (bf16[192,2240]{1,0:T(8,128)(2,1)}, bf16[192,2240]{1,0:T(8,128)(2,1)}, u32[]{:S(2)}, u32[]{:S(2)}) collective-permute-start(bf16[192,2240]{1,0:T(8,128)(2,1)} %bitcast.87), channel_id=1, source_target_pairs={{0,16},{16,0},{1,17},{17,1},{2,18},{18,2},{3,19},{19,3},{4,20},{20... | collective-permute-start | bytes 2580488 | tf_op jit(solution)/shard_map/tok/ppermute | solution.py:117
  3.7 2.5 %fusion.60 = (bf16[280,560]{1,0:T(8,128)(2,1)S(1)}, bf16[280,560]{1,0:T(8,128)(2,1)S(1)}, bf16[280,560]{1,0:T(8,128)(2,1)S(1)}, bf16[280,560]{1,0:T(8,128)(2,1)S...) fusion(bf16[280,3360]{1,0:T(8,128)(2,1)} %param.7), kind=kLoop, calls=%fused_computation.123 | loop fusion | bytes 3763200 | tf_op jit(solution)/shard_map/slice | solution.py:134
  10.1 4.5 %collective-permute-start.3 = (bf16[280,1680]{1,0:T(8,128)(2,1)}, bf16[280,1680]{1,0:T(8,128)(2,1)}, u32[]{:S(2)}, u32[]{:S(2)}) collective-permute-start(bf16[280,1680]{1,0:T(8,128)(2,1)} %broadcast_select_fusion), channel_id=1, source_target_pairs={{0,2},{2,4},{4,6},{14,12},{12,10},{10,8},{1,3},{3,5},{5,7},{15,13}... | collective-permute-start | bytes 2822408 | tf_op jit(solution)/shard_map/z1/ppermute | solution.py:122
  14.6 2.0 %slice_select_fusion = bf16[144,1680]{1,0:T(8,128)(2,1)} fusion(bf16[280,1680]{1,0:T(8,128)(2,1)} %broadcast_select_fusion, pred[]{:T(512)S(6)} %eq.43), kind=kLoop, calls=%fused_computation.35 | loop fusion | flops 241920 | bytes 1451521 | tf_op jit(solution)/shard_map/jit(_where)/select_n | solution.py:137
  19.3 2.6 %concatenate.49 = bf16[192,8,280]{2,1,0:T(8,128)(2,1)S(1)} reshape(bf16[2,4,24,2240]{3,2,1,0:T(8,128)(2,1)} %param.6) | data formatting | bytes 1720320 | tf_op jit(solution)/shard_map/concatenate | solution.py:156
  30.0 2.7 %fusion.13 = (bf16[560,640]{1,0:T(8,128)(2,1)}, bf16[560,640]{1,0:T(8,128)(2,1)}) fusion(s32[560]{0:T(1024)} %get-tuple-element.58, s32[560]{0:T(1024)} %get-tuple-element.59, s32[640]{0:T(1024)} %get-tuple-element.56, s32[640]{0:T(1024)} %get-tuple-element.61, s32[640]{0:T(1024)S(1)} %get-tuple-element.55, s32[640]{0:T(1024)} %get-tuple-element.62, ...), kind=kLoop, calls=%fused_computation.32 | loop fusion | flops 12544000 | bytes 1455204 | tf_op jit(solution)/shard_map/convert_element_type | solution.py:189
  33.7 2.6 %concatenate.50 = bf16[192,8,280]{2,1,0:T(8,128)(2,1)S(1)} reshape(bf16[192,2240]{1,0:T(8,128)(2,1)} %collective-permute-done) | data formatting | bytes 1720320 | tf_op jit(solution)/shard_map/concatenate | solution.py:156
  36.5 10.0 %constant_dynamic-slice_fusion = (bf16[384,1,280]{2,1,0:T(2,128)(2,1)S(1)}, bf16[384,1,280]{2,1,0:T(2,128)(2,1)}, bf16[384,1,280]{2,1,0:T(2,128)(2,1)}, bf16[384...) fusion(bf16[384,8,280]{2,1,0:T(8,128)(2,1)S(1)} %constant_dynam, ...), kind=kLoop, calls=%fused_computation.96 | loop fusion | bytes 6021176 | tf_op jit(solution)/shard_map/dynamic-slice.13
  46.5 2.1 %copy.69 = bf16[384,1,280]{0,2,1:T(8,128)(2,1)S(1)} copy(bf16[384,1,280]{2,1,0:T(2,128)(2,1)} %get-tuple-element.38) | data formatting | bytes 430080 | tf_op jit(solution)/shard_map/dynamic-slice
  48.7 2.2 %fusion.37 = f32[384,1680]{0,1:T(8,128)S(1)} fusion(bf16[280,1680]{1,0:T(8,128)(2,1)} %broadcast_select_fusion, bf16[384,1,280]{0,2,1:T(8,128)(2,1)S(1)} %copy.69), kind=kOutput, calls=%fused_computation.60 | convolution fusion | flops 361267200 | bytes 3736320 | tf_op jit(solution)/shard_map/dot_general | solution.py:170
  50.9 2.1 %copy.70 = bf16[384,1,280]{0,2,1:T(8,128)(2,1)S(1)} copy(bf16[384,1,280]{2,1,0:T(2,128)(2,1)} %get-tuple-element.37) | data formatting | bytes 430080 | tf_op jit(solution)/shard_map/dynamic-slice.1
  53.0 2.8 %copy.77 = bf16[384,1,280]{0,2,1:T(8,128)(2,1)} copy(bf16[384,1,280]{2,1,0:T(2,128)(2,1)} %get-tuple-element.34) | data formatting | bytes 430080 | tf_op jit(solution)/shard_map/dynamic-slice.4
  55.8 2.8 %copy.73 = bf16[384,1,280]{0,2,1:T(8,128)(2,1)} copy(bf16[384,1,280]{2,1,0:T(2,128)(2,1)} %get-tuple-element.36) | data formatting | bytes 430080 | tf_op jit(solution)/shard_map/dynamic-slice.2
  58.6 2.8 %copy.75 = bf16[384,1,280]{0,2,1:T(8,128)(2,1)} copy(bf16[384,1,280]{2,1,0:T(2,128)(2,1)} %get-tuple-element.35) | data formatting | bytes 430080 | tf_op jit(solution)/shard_map/dynamic-slice.3
  61.3 2.7 %copy.81 = bf16[384,1,280]{0,2,1:T(8,128)(2,1)} copy(bf16[384,1,280]{2,1,0:T(2,128)(2,1)} %get-tuple-element.32) | data formatting | bytes 430080 | tf_op jit(solution)/shard_map/dynamic-slice.6
  64.0 2.8 %copy.79 = bf16[384,1,280]{0,2,1:T(8,128)(2,1)} copy(bf16[384,1,280]{2,1,0:T(2,128)(2,1)} %get-tuple-element.33) | data formatting | bytes 430080 | tf_op jit(solution)/shard_map/dynamic-slice.5
  66.8 2.8 %copy.85 = bf16[384,1,280]{0,2,1:T(8,128)(2,1)} copy(bf16[384,1,280]{2,1,0:T(2,128)(2,1)} %get-tuple-element.30) | data formatting | bytes 430080 | tf_op jit(solution)/shard_map/dynamic-slice.8
  69.6 2.8 %copy.83 = bf16[384,1,280]{0,2,1:T(8,128)(2,1)} copy(bf16[384,1,280]{2,1,0:T(2,128)(2,1)} %get-tuple-element.31) | data formatting | bytes 430080 | tf_op jit(solution)/shard_map/dynamic-slice.7
  72.3 2.8 %copy.89 = bf16[384,1,280]{0,2,1:T(8,128)(2,1)} copy(bf16[384,1,280]{2,1,0:T(2,128)(2,1)} %get-tuple-element.28) | data formatting | bytes 430080 | tf_op jit(solution)/shard_map/dynamic-slice.10
  75.1 2.8 %copy.87 = bf16[384,1,280]{0,2,1:T(8,128)(2,1)} copy(bf16[384,1,280]{2,1,0:T(2,128)(2,1)} %get-tuple-element.29) | data formatting | bytes 430080 | tf_op jit(solution)/shard_map/dynamic-slice.9
  77.9 2.8 %copy.93 = bf16[384,1,280]{0,2,1:T(8,128)(2,1)} copy(bf16[384,1,280]{2,1,0:T(2,128)(2,1)} %get-tuple-element.26) | data formatting | bytes 430080 | tf_op jit(solution)/shard_map/dynamic-slice.12
  80.6 2.8 %copy.91 = bf16[384,1,280]{0,2,1:T(8,128)(2,1)} copy(bf16[384,1,280]{2,1,0:T(2,128)(2,1)} %get-tuple-element.27) | data formatting | bytes 430080 | tf_op jit(solution)/shard_map/dynamic-slice.11
  85.0 1.7 collective-permute-start.5
  87.7 1.8 collective-permute-start.7
  89.6 3.8 %fusion.35 = f32[384,1680]{1,0:T(8,128)} fusion(bf16[280,1680]{1,0:T(8,128)(2,1)} %collective-permute-done.3, bf16[384,1,280]{0,2,1:T(8,128)(2,1)} %copy.73), kind=kOutput, calls=%fused_computation.58 | convolution fusion | flops 361267200 | bytes 3736320 | tf_op jit(solution)/shard_map/dot_general | solution.py:170
  93.3 3.2 %convolution_add_fusion = f32[384,1680]{0,1:T(8,128)} fusion(f32[384,1680]{0,1:T(8,128)S(1)} %fusion.37, bf16[144,1680]{1,0:T(8,128)(2,1)} %collective-permute-done.1, bf16[144,1680]{1,0:T(8,128)(2,1)} %collective-permute-done.2, pred[]{:T(512)S(6)} %eq.43, bf16[384,280]{0,1:T(8,128)(2,1)S(1)} %bitcast.85), kind=kOutput, calls=%fused_computation.6 | convolution fusion | flops 186681600 | bytes 6239233 | tf_op jit(solution)/shard_map/dot_general | solution.py:170
  96.5 2.2 %copy.71 = f32[384,1680]{1,0:T(8,128)S(1)} copy(f32[384,1680]{0,1:T(8,128)} %convolution_add_fusion) | data formatting | bytes 5160960 | tf_op jit(solution)/shard_map/add | solution.py:179
  98.8 1.7 fusion.14
  101.4 5.0 %collective-permute-start.8 = (bf16[280,1680]{1,0:T(8,128)(2,1)}, bf16[280,1680]{1,0:T(8,128)(2,1)S(1)}, u32[]{:S(2)}, u32[]{:S(2)}) collective-permute-start(bf16[280,1680]{1,0:T(8,128)(2,1)} %collective-permute-done.7), channel_id=1, source_target_pairs={{0,8},{8,0},{1,9},{9,1},{2,10},{10,2},{3,11},{11,3},{4,12},{12,4},... | collective-permute-start | bytes 2822408 | tf_op jit(solution)/shard_map/ppermute | solution.py:117
  107.9 2.1 %fusion.32 = f32[384,1680]{1,0:T(8,128)S(1)} fusion(bf16[280,1680]{1,0:T(8,128)(2,1)} %collective-permute-done.5, bf16[384,1,280]{0,2,1:T(8,128)(2,1)S(1)} %copy-done.12), kind=kOutput, calls=%fused_computation.55 | convolution fusion | flops 361267200 | bytes 3736320 | tf_op jit(solution)/shard_map/dot_general | solution.py:170
  110.0 2.6 %fusion = f32[384,1680]{1,0:T(8,128)S(1)} fusion(f32[384,1680]{1,0:T(8,128)S(1)} %fusion.32, bf16[280,1680]{1,0:T(8,128)(2,1)} %collective-permute-done.4, f32[384,1680]{1,0:T(8,128)S(1)} %copy-done, f32[384,1680]{1,0:T(8,128)S(1)} %copy.71, f32[384,1680]{1,0:T(8,128)S(1)} %fusion.14, bf16[384,1,280]{0,2,1:T(8,128)(2,1)S(1)} %copy-done.13), kind=kOutput, calls=%fused_computation.13 | convolution fusion | flops 363847680 | bytes 14058240 | tf_op jit(solution)/shard_map/dot_general | solution.py:170
  112.6 2.2 %fusion.29 = f32[384,1680]{1,0:T(8,128)S(1)} fusion(bf16[280,1680]{1,0:T(8,128)(2,1)} %collective-permute-done.7, bf16[384,1,280]{0,2,1:T(8,128)(2,1)S(1)} %copy-done.11), kind=kOutput, calls=%fused_computation.52 | convolution fusion | flops 361267200 | bytes 3736320 | tf_op jit(solution)/shard_map/dot_general | solution.py:170
  115.7 8.3 %collective-permute-start.12 = (bf16[280,1680]{1,0:T(8,128)(2,1)S(1)}, bf16[280,1680]{1,0:T(8,128)(2,1)S(1)}, u32[]{:S(2)}, u32[]{:S(2)}) collective-permute-start(bf16[280,1680]{1,0:T(8,128)(2,1)S(1)} %collective-permute-done.11), channel_id=1, source_target_pairs={{0,8},{8,0},{1,9},{9,1},{2,10},{10,2},{3,11},{11,3},{4,12},{12,4},... | collective-permute-start | bytes 2822408 | tf_op jit(solution)/shard_map/ppermute | solution.py:117
  128.0 8.8 %collective-permute-start.14 = (bf16[280,1680]{1,0:T(8,128)(2,1)S(1)}, bf16[280,1680]{1,0:T(8,128)(2,1)S(1)}, u32[]{:S(2)}, u32[]{:S(2)}) collective-permute-start(bf16[280,1680]{1,0:T(8,128)(2,1)S(1)} %collective-permute-done.13), channel_id=1, source_target_pairs={{0,8},{8,0},{1,9},{9,1},{2,10},{10,2},{3,11},{11,3},{4,12},{12,4},... | collective-permute-start | bytes 2822408 | tf_op jit(solution)/shard_map/ppermute | solution.py:117
  139.7 2.5 %convolution_add_fusion.1.acc_ref = f32[384,1680]{1,0:T(8,128)} fusion(f32[384,1680]{1,0:T(8,128)S(1)} %fusion.4, bf16[280,1680]{1,0:T(8,128)(2,1)S(1)} %collective-permute-done.14, bf16[384,1,280]{0,2,1:T(8,128)(2,1)S(1)} %copy-done.7), kind=kOutput, calls=%fused_computation.7 | convolution fusion | flops 361912320 | bytes 6316800 | tf_op jit(solution)/shard_map/dot_general | solution.py:170
  142.9 5.2 %shard_map.85 = (bf16[384,560]{1,0:T(8,128)(2,1)}, bf16[20,16,128]{2,1,0:T(8,128)(2,1)}, bf16[20,16,128]{2,1,0:T(8,128)(2,1)}, bf16[20,16,128]{2,1,0:T(8,128)(2,...) custom-call(f32[384,1680]{1,0:T(8,128)} %convolution_add_fusion.1.ac, ...), custom_call_target="tpu_custom_call" | custom-call | flops 2000000000 | bytes 8000000 | tf_op jit(solution)/shard_map/pallas_call | solution.py:196
  148.1 4.8 %collective-permute-start.17 = (bf16[20,16,128]{2,1,0:T(8,128)(2,1)}, bf16[20,16,128]{2,1,0:T(8,128)(2,1)S(1)}, u32[]{:S(2)}, u32[]{:S(2)}) collective-permute-start(bf16[20,16,128]{2,1,0:T(8,128)(2,1)} %get-tuple-element.16), channel_id=1, source_target_pairs={{0,7},{1,6},{2,5},{3,4},{4,3},{5,2},{6,1},{7,0},{8,15},{9,14},{10,... | collective-permute-start | bytes 245768 | tf_op jit(solution)/shard_map/rs7/ppermute | solution.py:130
  154.4 3.7 %collective-permute-start.20 = (bf16[20,16,128]{2,1,0:T(8,128)(2,1)}, bf16[20,16,128]{2,1,0:T(8,128)(2,1)S(1)}, u32[]{:S(2)}, u32[]{:S(2)}) collective-permute-start(bf16[20,16,128]{2,1,0:T(8,128)(2,1)} %get-tuple-element.19), channel_id=1, source_target_pairs={{0,4},{1,5},{2,6},{3,7},{4,0},{5,1},{6,2},{7,3},{8,12},{9,13},{10,... | collective-permute-start | bytes 245768 | tf_op jit(solution)/shard_map/rs4/ppermute | solution.py:130
  161.8 3.9 %collective-permute-done.19 = bf16[20,16,128]{2,1,0:T(8,128)(2,1)S(1)} collective-permute-done((bf16[20,16,128]{2,1,0:T(8,128)(2,1)}, bf16[20,16,128]{2,1,0:T(8,128)(2,1)S(1)}, u32[]{:S(2)}, u32[]{:S(2)}) %collective-permute-start.19) | collective-permute-done | bytes 81952 | tf_op jit(solution)/shard_map/rs5/ppermute | solution.py:130
  170.3 1.8 fusion.61
  174.8 2.0 %collective-permute-start.27 = (bf16[20,16,128]{2,1,0:T(8,128)(2,1)S(1)}, bf16[20,16,128]{2,1,0:T(8,128)(2,1)S(1)}, u32[]{:S(2)}, u32[]{:S(2)}) collective-permute-start(bf16[20,16,128]{2,1,0:T(8,128)(2,1)S(1)} %fusion.39.refs_0_), channel_id=1, source_target_pairs={{0,3},{1,2},{2,1},{3,0},{4,7},{5,6},{6,5},{7,4},{8,11},{9,10},{10,... | collective-permute-start | bytes 245768 | tf_op jit(solution)/shard_map/ag3/ppermute | solution.py:130
  176.8 1.9 collective-permute-start.28
  178.7 2.0 %collective-permute-start.29 = (bf16[20,16,128]{2,1,0:T(8,128)(2,1)S(1)}, bf16[20,16,128]{2,1,0:T(8,128)(2,1)S(1)}, u32[]{:S(2)}, u32[]{:S(2)}) collective-permute-start(bf16[20,16,128]{2,1,0:T(8,128)(2,1)S(1)} %fusion.39.refs_0_), channel_id=1, source_target_pairs={{0,5},{1,4},{2,7},{3,6},{4,1},{5,0},{6,3},{7,2},{8,13},{9,12},{10,... | collective-permute-start | bytes 245768 | tf_op jit(solution)/shard_map/ag5/ppermute | solution.py:130
  180.9 3.1 %collective-permute-start.30 = (bf16[20,16,128]{2,1,0:T(8,128)(2,1)S(1)}, bf16[20,16,128]{2,1,0:T(8,128)(2,1)S(1)}, u32[]{:S(2)}, u32[]{:S(2)}) collective-permute-start(bf16[20,16,128]{2,1,0:T(8,128)(2,1)S(1)} %fusion.39.refs_0_), channel_id=1, source_target_pairs={{0,6},{1,7},{2,4},{3,5},{4,2},{5,3},{6,0},{7,1},{8,14},{9,15},{10,... | collective-permute-start | bytes 245768 | tf_op jit(solution)/shard_map/ag6/ppermute | solution.py:130
  185.4 1.9 collective-permute-start.33
  188.8 3.5 %collective-permute-done.29.refs_5_ = bf16[20,16,128]{2,1,0:T(8,128)(2,1)S(1)} collective-permute-done((bf16[20,16,128]{2,1,0:T(8,128)(2,1)S(1)}, bf16[20,16,128]{2,1,0:T(8,128)(2,1)S(1)}, u32[]{:S(2)}, u32[]{:S(2)}) %collective-permute-start.29) | collective-permute-done | bytes 81952 | tf_op jit(solution)/shard_map/ag5/ppermute | solution.py:130
  193.2 3.4 %shard_map.86 = bf16[192,1120]{1,0:T(8,128)(2,1)} custom-call(s32[1]{0:T(128)} %bitcast.y_ref, bf16[192,560]{1,0:T(8,128)(2,1)} %get-tuple-element.46.own_ref, bf16[192,560]{1,0:T(8,128)(2,1)} %copy-done.17, f32[192,128]{1,0:T(8,128)} %broadcast_in_dim.51.live_ref, bf16[560,640]{1,0:T(8,128)(2,1)} %get-tuple-element.48.group_ref, ...), custom_call_target="tpu_custom_call" | custom-call | flops 1500000000 | bytes 3000000 | tf_op jit(solution)/shard_map/pallas_call | solution.py:264
  197.3 1.7 shard_map.87
  (158 shorter events, 46.1 us)
Async XLA Ops:
  0.6 33.1 %collective-permute-start = (bf16[192,2240]{1,0:T(8,128)(2,1)}, bf16[192,2240]{1,0:T(8,128)(2,1)}, u32[]{:S(2)}, u32[]{:S(2)}) collective-permute-start(bf16[192,2240]{1,0:T(8,128)(2,1)} %bitcast.87), channel_id=1, source_target_pairs={{0,16},{16,0},{1,17},{17,1},{2,18},{18,2},{3,19},{19,3},{4,20},{20... | collective-permute-start | bytes 2580488 | tf_op jit(solution)/shard_map/tok/ppermute | solution.py:117
  9.0 9.1 %copy-start.25 = (s32[2]{0:T(128)S(1)}, s32[2]{0:T(128)}, u32[]{:S(2)}) copy-start(s32[2]{0:T(128)} %param.10) | copy-start | bytes 28
  10.1 74.9 %collective-permute-start.3 = (bf16[280,1680]{1,0:T(8,128)(2,1)}, bf16[280,1680]{1,0:T(8,128)(2,1)}, u32[]{:S(2)}, u32[]{:S(2)}) collective-permute-start(bf16[280,1680]{1,0:T(8,128)(2,1)} %broadcast_select_fusion), channel_id=1, source_target_pairs={{0,2},{2,4},{4,6},{14,12},{12,10},{10,8},{1,3},{3,5},{5,7},{15,13}... | collective-permute-start | bytes 2822408 | tf_op jit(solution)/shard_map/z1/ppermute | solution.py:122
  16.6 17.0 %collective-permute-start.1 = (bf16[144,1680]{1,0:T(8,128)(2,1)}, bf16[144,1680]{1,0:T(8,128)(2,1)}, u32[]{:S(2)}, u32[]{:S(2)}) collective-permute-start(bf16[144,1680]{1,0:T(8,128)(2,1)} %slice_select_fusion), channel_id=1, source_target_pairs={{0,1},{1,0},{2,3},{3,2},{4,5},{5,4},{6,7},{7,6},{8,9},{9,8},{10,11... | collective-permute-start | bytes 1451528 | tf_op jit(solution)/shard_map/x0/ppermute | solution.py:117
  18.8 13.9 %collective-permute-start.15 = (f32[2,4]{1,0:T(2,128)}, f32[2,4]{1,0:T(2,128)}, u32[]{:S(2)}, u32[]{:S(2)}) collective-permute-start(f32[2,4]{1,0:T(2,128)} %compare_convert_fusion), channel_id=1, source_target_pairs={{0,16},{16,0},{1,17},{17,1},{2,18},{18,2},{3,19},{19,3},{4,20},{20... | collective-permute-start | bytes 104 | tf_op jit(solution)/shard_map/ppermute | solution.py:117
  33.6 59.7 %collective-permute-start.2 = (bf16[144,1680]{1,0:T(8,128)(2,1)}, bf16[144,1680]{1,0:T(8,128)(2,1)}, u32[]{:S(2)}, u32[]{:S(2)}) collective-permute-start(bf16[144,1680]{1,0:T(8,128)(2,1)} %collective-permute-done.1), channel_id=1, source_target_pairs={{0,8},{8,0},{1,9},{9,1},{2,10},{10,2},{3,11},{11,3},{4,12},{12,4},... | collective-permute-start | bytes 1451528 | tf_op jit(solution)/shard_map/ppermute | solution.py:117
  85.0 22.2 %collective-permute-start.5 = (bf16[280,1680]{1,0:T(8,128)(2,1)}, bf16[280,1680]{1,0:T(8,128)(2,1)}, u32[]{:S(2)}, u32[]{:S(2)}) collective-permute-start(bf16[280,1680]{1,0:T(8,128)(2,1)} %collective-permute-done.3), channel_id=1, source_target_pairs={{2,3},{3,2},{4,5},{5,4},{6,7},{7,6},{8,9},{9,8},{10,11},{11,10},{1... | collective-permute-start | bytes 2822408 | tf_op jit(solution)/shard_map/x1/ppermute | solution.py:127
  86.7 23.3 %collective-permute-start.4 = (bf16[280,1680]{1,0:T(8,128)(2,1)}, bf16[280,1680]{1,0:T(8,128)(2,1)}, u32[]{:S(2)}, u32[]{:S(2)}) collective-permute-start(bf16[280,1680]{1,0:T(8,128)(2,1)} %collective-permute-done.3), channel_id=1, source_target_pairs={{0,8},{8,0},{1,9},{9,1},{2,10},{10,2},{3,11},{11,3},{4,12},{12,4},... | collective-permute-start | bytes 2822408 | tf_op jit(solution)/shard_map/ppermute | solution.py:117
  87.7 12.8 %collective-permute-start.7 = (bf16[280,1680]{1,0:T(8,128)(2,1)}, bf16[280,1680]{1,0:T(8,128)(2,1)}, u32[]{:S(2)}, u32[]{:S(2)}) collective-permute-start(bf16[280,1680]{1,0:T(8,128)(2,1)} %collective-permute-done.3), channel_id=1, source_target_pairs={{2,4},{4,6},{12,10},{10,8},{3,5},{5,7},{13,11},{11,9},{18,20},{20,... | collective-permute-start | bytes 2822408 | tf_op jit(solution)/shard_map/z2/ppermute | solution.py:122
  98.8 9.1 %copy-start.12 = (bf16[384,1,280]{0,2,1:T(8,128)(2,1)S(1)}, bf16[384,1,280]{0,2,1:T(8,128)(2,1)}, u32[]{:S(2)}) copy-start(bf16[384,1,280]{0,2,1:T(8,128)(2,1)} %copy.77) | copy-start | bytes 645124
  100.5 9.5 %copy-start = (f32[384,1680]{1,0:T(8,128)S(1)}, f32[384,1680]{1,0:T(8,128)}, u32[]{:S(2)}) copy-start(f32[384,1680]{1,0:T(8,128)} %fusion.35) | copy-start | bytes 7741444
  100.6 9.5 %copy-start.13 = (bf16[384,1,280]{0,2,1:T(8,128)(2,1)S(1)}, bf16[384,1,280]{0,2,1:T(8,128)(2,1)}, u32[]{:S(2)}) copy-start(bf16[384,1,280]{0,2,1:T(8,128)(2,1)} %copy.75) | copy-start | bytes 645124
  100.6 23.4 %collective-permute-start.9 = (bf16[280,1680]{1,0:T(8,128)(2,1)}, bf16[280,1680]{1,0:T(8,128)(2,1)S(1)}, u32[]{:S(2)}, u32[]{:S(2)}) collective-permute-start(bf16[280,1680]{1,0:T(8,128)(2,1)} %collective-permute-done.7), channel_id=1, source_target_pairs={{4,5},{5,4},{6,7},{7,6},{8,9},{9,8},{10,11},{11,10},{20,21},{21,20... | collective-permute-start | bytes 2822408 | tf_op jit(solution)/shard_map/x2/ppermute | solution.py:127
  101.4 24.6 %collective-permute-start.8 = (bf16[280,1680]{1,0:T(8,128)(2,1)}, bf16[280,1680]{1,0:T(8,128)(2,1)S(1)}, u32[]{:S(2)}, u32[]{:S(2)}) collective-permute-start(bf16[280,1680]{1,0:T(8,128)(2,1)} %collective-permute-done.7), channel_id=1, source_target_pairs={{0,8},{8,0},{1,9},{9,1},{2,10},{10,2},{3,11},{11,3},{4,12},{12,4},... | collective-permute-start | bytes 2822408 | tf_op jit(solution)/shard_map/ppermute | solution.py:117
  106.5 8.3 %collective-permute-start.11 = (bf16[280,1680]{1,0:T(8,128)(2,1)}, bf16[280,1680]{1,0:T(8,128)(2,1)S(1)}, u32[]{:S(2)}, u32[]{:S(2)}) collective-permute-start(bf16[280,1680]{1,0:T(8,128)(2,1)} %collective-permute-done.7), channel_id=1, source_target_pairs={{4,6},{10,8},{5,7},{11,9},{20,22},{26,24},{21,23},{27,25}} | collective-permute-start | bytes 2822408 | tf_op jit(solution)/shard_map/z3/ppermute | solution.py:122
  107.2 16.9 %collective-permute-start.6 = (bf16[280,1680]{1,0:T(8,128)(2,1)}, bf16[280,1680]{1,0:T(8,128)(2,1)S(1)}, u32[]{:S(2)}, u32[]{:S(2)}) collective-permute-start(bf16[280,1680]{1,0:T(8,128)(2,1)} %collective-permute-done.5), channel_id=1, source_target_pairs={{0,8},{8,0},{1,9},{9,1},{2,10},{10,2},{3,11},{11,3},{4,12},{12,4},... | collective-permute-start | bytes 2822408 | tf_op jit(solution)/shard_map/ppermute | solution.py:117
  112.6 11.4 %copy-start.6 = (bf16[384,1,280]{0,2,1:T(8,128)(2,1)S(1)}, bf16[384,1,280]{0,2,1:T(8,128)(2,1)}, u32[]{:S(2)}) copy-start(bf16[384,1,280]{0,2,1:T(8,128)(2,1)} %copy.79) | copy-start | bytes 645124
  114.8 10.3 %copy-start.10 = (bf16[384,1,280]{0,2,1:T(8,128)(2,1)S(1)}, bf16[384,1,280]{0,2,1:T(8,128)(2,1)}, u32[]{:S(2)}) copy-start(bf16[384,1,280]{0,2,1:T(8,128)(2,1)} %copy.85) | copy-start | bytes 645124
  114.8 13.2 %collective-permute-start.13 = (bf16[280,1680]{1,0:T(8,128)(2,1)S(1)}, bf16[280,1680]{1,0:T(8,128)(2,1)S(1)}, u32[]{:S(2)}, u32[]{:S(2)}) collective-permute-start(bf16[280,1680]{1,0:T(8,128)(2,1)S(1)} %collective-permute-done.11), channel_id=1, source_target_pairs={{6,7},{7,6},{8,9},{9,8},{22,23},{23,22},{24,25},{25,24}} | collective-permute-start | bytes 2822408 | tf_op jit(solution)/shard_map/x3/ppermute | solution.py:127
  115.7 23.0 %collective-permute-start.12 = (bf16[280,1680]{1,0:T(8,128)(2,1)S(1)}, bf16[280,1680]{1,0:T(8,128)(2,1)S(1)}, u32[]{:S(2)}, u32[]{:S(2)}) collective-permute-start(bf16[280,1680]{1,0:T(8,128)(2,1)S(1)} %collective-permute-done.11), channel_id=1, source_target_pairs={{0,8},{8,0},{1,9},{9,1},{2,10},{10,2},{3,11},{11,3},{4,12},{12,4},... | collective-permute-start | bytes 2822408 | tf_op jit(solution)/shard_map/ppermute | solution.py:117
  124.0 13.8 %collective-permute-start.10 = (bf16[280,1680]{1,0:T(8,128)(2,1)S(1)}, bf16[280,1680]{1,0:T(8,128)(2,1)S(1)}, u32[]{:S(2)}, u32[]{:S(2)}) collective-permute-start(bf16[280,1680]{1,0:T(8,128)(2,1)S(1)} %collective-permute-done.9), channel_id=1, source_target_pairs={{0,8},{8,0},{1,9},{9,1},{2,10},{10,2},{3,11},{11,3},{4,12},{12,4},... | collective-permute-start | bytes 2822408 | tf_op jit(solution)/shard_map/ppermute | solution.py:117
  127.0 9.8 %copy-start.8 = (bf16[384,1,280]{0,2,1:T(8,128)(2,1)S(1)}, bf16[384,1,280]{0,2,1:T(8,128)(2,1)}, u32[]{:S(2)}) copy-start(bf16[384,1,280]{0,2,1:T(8,128)(2,1)} %copy.93) | copy-start | bytes 645124
  128.0 9.8 %copy-start.4 = (bf16[384,1,280]{0,2,1:T(8,128)(2,1)S(1)}, bf16[384,1,280]{0,2,1:T(8,128)(2,1)}, u32[]{:S(2)}) copy-start(bf16[384,1,280]{0,2,1:T(8,128)(2,1)} %copy.87) | copy-start | bytes 645124
  128.0 11.7 %collective-permute-start.14 = (bf16[280,1680]{1,0:T(8,128)(2,1)S(1)}, bf16[280,1680]{1,0:T(8,128)(2,1)S(1)}, u32[]{:S(2)}, u32[]{:S(2)}) collective-permute-start(bf16[280,1680]{1,0:T(8,128)(2,1)S(1)} %collective-permute-done.13), channel_id=1, source_target_pairs={{0,8},{8,0},{1,9},{9,1},{2,10},{10,2},{3,11},{11,3},{4,12},{12,4},... | collective-permute-start | bytes 2822408 | tf_op jit(solution)/shard_map/ppermute | solution.py:117
  142.9 18.7 %copy-start.1 = (f32[20,14,1]{2,1,0:T(8,128)S(1)}, f32[20,14,1]{2,1,0:T(8,128)}, u32[]{:S(2)}) copy-start(f32[20,14,1]{2,1,0:T(8,128)} %copy.104) | copy-start | bytes 3364
  142.9 18.8 %copy-start.2 = (f32[2,10,14,112]{3,2,1,0:T(8,128)S(1)}, f32[2,10,14,112]{3,2,1,0:T(8,128)}, u32[]{:S(2)}) copy-start(f32[2,10,14,112]{3,2,1,0:T(8,128)} %copy.101) | copy-start | bytes 376324
  148.1 11.6 %collective-permute-start.17 = (bf16[20,16,128]{2,1,0:T(8,128)(2,1)}, bf16[20,16,128]{2,1,0:T(8,128)(2,1)S(1)}, u32[]{:S(2)}, u32[]{:S(2)}) collective-permute-start(bf16[20,16,128]{2,1,0:T(8,128)(2,1)} %get-tuple-element.16), channel_id=1, source_target_pairs={{0,7},{1,6},{2,5},{3,4},{4,3},{5,2},{6,1},{7,0},{8,15},{9,14},{10,... | collective-permute-start | bytes 245768 | tf_op jit(solution)/shard_map/rs7/ppermute | solution.py:130
  152.9 7.3 %collective-permute-start.18 = (bf16[20,16,128]{2,1,0:T(8,128)(2,1)}, bf16[20,16,128]{2,1,0:T(8,128)(2,1)S(1)}, u32[]{:S(2)}, u32[]{:S(2)}) collective-permute-start(bf16[20,16,128]{2,1,0:T(8,128)(2,1)} %get-tuple-element.17), channel_id=1, source_target_pairs={{0,6},{1,7},{2,4},{3,5},{4,2},{5,3},{6,0},{7,1},{8,14},{9,15},{10,... | collective-permute-start | bytes 245768 | tf_op jit(solution)/shard_map/rs6/ppermute | solution.py:130
  154.3 11.5 %collective-permute-start.19 = (bf16[20,16,128]{2,1,0:T(8,128)(2,1)}, bf16[20,16,128]{2,1,0:T(8,128)(2,1)S(1)}, u32[]{:S(2)}, u32[]{:S(2)}) collective-permute-start(bf16[20,16,128]{2,1,0:T(8,128)(2,1)} %get-tuple-element.18), channel_id=1, source_target_pairs={{0,5},{1,4},{2,7},{3,6},{4,1},{5,0},{6,3},{7,2},{8,13},{9,12},{10,... | collective-permute-start | bytes 245768 | tf_op jit(solution)/shard_map/rs5/ppermute | solution.py:130
  154.4 12.2 %collective-permute-start.20 = (bf16[20,16,128]{2,1,0:T(8,128)(2,1)}, bf16[20,16,128]{2,1,0:T(8,128)(2,1)S(1)}, u32[]{:S(2)}, u32[]{:S(2)}) collective-permute-start(bf16[20,16,128]{2,1,0:T(8,128)(2,1)} %get-tuple-element.19), channel_id=1, source_target_pairs={{0,4},{1,5},{2,6},{3,7},{4,0},{5,1},{6,2},{7,3},{8,12},{9,13},{10,... | collective-permute-start | bytes 245768 | tf_op jit(solution)/shard_map/rs4/ppermute | solution.py:130
  158.1 9.6 %collective-permute-start.21 = (bf16[20,16,128]{2,1,0:T(8,128)(2,1)}, bf16[20,16,128]{2,1,0:T(8,128)(2,1)S(1)}, u32[]{:S(2)}, u32[]{:S(2)}) collective-permute-start(bf16[20,16,128]{2,1,0:T(8,128)(2,1)} %get-tuple-element.20), channel_id=1, source_target_pairs={{0,3},{1,2},{2,1},{3,0},{4,7},{5,6},{6,5},{7,4},{8,11},{9,10},{10,... | collective-permute-start | bytes 245768 | tf_op jit(solution)/shard_map/rs3/ppermute | solution.py:130
  159.7 8.1 %collective-permute-start.22 = (bf16[20,16,128]{2,1,0:T(8,128)(2,1)}, bf16[20,16,128]{2,1,0:T(8,128)(2,1)S(1)}, u32[]{:S(2)}, u32[]{:S(2)}) collective-permute-start(bf16[20,16,128]{2,1,0:T(8,128)(2,1)} %get-tuple-element.21), channel_id=1, source_target_pairs={{0,2},{1,3},{2,0},{3,1},{4,6},{5,7},{6,4},{7,5},{8,10},{9,11},{10,... | collective-permute-start | bytes 245768 | tf_op jit(solution)/shard_map/rs2/ppermute | solution.py:130
  160.2 7.5 %collective-permute-start.23 = (bf16[20,16,128]{2,1,0:T(8,128)(2,1)}, bf16[20,16,128]{2,1,0:T(8,128)(2,1)S(1)}, u32[]{:S(2)}, u32[]{:S(2)}) collective-permute-start(bf16[20,16,128]{2,1,0:T(8,128)(2,1)} %get-tuple-element.22), channel_id=1, source_target_pairs={{0,1},{1,0},{2,3},{3,2},{4,5},{5,4},{6,7},{7,6},{8,9},{9,8},{10,11... | collective-permute-start | bytes 245768 | tf_op jit(solution)/shard_map/rs1/ppermute | solution.py:130
  168.8 4.1 %collective-permute-start.24 = (bf16[10,16,128]{2,1,0:T(8,128)(2,1)S(1)}, bf16[10,16,128]{2,1,0:T(8,128)(2,1)S(1)}, u32[]{:S(2)}, u32[]{:S(2)}) collective-permute-start(bf16[10,16,128]{2,1,0:T(8,128)(2,1)S(1)} %slice.87), channel_id=1, source_target_pairs={{0,16},{16,0},{1,17},{17,1},{2,18},{18,2},{3,19},{19,3},{4,20},{20... | collective-permute-start | bytes 122888 | tf_op jit(solution)/shard_map/sy/ppermute | solution.py:117
  172.1 20.2 %collective-permute-start.16 = (bf16[192,560]{1,0:T(8,128)(2,1)S(1)}, bf16[192,560]{1,0:T(8,128)(2,1)S(1)}, u32[]{:S(2)}, u32[]{:S(2)}) collective-permute-start(bf16[192,560]{1,0:T(8,128)(2,1)S(1)} %get-tuple-element.45), channel_id=1, source_target_pairs={{0,16},{16,0},{1,17},{17,1},{2,18},{18,2},{3,19},{19,3},{4,20},{20... | collective-permute-start | bytes 645128 | tf_op jit(solution)/shard_map/qy/ppermute | solution.py:117
  173.0 3.8 %collective-permute-start.32 = (bf16[1,20,16,128]{3,2,1,0:T(8,128)(2,1)S(1)}, bf16[1,20,16,128]{3,2,1,0:T(8,128)(2,1)S(1)}, u32[]{:S(2)}, u32[]{:S(2)}) collective-permute-start(bf16[1,20,16,128]{3,2,1,0:T(8,128)(2,1)S(1)} %fusion.40), channel_id=1, source_target_pairs={{0,8},{8,0},{16,24},{24,16},{1,9},{9,1},{17,25},{25,17},{2,10},{10... | collective-permute-start | bytes 245768 | tf_op jit(solution)/shard_map/mv1/ppermute | solution.py:242
  173.2 19.9 %copy-start.14 = (bf16[20,16,128]{2,1,0:T(8,128)(2,1)}, bf16[20,16,128]{2,1,0:T(8,128)(2,1)S(1)}, u32[]{:S(2)}) copy-start(bf16[20,16,128]{2,1,0:T(8,128)(2,1)S(1)} %fusion.39.refs_0_) | copy-start | bytes 245764
  173.2 5.4 %collective-permute-start.25 = (bf16[20,16,128]{2,1,0:T(8,128)(2,1)S(1)}, bf16[20,16,128]{2,1,0:T(8,128)(2,1)S(1)}, u32[]{:S(2)}, u32[]{:S(2)}) collective-permute-start(bf16[20,16,128]{2,1,0:T(8,128)(2,1)S(1)} %fusion.39.refs_0_), channel_id=1, source_target_pairs={{0,1},{1,0},{2,3},{3,2},{4,5},{5,4},{6,7},{7,6},{8,9},{9,8},{10,11... | collective-permute-start | bytes 245768 | tf_op jit(solution)/shard_map/ag1/ppermute | solution.py:130
  174.7 6.2 %collective-permute-start.26 = (bf16[20,16,128]{2,1,0:T(8,128)(2,1)S(1)}, bf16[20,16,128]{2,1,0:T(8,128)(2,1)S(1)}, u32[]{:S(2)}, u32[]{:S(2)}) collective-permute-start(bf16[20,16,128]{2,1,0:T(8,128)(2,1)S(1)} %fusion.39.refs_0_), channel_id=1, source_target_pairs={{0,2},{1,3},{2,0},{3,1},{4,6},{5,7},{6,4},{7,5},{8,10},{9,11},{10,... | collective-permute-start | bytes 245768 | tf_op jit(solution)/shard_map/ag2/ppermute | solution.py:130
  174.8 9.3 %collective-permute-start.27 = (bf16[20,16,128]{2,1,0:T(8,128)(2,1)S(1)}, bf16[20,16,128]{2,1,0:T(8,128)(2,1)S(1)}, u32[]{:S(2)}, u32[]{:S(2)}) collective-permute-start(bf16[20,16,128]{2,1,0:T(8,128)(2,1)S(1)} %fusion.39.refs_0_), channel_id=1, source_target_pairs={{0,3},{1,2},{2,1},{3,0},{4,7},{5,6},{6,5},{7,4},{8,11},{9,10},{10,... | collective-permute-start | bytes 245768 | tf_op jit(solution)/shard_map/ag3/ppermute | solution.py:130
  176.8 8.6 %collective-permute-start.28 = (bf16[20,16,128]{2,1,0:T(8,128)(2,1)S(1)}, bf16[20,16,128]{2,1,0:T(8,128)(2,1)S(1)}, u32[]{:S(2)}, u32[]{:S(2)}) collective-permute-start(bf16[20,16,128]{2,1,0:T(8,128)(2,1)S(1)} %fusion.39.refs_0_), channel_id=1, source_target_pairs={{0,4},{1,5},{2,6},{3,7},{4,0},{5,1},{6,2},{7,3},{8,12},{9,13},{10,... | collective-permute-start | bytes 245768 | tf_op jit(solution)/shard_map/ag4/ppermute | solution.py:130
  178.7 14.4 %copy-start.18 = (bf16[20,16,128]{2,1,0:T(8,128)(2,1)}, bf16[20,16,128]{2,1,0:T(8,128)(2,1)S(1)}, u32[]{:S(2)}) copy-start(bf16[20,16,128]{2,1,0:T(8,128)(2,1)S(1)} %collective-permute-done.25.refs_1_) | copy-start | bytes 245764
  178.7 13.6 %collective-permute-start.29 = (bf16[20,16,128]{2,1,0:T(8,128)(2,1)S(1)}, bf16[20,16,128]{2,1,0:T(8,128)(2,1)S(1)}, u32[]{:S(2)}, u32[]{:S(2)}) collective-permute-start(bf16[20,16,128]{2,1,0:T(8,128)(2,1)S(1)} %fusion.39.refs_0_), channel_id=1, source_target_pairs={{0,5},{1,4},{2,7},{3,6},{4,1},{5,0},{6,3},{7,2},{8,13},{9,12},{10,... | collective-permute-start | bytes 245768 | tf_op jit(solution)/shard_map/ag5/ppermute | solution.py:130
  180.9 12.2 %copy-start.19 = (bf16[20,16,128]{2,1,0:T(8,128)(2,1)}, bf16[20,16,128]{2,1,0:T(8,128)(2,1)S(1)}, u32[]{:S(2)}) copy-start(bf16[20,16,128]{2,1,0:T(8,128)(2,1)S(1)} %collective-permute-done.26.refs_2_) | copy-start | bytes 245764
  180.9 11.4 %collective-permute-start.30 = (bf16[20,16,128]{2,1,0:T(8,128)(2,1)S(1)}, bf16[20,16,128]{2,1,0:T(8,128)(2,1)S(1)}, u32[]{:S(2)}, u32[]{:S(2)}) collective-permute-start(bf16[20,16,128]{2,1,0:T(8,128)(2,1)S(1)} %fusion.39.refs_0_), channel_id=1, source_target_pairs={{0,6},{1,7},{2,4},{3,5},{4,2},{5,3},{6,0},{7,1},{8,14},{9,15},{10,... | collective-permute-start | bytes 245768 | tf_op jit(solution)/shard_map/ag6/ppermute | solution.py:130
  184.0 9.1 %copy-start.20 = (bf16[20,16,128]{2,1,0:T(8,128)(2,1)}, bf16[20,16,128]{2,1,0:T(8,128)(2,1)S(1)}, u32[]{:S(2)}) copy-start(bf16[20,16,128]{2,1,0:T(8,128)(2,1)S(1)} %collective-permute-done.27.refs_3_) | copy-start | bytes 245764
  184.0 8.3 %collective-permute-start.31 = (bf16[20,16,128]{2,1,0:T(8,128)(2,1)S(1)}, bf16[20,16,128]{2,1,0:T(8,128)(2,1)S(1)}, u32[]{:S(2)}, u32[]{:S(2)}) collective-permute-start(bf16[20,16,128]{2,1,0:T(8,128)(2,1)S(1)} %fusion.39.refs_0_), channel_id=1, source_target_pairs={{0,7},{1,6},{2,5},{3,4},{4,3},{5,2},{6,1},{7,0},{8,15},{9,14},{10,... | collective-permute-start | bytes 245768 | tf_op jit(solution)/shard_map/ag7/ppermute | solution.py:130
  185.4 11.1 %collective-permute-start.33 = (bf16[2,20,16,128]{3,2,1,0:T(8,128)(2,1)S(1)}, bf16[2,20,16,128]{3,2,1,0:T(8,128)(2,1)S(1)}, u32[]{:S(2)}, u32[]{:S(2)}) collective-permute-start(bf16[2,20,16,128]{3,2,1,0:T(8,128)(2,1)S(1)} %pad_maximum_fusion.1), channel_id=1, source_target_pairs={{0,16},{8,24},{16,0},{24,8},{1,17},{9,25},{17,1},{25,9},{2,18},{10... | collective-permute-start | bytes 491528 | tf_op jit(solution)/shard_map/mv2/ppermute | solution.py:242
  (12 other events, 28.7 us)

commit v2 on v1

v2 whole, which is shorter than its diff:
```python
import functools

import jax
import jax.numpy as jnp
from jax import lax
from jax.experimental import pallas as pl
from jax.experimental.pallas import tpu as pltpu
from jax.sharding import Mesh
from jax.sharding import PartitionSpec as P


F32 = jnp.float32
BF16 = jnp.bfloat16
LANES = 128
VMEM = pl.BlockSpec(memory_space=pltpu.VMEM)
SMEM = pl.BlockSpec(memory_space=pltpu.SMEM)
SWAP = [(0, 1), (1, 0)]


def phi(u):
    return jnp.where(u > 0.0, u + 1.0, jnp.exp(jnp.minimum(u, 0.0)))


def whole_call(kernel, out_shape, kinds, flops, moved, scratch=(), alias=None, smem=False):
    return pl.pallas_call(
        kernel,
        out_shape=out_shape,
        in_specs=[SMEM if kind == "s" else VMEM for kind in kinds],
        scratch_shapes=scratch,
        input_output_aliases=alias or {},
        out_specs=SMEM if smem else jax.tree.map(lambda _: VMEM, out_shape),
        cost_estimate=pl.CostEstimate(flops=flops, bytes_accessed=moved, transcendentals=0),
        compiler_params=pltpu.CompilerParams(vmem_limit_bytes=20 * 1024 * 1024),
    )


def prep_kernel(pos_ref, w_ref, mine_ref, piece_ref):
    depth, total = w_ref.shape
    half = piece_ref.shape[0]
    width = total // 6
    wide = mine_ref.shape[1]
    for turn in range(2):

        @pl.when(pos_ref[3] == turn)
        def _():
            for j, part in enumerate((1, 2, 0)):
                start = (2 * part + turn) * width
                mine_ref[:, j * width : (j + 1) * width] = w_ref[:, start : start + width]

    mine_ref[:, 3 * width :] = jnp.zeros((depth, wide - 3 * width), BF16)

    @pl.when(pos_ref[2] == 0)
    def _():
        piece_ref[...] = mine_ref[:half]

    @pl.when(pos_ref[2] == 1)
    def _():
        piece_ref[: depth - half] = mine_ref[half:]
        piece_ref[depth - half :] = jnp.zeros((2 * half - depth, wide), BF16)


def table_kernel(heads, rows, pos_ref, state_ref, ksum_ref, group_ref, plain_ref, old_ref):
    units, share, size = state_ref.shape
    m = pos_ref[4]
    src = lax.broadcasted_iota(jnp.int32, (size, LANES), 0)
    lane = lax.broadcasted_iota(jnp.int32, (size, LANES), 1)
    plain = jnp.where(src == lane, 1.0, 0.0).astype(BF16)
    spot = ((lane // rows) ^ m) * share + lane % rows
    group = jnp.where((src == spot) & (lane % rows < share), 1.0, 0.0).astype(BF16)
    group_ref[...] = jnp.zeros_like(group_ref)
    plain_ref[...] = jnp.zeros_like(plain_ref)
    for h in range(heads):
        group_ref[h * size : (h + 1) * size, h * LANES : (h + 1) * LANES] = group
        plain_ref[h * size : (h + 1) * size, h * LANES : (h + 1) * LANES] = plain
    row = lax.broadcasted_iota(jnp.int32, (rows, size), 0)
    col = lax.broadcasted_iota(jnp.int32, (rows, size), 1)
    chosen = jnp.where((col == m * share + row) & (row < share), 1.0, 0.0)
    ksum = ksum_ref[...]
    turned = lax.dot_general(
        chosen,
        ksum,
        (((1,), (1,)), ((), ())),
        precision=lax.Precision.HIGHEST,
        preferred_element_type=F32,
    )
    old_ref[...] = jnp.zeros_like(old_ref)
    for u in range(units):
        old_ref[u, :, size : size + 1] = turned[:, u : u + 1]
        old_ref[u, :share, :size] = state_ref[u]
        old_ref[u, rows - 1 :, :size] = ksum[u : u + 1]


def block_kernel(pos_ref, own_ref, other_ref, out_ref):
    members, both, wide = out_ref.shape
    count = both // 2
    depth = own_ref.shape[1] // members
    for b in range(members):
        out_ref[b, :count, :depth] = own_ref[:, b * depth : (b + 1) * depth]
        out_ref[b, count:, :depth] = other_ref[:, b * depth : (b + 1) * depth]
        if wide > depth:
            out_ref[b, :, depth:] = jnp.zeros((both, wide - depth), BF16)


def hops(n, pos_ref, k, cross):
    z, x, c = pos_ref[0], pos_ref[1], pos_ref[2]
    col = 1 - x if cross else x
    first = 2 if cross and k == 1 else k
    up, down = lax.rem(z - k + n, n), lax.rem(z + k, n)
    if 2 * first > n - 1:
        return (jnp.where(z >= first, up, down) * 2 + col,)
    return (jnp.where(c == 0, up, down) * 2 + col, jnp.where(c == 0, down, up) * 2 + col)


def add_products(n, plan, pos_ref, blocks_ref, refs, tile):
    total = None
    refs = list(refs)
    for kind, k in plan:
        if kind == "own":
            terms = [(pos_ref[0] * 2 + pos_ref[1], refs.pop(0)[:, tile])]
        elif kind in ("beside", "corner"):
            here, there = refs.pop(0)[:, tile], refs.pop(0)[:, tile]
            first = pos_ref[2] == 0
            line = pos_ref[0]
            if kind == "corner":
                line = jnp.where(line <= 1, 0, n - 1)
            both = jnp.concatenate(
                [jnp.where(first, here, there), jnp.where(first, there, here)], axis=0
            )
            terms = [(line * 2 + 1 - pos_ref[1], both)]
        else:
            here, there = refs.pop(0)[:, tile], refs.pop(0)[:, tile]
            ids = hops(n, pos_ref, k, kind == "across")
            terms = [(ids[0], here + there)] if len(ids) == 1 else list(zip(ids, (here, there)))
        for index, weight in terms:
            lhs = blocks_ref[index, :, : weight.shape[0]]
            term = jnp.dot(lhs, weight, preferred_element_type=F32)
            total = term if total is None else total + term
    return total


def mul_kernel(n, plan, fresh, pos_ref, blocks_ref, *refs):
    acc_ref = refs[-1]
    given = refs[:-1] if fresh else refs[1:-1]
    wide = acc_ref.shape[1]
    step = 256 if wide % 256 == 0 else LANES

    @pl.loop(0, wide // step)
    def _(t):
        tile = pl.ds(pl.multiple_of(t * step, step), step)
        term = add_products(n, plan, pos_ref, blocks_ref, given, tile)
        acc_ref[:, tile] = term if fresh else refs[0][:, tile] + term


def kv_kernel(n, plan, streams, frames, heads, size, rows, pos_ref, near_ref, far_ref, *refs):
    blocks_ref, old_ref, refs = refs[0], refs[1], refs[2:]
    given, refs = refs[: 2 * len(plan)], refs[2 * len(plan) :]
    group_ref, plain_ref, mine_ref, give_ref = refs[:4]
    chunks, acc_ref = refs[4:-1], refs[-1]
    wide = acc_ref.shape[1]
    step = 256 if wide % 256 == 0 else LANES

    @pl.loop(0, wide // step)
    def _(t):
        tile = pl.ds(pl.multiple_of(t * step, step), step)
        acc_ref[:, tile] = old_ref[:, tile] + add_products(
            n, plan, pos_ref, blocks_ref, given, tile
        )

    width = heads * size
    count = acc_ref.shape[0] // 2
    tokens = count // streams
    asked = acc_ref[:, 2 * width : 3 * width].astype(BF16)
    mine_ref[...] = asked[:count]
    give_ref[...] = asked[count:]
    frame = lax.broadcasted_iota(jnp.int32, (tokens, width), 0) // (tokens // frames)
    masks = [frame < ref[s] for ref in (near_ref, far_ref) for s in range(streams)]
    live = jnp.concatenate([jnp.where(mask, 1.0, 0.0) for mask in masks], axis=0)
    keys = acc_ref[:, :width].astype(BF16).astype(F32)
    keyed = (phi(keys) * live).astype(BF16)
    values = acc_ref[:, width : 2 * width].astype(BF16)
    grouped = jnp.dot(keyed, group_ref[...], preferred_element_type=F32).astype(BF16)
    plain = jnp.dot(keyed, plain_ref[...], preferred_element_type=F32)
    spread = jnp.dot(values, plain_ref[...], preferred_element_type=F32)
    lane = lax.broadcasted_iota(jnp.int32, spread.shape, 1) % LANES
    spread = jnp.where(lane == size, 1.0, spread).astype(BF16)
    row = lax.broadcasted_iota(jnp.int32, (LANES, LANES), 0) % rows
    for s in range(2 * streams):
        span = slice(s * tokens, (s + 1) * tokens)
        sums = jnp.sum(plain[span], axis=0, keepdims=True)
        for h in range(heads):
            cols = slice(h * LANES, (h + 1) * LANES)
            outer = lax.dot_general(
                grouped[span, cols],
                spread[span, cols],
                (((0,), (0,)), ((), ())),
                preferred_element_type=F32,
            )
            outer = jnp.where(row == rows - 1, sums[:, cols], outer).astype(BF16)
            for r, chunk in enumerate(chunks):
                chunk[s * heads + h] = outer[r * rows : (r + 1) * rows]


def sum_kernel(*refs):
    parts, keep_ref, give_ref = refs[1:-2], refs[-2], refs[-1]
    half = keep_ref.shape[0]
    for lo, out in ((0, keep_ref), (half, give_ref)):
        total = parts[0][lo : lo + half].astype(F32)
        for part in parts[1:]:
            total = total + part[lo : lo + half].astype(F32)
        out[...] = total.astype(out.dtype)


def join_kernel(heads, pos_ref, keep_ref, got_ref, old_ref, new_ref):
    first = pos_ref[3] == 0
    for s in range(keep_ref.shape[0] // heads):
        keep = keep_ref[s * heads : (s + 1) * heads]
        got = got_ref[s * heads : (s + 1) * heads].astype(F32)
        at = 2 * s * heads
        low = jnp.where(first, keep, got) + old_ref[at : at + heads]
        high = jnp.where(first, got, keep) + old_ref[at + heads : at + 2 * heads]
        new_ref[at : at + heads] = low.astype(BF16)
        new_ref[at + heads : at + 2 * heads] = high.astype(BF16)


def query_kernel(pos_ref, raw_ref, group_ref, out_ref):
    queried = phi(raw_ref[...].astype(F32)).astype(BF16)
    out_ref[...] = jnp.dot(queried, group_ref[...], preferred_element_type=F32).astype(BF16)


def read_kernel(streams, frames, heads, size, pos_ref, near_ref, own_ref, other_ref, *refs):
    pieces, out_ref = refs[:-1], refs[-1]
    tokens = own_ref.shape[0] // streams
    first = pos_ref[3] == 0
    frame = lax.broadcasted_iota(jnp.int32, (tokens, 1), 0) // (tokens // frames)
    own, other = own_ref[...], other_ref[...]
    halves = (jnp.where(first, own, other), jnp.where(first, other, own))
    for s in range(streams):
        span = slice(s * tokens, (s + 1) * tokens)
        live = jnp.where(frame < near_ref[s], 1.0, 0.0)
        for half, grouped in enumerate(halves):
            for h in range(heads):
                pair = s * 2 * heads + half * heads + h
                state = jnp.concatenate([piece[pair] for piece in pieces], axis=0)
                top = jnp.dot(
                    grouped[span, h * LANES : (h + 1) * LANES],
                    state,
                    preferred_element_type=F32,
                )
                result = top[:, :size] / top[:, size : size + 1] * live
                col = (half * heads + h) * size
                out_ref[span, col : col + size] = result.astype(BF16)


def place_kernel(units, pos_ref, new_ref, place_ref):
    me = pos_ref[5]

    @pl.loop(0, new_ref.shape[0])
    def _(g):
        spot = new_ref[g]

        @pl.when(spot // units == me)
        def _():
            place_ref[spot % units] = ((g // units) ^ me) * units + g % units


def pick_kernel(share, size, rows, spots, place_ref, *refs):
    given, (state_ref, ksum_ref, all_ref) = refs[:-3], refs[-3:]
    units = state_ref.shape[0]
    for spot, ref in zip(spots, given):
        all_ref[spot * units : (spot + 1) * units] = ref[...]
    for u in range(units):
        block = all_ref[place_ref[u]].astype(F32)
        state_ref[u] = block[:share, :size]
        ksum_ref[u : u + 1] = block[rows - 1 :, :size]


def body(n, *given):
    return layer(n, *given)


def layer(n, latents, w_qkv, state_in, ksum_in, frames_live, new_place):
    streams, frames, spatial, model = latents.shape
    heads_all, size = ksum_in.shape[1:]
    heads = heads_all // 2
    share = state_in.shape[2]
    members = size // share
    rows = LANES // members
    width = heads * size
    depth = w_qkv.shape[0]
    units = streams * heads_all
    o, y, c = lax.axis_index("o"), lax.axis_index("y"), lax.axis_index("c")
    z, x = lax.axis_index("z"), lax.axis_index("x")
    m = z * 2 + x
    owners = lax.axis_size("o") * 4
    me = (o * 2 + y) * 2 + c

    def flat(cc, zz, xx):
        return (cc * n + zz) * 2 + xx

    def swap(axis, v):
        return lax.ppermute(v, axis, SWAP)

    def hop(k, v):
        pairs = [(i, i + 1) for i in range(k - 1, n - 1)]
        pairs += [(n + i, n + i - 1) for i in range(n - k, 0, -1)]
        return lax.ppermute(v, ("c", "z"), pairs)

    def across(k, v):
        first = 2 if k == 1 else k
        pairs = [(flat(0, i, a), flat(0, i, 1 - a)) for i in range(first, n) for a in range(2)]
        pairs += [(flat(1, i, a), flat(1, i, 1 - a)) for i in range(n - first) for a in range(2)]
        return lax.ppermute(v, ("c", "z", "x"), pairs)

    def xor(k, v):
        return lax.ppermute(v, ("z", "x"), [(i, i ^ k) for i in range(members)])

    def near_end(v):
        pairs = [(flat(i, 0, a), flat(i, 1, a)) for i in range(2) for a in range(2)]
        pairs += [(flat(i, n - 1, a), flat(i, n - 2, a)) for i in range(2) for a in range(2)]
        return lax.ppermute(v, ("c", "z", "x"), pairs)

    pos = jnp.stack([z, x, c, y, m, me]).astype(jnp.int32)
    wide = -(-3 * width // LANES) * LANES
    half = -(-depth // 32) * 16
    mine, piece = whole_call(
        prep_kernel,
        [jax.ShapeDtypeStruct((depth, wide), BF16), jax.ShapeDtypeStruct((half, wide), BF16)],
        "sv",
        0,
        4_000_000,
    )(pos, w_qkv)

    own_tokens = latents.reshape(-1, model)
    count = own_tokens.shape[0]
    Z, X, ZC, XC = ([None] * n for _ in range(4))
    Z[1] = hop(1, mine)
    X[0] = swap("x", piece)
    other_tokens = swap("y", own_tokens)
    far_live = swap("y", frames_live)
    for k in range(1, n):
        if k > 1:
            Z[k] = hop(k, Z[k - 1])
        X[k] = across(k, Z[k])
        ZC[k] = swap("c", Z[k])
    Y = near_end(X[0])
    YC = swap("c", Y)
    for k in range(n):
        XC[k] = swap("c", X[k])

    group, plain, old = whole_call(
        functools.partial(table_kernel, heads, rows),
        [
            jax.ShapeDtypeStruct((width, heads * LANES), BF16),
            jax.ShapeDtypeStruct((width, heads * LANES), BF16),
            jax.ShapeDtypeStruct((units, rows, LANES), F32),
        ],
        "svv",
        0,
        2_000_000,
    )(pos, state_in.reshape(units, share, size), ksum_in.reshape(units, size))
    blocks = whole_call(
        block_kernel,
        jax.ShapeDtypeStruct((members, 2 * count, 2 * half), BF16),
        "svv",
        0,
        4_000_000,
    )(pos, own_tokens, other_tokens)

    def multiply(plan, acc, *given):
        first = [] if acc is None else [acc]
        return whole_call(
            functools.partial(mul_kernel, n, plan, acc is None),
            jax.ShapeDtypeStruct((2 * count, wide), F32),
            "sv" + "v" * (len(first) + len(given)),
            2_000_000_000,
            8_000_000,
            alias={2: 0} if first else None,
        )(pos, blocks, *first, *given)

    acc = multiply([("own", 0), ("beside", 0), ("along", 1)], None, mine, X[0], XC[0], Z[1], ZC[1])
    for k in range(2, n):
        plan = [("across", k - 1), ("along", k)]
        given = [X[k - 1], XC[k - 1], Z[k], ZC[k]]
        if k == 2:
            plan, given = plan + [("corner", 0)], given + [Y, YC]
        acc = multiply(plan, acc, *given)

    pairs = 2 * streams * heads
    chunk = jax.ShapeDtypeStruct((pairs, rows, LANES), BF16)
    asked = jax.ShapeDtypeStruct((count, width), BF16)
    q, q_give, *parts = whole_call(
        functools.partial(
            kv_kernel, n, [("across", n - 1)], streams, frames, heads, size, rows
        ),
        [asked, asked] + [chunk] * members,
        "sssvvvvvv",
        2_000_000_000,
        8_000_000,
        scratch=[pltpu.VMEM((2 * count, wide), F32)],
    )(pos, frames_live, far_live, blocks, acc, X[n - 1], XC[n - 1], group, plain)

    for k in range(members - 1, 0, -1):
        parts[k] = xor(k, parts[k])
    q_other = swap("y", q_give)

    def ask(raw):
        return whole_call(
            query_kernel,
            jax.ShapeDtypeStruct((count, heads * LANES), BF16),
            "svv",
            140_000_000,
            1_500_000,
        )(pos, raw, group)

    q = ask(q)
    keep, give = whole_call(
        sum_kernel,
        [
            jax.ShapeDtypeStruct((pairs // 2, rows, LANES), F32),
            jax.ShapeDtypeStruct((pairs // 2, rows, LANES), BF16),
        ],
        "s" + "v" * members,
        0,
        1_000_000,
    )(pos, *parts)
    got = swap("y", give)
    new = whole_call(
        functools.partial(join_kernel, heads),
        jax.ShapeDtypeStruct((units, rows, LANES), BF16),
        "svvv",
        0,
        500_000,
    )(pos, keep, got, old)

    gathered = [new] + [xor(k, new) for k in range(1, members)]
    q_other = ask(q_other)

    every, spots, bit = [new], [0], owners // 2
    while bit:
        step = [(i, i ^ bit) for i in range(owners)]
        for i in range(len(every)):
            moved = lax.ppermute(every[i], ("o", "y", "c"), step)
            every.append(moved)
            spots.append(spots[i] ^ bit)
        bit //= 2
    place = whole_call(
        functools.partial(place_kernel, units),
        jax.ShapeDtypeStruct((units,), jnp.int32),
        "ss",
        0,
        1_000,
        smem=True,
    )(pos, new_place)
    moved_state, moved_ksum = whole_call(
        functools.partial(pick_kernel, share, size, rows, spots),
        [
            jax.ShapeDtypeStruct((units, share, size), F32),
            jax.ShapeDtypeStruct((units, size), F32),
        ],
        "s" + "v" * owners,
        1_000_000,
        800_000,
        scratch=[pltpu.VMEM((owners * units, rows, LANES), BF16)],
    )(place, *every)

    attended = whole_call(
        functools.partial(read_kernel, streams, frames, heads, size),
        jax.ShapeDtypeStruct((count, 2 * width), BF16),
        "ssvv" + "v" * members,
        1_500_000_000,
        3_000_000,
    )(pos, frames_live, q, q_other, *gathered)
    return (
        attended.reshape(streams, frames, spatial, 2 * width),
        moved_state,
        moved_ksum,
    )


def solution(mesh):
    owners, members = mesh.shape["req"], mesh.shape["mp"]
    split = Mesh(
        mesh.devices.reshape(owners // 4, 2, 2, members // 2, 2), ("o", "y", "c", "z", "x")
    )
    req, mp = ("o", "y", "c"), ("z", "x")
    return jax.shard_map(
        functools.partial(body, members // 2),
        mesh=split,
        in_specs=(
            P(req, None, mp, None),
            P(mp, None),
            P(req, None, mp, None),
            P(req, None, None),
            P(req),
            P(),
        ),
        out_specs=(P(req, None, mp, None), P(req, mp, None), P(req, None)),
        check_vma=False,
    )
```

time: 202 us -> 159 us (0.79); the launches traced: 199 us -> 158 us
  local copies, waits for them, and re-layouts: 67.8 us -> 11.7 us
  matrix products: 26.8 us -> 0 us
  waiting for transfers between devices: 9.93 us -> 33.9 us
  Pallas kernels: 10.2 us -> 31.5 us
  other arithmetic: 15.3 us -> 0 us
  starting transfers between devices: 67.6 us -> 80 us
    another operation x15 -> x1, local copies, waits for them, and re-layouts: 46.2 us -> 0.08 us  [layer(): pos = jnp.stack([z, x, c, y, m, me]).astype(jnp.int32)]
    dot_general x15 -> x0, matrix products: 26.8 us -> none  [mul(): return jnp.dot(a, b, preferred_element_type=F32)]
    pallas_call x3 -> x14, Pallas kernels: 10.2 us -> 31.5 us  [the longest x3 13.8 us: multiply(): whole_call(functools.partial(mul_kernel, n, plan, acc is None), jax.Shape...]
    ppermute x12 -> x13, waiting for transfers between devices: 0.19 us -> 14 us  [swap(): return lax.ppermute(v, axis, SWAP)]
    ppermute x3, waiting for transfers between devices: 0.01 us -> 11.8 us  [hop(): return lax.ppermute(v, ('c', 'z'), pairs)]
    unnamed x55 -> x38, local copies, waits for them, and re-layouts: 1.82 us -> 11.6 us
    concatenate x8 -> x0, local copies, waits for them, and re-layouts: 8.31 us -> none  [the longest x3 5.41 us: body(): tokens = jnp.concatenate([own_tokens, other_tokens], axis=0)]
    ppermute x14, starting transfers between devices: 24.1 us -> 30.2 us  [xor(): return lax.ppermute(v, ('z', 'x'), [(i, i ^ k) for i in range(members)])]
  transfers between devices with their start and end apart: 34 -> 37, of which waited for: 6 -> 7; matrix products, arithmetic and copies ran while one was open for 53% -> 1% of each run, Pallas kernels for 2% -> 15%
where the time goes in v2:
time: 159 us; the launch traced here: 158 us
  starting transfers between devices  80 us (50%)
  waiting for transfers between devices  33.9 us (21%)
  Pallas kernels  31.5 us (20%)
  local copies, waits for them, and re-layouts  11.7 us (7%)
    ppermute x13, starting transfers between devices, swap(): return lax.ppermute(v, axis, SWAP)  32.1 us
    ppermute x14, starting transfers between devices, xor(): return lax.ppermute(v, ('z', 'x'), [(i, i ^ k) for i in range(members)])  30.2 us
    ppermute x13, waiting for transfers between devices, swap(): return lax.ppermute(v, axis, SWAP)  14 us
    pallas_call x3, Pallas kernels, multiply(): whole_call(functools.partial(mul_kernel, n, plan, acc is None), jax.Shape...  13.8 us
    ppermute x3, waiting for transfers between devices, hop(): return lax.ppermute(v, ('c', 'z'), pairs)  11.8 us
    unnamed x38, local copies, waits for them, and re-layouts  11.6 us
    ppermute x14, waiting for transfers between devices, xor(): return lax.ppermute(v, ('z', 'x'), [(i, i ^ k) for i in range(members)])  6.67 us
    ppermute x3, starting transfers between devices, hop(): return lax.ppermute(v, ('c', 'z'), pairs)  6.45 us
  transfers between devices with their start and end apart: 37, of which 7 were waited for; matrix products, arithmetic and copies ran while one was open for 1% of the time, Pallas kernels for 15%

profile of v2, /device:TPU:0, one launch (start us, length us, event | category | flops | bytes accessed | tf_op | source)
XLA Modules:
  0.0 158.2 jit_solution(8654118059579804951)
XLA Ops:
  0.7 1.5 copy-done
  2.3 1.0 shard_map.86
  3.3 5.0 %collective-permute-start.4 = (bf16[280,1792]{1,0:T(8,128)(2,1)S(1)}, bf16[280,1792]{1,0:T(8,128)(2,1)S(1)}, u32[]{:S(2)}, u32[]{:S(2)}) collective-permute-start(bf16[280,1792]{1,0:T(8,128)(2,1)S(1)} %get-tuple-element.22.refs_0_), channel_id=1, source_target_pairs={{0,2},{2,4},{4,6},{14,12},{12,10},{10,8},{1,3},{3,5},{5,7},{15,13}... | collective-permute-start | bytes 3010568 | tf_op jit(solution)/shard_map/ppermute | solution.py:306
  8.3 11.8 %collective-permute-done.4.refs_3_ = bf16[280,1792]{1,0:T(8,128)(2,1)S(1)} collective-permute-done((bf16[280,1792]{1,0:T(8,128)(2,1)S(1)}, bf16[280,1792]{1,0:T(8,128)(2,1)S(1)}, u32[]{:S(2)}, u32[]{:S(2)}) %collective-permute-start.4) | collective-permute-done | bytes 1003552 | tf_op jit(solution)/shard_map/ppermute | solution.py:306
  20.8 1.6 collective-permute-start.2
  22.3 1.5 collective-permute-start.1
  24.6 9.9 %collective-permute-done.2.refs_1_ = bf16[144,1792]{1,0:T(8,128)(2,1)S(1)} collective-permute-done((bf16[144,1792]{1,0:T(8,128)(2,1)S(1)}, bf16[144,1792]{1,0:T(8,128)(2,1)S(1)}, u32[]{:S(2)}, u32[]{:S(2)}) %collective-permute-start.2) | collective-permute-done | bytes 516128 | tf_op jit(solution)/shard_map/ppermute | solution.py:301
  34.5 2.0 %collective-permute-start.3 = (bf16[144,1792]{1,0:T(8,128)(2,1)S(1)}, bf16[144,1792]{1,0:T(8,128)(2,1)S(1)}, u32[]{:S(2)}, u32[]{:S(2)}) collective-permute-start(bf16[144,1792]{1,0:T(8,128)(2,1)S(1)} %collective-permute-done.2.refs_1_), channel_id=1, source_target_pairs={{0,8},{8,0},{1,9},{9,1},{2,10},{10,2},{3,11},{11,3},{4,12},{12,4},... | collective-permute-start | bytes 1548296 | tf_op jit(solution)/shard_map/ppermute | solution.py:301
  36.5 4.3 %collective-permute-start.10 = (bf16[144,1792]{1,0:T(8,128)(2,1)S(1)}, bf16[144,1792]{1,0:T(8,128)(2,1)S(1)}, u32[]{:S(2)}, u32[]{:S(2)}) collective-permute-start(bf16[144,1792]{1,0:T(8,128)(2,1)S(1)} %collective-permute-done.2.refs_1_), channel_id=1, source_target_pairs={{0,2},{1,3},{8,10},{9,11},{6,4},{7,5},{14,12},{15,13},{16,18},{17,... | collective-permute-start | bytes 1548296 | tf_op jit(solution)/shard_map/ppermute | solution.py:320
  41.6 1.6 %collective-permute-start.6 = (bf16[280,1792]{1,0:T(8,128)(2,1)S(1)}, bf16[280,1792]{1,0:T(8,128)(2,1)}, u32[]{:S(2)}, u32[]{:S(2)}) collective-permute-start(bf16[280,1792]{1,0:T(8,128)(2,1)S(1)} %collective-permute-done.4.refs_3_), channel_id=1, source_target_pairs={{4,5},{5,4},{6,7},{7,6},{8,9},{9,8},{10,11},{11,10},{20,21},{21,20... | collective-permute-start | bytes 3010568 | tf_op jit(solution)/shard_map/ppermute | solution.py:312
  45.6 1.0 copy-done.1
  47.4 1.6 %collective-permute-start.12 = (bf16[280,1792]{1,0:T(8,128)(2,1)S(1)}, bf16[280,1792]{1,0:T(8,128)(2,1)}, u32[]{:S(2)}, u32[]{:S(2)}) collective-permute-start(bf16[280,1792]{1,0:T(8,128)(2,1)S(1)} %collective-permute-done.8.refs_3_), channel_id=1, source_target_pairs={{4,5},{5,4},{6,7},{7,6},{8,9},{9,8},{10,11},{11,10},{20,21},{21,20... | collective-permute-start | bytes 3010568 | tf_op jit(solution)/shard_map/ppermute | solution.py:312
  49.0 1.6 %collective-permute-start.16 = (bf16[280,1792]{1,0:T(8,128)(2,1)S(1)}, bf16[280,1792]{1,0:T(8,128)(2,1)}, u32[]{:S(2)}, u32[]{:S(2)}) collective-permute-start(bf16[280,1792]{1,0:T(8,128)(2,1)S(1)} %collective-permute-done.14.refs_3_), channel_id=1, source_target_pairs={{6,7},{7,6},{8,9},{9,8},{22,23},{23,22},{24,25},{25,24}} | collective-permute-start | bytes 3010568 | tf_op jit(solution)/shard_map/ppermute | solution.py:312
  50.7 1.5 collective-permute-done.10.refs_5_
  52.2 1.2 collective-permute-start.11
  56.7 1.0 copy-done.3
  57.7 9.7 %collective-permute-start.13 = (bf16[280,1792]{1,0:T(8,128)(2,1)}, bf16[280,1792]{1,0:T(8,128)(2,1)}, u32[]{:S(2)}, u32[]{:S(2)}) collective-permute-start(bf16[280,1792]{1,0:T(8,128)(2,1)} %collective-permute-done.12.refs_1_), channel_id=1, source_target_pairs={{0,8},{8,0},{1,9},{9,1},{2,10},{10,2},{3,11},{11,3},{4,12},{12,4},... | collective-permute-start | bytes 3010568 | tf_op jit(solution)/shard_map/ppermute | solution.py:301
  67.5 10.7 %collective-permute-start.17 = (bf16[280,1792]{1,0:T(8,128)(2,1)}, bf16[280,1792]{1,0:T(8,128)(2,1)}, u32[]{:S(2)}, u32[]{:S(2)}) collective-permute-start(bf16[280,1792]{1,0:T(8,128)(2,1)} %collective-permute-done.16.refs_2_), channel_id=1, source_target_pairs={{0,8},{8,0},{1,9},{9,1},{2,10},{10,2},{3,11},{11,3},{4,12},{12,4},... | collective-permute-start | bytes 3010568 | tf_op jit(solution)/shard_map/ppermute | solution.py:301
  78.2 0.9 copy.13
  79.9 0.9 shard_map.90
  80.8 1.2 copy-done.5
  82.0 1.2 copy-done.7
  83.1 1.3 shard_map.85.blocks_ref.refs_0_
  84.5 4.4 %shard_map.87.refs_0_ = f32[384,1792]{1,0:T(8,128)S(1)} custom-call(s32[6]{0:T(128)S(1)} %stack.27.pos_ref.refs_0_, bf16[8,384,288]{2,1,0:T(8,128)(2,1)S(1)} %shard_map.85.blocks_ref.refs_0_, bf16[280,1792]{1,0:T(8,128)(2,1)S(1)} %get-tuple-element.22.refs_0_, bf16[144,1792]{1,0:T(8,128)(2,1)S(1)} %copy-done.9, bf16[144,1792]{1,0:T(8,128)(2,1)S(1)} %copy-done.13, ...), custom_call_target="tpu_custom_call" | custom-call | flops 2000000000 | bytes 8000000 | tf_op jit(solution)/shard_map/pallas_call | solution.py:371
  89.0 1.6 %collective-permute-start = (s32[2]{0:T(128)S(1)}, s32[2]{0:T(128)S(1)}, u32[]{:S(2)}, u32[]{:S(2)}) collective-permute-start(s32[2]{0:T(128)S(1)} %copy-done.16), channel_id=1, source_target_pairs={{0,16},{16,0},{1,17},{17,1},{2,18},{18,2},{3,19},{19,3},{4,20},{20... | collective-permute-start | bytes 32 | tf_op jit(solution)/shard_map/ppermute | solution.py:301
  90.6 5.0 %shard_map.88.refs_0_ = f32[384,1792]{1,0:T(8,128)S(1)} custom-call(s32[6]{0:T(128)S(1)} %stack.27.pos_ref.refs_0_, bf16[8,384,288]{2,1,0:T(8,128)(2,1)S(1)} %shard_map.85.blocks_ref.refs_0_, f32[384,1792]{1,0:T(8,128)S(1)} %shard_map.87.refs_0_, bf16[280,1792]{1,0:T(8,128)(2,1)} %collective-permute-done.6.refs_1_, ...), custom_call_target="tpu_custom_call", output_to_operand_aliasing={{}: (2, {})} | custom-call | flops 2000000000 | bytes 8000000 | tf_op jit(solution)/shard_map/pallas_call | solution.py:371
  95.6 4.4 %shard_map.89.refs_1_ = f32[384,1792]{1,0:T(8,128)S(1)} custom-call(s32[6]{0:T(128)S(1)} %stack.27.pos_ref.refs_0_, bf16[8,384,288]{2,1,0:T(8,128)(2,1)S(1)} %shard_map.85.blocks_ref.refs_0_, f32[384,1792]{1,0:T(8,128)S(1)} %shard_map.88.refs_0_, bf16[280,1792]{1,0:T(8,128)(2,1)} %collective-permute-done.12.refs_1_, ...), custom_call_target="tpu_custom_call", output_to_operand_aliasing={{}: (2, {})} | custom-call | flops 2000000000 | bytes 8000000 | tf_op jit(solution)/shard_map/pallas_call | solution.py:371
  100.0 5.2 %shard_map.91 = (bf16[192,560]{1,0:T(8,128)(2,1)S(1)}, bf16[192,560]{1,0:T(8,128)(2,1)S(1)}, bf16[20,16,128]{2,1,0:T(8,128)(2,1)S(1)}, bf16[20,16,128]{2,1,0:T(8...) custom-call(s32[6]{0:T(128)S(1)} %stack.27.pos_ref.refs_0_, ...), custom_call_target="tpu_custom_call" | custom-call | flops 2000000000 | bytes 8000000 | tf_op jit(solution)/shard_map/pallas_call | solution.py:391
  105.3 1.6 collective-permute-start.19
  106.8 2.0 %collective-permute-start.21 = (bf16[20,16,128]{2,1,0:T(8,128)(2,1)S(1)}, bf16[20,16,128]{2,1,0:T(8,128)(2,1)S(1)}, u32[]{:S(2)}, u32[]{:S(2)}) collective-permute-start(bf16[20,16,128]{2,1,0:T(8,128)(2,1)S(1)} %get-tuple-element.31), channel_id=1, source_target_pairs={{0,3},{1,2},{2,1},{3,0},{4,7},{5,6},{6,5},{7,4},{8,11},{9,10},{10,... | collective-permute-start | bytes 245768 | tf_op jit(solution)/shard_map/ppermute | solution.py:315
  109.3 5.7 %collective-permute-start.22 = (bf16[20,16,128]{2,1,0:T(8,128)(2,1)S(1)}, bf16[20,16,128]{2,1,0:T(8,128)(2,1)S(1)}, u32[]{:S(2)}, u32[]{:S(2)}) collective-permute-start(bf16[20,16,128]{2,1,0:T(8,128)(2,1)S(1)} %get-tuple-element.32), channel_id=1, source_target_pairs={{0,4},{1,5},{2,6},{3,7},{4,0},{5,1},{6,2},{7,3},{8,12},{9,13},{10,... | collective-permute-start | bytes 245768 | tf_op jit(solution)/shard_map/ppermute | solution.py:315
  115.1 0.9 collective-permute-start.23
  116.0 4.4 %collective-permute-start.24 = (bf16[20,16,128]{2,1,0:T(8,128)(2,1)S(1)}, bf16[20,16,128]{2,1,0:T(8,128)(2,1)S(1)}, u32[]{:S(2)}, u32[]{:S(2)}) collective-permute-start(bf16[20,16,128]{2,1,0:T(8,128)(2,1)S(1)} %get-tuple-element.34), channel_id=1, source_target_pairs={{0,6},{1,7},{2,4},{3,5},{4,2},{5,3},{6,0},{7,1},{8,14},{9,15},{10,... | collective-permute-start | bytes 245768 | tf_op jit(solution)/shard_map/ppermute | solution.py:315
  121.0 6.6 %collective-permute-done.23.refs_6_ = bf16[20,16,128]{2,1,0:T(8,128)(2,1)S(1)} collective-permute-done((bf16[20,16,128]{2,1,0:T(8,128)(2,1)S(1)}, bf16[20,16,128]{2,1,0:T(8,128)(2,1)S(1)}, u32[]{:S(2)}, u32[]{:S(2)}) %collective-permute-start.23) | collective-permute-done | bytes 81952 | tf_op jit(solution)/shard_map/ppermute | solution.py:315
  128.3 1.5 collective-permute-start.26
  129.8 2.6 %collective-permute-done.26.got_ref = bf16[10,16,128]{2,1,0:T(8,128)(2,1)S(1)} collective-permute-done((bf16[10,16,128]{2,1,0:T(8,128)(2,1)S(1)}, bf16[10,16,128]{2,1,0:T(8,128)(2,1)S(1)}, u32[]{:S(2)}, u32[]{:S(2)}) %collective-permute-start.26) | collective-permute-done | bytes 40992 | tf_op jit(solution)/shard_map/ppermute | solution.py:301
  133.0 1.5 collective-permute-start.34
  135.3 3.2 %collective-permute-start.28 = (bf16[20,16,128]{2,1,0:T(8,128)(2,1)S(1)}, bf16[20,16,128]{2,1,0:T(8,128)(2,1)S(1)}, u32[]{:S(2)}, u32[]{:S(2)}) collective-permute-start(bf16[20,16,128]{2,1,0:T(8,128)(2,1)S(1)} %shard_map.95.refs_0_), channel_id=1, source_target_pairs={{0,2},{1,3},{2,0},{3,1},{4,6},{5,7},{6,4},{7,5},{8,10},{9,11},{10,... | collective-permute-start | bytes 245768 | tf_op jit(solution)/shard_map/ppermute | solution.py:315
  138.5 0.9 collective-permute-start.29
  139.5 3.8 %collective-permute-start.30 = (bf16[20,16,128]{2,1,0:T(8,128)(2,1)S(1)}, bf16[20,16,128]{2,1,0:T(8,128)(2,1)S(1)}, u32[]{:S(2)}, u32[]{:S(2)}) collective-permute-start(bf16[20,16,128]{2,1,0:T(8,128)(2,1)S(1)} %shard_map.95.refs_0_), channel_id=1, source_target_pairs={{0,4},{1,5},{2,6},{3,7},{4,0},{5,1},{6,2},{7,3},{8,12},{9,13},{10,... | collective-permute-start | bytes 245768 | tf_op jit(solution)/shard_map/ppermute | solution.py:315
  143.2 1.5 collective-permute-start.31
  144.8 1.8 %collective-permute-start.32 = (bf16[20,16,128]{2,1,0:T(8,128)(2,1)S(1)}, bf16[20,16,128]{2,1,0:T(8,128)(2,1)S(1)}, u32[]{:S(2)}, u32[]{:S(2)}) collective-permute-start(bf16[20,16,128]{2,1,0:T(8,128)(2,1)S(1)} %shard_map.95.refs_0_), channel_id=1, source_target_pairs={{0,6},{1,7},{2,4},{3,5},{4,2},{5,3},{6,0},{7,1},{8,14},{9,15},{10,... | collective-permute-start | bytes 245768 | tf_op jit(solution)/shard_map/ppermute | solution.py:315
  146.6 2.9 %collective-permute-start.33 = (bf16[20,16,128]{2,1,0:T(8,128)(2,1)S(1)}, bf16[20,16,128]{2,1,0:T(8,128)(2,1)S(1)}, u32[]{:S(2)}, u32[]{:S(2)}) collective-permute-start(bf16[20,16,128]{2,1,0:T(8,128)(2,1)S(1)} %shard_map.95.refs_0_), channel_id=1, source_target_pairs={{0,7},{1,6},{2,5},{3,4},{4,3},{5,2},{6,1},{7,0},{8,15},{9,14},{10,... | collective-permute-start | bytes 245768 | tf_op jit(solution)/shard_map/ppermute | solution.py:315
  149.5 2.8 %shard_map.97.place_ref = s32[20]{0:T(128)S(1)} custom-call(s32[6]{0:T(128)S(1)} %stack.27.pos_ref.refs_0_, s32[80]{0:T(128)S(1)} %copy-done.17), custom_call_target="tpu_custom_call" | custom-call | bytes 1000 | tf_op jit(solution)/shard_map/pallas_call | solution.py:446
  152.3 0.9 shard_map.92.own_ref
  153.2 0.9 shard_map.93.other_ref
  154.7 2.2 %shard_map.96 = bf16[192,1120]{1,0:T(8,128)(2,1)} custom-call(s32[6]{0:T(128)S(1)} %stack.27.pos_ref.refs_0_, s32[2]{0:T(128)S(1)} %copy-done.16, bf16[192,640]{1,0:T(8,128)(2,1)S(1)} %shard_map.92.own_ref, bf16[192,640]{1,0:T(8,128)(2,1)S(1)} %shard_map.93.other_ref, bf16[20,16,128]{2,1,0:T(8,128)(2,1)S(1)} %shard_map.95.refs_0_, ...), custom_call_target="tpu_custom_call" | custom-call | flops 1500000000 | bytes 3000000 | tf_op jit(solution)/shard_map/pallas_call | solution.py:466
  156.9 1.3 shard_map.98
  (80 shorter events, 13.5 us)
Async XLA Ops:
  0.7 1.5 copy-start
  3.3 16.8 %collective-permute-start.4 = (bf16[280,1792]{1,0:T(8,128)(2,1)S(1)}, bf16[280,1792]{1,0:T(8,128)(2,1)S(1)}, u32[]{:S(2)}, u32[]{:S(2)}) collective-permute-start(bf16[280,1792]{1,0:T(8,128)(2,1)S(1)} %get-tuple-element.22.refs_0_), channel_id=1, source_target_pairs={{0,2},{2,4},{4,6},{14,12},{12,10},{10,8},{1,3},{3,5},{5,7},{15,13}... | collective-permute-start | bytes 3010568 | tf_op jit(solution)/shard_map/ppermute | solution.py:306
  20.0 3.8 %collective-permute-start.8 = (bf16[280,1792]{1,0:T(8,128)(2,1)S(1)}, bf16[280,1792]{1,0:T(8,128)(2,1)S(1)}, u32[]{:S(2)}, u32[]{:S(2)}) collective-permute-start(bf16[280,1792]{1,0:T(8,128)(2,1)S(1)} %collective-permute-done.4.refs_3_), channel_id=1, source_target_pairs={{2,4},{4,6},{12,10},{10,8},{3,5},{5,7},{13,11},{11,9},{18,20},{20,... | collective-permute-start | bytes 3010568 | tf_op jit(solution)/shard_map/ppermute | solution.py:306
  20.8 13.7 %collective-permute-start.2 = (bf16[144,1792]{1,0:T(8,128)(2,1)S(1)}, bf16[144,1792]{1,0:T(8,128)(2,1)S(1)}, u32[]{:S(2)}, u32[]{:S(2)}) collective-permute-start(bf16[144,1792]{1,0:T(8,128)(2,1)S(1)} %get-tuple-element.23), channel_id=1, source_target_pairs={{0,1},{1,0},{2,3},{3,2},{4,5},{5,4},{6,7},{7,6},{8,9},{9,8},{10,11... | collective-permute-start | bytes 1548296 | tf_op jit(solution)/shard_map/ppermute | solution.py:301
  22.3 21.6 %collective-permute-start.1 = (bf16[192,2240]{1,0:T(8,128)(2,1)}, bf16[192,2240]{1,0:T(8,128)(2,1)S(1)}, u32[]{:S(2)}, u32[]{:S(2)}) collective-permute-start(bf16[192,2240]{1,0:T(8,128)(2,1)} %bitcast.9), channel_id=1, source_target_pairs={{0,16},{16,0},{1,17},{17,1},{2,18},{18,2},{3,19},{19,3},{4,20},{20... | collective-permute-start | bytes 2580488 | tf_op jit(solution)/shard_map/ppermute | solution.py:301
  23.9 25.2 %collective-permute-start.14 = (bf16[280,1792]{1,0:T(8,128)(2,1)S(1)}, bf16[280,1792]{1,0:T(8,128)(2,1)S(1)}, u32[]{:S(2)}, u32[]{:S(2)}) collective-permute-start(bf16[280,1792]{1,0:T(8,128)(2,1)S(1)} %collective-permute-done.8.refs_3_), channel_id=1, source_target_pairs={{4,6},{10,8},{5,7},{11,9},{20,22},{26,24},{21,23},{27,25}} | collective-permute-start | bytes 3010568 | tf_op jit(solution)/shard_map/ppermute | solution.py:306
  34.5 12.1 %collective-permute-start.3 = (bf16[144,1792]{1,0:T(8,128)(2,1)S(1)}, bf16[144,1792]{1,0:T(8,128)(2,1)S(1)}, u32[]{:S(2)}, u32[]{:S(2)}) collective-permute-start(bf16[144,1792]{1,0:T(8,128)(2,1)S(1)} %collective-permute-done.2.refs_1_), channel_id=1, source_target_pairs={{0,8},{8,0},{1,9},{9,1},{2,10},{10,2},{3,11},{11,3},{4,12},{12,4},... | collective-permute-start | bytes 1548296 | tf_op jit(solution)/shard_map/ppermute | solution.py:301
  36.5 15.7 %collective-permute-start.10 = (bf16[144,1792]{1,0:T(8,128)(2,1)S(1)}, bf16[144,1792]{1,0:T(8,128)(2,1)S(1)}, u32[]{:S(2)}, u32[]{:S(2)}) collective-permute-start(bf16[144,1792]{1,0:T(8,128)(2,1)S(1)} %collective-permute-done.2.refs_1_), channel_id=1, source_target_pairs={{0,2},{1,3},{8,10},{9,11},{6,4},{7,5},{14,12},{15,13},{16,18},{17,... | collective-permute-start | bytes 1548296 | tf_op jit(solution)/shard_map/ppermute | solution.py:320
  41.6 14.5 %collective-permute-start.6 = (bf16[280,1792]{1,0:T(8,128)(2,1)S(1)}, bf16[280,1792]{1,0:T(8,128)(2,1)}, u32[]{:S(2)}, u32[]{:S(2)}) collective-permute-start(bf16[280,1792]{1,0:T(8,128)(2,1)S(1)} %collective-permute-done.4.refs_3_), channel_id=1, source_target_pairs={{4,5},{5,4},{6,7},{7,6},{8,9},{9,8},{10,11},{11,10},{20,21},{21,20... | collective-permute-start | bytes 3010568 | tf_op jit(solution)/shard_map/ppermute | solution.py:312
  44.9 11.9 %collective-permute-start.5 = (bf16[280,1792]{1,0:T(8,128)(2,1)S(1)}, bf16[280,1792]{1,0:T(8,128)(2,1)S(1)}, u32[]{:S(2)}, u32[]{:S(2)}) collective-permute-start(bf16[280,1792]{1,0:T(8,128)(2,1)S(1)} %collective-permute-done.4.refs_3_), channel_id=1, source_target_pairs={{0,8},{8,0},{1,9},{9,1},{2,10},{10,2},{3,11},{11,3},{4,12},{12,4},... | collective-permute-start | bytes 3010568 | tf_op jit(solution)/shard_map/ppermute | solution.py:301
  47.4 10.3 %collective-permute-start.12 = (bf16[280,1792]{1,0:T(8,128)(2,1)S(1)}, bf16[280,1792]{1,0:T(8,128)(2,1)}, u32[]{:S(2)}, u32[]{:S(2)}) collective-permute-start(bf16[280,1792]{1,0:T(8,128)(2,1)S(1)} %collective-permute-done.8.refs_3_), channel_id=1, source_target_pairs={{4,5},{5,4},{6,7},{7,6},{8,9},{9,8},{10,11},{11,10},{20,21},{21,20... | collective-permute-start | bytes 3010568 | tf_op jit(solution)/shard_map/ppermute | solution.py:312
  49.0 18.5 %collective-permute-start.16 = (bf16[280,1792]{1,0:T(8,128)(2,1)S(1)}, bf16[280,1792]{1,0:T(8,128)(2,1)}, u32[]{:S(2)}, u32[]{:S(2)}) collective-permute-start(bf16[280,1792]{1,0:T(8,128)(2,1)S(1)} %collective-permute-done.14.refs_3_), channel_id=1, source_target_pairs={{6,7},{7,6},{8,9},{9,8},{22,23},{23,22},{24,25},{25,24}} | collective-permute-start | bytes 3010568 | tf_op jit(solution)/shard_map/ppermute | solution.py:312
  52.2 2.7 %collective-permute-start.11 = (bf16[144,1792]{1,0:T(8,128)(2,1)S(1)}, bf16[144,1792]{1,0:T(8,128)(2,1)S(1)}, u32[]{:S(2)}, u32[]{:S(2)}) collective-permute-start(bf16[144,1792]{1,0:T(8,128)(2,1)S(1)} %collective-permute-done.10.refs_5_), channel_id=1, source_target_pairs={{0,8},{8,0},{1,9},{9,1},{2,10},{10,2},{3,11},{11,3},{4,12},{12,4},... | collective-permute-start | bytes 1548296 | tf_op jit(solution)/shard_map/ppermute | solution.py:301
  55.7 33.3 %collective-permute-start.9 = (bf16[280,1792]{1,0:T(8,128)(2,1)S(1)}, bf16[280,1792]{1,0:T(8,128)(2,1)}, u32[]{:S(2)}, u32[]{:S(2)}) collective-permute-start(bf16[280,1792]{1,0:T(8,128)(2,1)S(1)} %collective-permute-done.8.refs_3_), channel_id=1, source_target_pairs={{0,8},{8,0},{1,9},{9,1},{2,10},{10,2},{3,11},{11,3},{4,12},{12,4},... | collective-permute-start | bytes 3010568 | tf_op jit(solution)/shard_map/ppermute | solution.py:301
  56.1 34.5 %collective-permute-start.7 = (bf16[280,1792]{1,0:T(8,128)(2,1)}, bf16[280,1792]{1,0:T(8,128)(2,1)}, u32[]{:S(2)}, u32[]{:S(2)}) collective-permute-start(bf16[280,1792]{1,0:T(8,128)(2,1)} %collective-permute-done.6.refs_1_), channel_id=1, source_target_pairs={{0,8},{8,0},{1,9},{9,1},{2,10},{10,2},{3,11},{11,3},{4,12},{12,4},... | collective-permute-start | bytes 3010568 | tf_op jit(solution)/shard_map/ppermute | solution.py:301
  57.7 37.9 %collective-permute-start.15 = (bf16[280,1792]{1,0:T(8,128)(2,1)S(1)}, bf16[280,1792]{1,0:T(8,128)(2,1)}, u32[]{:S(2)}, u32[]{:S(2)}) collective-permute-start(bf16[280,1792]{1,0:T(8,128)(2,1)S(1)} %collective-permute-done.14.refs_3_), channel_id=1, source_target_pairs={{0,8},{8,0},{1,9},{9,1},{2,10},{10,2},{3,11},{11,3},{4,12},{12,4},... | collective-permute-start | bytes 3010568 | tf_op jit(solution)/shard_map/ppermute | solution.py:301
  57.7 37.9 %collective-permute-start.13 = (bf16[280,1792]{1,0:T(8,128)(2,1)}, bf16[280,1792]{1,0:T(8,128)(2,1)}, u32[]{:S(2)}, u32[]{:S(2)}) collective-permute-start(bf16[280,1792]{1,0:T(8,128)(2,1)} %collective-permute-done.12.refs_1_), channel_id=1, source_target_pairs={{0,8},{8,0},{1,9},{9,1},{2,10},{10,2},{3,11},{11,3},{4,12},{12,4},... | collective-permute-start | bytes 3010568 | tf_op jit(solution)/shard_map/ppermute | solution.py:301
  67.5 32.5 %collective-permute-start.17 = (bf16[280,1792]{1,0:T(8,128)(2,1)}, bf16[280,1792]{1,0:T(8,128)(2,1)}, u32[]{:S(2)}, u32[]{:S(2)}) collective-permute-start(bf16[280,1792]{1,0:T(8,128)(2,1)} %collective-permute-done.16.refs_2_), channel_id=1, source_target_pairs={{0,8},{8,0},{1,9},{9,1},{2,10},{10,2},{3,11},{11,3},{4,12},{12,4},... | collective-permute-start | bytes 3010568 | tf_op jit(solution)/shard_map/ppermute | solution.py:301
  79.9 4.6 %copy-start.2 = (bf16[280,1792]{1,0:T(8,128)(2,1)S(1)}, bf16[280,1792]{1,0:T(8,128)(2,1)}, u32[]{:S(2)}) copy-start(bf16[280,1792]{1,0:T(8,128)(2,1)} %copy-done.1) | copy-start | bytes 3010564
  79.9 4.6 %copy-start.4 = (bf16[280,1792]{1,0:T(8,128)(2,1)S(1)}, bf16[280,1792]{1,0:T(8,128)(2,1)}, u32[]{:S(2)}) copy-start(bf16[280,1792]{1,0:T(8,128)(2,1)} %copy-done.3) | copy-start | bytes 3010564
  80.8 1.2 copy-start.5
  82.0 1.2 copy-start.7
  83.1 1.3 copy-start.9
  83.1 1.4 copy-start.13
  84.5 4.5 %copy-start.16 = (s32[2]{0:T(128)S(1)}, s32[2]{0:T(128)}, u32[]{:S(2)}) copy-start(s32[2]{0:T(128)} %near_ref.3) | copy-start | bytes 28
  84.5 6.1 %copy-start.11 = (bf16[144,1792]{1,0:T(8,128)(2,1)S(1)}, bf16[144,1792]{1,0:T(8,128)(2,1)}, u32[]{:S(2)}) copy-start(bf16[144,1792]{1,0:T(8,128)(2,1)} %copy-done.10) | copy-start | bytes 1548292
  84.5 6.1 %copy-start.15 = (bf16[144,1792]{1,0:T(8,128)(2,1)S(1)}, bf16[144,1792]{1,0:T(8,128)(2,1)}, u32[]{:S(2)}) copy-start(bf16[144,1792]{1,0:T(8,128)(2,1)} %copy-done.14) | copy-start | bytes 1548292
  89.0 11.0 %collective-permute-start = (s32[2]{0:T(128)S(1)}, s32[2]{0:T(128)S(1)}, u32[]{:S(2)}, u32[]{:S(2)}) collective-permute-start(s32[2]{0:T(128)S(1)} %copy-done.16), channel_id=1, source_target_pairs={{0,16},{16,0},{1,17},{17,1},{2,18},{18,2},{3,19},{19,3},{4,20},{20... | collective-permute-start | bytes 32 | tf_op jit(solution)/shard_map/ppermute | solution.py:301
  100.0 49.4 %copy-start.17 = (s32[80]{0:T(128)S(1)}, s32[80]{0:T(128)}, u32[]{:S(2)}) copy-start(s32[80]{0:T(128)} %new_ref.1) | copy-start | bytes 964
  105.3 9.8 %collective-permute-start.19 = (bf16[20,16,128]{2,1,0:T(8,128)(2,1)S(1)}, bf16[20,16,128]{2,1,0:T(8,128)(2,1)S(1)}, u32[]{:S(2)}, u32[]{:S(2)}) collective-permute-start(bf16[20,16,128]{2,1,0:T(8,128)(2,1)S(1)} %get-tuple-element.29), channel_id=1, source_target_pairs={{0,1},{1,0},{2,3},{3,2},{4,5},{5,4},{6,7},{7,6},{8,9},{9,8},{10,11... | collective-permute-start | bytes 245768 | tf_op jit(solution)/shard_map/ppermute | solution.py:315
  106.8 9.1 %collective-permute-start.20 = (bf16[20,16,128]{2,1,0:T(8,128)(2,1)S(1)}, bf16[20,16,128]{2,1,0:T(8,128)(2,1)S(1)}, u32[]{:S(2)}, u32[]{:S(2)}) collective-permute-start(bf16[20,16,128]{2,1,0:T(8,128)(2,1)S(1)} %get-tuple-element.30), channel_id=1, source_target_pairs={{0,2},{1,3},{2,0},{3,1},{4,6},{5,7},{6,4},{7,5},{8,10},{9,11},{10,... | collective-permute-start | bytes 245768 | tf_op jit(solution)/shard_map/ppermute | solution.py:315
  106.8 13.5 %collective-permute-start.21 = (bf16[20,16,128]{2,1,0:T(8,128)(2,1)S(1)}, bf16[20,16,128]{2,1,0:T(8,128)(2,1)S(1)}, u32[]{:S(2)}, u32[]{:S(2)}) collective-permute-start(bf16[20,16,128]{2,1,0:T(8,128)(2,1)S(1)} %get-tuple-element.31), channel_id=1, source_target_pairs={{0,3},{1,2},{2,1},{3,0},{4,7},{5,6},{6,5},{7,4},{8,11},{9,10},{10,... | collective-permute-start | bytes 245768 | tf_op jit(solution)/shard_map/ppermute | solution.py:315
  108.8 37.8 %collective-permute-start.18 = (bf16[192,560]{1,0:T(8,128)(2,1)S(1)}, bf16[192,560]{1,0:T(8,128)(2,1)S(1)}, u32[]{:S(2)}, u32[]{:S(2)}) collective-permute-start(bf16[192,560]{1,0:T(8,128)(2,1)S(1)} %get-tuple-element.27), channel_id=1, source_target_pairs={{0,16},{16,0},{1,17},{17,1},{2,18},{18,2},{3,19},{19,3},{4,20},{20... | collective-permute-start | bytes 645128 | tf_op jit(solution)/shard_map/ppermute | solution.py:301
  109.3 11.7 %collective-permute-start.22 = (bf16[20,16,128]{2,1,0:T(8,128)(2,1)S(1)}, bf16[20,16,128]{2,1,0:T(8,128)(2,1)S(1)}, u32[]{:S(2)}, u32[]{:S(2)}) collective-permute-start(bf16[20,16,128]{2,1,0:T(8,128)(2,1)S(1)} %get-tuple-element.32), channel_id=1, source_target_pairs={{0,4},{1,5},{2,6},{3,7},{4,0},{5,1},{6,2},{7,3},{8,12},{9,13},{10,... | collective-permute-start | bytes 245768 | tf_op jit(solution)/shard_map/ppermute | solution.py:315
  115.1 12.6 %collective-permute-start.23 = (bf16[20,16,128]{2,1,0:T(8,128)(2,1)S(1)}, bf16[20,16,128]{2,1,0:T(8,128)(2,1)S(1)}, u32[]{:S(2)}, u32[]{:S(2)}) collective-permute-start(bf16[20,16,128]{2,1,0:T(8,128)(2,1)S(1)} %get-tuple-element.33), channel_id=1, source_target_pairs={{0,5},{1,4},{2,7},{3,6},{4,1},{5,0},{6,3},{7,2},{8,13},{9,12},{10,... | collective-permute-start | bytes 245768 | tf_op jit(solution)/shard_map/ppermute | solution.py:315
  116.0 11.7 %collective-permute-start.24 = (bf16[20,16,128]{2,1,0:T(8,128)(2,1)S(1)}, bf16[20,16,128]{2,1,0:T(8,128)(2,1)S(1)}, u32[]{:S(2)}, u32[]{:S(2)}) collective-permute-start(bf16[20,16,128]{2,1,0:T(8,128)(2,1)S(1)} %get-tuple-element.34), channel_id=1, source_target_pairs={{0,6},{1,7},{2,4},{3,5},{4,2},{5,3},{6,0},{7,1},{8,14},{9,15},{10,... | collective-permute-start | bytes 245768 | tf_op jit(solution)/shard_map/ppermute | solution.py:315
  120.4 7.3 %collective-permute-start.25 = (bf16[20,16,128]{2,1,0:T(8,128)(2,1)S(1)}, bf16[20,16,128]{2,1,0:T(8,128)(2,1)S(1)}, u32[]{:S(2)}, u32[]{:S(2)}) collective-permute-start(bf16[20,16,128]{2,1,0:T(8,128)(2,1)S(1)} %get-tuple-element.35), channel_id=1, source_target_pairs={{0,7},{1,6},{2,5},{3,4},{4,3},{5,2},{6,1},{7,0},{8,15},{9,14},{10,... | collective-permute-start | bytes 245768 | tf_op jit(solution)/shard_map/ppermute | solution.py:315
  128.3 4.1 %collective-permute-start.26 = (bf16[10,16,128]{2,1,0:T(8,128)(2,1)S(1)}, bf16[10,16,128]{2,1,0:T(8,128)(2,1)S(1)}, u32[]{:S(2)}, u32[]{:S(2)}) collective-permute-start(bf16[10,16,128]{2,1,0:T(8,128)(2,1)S(1)} %get-tuple-element.37), channel_id=1, source_target_pairs={{0,16},{16,0},{1,17},{17,1},{2,18},{18,2},{3,19},{19,3},{4,20},{20... | collective-permute-start | bytes 122888 | tf_op jit(solution)/shard_map/ppermute | solution.py:301
  133.0 6.5 %collective-permute-start.34 = (bf16[20,16,128]{2,1,0:T(8,128)(2,1)S(1)}, bf16[20,16,128]{2,1,0:T(8,128)(2,1)S(1)}, u32[]{:S(2)}, u32[]{:S(2)}) collective-permute-start(bf16[20,16,128]{2,1,0:T(8,128)(2,1)S(1)} %shard_map.95.refs_0_), channel_id=1, source_target_pairs={{0,16},{8,24},{16,0},{24,8},{1,17},{9,25},{17,1},{25,9},{2,18},{10... | collective-permute-start | bytes 245768 | tf_op jit(solution)/shard_map/ppermute | solution.py:442
  134.5 8.8 %collective-permute-start.27 = (bf16[20,16,128]{2,1,0:T(8,128)(2,1)S(1)}, bf16[20,16,128]{2,1,0:T(8,128)(2,1)S(1)}, u32[]{:S(2)}, u32[]{:S(2)}) collective-permute-start(bf16[20,16,128]{2,1,0:T(8,128)(2,1)S(1)} %shard_map.95.refs_0_), channel_id=1, source_target_pairs={{0,1},{1,0},{2,3},{3,2},{4,5},{5,4},{6,7},{7,6},{8,9},{9,8},{10,11... | collective-permute-start | bytes 245768 | tf_op jit(solution)/shard_map/ppermute | solution.py:315
  135.3 9.5 %collective-permute-start.28 = (bf16[20,16,128]{2,1,0:T(8,128)(2,1)S(1)}, bf16[20,16,128]{2,1,0:T(8,128)(2,1)S(1)}, u32[]{:S(2)}, u32[]{:S(2)}) collective-permute-start(bf16[20,16,128]{2,1,0:T(8,128)(2,1)S(1)} %shard_map.95.refs_0_), channel_id=1, source_target_pairs={{0,2},{1,3},{2,0},{3,1},{4,6},{5,7},{6,4},{7,5},{8,10},{9,11},{10,... | collective-permute-start | bytes 245768 | tf_op jit(solution)/shard_map/ppermute | solution.py:315
  138.5 15.6 %collective-permute-start.29 = (bf16[20,16,128]{2,1,0:T(8,128)(2,1)S(1)}, bf16[20,16,128]{2,1,0:T(8,128)(2,1)S(1)}, u32[]{:S(2)}, u32[]{:S(2)}) collective-permute-start(bf16[20,16,128]{2,1,0:T(8,128)(2,1)S(1)} %shard_map.95.refs_0_), channel_id=1, source_target_pairs={{0,3},{1,2},{2,1},{3,0},{4,7},{5,6},{6,5},{7,4},{8,11},{9,10},{10,... | collective-permute-start | bytes 245768 | tf_op jit(solution)/shard_map/ppermute | solution.py:315
  139.5 14.7 %collective-permute-start.30 = (bf16[20,16,128]{2,1,0:T(8,128)(2,1)S(1)}, bf16[20,16,128]{2,1,0:T(8,128)(2,1)S(1)}, u32[]{:S(2)}, u32[]{:S(2)}) collective-permute-start(bf16[20,16,128]{2,1,0:T(8,128)(2,1)S(1)} %shard_map.95.refs_0_), channel_id=1, source_target_pairs={{0,4},{1,5},{2,6},{3,7},{4,0},{5,1},{6,2},{7,3},{8,12},{9,13},{10,... | collective-permute-start | bytes 245768 | tf_op jit(solution)/shard_map/ppermute | solution.py:315
  143.2 11.4 %collective-permute-start.31 = (bf16[20,16,128]{2,1,0:T(8,128)(2,1)S(1)}, bf16[20,16,128]{2,1,0:T(8,128)(2,1)S(1)}, u32[]{:S(2)}, u32[]{:S(2)}) collective-permute-start(bf16[20,16,128]{2,1,0:T(8,128)(2,1)S(1)} %shard_map.95.refs_0_), channel_id=1, source_target_pairs={{0,5},{1,4},{2,7},{3,6},{4,1},{5,0},{6,3},{7,2},{8,13},{9,12},{10,... | collective-permute-start | bytes 245768 | tf_op jit(solution)/shard_map/ppermute | solution.py:315
  144.8 9.9 %collective-permute-start.32 = (bf16[20,16,128]{2,1,0:T(8,128)(2,1)S(1)}, bf16[20,16,128]{2,1,0:T(8,128)(2,1)S(1)}, u32[]{:S(2)}, u32[]{:S(2)}) collective-permute-start(bf16[20,16,128]{2,1,0:T(8,128)(2,1)S(1)} %shard_map.95.refs_0_), channel_id=1, source_target_pairs={{0,6},{1,7},{2,4},{3,5},{4,2},{5,3},{6,0},{7,1},{8,14},{9,15},{10,... | collective-permute-start | bytes 245768 | tf_op jit(solution)/shard_map/ppermute | solution.py:315
  146.6 8.1 %collective-permute-start.33 = (bf16[20,16,128]{2,1,0:T(8,128)(2,1)S(1)}, bf16[20,16,128]{2,1,0:T(8,128)(2,1)S(1)}, u32[]{:S(2)}, u32[]{:S(2)}) collective-permute-start(bf16[20,16,128]{2,1,0:T(8,128)(2,1)S(1)} %shard_map.95.refs_0_), channel_id=1, source_target_pairs={{0,7},{1,6},{2,5},{3,4},{4,3},{5,2},{6,1},{7,0},{8,15},{9,14},{10,... | collective-permute-start | bytes 245768 | tf_op jit(solution)/shard_map/ppermute | solution.py:315
  154.1 2.8 %collective-permute-start.35 = (bf16[20,16,128]{2,1,0:T(8,128)(2,1)S(1)}, bf16[20,16,128]{2,1,0:T(8,128)(2,1)S(1)}, u32[]{:S(2)}, u32[]{:S(2)}) collective-permute-start(bf16[20,16,128]{2,1,0:T(8,128)(2,1)S(1)} %shard_map.95.refs_0_), channel_id=1, source_target_pairs={{0,8},{8,0},{16,24},{24,16},{1,9},{9,1},{17,25},{25,17},{2,10},{10... | collective-permute-start | bytes 245768 | tf_op jit(solution)/shard_map/ppermute | solution.py:442
  154.2 2.7 %collective-permute-start.36 = (bf16[20,16,128]{2,1,0:T(8,128)(2,1)S(1)}, bf16[20,16,128]{2,1,0:T(8,128)(2,1)S(1)}, u32[]{:S(2)}, u32[]{:S(2)}) collective-permute-start(bf16[20,16,128]{2,1,0:T(8,128)(2,1)S(1)} %collective-permute-done.34.refs_1_), channel_id=1, source_target_pairs={{0,8},{8,0},{16,24},{24,16},{1,9},{9,1},{17,25},{25,17},{2,10},{10... | collective-permute-start | bytes 245768 | tf_op jit(solution)/shard_map/ppermute | solution.py:442
  (7 other events, 6.1 us)

commit v3 on v2

--- a/solution.py
+++ b/solution.py
@@ -14,7 +14,34 @@
 LANES = 128
 VMEM = pl.BlockSpec(memory_space=pltpu.VMEM)
 SMEM = pl.BlockSpec(memory_space=pltpu.SMEM)
+SPECS = {"s": SMEM, "v": VMEM, "h": pl.BlockSpec(memory_space=pltpu.HBM)}
 SWAP = [(0, 1), (1, 0)]
+
+
+def swap_plan():
+    spots = [(c, z, x) for c in range(2) for z in range(4) for x in range(2)]
+    partners, sent, held = [], [], [{(c, z, x): (z, x) for c, z, x in spots}]
+    for k in range(1, 5):
+        pair, send = {}, {}
+        for c, z, x in spots:
+            end = z in (0, 3)
+            line = (c, z ^ 1, x)
+            side = (c, z, 1 - x)
+            middle = side if end else (c, 3 - z, x)
+            straight = c == (k + 1) % 2
+            if k < 3:
+                pair[c, z, x] = line if straight else middle
+            else:
+                pair[c, z, x] = line if straight == (k == 3) else side
+            send[c, z, x] = k - 1
+            if k == 4:
+                pair[c, z, x] = side if c == 0 else line
+            if not end and ((k == 3 and c == 1) or (k == 4 and c == 0)):
+                send[c, z, x] = k - 2
+        partners.append(pair)
+        sent.append(send)
+        held.append({spot: held[send[pair[spot]]][pair[spot]] for spot in spots})
+    return partners, sent, held
 
 
 def phi(u):
@@ -25,7 +52,7 @@
     return pl.pallas_call(
         kernel,
         out_shape=out_shape,
-        in_specs=[SMEM if kind == "s" else VMEM for kind in kinds],
+        in_specs=[SPECS[kind] for kind in kinds],
         scratch_shapes=scratch,
         input_output_aliases=alias or {},
         out_specs=SMEM if smem else jax.tree.map(lambda _: VMEM, out_shape),
@@ -34,29 +61,49 @@
     )
 
 
-def prep_kernel(pos_ref, w_ref, mine_ref, piece_ref):
-    depth, total = w_ref.shape
-    half = piece_ref.shape[0]
+def prep_kernel(kinds, pos_ref, w_hbm, out_ref, w_ref, sems):
+    depth, total = w_hbm.shape
     width = total // 6
-    wide = mine_ref.shape[1]
-    for turn in range(2):
-
-        @pl.when(pos_ref[3] == turn)
-        def _():
-            for j, part in enumerate((1, 2, 0)):
-                start = (2 * part + turn) * width
-                mine_ref[:, j * width : (j + 1) * width] = w_ref[:, start : start + width]
-
-    mine_ref[:, 3 * width :] = jnp.zeros((depth, wide - 3 * width), BF16)
-
-    @pl.when(pos_ref[2] == 0)
+    cuts = sems.shape[0]
+    edges = [depth * i // cuts // 8 * 8 for i in range(cuts)] + [depth]
+    spans = list(zip(edges, edges[1:]))
+    low = min(kinds) * 2 * width // LANES * LANES
+    high = min(-(-(max(kinds) + 1) * 2 * width // LANES) * LANES, total)
+    copies = []
+    for i, (lo, hi) in enumerate(spans):
+        if high == total:
+            low, source, target = 0, w_hbm.at[lo:hi], w_ref.at[lo:hi]
+        else:
+            source, target = w_hbm.at[lo:hi, low:high], w_ref.at[lo:hi, : high - low]
+        copies.append(pltpu.make_async_copy(source, target, sems.at[i]))
+    for copy in copies:
+        copy.start()
+    used = len(kinds) * width
+    if used < out_ref.shape[1]:
+        out_ref[:, used:] = jnp.zeros((depth, out_ref.shape[1] - used), BF16)
+    for copy, (lo, hi) in zip(copies, spans):
+        copy.wait()
+        for turn in range(2):
+
+            @pl.when(pos_ref[3] == turn)
+            def _():
+                for j, kind in enumerate(kinds):
+                    start = (2 * kind + turn) * width - low
+                    out_ref[lo:hi, j * width : (j + 1) * width] = w_ref[
+                        lo:hi, start : start + width
+                    ]
+
+
+def choose_kernel(core, pos_ref, early_ref, late_ref, out_ref):
+    early = (pos_ref[6] == 1) & (pos_ref[2] == core)
+
+    @pl.when(early)
     def _():
-        piece_ref[...] = mine_ref[:half]
-
-    @pl.when(pos_ref[2] == 1)
+        out_ref[...] = early_ref[...]
+
+    @pl.when(jnp.logical_not(early))
     def _():
-        piece_ref[: depth - half] = mine_ref[half:]
-        piece_ref[depth - half :] = jnp.zeros((2 * half - depth, wide), BF16)
+        out_ref[...] = late_ref[...]
 
 
 def table_kernel(heads, rows, pos_ref, state_ref, ksum_ref, group_ref, plain_ref, old_ref):
@@ -91,87 +138,83 @@
 
 
 def block_kernel(pos_ref, own_ref, other_ref, out_ref):
-    members, both, wide = out_ref.shape
+    members, both, _ = out_ref.shape
     count = both // 2
     depth = own_ref.shape[1] // members
     for b in range(members):
         out_ref[b, :count, :depth] = own_ref[:, b * depth : (b + 1) * depth]
         out_ref[b, count:, :depth] = other_ref[:, b * depth : (b + 1) * depth]
-        if wide > depth:
-            out_ref[b, :, depth:] = jnp.zeros((both, wide - depth), BF16)
-
-
-def hops(n, pos_ref, k, cross):
-    z, x, c = pos_ref[0], pos_ref[1], pos_ref[2]
-    col = 1 - x if cross else x
-    first = 2 if cross and k == 1 else k
-    up, down = lax.rem(z - k + n, n), lax.rem(z + k, n)
-    if 2 * first > n - 1:
-        return (jnp.where(z >= first, up, down) * 2 + col,)
-    return (jnp.where(c == 0, up, down) * 2 + col, jnp.where(c == 0, down, up) * 2 + col)
-
-
-def add_products(n, plan, pos_ref, blocks_ref, refs, tile):
+
+
+def add_products(slots, pos_ref, blocks_ref, refs, tile):
+    terms = []
+    if slots == ("core",):
+        first = pos_ref[2] == 0
+        weight = jnp.where(first, refs[0][:, tile], refs[1][:, tile])
+        terms = [(jnp.where(first, pos_ref[14], pos_ref[15]), weight)]
+    elif slots == ("all",):
+        terms = [(b, refs[0][b, :, tile]) for b in range(refs[0].shape[0])]
+    else:
+        terms = [(pos_ref[slot], ref[:, tile]) for slot, ref in zip(slots, refs)]
     total = None
-    refs = list(refs)
-    for kind, k in plan:
-        if kind == "own":
-            terms = [(pos_ref[0] * 2 + pos_ref[1], refs.pop(0)[:, tile])]
-        elif kind in ("beside", "corner"):
-            here, there = refs.pop(0)[:, tile], refs.pop(0)[:, tile]
-            first = pos_ref[2] == 0
-            line = pos_ref[0]
-            if kind == "corner":
-                line = jnp.where(line <= 1, 0, n - 1)
-            both = jnp.concatenate(
-                [jnp.where(first, here, there), jnp.where(first, there, here)], axis=0
-            )
-            terms = [(line * 2 + 1 - pos_ref[1], both)]
-        else:
-            here, there = refs.pop(0)[:, tile], refs.pop(0)[:, tile]
-            ids = hops(n, pos_ref, k, kind == "across")
-            terms = [(ids[0], here + there)] if len(ids) == 1 else list(zip(ids, (here, there)))
-        for index, weight in terms:
-            lhs = blocks_ref[index, :, : weight.shape[0]]
-            term = jnp.dot(lhs, weight, preferred_element_type=F32)
-            total = term if total is None else total + term
+    for index, weight in terms:
+        term = jnp.dot(blocks_ref[index], weight, preferred_element_type=F32)
+        total = term if total is None else total + term
     return total
 
 
-def mul_kernel(n, plan, fresh, pos_ref, blocks_ref, *refs):
+def column_step(wide):
+    return next(step for step in (384, 256, LANES) if wide % step == 0)
+
+
+def mul_kernel(slots, fresh, pos_ref, blocks_ref, *refs):
     acc_ref = refs[-1]
     given = refs[:-1] if fresh else refs[1:-1]
-    wide = acc_ref.shape[1]
-    step = 256 if wide % 256 == 0 else LANES
-
-    @pl.loop(0, wide // step)
+    step = column_step(acc_ref.shape[1])
+
+    @pl.loop(0, acc_ref.shape[1] // step)
     def _(t):
         tile = pl.ds(pl.multiple_of(t * step, step), step)
-        term = add_products(n, plan, pos_ref, blocks_ref, given, tile)
+        term = add_products(slots, pos_ref, blocks_ref, given, tile)
         acc_ref[:, tile] = term if fresh else refs[0][:, tile] + term
 
 
-def kv_kernel(n, plan, streams, frames, heads, size, rows, pos_ref, near_ref, far_ref, *refs):
-    blocks_ref, old_ref, refs = refs[0], refs[1], refs[2:]
-    given, refs = refs[: 2 * len(plan)], refs[2 * len(plan) :]
-    group_ref, plain_ref, mine_ref, give_ref = refs[:4]
-    chunks, acc_ref = refs[4:-1], refs[-1]
-    wide = acc_ref.shape[1]
-    step = 256 if wide % 256 == 0 else LANES
-
-    @pl.loop(0, wide // step)
+def ask_kernel(slots, width, pos_ref, blocks_ref, old_ref, group_ref, *refs):
+    given, (mine_ref, give_ref, acc_ref) = refs[:-3], refs[-3:]
+    step = column_step(acc_ref.shape[1])
+
+    @pl.loop(0, acc_ref.shape[1] // step)
     def _(t):
         tile = pl.ds(pl.multiple_of(t * step, step), step)
         acc_ref[:, tile] = old_ref[:, tile] + add_products(
-            n, plan, pos_ref, blocks_ref, given, tile
+            slots, pos_ref, blocks_ref, given, tile
+        )
+
+    count = acc_ref.shape[0] // 2
+    give_ref[...] = acc_ref[count:, :width].astype(BF16)
+    raw = acc_ref[:count, :width].astype(BF16)
+    queried = phi(raw.astype(F32)).astype(BF16)
+    mine_ref[...] = jnp.dot(queried, group_ref[...], preferred_element_type=F32).astype(BF16)
+
+
+def kv_kernel(slots, streams, frames, heads, size, rows, pos_ref, near_ref, far_ref, *refs):
+    blocks_ref, old_ref, refs = refs[0], refs[1], refs[2:]
+    count = 2 if slots == ("core",) else 1
+    given, refs = refs[:count], refs[count:]
+    group_ref, plain_ref = refs[:2]
+    chunks, acc_ref = refs[2:-1], refs[-1]
+    step = column_step(acc_ref.shape[1])
+
+    @pl.loop(0, acc_ref.shape[1] // step)
+    def _(t):
+        tile = pl.ds(pl.multiple_of(t * step, step), step)
+        acc_ref[:, tile] = old_ref[:, tile] + add_products(
+            slots, pos_ref, blocks_ref, given, tile
         )
 
     width = heads * size
     count = acc_ref.shape[0] // 2
     tokens = count // streams
-    asked = acc_ref[:, 2 * width : 3 * width].astype(BF16)
-    mine_ref[...] = asked[:count]
-    give_ref[...] = asked[count:]
     frame = lax.broadcasted_iota(jnp.int32, (tokens, width), 0) // (tokens // frames)
     masks = [frame < ref[s] for ref in (near_ref, far_ref) for s in range(streams)]
     live = jnp.concatenate([jnp.where(mask, 1.0, 0.0) for mask in masks], axis=0)
@@ -294,59 +337,73 @@
     owners = lax.axis_size("o") * 4
     me = (o * 2 + y) * 2 + c
 
-    def flat(cc, zz, xx):
-        return (cc * n + zz) * 2 + xx
-
     def swap(axis, v):
         return lax.ppermute(v, axis, SWAP)
 
-    def hop(k, v):
-        pairs = [(i, i + 1) for i in range(k - 1, n - 1)]
-        pairs += [(n + i, n + i - 1) for i in range(n - k, 0, -1)]
-        return lax.ppermute(v, ("c", "z"), pairs)
-
-    def across(k, v):
-        first = 2 if k == 1 else k
-        pairs = [(flat(0, i, a), flat(0, i, 1 - a)) for i in range(first, n) for a in range(2)]
-        pairs += [(flat(1, i, a), flat(1, i, 1 - a)) for i in range(n - first) for a in range(2)]
-        return lax.ppermute(v, ("c", "z", "x"), pairs)
-
     def xor(k, v):
         return lax.ppermute(v, ("z", "x"), [(i, i ^ k) for i in range(members)])
 
-    def near_end(v):
-        pairs = [(flat(i, 0, a), flat(i, 1, a)) for i in range(2) for a in range(2)]
-        pairs += [(flat(i, n - 1, a), flat(i, n - 2, a)) for i in range(2) for a in range(2)]
-        return lax.ppermute(v, ("c", "z", "x"), pairs)
-
-    pos = jnp.stack([z, x, c, y, m, me]).astype(jnp.int32)
-    wide = -(-3 * width // LANES) * LANES
-    half = -(-depth // 32) * 16
-    mine, piece = whole_call(
-        prep_kernel,
-        [jax.ShapeDtypeStruct((depth, wide), BF16), jax.ShapeDtypeStruct((half, wide), BF16)],
-        "sv",
-        0,
-        4_000_000,
-    )(pos, w_qkv)
+    fast = n == 4
+    spot = (c * n + z) * 2 + x
+    pos = [z, x, c, y, m, me]
+    if fast:
+        partners, sent, held = swap_plan()
+        spots = [(i, j, k) for i in range(2) for j in range(n) for k in range(2)]
+        table = []
+        for i, j, k in spots:
+            row = [int(sent[2][i, j, k] == 1 or sent[3][i, j, k] == 2), j * 2 + k]
+            for got in held[1:]:
+                for line, side in (got[i, j, k], got[1 - i, j, k]):
+                    row.append(line * 2 + side)
+            table.append(row)
+        own_row = jnp.asarray(table, jnp.int32)[spot]
+        place_of = jnp.stack(pos).astype(jnp.int32)
+        pos = jnp.concatenate([place_of, own_row])
+    else:
+        pos = place_of = jnp.stack(pos).astype(jnp.int32)
+    wide_kv = -(-2 * width // LANES) * LANES
+    wide_q = -(-width // LANES) * LANES
+
+    def prep(kinds, wide):
+        return whole_call(
+            functools.partial(prep_kernel, kinds),
+            jax.ShapeDtypeStruct((depth, wide), BF16),
+            "sh",
+            0,
+            2_000_000,
+            scratch=[pltpu.VMEM(w_qkv.shape, BF16), pltpu.SemaphoreType.DMA((5,))],
+        )(place_of, w_qkv)
+
+    pieces = [prep((1, 2), wide_kv), prep((0,), wide_q)]
+
+    def choose(core, early, late):
+        return whole_call(
+            functools.partial(choose_kernel, core),
+            jax.ShapeDtypeStruct(early.shape, BF16),
+            "svv",
+            0,
+            1_000_000,
+        )(pos, early, late)
+
+    def rounds(piece):
+        got, both = [piece], []
+        for k in range(1, 5):
+            give = got[-1]
+            if k > 2:
+                give = choose(4 - k, got[k - 2], got[k - 1])
+            pair = partners[k - 1]
+            step = [
+                ((i * n + j) * 2 + l, (pair[i, j, l][0] * n + pair[i, j, l][1]) * 2 + pair[i, j, l][2])
+                for i, j, l in spots
+            ]
+            got.append(lax.ppermute(give, ("c", "z", "x"), step))
+            both.append((got[k], swap("c", got[k])))
+        return both
 
     own_tokens = latents.reshape(-1, model)
     count = own_tokens.shape[0]
-    Z, X, ZC, XC = ([None] * n for _ in range(4))
-    Z[1] = hop(1, mine)
-    X[0] = swap("x", piece)
     other_tokens = swap("y", own_tokens)
     far_live = swap("y", frames_live)
-    for k in range(1, n):
-        if k > 1:
-            Z[k] = hop(k, Z[k - 1])
-        X[k] = across(k, Z[k])
-        ZC[k] = swap("c", Z[k])
-    Y = near_end(X[0])
-    YC = swap("c", Y)
-    for k in range(n):
-        XC[k] = swap("c", X[k])
-
     group, plain, old = whole_call(
         functools.partial(table_kernel, heads, rows),
         [
@@ -359,60 +416,62 @@
         2_000_000,
     )(pos, state_in.reshape(units, share, size), ksum_in.reshape(units, size))
     blocks = whole_call(
-        block_kernel,
-        jax.ShapeDtypeStruct((members, 2 * count, 2 * half), BF16),
-        "svv",
-        0,
-        4_000_000,
+        block_kernel, jax.ShapeDtypeStruct((members, 2 * count, depth), BF16), "svv", 0, 4_000_000
     )(pos, own_tokens, other_tokens)
 
-    def multiply(plan, acc, *given):
+    def multiply(slots, acc, *given):
         first = [] if acc is None else [acc]
+        wide = given[0].shape[-1]
         return whole_call(
-            functools.partial(mul_kernel, n, plan, acc is None),
+            functools.partial(mul_kernel, slots, acc is None),
             jax.ShapeDtypeStruct((2 * count, wide), F32),
             "sv" + "v" * (len(first) + len(given)),
-            2_000_000_000,
-            8_000_000,
+            1_500_000_000,
+            5_000_000,
             alias={2: 0} if first else None,
         )(pos, blocks, *first, *given)
 
-    acc = multiply([("own", 0), ("beside", 0), ("along", 1)], None, mine, X[0], XC[0], Z[1], ZC[1])
-    for k in range(2, n):
-        plan = [("across", k - 1), ("along", k)]
-        given = [X[k - 1], XC[k - 1], Z[k], ZC[k]]
-        if k == 2:
-            plan, given = plan + [("corner", 0)], given + [Y, YC]
-        acc = multiply(plan, acc, *given)
+    if fast:
+        kvs, qs = rounds(pieces[0]), rounds(pieces[1])
+        acc = multiply((7, 8, 9), None, pieces[0], *kvs[0])
+        acc = multiply((10, 11), acc, *kvs[1])
+        acc = multiply((12, 13), acc, *kvs[2])
+        last, last_kv, last_q = ("core",), kvs[3], qs[3]
+        asked = multiply((7, 8, 9, 10, 11), None, pieces[1], *qs[0], *qs[1])
+        asked = multiply((12, 13), asked, *qs[2])
+    else:
+        last, last_kv, last_q = ("all",), *(
+            (lax.all_gather(piece, ("z", "x"), axis=0, tiled=False),) for piece in pieces
+        )
+        acc, asked = (jnp.zeros((2 * count, piece.shape[1]), F32) for piece in pieces)
 
     pairs = 2 * streams * heads
     chunk = jax.ShapeDtypeStruct((pairs, rows, LANES), BF16)
-    asked = jax.ShapeDtypeStruct((count, width), BF16)
-    q, q_give, *parts = whole_call(
-        functools.partial(
-            kv_kernel, n, [("across", n - 1)], streams, frames, heads, size, rows
-        ),
-        [asked, asked] + [chunk] * members,
-        "sssvvvvvv",
-        2_000_000_000,
-        8_000_000,
-        scratch=[pltpu.VMEM((2 * count, wide), F32)],
-    )(pos, frames_live, far_live, blocks, acc, X[n - 1], XC[n - 1], group, plain)
+    parts = whole_call(
+        functools.partial(kv_kernel, last, streams, frames, heads, size, rows),
+        [chunk] * members,
+        "sss" + "v" * (4 + len(last_kv)),
+        1_500_000_000,
+        5_000_000,
+        scratch=[pltpu.VMEM(acc.shape, F32)],
+    )(pos, frames_live, far_live, blocks, acc, *last_kv, group, plain)
+    parts = list(parts)
+    q, q_give = whole_call(
+        functools.partial(ask_kernel, last, width),
+        [
+            jax.ShapeDtypeStruct((count, heads * LANES), BF16),
+            jax.ShapeDtypeStruct((count, width), BF16),
+        ],
+        "svvv" + "v" * len(last_q),
+        700_000_000,
+        3_000_000,
+        scratch=[pltpu.VMEM(asked.shape, F32)],
+    )(pos, blocks, asked, group, *last_q)
 
     for k in range(members - 1, 0, -1):
         parts[k] = xor(k, parts[k])
     q_other = swap("y", q_give)
 
-    def ask(raw):
-        return whole_call(
-            query_kernel,
-            jax.ShapeDtypeStruct((count, heads * LANES), BF16),
-            "svv",
-            140_000_000,
-            1_500_000,
-        )(pos, raw, group)
-
-    q = ask(q)
     keep, give = whole_call(
         sum_kernel,
         [
@@ -433,7 +492,13 @@
     )(pos, keep, got, old)
 
     gathered = [new] + [xor(k, new) for k in range(1, members)]
-    q_other = ask(q_other)
+    q_other = whole_call(
+        query_kernel,
+        jax.ShapeDtypeStruct((count, heads * LANES), BF16),
+        "svv",
+        140_000_000,
+        1_500_000,
+    )(pos, q_other, group)
 
     every, spots, bit = [new], [0], owners // 2
     while bit:

time: 159 us -> 140 us (0.88)
  starting transfers between devices: 80 us -> 46.9 us
  waiting for transfers between devices: 33.9 us -> 46.6 us
  Pallas kernels: 31.5 us -> 37.3 us
  local copies, waits for them, and re-layouts: 11.7 us -> 7.45 us
    ppermute x13 -> x12, starting transfers between devices: 32.1 us -> 7.24 us  [swap(): return lax.ppermute(v, axis, SWAP)]
    ppermute x7 -> x8, waiting for transfers between devices: 13.3 us -> 35.3 us  [rounds(): got.append(lax.ppermute(give, ('c', 'z', 'x'), step))]
    ppermute x13 -> x12, waiting for transfers between devices: 14 us -> 2.51 us  [swap(): return lax.ppermute(v, axis, SWAP)]
    ppermute x14, starting transfers between devices: 30.2 us -> 24.3 us  [xor(): return lax.ppermute(v, ('z', 'x'), [(i, i ^ k) for i in range(members)])]
    pallas_call x8 -> x15, Pallas kernels: 23.2 us -> 28.9 us  [the longest x5 13.8 us: multiply(): whole_call(functools.partial(mul_kernel, slots, acc is None), jax.ShapeDt...]
    unnamed x38 -> x46, local copies, waits for them, and re-layouts: 11.6 us -> 6.59 us
    ppermute x7 -> x8, starting transfers between devices: 15.7 us -> 13.2 us  [rounds(): got.append(lax.ppermute(give, ('c', 'z', 'x'), step))]
    ppermute x14, waiting for transfers between devices: 6.67 us -> 8.76 us  [xor(): return lax.ppermute(v, ('z', 'x'), [(i, i ^ k) for i in range(members)])]
  transfers between devices with their start and end apart: 37 -> 37, of which waited for: 7 -> 10; matrix products, arithmetic and copies ran while one was open for 1% -> 1% of each run, Pallas kernels for 15% -> 24%
where the time goes in v3:
time: 140 us; the launch traced here: 139 us
  starting transfers between devices  46.9 us (34%)
  waiting for transfers between devices  46.6 us (33%)
  Pallas kernels  37.3 us (27%)
  local copies, waits for them, and re-layouts  7.45 us (5%)
    ppermute x8, waiting for transfers between devices, rounds(): got.append(lax.ppermute(give, ('c', 'z', 'x'), step))  35.3 us
    ppermute x14, starting transfers between devices, xor(): return lax.ppermute(v, ('z', 'x'), [(i, i ^ k) for i in range(members)])  24.3 us
    pallas_call x5, Pallas kernels, multiply(): whole_call(functools.partial(mul_kernel, slots, acc is None), jax.ShapeDt...  13.8 us
    ppermute x8, starting transfers between devices, rounds(): got.append(lax.ppermute(give, ('c', 'z', 'x'), step))  13.2 us
    ppermute x14, waiting for transfers between devices, xor(): return lax.ppermute(v, ('z', 'x'), [(i, i ^ k) for i in range(members)])  8.76 us
    ppermute x12, starting transfers between devices, swap(): return lax.ppermute(v, axis, SWAP)  7.24 us
    unnamed x46, local copies, waits for them, and re-layouts  6.59 us
    pallas_call x1, Pallas kernels, layer(): whole_call(functools.partial(kv_kernel, last, streams, frames, heads, siz...  4.15 us
  transfers between devices with their start and end apart: 37, of which 10 were waited for; matrix products, arithmetic and copies ran while one was open for 1% of the time, Pallas kernels for 24%

profile of v3, /device:TPU:0, one launch (start us, length us, event | category | flops | bytes accessed | tf_op | source)
XLA Modules:
  0.0 139.2 jit_solution(11819801889452352896)
XLA Ops:
  0.7 1.5 %copy-done = bf16[280,3360]{1,0:T(8,128)(2,1)S(1)} copy-done((bf16[280,3360]{1,0:T(8,128)(2,1)S(1)}, bf16[280,3360]{1,0:T(8,128)(2,1)}, u32[]{:S(2)}) %copy-start) | copy-done | bytes 1881624
  2.3 2.1 %shard_map.103.refs_0_ = bf16[280,1152]{1,0:T(8,128)(2,1)S(1)} custom-call(s32[6]{0:T(128)S(1)} %stack.27.pos_ref, bf16[280,3360]{1,0:T(8,128)(2,1)S(1)} %copy-done), custom_call_target="tpu_custom_call" | custom-call | bytes 2000000 | tf_op jit(solution)/shard_map/pallas_call | solution.py:368
  4.3 3.1 %collective-permute-start.11 = (bf16[280,1152]{1,0:T(8,128)(2,1)S(1)}, bf16[280,1152]{1,0:T(8,128)(2,1)S(1)}, u32[]{:S(2)}, u32[]{:S(2)}) collective-permute-start(bf16[280,1152]{1,0:T(8,128)(2,1)S(1)} %shard_map.103.refs_0_), channel_id=1, source_target_pairs={{0,2},{1,3},{2,0},{3,1},{4,6},{5,7},{6,4},{7,5},{8,9},{9,8},{10,12... | collective-permute-start | bytes 1935368 | tf_op jit(solution)/shard_map/ppermute | solution.py:399
  8.3 7.6 %collective-permute-done.11.refs_1_.early_ref = bf16[280,1152]{1,0:T(8,128)(2,1)S(1)} collective-permute-done((bf16[280,1152]{1,0:T(8,128)(2,1)S(1)}, bf16[280,1152]{1,0:T(8,128)(2,1)S(1)}, u32[]{:S(2)}, u32[]{:S(2)}) %collective-permute-start.11) | collective-permute-done | bytes 645152 | tf_op jit(solution)/shard_map/ppermute | solution.py:399
  15.9 1.9 %collective-permute-start.13 = (bf16[280,1152]{1,0:T(8,128)(2,1)S(1)}, bf16[280,1152]{1,0:T(8,128)(2,1)S(1)}, u32[]{:S(2)}, u32[]{:S(2)}) collective-permute-start(bf16[280,1152]{1,0:T(8,128)(2,1)S(1)} %collective-permute-done.11.refs_1_.early_ref), channel_id=1, source_target_pairs={{0,1},{1,0},{2,4},{3,5},{4,2},{5,3},{6,7},{7,6},{8,10},{9,11},{10,... | collective-permute-start | bytes 1935368 | tf_op jit(solution)/shard_map/ppermute | solution.py:399
  18.6 7.8 %collective-permute-done.13.refs_1_.late_ref.early_ref = bf16[280,1152]{1,0:T(8,128)(2,1)S(1)} collective-permute-done((bf16[280,1152]{1,0:T(8,128)(2,1)S(1)}, bf16[280,1152]{1,0:T(8,128)(2,1)S(1)}, u32[]{:S(2)}, u32[]{:S(2)}) %collective-permute-start.13) | collective-permute-done | bytes 645152 | tf_op jit(solution)/shard_map/ppermute | solution.py:399
  27.0 2.1 %collective-permute-start.15 = (bf16[280,1152]{1,0:T(8,128)(2,1)S(1)}, bf16[280,1152]{1,0:T(8,128)(2,1)}, u32[]{:S(2)}, u32[]{:S(2)}) collective-permute-start(bf16[280,1152]{1,0:T(8,128)(2,1)S(1)} %shard_map.106), channel_id=1, source_target_pairs={{0,2},{1,3},{2,0},{3,1},{4,6},{5,7},{6,4},{7,5},{8,9},{9,8},{10,11... | collective-permute-start | bytes 1935368 | tf_op jit(solution)/shard_map/ppermute | solution.py:399
  30.7 2.3 %collective-permute-start = (bf16[192,2240]{1,0:T(8,128)(2,1)S(1)}, bf16[192,2240]{1,0:T(8,128)(2,1)S(1)}, u32[]{:S(2)}, u32[]{:S(2)}) collective-permute-start(bf16[192,2240]{1,0:T(8,128)(2,1)S(1)} %bitcast.11), channel_id=1, source_target_pairs={{0,16},{16,0},{1,17},{17,1},{2,18},{18,2},{3,19},{19,3},{4,20},{20... | collective-permute-start | bytes 2580488 | tf_op jit(solution)/shard_map/ppermute | solution.py:341
  33.1 9.4 %collective-permute-done.1.refs_1_.early_ref = bf16[280,640]{1,0:T(8,128)(2,1)S(1)} collective-permute-done((bf16[280,640]{1,0:T(8,128)(2,1)S(1)}, bf16[280,640]{1,0:T(8,128)(2,1)S(1)}, u32[]{:S(2)}, u32[]{:S(2)}) %collective-permute-start.1) | collective-permute-done | bytes 358432 | tf_op jit(solution)/shard_map/ppermute | solution.py:399
  42.5 1.3 collective-permute-start.3
  43.8 1.1 shard_map.108
  45.8 4.1 %collective-permute-done.3.refs_3_.late_ref.early_ref = bf16[280,640]{1,0:T(8,128)(2,1)S(1)} collective-permute-done((bf16[280,640]{1,0:T(8,128)(2,1)S(1)}, bf16[280,640]{1,0:T(8,128)(2,1)S(1)}, u32[]{:S(2)}, u32[]{:S(2)}) %collective-permute-start.3) | collective-permute-done | bytes 358432 | tf_op jit(solution)/shard_map/ppermute | solution.py:399
  50.5 2.5 %collective-permute-start.5 = (bf16[280,640]{1,0:T(8,128)(2,1)S(1)}, bf16[280,640]{1,0:T(8,128)(2,1)S(1)}, u32[]{:S(2)}, u32[]{:S(2)}) collective-permute-start(bf16[280,640]{1,0:T(8,128)(2,1)S(1)} %shard_map.97), channel_id=1, source_target_pairs={{0,2},{1,3},{2,0},{3,1},{4,6},{5,7},{6,4},{7,5},{8,9},{9,8},{10,11... | collective-permute-start | bytes 1075208 | tf_op jit(solution)/shard_map/ppermute | solution.py:399
  54.4 4.6 %collective-permute-done.5.refs_1_.late_ref = bf16[280,640]{1,0:T(8,128)(2,1)S(1)} collective-permute-done((bf16[280,640]{1,0:T(8,128)(2,1)S(1)}, bf16[280,640]{1,0:T(8,128)(2,1)S(1)}, u32[]{:S(2)}, u32[]{:S(2)}) %collective-permute-start.5) | collective-permute-done | bytes 358432 | tf_op jit(solution)/shard_map/ppermute | solution.py:399
  58.9 1.8 %collective-permute-done.17.refs_2_ = bf16[280,1152]{1,0:T(8,128)(2,1)} collective-permute-done((bf16[280,1152]{1,0:T(8,128)(2,1)S(1)}, bf16[280,1152]{1,0:T(8,128)(2,1)}, u32[]{:S(2)}, u32[]{:S(2)}) %collective-permute-start.17) | collective-permute-done | bytes 645152 | tf_op jit(solution)/shard_map/ppermute | solution.py:399
  60.8 1.3 shard_map.100
  63.6 1.3 collective-permute-start.7
  65.0 0.9 shard_map.99
  65.9 1.2 copy-done.7
  67.1 1.3 shard_map.94.blocks_ref.refs_0_
  68.5 3.2 %shard_map.96.refs_0_ = f32[384,640]{1,0:T(8,128)S(1)} custom-call(s32[16]{0:T(128)S(1)} %concatenate.4.pos_ref.refs_0_, bf16[8,384,280]{2,1,0:T(8,128)(2,1)S(1)} %shard_map.94.blocks_ref.refs_0_, bf16[280,640]{1,0:T(8,128)(2,1)S(1)} %copy-done.11, bf16[280,640]{1,0:T(8,128)(2,1)S(1)} %copy-done.13, bf16[280,640]{1,0:T(8,128)(2,1)S(1)} %copy-done.16, ...), custom_call_target="tpu_custom_call" | custom-call | flops 1500000000 | bytes 5000000 | tf_op jit(solution)/shard_map/pallas_call | solution.py:425
  71.7 1.6 %collective-permute-start.10 = (s32[2]{0:T(128)S(1)}, s32[2]{0:T(128)S(1)}, u32[]{:S(2)}, u32[]{:S(2)}) collective-permute-start(s32[2]{0:T(128)S(1)} %copy-done.14), channel_id=1, source_target_pairs={{0,16},{16,0},{1,17},{17,1},{2,18},{18,2},{3,19},{19,3},{4,20},{20... | collective-permute-start | bytes 32 | tf_op jit(solution)/shard_map/ppermute | solution.py:341
  73.3 3.2 %shard_map.104.refs_0_ = f32[384,1152]{1,0:T(8,128)S(1)} custom-call(s32[16]{0:T(128)S(1)} %concatenate.4.pos_ref.refs_0_, bf16[8,384,280]{2,1,0:T(8,128)(2,1)S(1)} %shard_map.94.blocks_ref.refs_0_, bf16[280,1152]{1,0:T(8,128)(2,1)S(1)} %copy-done.3, bf16[280,1152]{1,0:T(8,128)(2,1)S(1)} %collective-permute-done.11.refs_1_.early_ref, ...), custom_call_target="tpu_custom_call" | custom-call | flops 1500000000 | bytes 5000000 | tf_op jit(solution)/shard_map/pallas_call | solution.py:425
  77.1 2.6 %shard_map.105.refs_0_ = f32[384,1152]{1,0:T(8,128)S(1)} custom-call(s32[16]{0:T(128)S(1)} %concatenate.4.pos_ref.refs_0_, bf16[8,384,280]{2,1,0:T(8,128)(2,1)S(1)} %shard_map.94.blocks_ref.refs_0_, f32[384,1152]{1,0:T(8,128)S(1)} %shard_map.104.refs_0_, ...), custom_call_target="tpu_custom_call", output_to_operand_aliasing={{}: (2, {})} | custom-call | flops 1500000000 | bytes 5000000 | tf_op jit(solution)/shard_map/pallas_call | solution.py:425
  79.7 2.8 %shard_map.107.refs_1_ = f32[384,1152]{1,0:T(8,128)S(1)} custom-call(s32[16]{0:T(128)S(1)} %concatenate.4.pos_ref.refs_0_, bf16[8,384,280]{2,1,0:T(8,128)(2,1)S(1)} %shard_map.94.blocks_ref.refs_0_, f32[384,1152]{1,0:T(8,128)S(1)} %shard_map.105.refs_0_, bf16[280,1152]{1,0:T(8,128)(2,1)} %collective-permute-done.15.refs_1_.late_ref, ...), custom_call_target="tpu_custom_call", output_to_operand_aliasing={{}: (2, {})} | custom-call | flops 1500000000 | bytes 5000000 | tf_op jit(solution)/shard_map/pallas_call | solution.py:425
  82.5 4.2 %shard_map.109 = (bf16[20,16,128]{2,1,0:T(8,128)(2,1)S(1)}, bf16[20,16,128]{2,1,0:T(8,128)(2,1)S(1)}, bf16[20,16,128]{2,1,0:T(8,128)(2,1)S(1)}, bf16[20,16,128]{...) custom-call(s32[16]{0:T(128)S(1)} %concatenate.4.pos_ref.refs_0_, ...), custom_call_target="tpu_custom_call" | custom-call | flops 1500000000 | bytes 5000000 | tf_op jit(solution)/shard_map/pallas_call | solution.py:450
  87.3 1.0 collective-permute-start.20
  88.3 1.9 %collective-permute-start.21 = (bf16[20,16,128]{2,1,0:T(8,128)(2,1)S(1)}, bf16[20,16,128]{2,1,0:T(8,128)(2,1)S(1)}, u32[]{:S(2)}, u32[]{:S(2)}) collective-permute-start(bf16[20,16,128]{2,1,0:T(8,128)(2,1)S(1)} %get-tuple-element.27), channel_id=1, source_target_pairs={{0,3},{1,2},{2,1},{3,0},{4,7},{5,6},{6,5},{7,4},{8,11},{9,10},{10,... | collective-permute-start | bytes 245768 | tf_op jit(solution)/shard_map/ppermute | solution.py:344
  90.2 2.0 %shard_map.98.old_ref = f32[384,640]{1,0:T(8,128)S(1)} custom-call(s32[16]{0:T(128)S(1)} %concatenate.4.pos_ref.refs_0_, bf16[8,384,280]{2,1,0:T(8,128)(2,1)S(1)} %shard_map.94.blocks_ref.refs_0_, f32[384,640]{1,0:T(8,128)S(1)} %shard_map.96.refs_0_, bf16[280,640]{1,0:T(8,128)(2,1)S(1)} %copy-done.9, ...), custom_call_target="tpu_custom_call", output_to_operand_aliasing={{}: (2, {})} | custom-call | flops 1500000000 | bytes 5000000 | tf_op jit(solution)/shard_map/pallas_call | solution.py:425
  92.3 2.2 %shard_map.101 = (bf16[192,640]{1,0:T(8,128)(2,1)S(1)}, bf16[192,560]{1,0:T(8,128)(2,1)S(1)}) custom-call(s32[16]{0:T(128)S(1)} %concatenate.4.pos_ref.refs_0_, bf16[8,384,280]{2,1,0:T(8,128)(2,1)S(1)} %shard_map.94.blocks_ref.refs_0_, f32[384,640]{1,0:T(8,128)S(1)} %shard_map.98.old_ref, bf16[560,640]{1,0:T(8,128)(2,1)S(1)} %get-tuple-element.20.group_ref.refs_4_, ...), custom_call_target="tpu_custom_call" | custom-call | flops 700000000 | bytes 3000000 | tf_op jit(solution)/shard_map/pallas_call | solution.py:459
  95.1 1.8 %collective-permute-start.22 = (bf16[20,16,128]{2,1,0:T(8,128)(2,1)S(1)}, bf16[20,16,128]{2,1,0:T(8,128)(2,1)S(1)}, u32[]{:S(2)}, u32[]{:S(2)}) collective-permute-start(bf16[20,16,128]{2,1,0:T(8,128)(2,1)S(1)} %get-tuple-element.28), channel_id=1, source_target_pairs={{0,4},{1,5},{2,6},{3,7},{4,0},{5,1},{6,2},{7,3},{8,12},{9,13},{10,... | collective-permute-start | bytes 245768 | tf_op jit(solution)/shard_map/ppermute | solution.py:344
  96.9 1.2 collective-permute-start.23
  98.1 3.0 %collective-permute-start.24 = (bf16[20,16,128]{2,1,0:T(8,128)(2,1)S(1)}, bf16[20,16,128]{2,1,0:T(8,128)(2,1)S(1)}, u32[]{:S(2)}, u32[]{:S(2)}) collective-permute-start(bf16[20,16,128]{2,1,0:T(8,128)(2,1)S(1)} %get-tuple-element.30), channel_id=1, source_target_pairs={{0,6},{1,7},{2,4},{3,5},{4,2},{5,3},{6,0},{7,1},{8,14},{9,15},{10,... | collective-permute-start | bytes 245768 | tf_op jit(solution)/shard_map/ppermute | solution.py:344
  101.2 1.6 %collective-permute-start.25 = (bf16[20,16,128]{2,1,0:T(8,128)(2,1)S(1)}, bf16[20,16,128]{2,1,0:T(8,128)(2,1)S(1)}, u32[]{:S(2)}, u32[]{:S(2)}) collective-permute-start(bf16[20,16,128]{2,1,0:T(8,128)(2,1)S(1)} %get-tuple-element.31), channel_id=1, source_target_pairs={{0,7},{1,6},{2,5},{3,4},{4,3},{5,2},{6,1},{7,0},{8,15},{9,14},{10,... | collective-permute-start | bytes 245768 | tf_op jit(solution)/shard_map/ppermute | solution.py:344
  102.7 3.4 %collective-permute-done.22.refs_5_ = bf16[20,16,128]{2,1,0:T(8,128)(2,1)S(1)} collective-permute-done((bf16[20,16,128]{2,1,0:T(8,128)(2,1)S(1)}, bf16[20,16,128]{2,1,0:T(8,128)(2,1)S(1)}, u32[]{:S(2)}, u32[]{:S(2)}) %collective-permute-start.22) | collective-permute-done | bytes 81952 | tf_op jit(solution)/shard_map/ppermute | solution.py:344
  106.2 2.9 %collective-permute-done.23.refs_6_ = bf16[20,16,128]{2,1,0:T(8,128)(2,1)S(1)} collective-permute-done((bf16[20,16,128]{2,1,0:T(8,128)(2,1)S(1)}, bf16[20,16,128]{2,1,0:T(8,128)(2,1)S(1)}, u32[]{:S(2)}, u32[]{:S(2)}) %collective-permute-start.23) | collective-permute-done | bytes 81952 | tf_op jit(solution)/shard_map/ppermute | solution.py:344
  109.7 1.6 %collective-permute-start.26 = (bf16[10,16,128]{2,1,0:T(8,128)(2,1)S(1)}, bf16[10,16,128]{2,1,0:T(8,128)(2,1)S(1)}, u32[]{:S(2)}, u32[]{:S(2)}) collective-permute-start(bf16[10,16,128]{2,1,0:T(8,128)(2,1)S(1)} %get-tuple-element.33), channel_id=1, source_target_pairs={{0,16},{16,0},{1,17},{17,1},{2,18},{18,2},{3,19},{19,3},{4,20},{20... | collective-permute-start | bytes 122888 | tf_op jit(solution)/shard_map/ppermute | solution.py:341
  111.2 2.5 %collective-permute-done.26.got_ref = bf16[10,16,128]{2,1,0:T(8,128)(2,1)S(1)} collective-permute-done((bf16[10,16,128]{2,1,0:T(8,128)(2,1)S(1)}, bf16[10,16,128]{2,1,0:T(8,128)(2,1)S(1)}, u32[]{:S(2)}, u32[]{:S(2)}) %collective-permute-start.26) | collective-permute-done | bytes 40992 | tf_op jit(solution)/shard_map/ppermute | solution.py:341
  114.3 1.6 %collective-permute-start.34 = (bf16[20,16,128]{2,1,0:T(8,128)(2,1)S(1)}, bf16[20,16,128]{2,1,0:T(8,128)(2,1)S(1)}, u32[]{:S(2)}, u32[]{:S(2)}) collective-permute-start(bf16[20,16,128]{2,1,0:T(8,128)(2,1)S(1)} %shard_map.111.refs_0_), channel_id=1, source_target_pairs={{0,16},{8,24},{16,0},{24,8},{1,17},{9,25},{17,1},{25,9},{2,18},{10... | collective-permute-start | bytes 245768 | tf_op jit(solution)/shard_map/ppermute | solution.py:507
  115.9 1.2 collective-permute-start.27
  117.1 3.6 %collective-permute-start.28 = (bf16[20,16,128]{2,1,0:T(8,128)(2,1)S(1)}, bf16[20,16,128]{2,1,0:T(8,128)(2,1)S(1)}, u32[]{:S(2)}, u32[]{:S(2)}) collective-permute-start(bf16[20,16,128]{2,1,0:T(8,128)(2,1)S(1)} %shard_map.111.refs_0_), channel_id=1, source_target_pairs={{0,2},{1,3},{2,0},{3,1},{4,6},{5,7},{6,4},{7,5},{8,10},{9,11},{10,... | collective-permute-start | bytes 245768 | tf_op jit(solution)/shard_map/ppermute | solution.py:344
  120.9 3.3 %collective-permute-start.30 = (bf16[20,16,128]{2,1,0:T(8,128)(2,1)S(1)}, bf16[20,16,128]{2,1,0:T(8,128)(2,1)S(1)}, u32[]{:S(2)}, u32[]{:S(2)}) collective-permute-start(bf16[20,16,128]{2,1,0:T(8,128)(2,1)S(1)} %shard_map.111.refs_0_), channel_id=1, source_target_pairs={{0,4},{1,5},{2,6},{3,7},{4,0},{5,1},{6,2},{7,3},{8,12},{9,13},{10,... | collective-permute-start | bytes 245768 | tf_op jit(solution)/shard_map/ppermute | solution.py:344
  125.0 2.3 %collective-permute-start.32 = (bf16[20,16,128]{2,1,0:T(8,128)(2,1)S(1)}, bf16[20,16,128]{2,1,0:T(8,128)(2,1)S(1)}, u32[]{:S(2)}, u32[]{:S(2)}) collective-permute-start(bf16[20,16,128]{2,1,0:T(8,128)(2,1)S(1)} %shard_map.111.refs_0_), channel_id=1, source_target_pairs={{0,6},{1,7},{2,4},{3,5},{4,2},{5,3},{6,0},{7,1},{8,14},{9,15},{10,... | collective-permute-start | bytes 245768 | tf_op jit(solution)/shard_map/ppermute | solution.py:344
  127.3 1.7 %collective-permute-start.33 = (bf16[20,16,128]{2,1,0:T(8,128)(2,1)S(1)}, bf16[20,16,128]{2,1,0:T(8,128)(2,1)S(1)}, u32[]{:S(2)}, u32[]{:S(2)}) collective-permute-start(bf16[20,16,128]{2,1,0:T(8,128)(2,1)S(1)} %shard_map.111.refs_0_), channel_id=1, source_target_pairs={{0,7},{1,6},{2,5},{3,4},{4,3},{5,2},{6,1},{7,0},{8,15},{9,14},{10,... | collective-permute-start | bytes 245768 | tf_op jit(solution)/shard_map/ppermute | solution.py:344
  129.0 2.8 %shard_map.113.place_ref = s32[20]{0:T(128)S(1)} custom-call(s32[16]{0:T(128)S(1)} %concatenate.4.pos_ref.refs_0_, s32[80]{0:T(128)S(1)} %copy-done.19), custom_call_target="tpu_custom_call" | custom-call | bytes 1000 | tf_op jit(solution)/shard_map/pallas_call | solution.py:511
  133.3 2.4 %collective-permute-done.31.refs_5_ = bf16[20,16,128]{2,1,0:T(8,128)(2,1)S(1)} collective-permute-done((bf16[20,16,128]{2,1,0:T(8,128)(2,1)S(1)}, bf16[20,16,128]{2,1,0:T(8,128)(2,1)S(1)}, u32[]{:S(2)}, u32[]{:S(2)}) %collective-permute-start.31) | collective-permute-done | bytes 81952 | tf_op jit(solution)/shard_map/ppermute | solution.py:344
  135.7 2.2 %shard_map.112 = bf16[192,1120]{1,0:T(8,128)(2,1)} custom-call(s32[16]{0:T(128)S(1)} %concatenate.4.pos_ref.refs_0_, s32[2]{0:T(128)S(1)} %copy-done.14, bf16[192,640]{1,0:T(8,128)(2,1)S(1)} %get-tuple-element.21.own_ref, bf16[192,640]{1,0:T(8,128)(2,1)S(1)} %shard_map.102.other_ref, bf16[20,16,128]{2,1,0:T(8,128)(2,1)S(1)} %shard_map.111.refs_0_, ...), custom_call_target="tpu_custom_call" | custom-call | flops 1500000000 | bytes 3000000 | tf_op jit(solution)/shard_map/pallas_call | solution.py:531
  138.0 1.3 shard_map.114
  (97 shorter events, 13.7 us)
Async XLA Ops:
  2.3 26.8 %copy-start.1 = (bf16[280,3360]{1,0:T(8,128)(2,1)S(1)}, bf16[280,3360]{1,0:T(8,128)(2,1)}, u32[]{:S(2)}) copy-start(bf16[280,3360]{1,0:T(8,128)(2,1)} %w_hbm.3) | copy-start | bytes 5644804
  4.3 11.6 %collective-permute-start.11 = (bf16[280,1152]{1,0:T(8,128)(2,1)S(1)}, bf16[280,1152]{1,0:T(8,128)(2,1)S(1)}, u32[]{:S(2)}, u32[]{:S(2)}) collective-permute-start(bf16[280,1152]{1,0:T(8,128)(2,1)S(1)} %shard_map.103.refs_0_), channel_id=1, source_target_pairs={{0,2},{1,3},{2,0},{3,1},{4,6},{5,7},{6,4},{7,5},{8,9},{9,8},{10,12... | collective-permute-start | bytes 1935368 | tf_op jit(solution)/shard_map/ppermute | solution.py:399
  15.9 10.5 %collective-permute-start.13 = (bf16[280,1152]{1,0:T(8,128)(2,1)S(1)}, bf16[280,1152]{1,0:T(8,128)(2,1)S(1)}, u32[]{:S(2)}, u32[]{:S(2)}) collective-permute-start(bf16[280,1152]{1,0:T(8,128)(2,1)S(1)} %collective-permute-done.11.refs_1_.early_ref), channel_id=1, source_target_pairs={{0,1},{1,0},{2,4},{3,5},{4,2},{5,3},{6,7},{7,6},{8,10},{9,11},{10,... | collective-permute-start | bytes 1935368 | tf_op jit(solution)/shard_map/ppermute | solution.py:399
  18.6 12.1 %copy-start.4 = (bf16[2,4,24,2240]{3,2,1,0:T(8,128)(2,1)S(1)}, bf16[2,4,24,2240]{3,2,1,0:T(8,128)(2,1)}, u32[]{:S(2)}) copy-start(bf16[2,4,24,2240]{3,2,1,0:T(8,128)(2,1)} %param.7) | copy-start | bytes 2580484
  27.0 16.8 %collective-permute-start.15 = (bf16[280,1152]{1,0:T(8,128)(2,1)S(1)}, bf16[280,1152]{1,0:T(8,128)(2,1)}, u32[]{:S(2)}, u32[]{:S(2)}) collective-permute-start(bf16[280,1152]{1,0:T(8,128)(2,1)S(1)} %shard_map.106), channel_id=1, source_target_pairs={{0,2},{1,3},{2,0},{3,1},{4,6},{5,7},{6,4},{7,5},{8,9},{9,8},{10,11... | collective-permute-start | bytes 1935368 | tf_op jit(solution)/shard_map/ppermute | solution.py:399
  29.9 12.6 %collective-permute-start.1 = (bf16[280,640]{1,0:T(8,128)(2,1)S(1)}, bf16[280,640]{1,0:T(8,128)(2,1)S(1)}, u32[]{:S(2)}, u32[]{:S(2)}) collective-permute-start(bf16[280,640]{1,0:T(8,128)(2,1)S(1)} %shard_map.95.refs_0_), channel_id=1, source_target_pairs={{0,2},{1,3},{2,0},{3,1},{4,6},{5,7},{6,4},{7,5},{8,9},{9,8},{10,12... | collective-permute-start | bytes 1075208 | tf_op jit(solution)/shard_map/ppermute | solution.py:399
  30.7 34.2 %copy-start.20 = (f32[2,10,14,112]{3,0,2,1:T(2,128)S(1)}, f32[2,10,14,112]{3,0,2,1:T(2,128)}, u32[]{:S(2)}) copy-start(f32[2,10,14,112]{3,0,2,1:T(2,128)} %param.9) | copy-start | bytes 376324
  30.7 34.2 %copy-start.21 = (f32[2,10,112]{2,0,1:T(2,128)S(1)}, f32[2,10,112]{2,0,1:T(2,128)}, u32[]{:S(2)}) copy-start(f32[2,10,112]{2,0,1:T(2,128)} %param.10) | copy-start | bytes 26884
  30.7 23.6 %collective-permute-start = (bf16[192,2240]{1,0:T(8,128)(2,1)S(1)}, bf16[192,2240]{1,0:T(8,128)(2,1)S(1)}, u32[]{:S(2)}, u32[]{:S(2)}) collective-permute-start(bf16[192,2240]{1,0:T(8,128)(2,1)S(1)} %bitcast.11), channel_id=1, source_target_pairs={{0,16},{16,0},{1,17},{17,1},{2,18},{18,2},{3,19},{19,3},{4,20},{20... | collective-permute-start | bytes 2580488 | tf_op jit(solution)/shard_map/ppermute | solution.py:341
  42.5 19.6 %copy-start.12 = (bf16[280,640]{1,0:T(8,128)(2,1)}, bf16[280,640]{1,0:T(8,128)(2,1)S(1)}, u32[]{:S(2)}) copy-start(bf16[280,640]{1,0:T(8,128)(2,1)S(1)} %collective-permute-done.1.refs_1_.early_ref) | copy-start | bytes 1075204
  42.5 7.4 %collective-permute-start.3 = (bf16[280,640]{1,0:T(8,128)(2,1)S(1)}, bf16[280,640]{1,0:T(8,128)(2,1)S(1)}, u32[]{:S(2)}, u32[]{:S(2)}) collective-permute-start(bf16[280,640]{1,0:T(8,128)(2,1)S(1)} %collective-permute-done.1.refs_1_.early_ref), channel_id=1, source_target_pairs={{0,1},{1,0},{2,4},{3,5},{4,2},{5,3},{6,7},{7,6},{8,10},{9,11},{10,... | collective-permute-start | bytes 1075208 | tf_op jit(solution)/shard_map/ppermute | solution.py:399
  43.8 9.2 %collective-permute-start.2 = (bf16[280,640]{1,0:T(8,128)(2,1)S(1)}, bf16[280,640]{1,0:T(8,128)(2,1)S(1)}, u32[]{:S(2)}, u32[]{:S(2)}) collective-permute-start(bf16[280,640]{1,0:T(8,128)(2,1)S(1)} %collective-permute-done.1.refs_1_.early_ref), channel_id=1, source_target_pairs={{0,8},{8,0},{1,9},{9,1},{2,10},{10,2},{3,11},{11,3},{4,12},{12,4},... | collective-permute-start | bytes 1075208 | tf_op jit(solution)/shard_map/ppermute | solution.py:341
  45.0 20.9 %copy-start.5 = (bf16[2,4,24,2240]{3,2,1,0:T(8,128)(2,1)S(1)}, bf16[2,4,24,2240]{3,2,1,0:T(8,128)(2,1)}, u32[]{:S(2)}) copy-start(bf16[2,4,24,2240]{3,2,1,0:T(8,128)(2,1)} %param.7) | copy-start | bytes 2580484
  45.0 15.8 %collective-permute-start.17 = (bf16[280,1152]{1,0:T(8,128)(2,1)S(1)}, bf16[280,1152]{1,0:T(8,128)(2,1)}, u32[]{:S(2)}, u32[]{:S(2)}) collective-permute-start(bf16[280,1152]{1,0:T(8,128)(2,1)S(1)} %shard_map.108), channel_id=1, source_target_pairs={{0,1},{1,0},{2,3},{3,2},{4,5},{5,4},{6,7},{7,6},{8,10},{9,11},{10,... | collective-permute-start | bytes 1935368 | tf_op jit(solution)/shard_map/ppermute | solution.py:399
  50.5 8.4 %collective-permute-start.5 = (bf16[280,640]{1,0:T(8,128)(2,1)S(1)}, bf16[280,640]{1,0:T(8,128)(2,1)S(1)}, u32[]{:S(2)}, u32[]{:S(2)}) collective-permute-start(bf16[280,640]{1,0:T(8,128)(2,1)S(1)} %shard_map.97), channel_id=1, source_target_pairs={{0,2},{1,3},{2,0},{3,1},{4,6},{5,7},{6,4},{7,5},{8,9},{9,8},{10,11... | collective-permute-start | bytes 1075208 | tf_op jit(solution)/shard_map/ppermute | solution.py:399
  53.1 18.6 %collective-permute-start.12 = (bf16[280,1152]{1,0:T(8,128)(2,1)S(1)}, bf16[280,1152]{1,0:T(8,128)(2,1)}, u32[]{:S(2)}, u32[]{:S(2)}) collective-permute-start(bf16[280,1152]{1,0:T(8,128)(2,1)S(1)} %collective-permute-done.11.refs_1_.early_ref), channel_id=1, source_target_pairs={{0,8},{8,0},{1,9},{9,1},{2,10},{10,2},{3,11},{11,3},{4,12},{12,4},... | collective-permute-start | bytes 1935368 | tf_op jit(solution)/shard_map/ppermute | solution.py:341
  53.8 9.0 %collective-permute-start.4 = (bf16[280,640]{1,0:T(8,128)(2,1)S(1)}, bf16[280,640]{1,0:T(8,128)(2,1)S(1)}, u32[]{:S(2)}, u32[]{:S(2)}) collective-permute-start(bf16[280,640]{1,0:T(8,128)(2,1)S(1)} %collective-permute-done.3.refs_3_.late_ref.early_ref), channel_id=1, source_target_pairs={{0,8},{8,0},{1,9},{9,1},{2,10},{10,2},{3,11},{11,3},{4,12},{12,4},... | collective-permute-start | bytes 1075208 | tf_op jit(solution)/shard_map/ppermute | solution.py:341
  54.3 8.5 %copy-start.6 = (bf16[192,2240]{1,0:T(8,128)(2,1)}, bf16[192,2240]{1,0:T(8,128)(2,1)S(1)}, u32[]{:S(2)}) copy-start(bf16[192,2240]{1,0:T(8,128)(2,1)S(1)} %collective-permute-done.other_ref) | copy-start | bytes 2580484
  54.3 22.2 %collective-permute-start.14 = (bf16[280,1152]{1,0:T(8,128)(2,1)S(1)}, bf16[280,1152]{1,0:T(8,128)(2,1)}, u32[]{:S(2)}, u32[]{:S(2)}) collective-permute-start(bf16[280,1152]{1,0:T(8,128)(2,1)S(1)} %collective-permute-done.13.refs_1_.late_ref.early_ref), channel_id=1, source_target_pairs={{0,8},{8,0},{1,9},{9,1},{2,10},{10,2},{3,11},{11,3},{4,12},{12,4},... | collective-permute-start | bytes 1935368 | tf_op jit(solution)/shard_map/ppermute | solution.py:341
  58.9 20.7 %collective-permute-start.16 = (bf16[280,1152]{1,0:T(8,128)(2,1)}, bf16[280,1152]{1,0:T(8,128)(2,1)}, u32[]{:S(2)}, u32[]{:S(2)}) collective-permute-start(bf16[280,1152]{1,0:T(8,128)(2,1)} %collective-permute-done.15.refs_1_.late_ref), channel_id=1, source_target_pairs={{0,8},{8,0},{1,9},{9,1},{2,10},{10,2},{3,11},{11,3},{4,12},{12,4},... | collective-permute-start | bytes 1935368 | tf_op jit(solution)/shard_map/ppermute | solution.py:341
  60.8 21.7 %collective-permute-start.18 = (bf16[280,1152]{1,0:T(8,128)(2,1)}, bf16[280,1152]{1,0:T(8,128)(2,1)}, u32[]{:S(2)}, u32[]{:S(2)}) collective-permute-start(bf16[280,1152]{1,0:T(8,128)(2,1)} %collective-permute-done.17.refs_2_), channel_id=1, source_target_pairs={{0,8},{8,0},{1,9},{9,1},{2,10},{10,2},{3,11},{11,3},{4,12},{12,4},... | collective-permute-start | bytes 1935368 | tf_op jit(solution)/shard_map/ppermute | solution.py:341
  63.6 12.9 %collective-permute-start.7 = (bf16[280,640]{1,0:T(8,128)(2,1)}, bf16[280,640]{1,0:T(8,128)(2,1)S(1)}, u32[]{:S(2)}, u32[]{:S(2)}) collective-permute-start(bf16[280,640]{1,0:T(8,128)(2,1)} %shard_map.100), channel_id=1, source_target_pairs={{0,1},{1,0},{2,3},{3,2},{4,5},{5,4},{6,7},{7,6},{8,10},{9,11},{10,... | collective-permute-start | bytes 1075208 | tf_op jit(solution)/shard_map/ppermute | solution.py:399
  68.4 3.3 %copy-start.14 = (s32[2]{0:T(128)S(1)}, s32[2]{0:T(128)}, u32[]{:S(2)}) copy-start(s32[2]{0:T(128)} %near_ref.3) | copy-start | bytes 28
  68.4 4.8 %copy-start.3 = (bf16[280,1152]{1,0:T(8,128)(2,1)S(1)}, bf16[280,1152]{1,0:T(8,128)(2,1)}, u32[]{:S(2)}) copy-start(bf16[280,1152]{1,0:T(8,128)(2,1)} %copy-done.2) | copy-start | bytes 1935364
  71.7 4.8 %copy-start.9 = (bf16[280,640]{1,0:T(8,128)(2,1)S(1)}, bf16[280,640]{1,0:T(8,128)(2,1)}, u32[]{:S(2)}) copy-start(bf16[280,640]{1,0:T(8,128)(2,1)} %copy-done.8) | copy-start | bytes 1075204
  71.7 10.8 %collective-permute-start.10 = (s32[2]{0:T(128)S(1)}, s32[2]{0:T(128)S(1)}, u32[]{:S(2)}, u32[]{:S(2)}) collective-permute-start(s32[2]{0:T(128)S(1)} %copy-done.14), channel_id=1, source_target_pairs={{0,16},{16,0},{1,17},{17,1},{2,18},{18,2},{3,19},{19,3},{4,20},{20... | collective-permute-start | bytes 32 | tf_op jit(solution)/shard_map/ppermute | solution.py:341
  76.5 13.8 %collective-permute-start.6 = (bf16[280,640]{1,0:T(8,128)(2,1)S(1)}, bf16[280,640]{1,0:T(8,128)(2,1)S(1)}, u32[]{:S(2)}, u32[]{:S(2)}) collective-permute-start(bf16[280,640]{1,0:T(8,128)(2,1)S(1)} %copy-done.9), channel_id=1, source_target_pairs={{0,8},{8,0},{1,9},{9,1},{2,10},{10,2},{3,11},{11,3},{4,12},{12,4},... | collective-permute-start | bytes 1075208 | tf_op jit(solution)/shard_map/ppermute | solution.py:341
  76.6 15.7 %collective-permute-start.8 = (bf16[280,640]{1,0:T(8,128)(2,1)S(1)}, bf16[280,640]{1,0:T(8,128)(2,1)S(1)}, u32[]{:S(2)}, u32[]{:S(2)}) collective-permute-start(bf16[280,640]{1,0:T(8,128)(2,1)S(1)} %collective-permute-done.7.refs_0_), channel_id=1, source_target_pairs={{0,8},{8,0},{1,9},{9,1},{2,10},{10,2},{3,11},{11,3},{4,12},{12,4},... | collective-permute-start | bytes 1075208 | tf_op jit(solution)/shard_map/ppermute | solution.py:341
  86.7 10.2 %collective-permute-start.19 = (bf16[20,16,128]{2,1,0:T(8,128)(2,1)S(1)}, bf16[20,16,128]{2,1,0:T(8,128)(2,1)S(1)}, u32[]{:S(2)}, u32[]{:S(2)}) collective-permute-start(bf16[20,16,128]{2,1,0:T(8,128)(2,1)S(1)} %get-tuple-element.25), channel_id=1, source_target_pairs={{0,1},{1,0},{2,3},{3,2},{4,5},{5,4},{6,7},{7,6},{8,9},{9,8},{10,11... | collective-permute-start | bytes 245768 | tf_op jit(solution)/shard_map/ppermute | solution.py:344
  87.3 10.8 %collective-permute-start.20 = (bf16[20,16,128]{2,1,0:T(8,128)(2,1)S(1)}, bf16[20,16,128]{2,1,0:T(8,128)(2,1)S(1)}, u32[]{:S(2)}, u32[]{:S(2)}) collective-permute-start(bf16[20,16,128]{2,1,0:T(8,128)(2,1)S(1)} %get-tuple-element.26), channel_id=1, source_target_pairs={{0,2},{1,3},{2,0},{3,1},{4,6},{5,7},{6,4},{7,5},{8,10},{9,11},{10,... | collective-permute-start | bytes 245768 | tf_op jit(solution)/shard_map/ppermute | solution.py:344
  88.3 12.9 %collective-permute-start.21 = (bf16[20,16,128]{2,1,0:T(8,128)(2,1)S(1)}, bf16[20,16,128]{2,1,0:T(8,128)(2,1)S(1)}, u32[]{:S(2)}, u32[]{:S(2)}) collective-permute-start(bf16[20,16,128]{2,1,0:T(8,128)(2,1)S(1)} %get-tuple-element.27), channel_id=1, source_target_pairs={{0,3},{1,2},{2,1},{3,0},{4,7},{5,6},{6,5},{7,4},{8,11},{9,10},{10,... | collective-permute-start | bytes 245768 | tf_op jit(solution)/shard_map/ppermute | solution.py:344
  92.3 36.7 %copy-start.19 = (s32[80]{0:T(128)S(1)}, s32[80]{0:T(128)}, u32[]{:S(2)}) copy-start(s32[80]{0:T(128)} %new_ref.1) | copy-start | bytes 964
  94.5 26.4 %collective-permute-start.9 = (bf16[192,560]{1,0:T(8,128)(2,1)S(1)}, bf16[192,560]{1,0:T(8,128)(2,1)S(1)}, u32[]{:S(2)}, u32[]{:S(2)}) collective-permute-start(bf16[192,560]{1,0:T(8,128)(2,1)S(1)} %get-tuple-element.22), channel_id=1, source_target_pairs={{0,16},{16,0},{1,17},{17,1},{2,18},{18,2},{3,19},{19,3},{4,20},{20... | collective-permute-start | bytes 645128 | tf_op jit(solution)/shard_map/ppermute | solution.py:341
  95.1 11.1 %collective-permute-start.22 = (bf16[20,16,128]{2,1,0:T(8,128)(2,1)S(1)}, bf16[20,16,128]{2,1,0:T(8,128)(2,1)S(1)}, u32[]{:S(2)}, u32[]{:S(2)}) collective-permute-start(bf16[20,16,128]{2,1,0:T(8,128)(2,1)S(1)} %get-tuple-element.28), channel_id=1, source_target_pairs={{0,4},{1,5},{2,6},{3,7},{4,0},{5,1},{6,2},{7,3},{8,12},{9,13},{10,... | collective-permute-start | bytes 245768 | tf_op jit(solution)/shard_map/ppermute | solution.py:344
  96.9 12.2 %collective-permute-start.23 = (bf16[20,16,128]{2,1,0:T(8,128)(2,1)S(1)}, bf16[20,16,128]{2,1,0:T(8,128)(2,1)S(1)}, u32[]{:S(2)}, u32[]{:S(2)}) collective-permute-start(bf16[20,16,128]{2,1,0:T(8,128)(2,1)S(1)} %get-tuple-element.29), channel_id=1, source_target_pairs={{0,5},{1,4},{2,7},{3,6},{4,1},{5,0},{6,3},{7,2},{8,13},{9,12},{10,... | collective-permute-start | bytes 245768 | tf_op jit(solution)/shard_map/ppermute | solution.py:344
  98.1 10.9 %collective-permute-start.24 = (bf16[20,16,128]{2,1,0:T(8,128)(2,1)S(1)}, bf16[20,16,128]{2,1,0:T(8,128)(2,1)S(1)}, u32[]{:S(2)}, u32[]{:S(2)}) collective-permute-start(bf16[20,16,128]{2,1,0:T(8,128)(2,1)S(1)} %get-tuple-element.30), channel_id=1, source_target_pairs={{0,6},{1,7},{2,4},{3,5},{4,2},{5,3},{6,0},{7,1},{8,14},{9,15},{10,... | collective-permute-start | bytes 245768 | tf_op jit(solution)/shard_map/ppermute | solution.py:344
  101.2 7.9 %collective-permute-start.25 = (bf16[20,16,128]{2,1,0:T(8,128)(2,1)S(1)}, bf16[20,16,128]{2,1,0:T(8,128)(2,1)S(1)}, u32[]{:S(2)}, u32[]{:S(2)}) collective-permute-start(bf16[20,16,128]{2,1,0:T(8,128)(2,1)S(1)} %get-tuple-element.31), channel_id=1, source_target_pairs={{0,7},{1,6},{2,5},{3,4},{4,3},{5,2},{6,1},{7,0},{8,15},{9,14},{10,... | collective-permute-start | bytes 245768 | tf_op jit(solution)/shard_map/ppermute | solution.py:344
  109.7 4.1 %collective-permute-start.26 = (bf16[10,16,128]{2,1,0:T(8,128)(2,1)S(1)}, bf16[10,16,128]{2,1,0:T(8,128)(2,1)S(1)}, u32[]{:S(2)}, u32[]{:S(2)}) collective-permute-start(bf16[10,16,128]{2,1,0:T(8,128)(2,1)S(1)} %get-tuple-element.33), channel_id=1, source_target_pairs={{0,16},{16,0},{1,17},{17,1},{2,18},{18,2},{3,19},{19,3},{4,20},{20... | collective-permute-start | bytes 122888 | tf_op jit(solution)/shard_map/ppermute | solution.py:341
  114.3 9.9 %collective-permute-start.34 = (bf16[20,16,128]{2,1,0:T(8,128)(2,1)S(1)}, bf16[20,16,128]{2,1,0:T(8,128)(2,1)S(1)}, u32[]{:S(2)}, u32[]{:S(2)}) collective-permute-start(bf16[20,16,128]{2,1,0:T(8,128)(2,1)S(1)} %shard_map.111.refs_0_), channel_id=1, source_target_pairs={{0,16},{8,24},{16,0},{24,8},{1,17},{9,25},{17,1},{25,9},{2,18},{10... | collective-permute-start | bytes 245768 | tf_op jit(solution)/shard_map/ppermute | solution.py:507
  115.9 9.1 %collective-permute-start.27 = (bf16[20,16,128]{2,1,0:T(8,128)(2,1)S(1)}, bf16[20,16,128]{2,1,0:T(8,128)(2,1)S(1)}, u32[]{:S(2)}, u32[]{:S(2)}) collective-permute-start(bf16[20,16,128]{2,1,0:T(8,128)(2,1)S(1)} %shard_map.111.refs_0_), channel_id=1, source_target_pairs={{0,1},{1,0},{2,3},{3,2},{4,5},{5,4},{6,7},{7,6},{8,9},{9,8},{10,11... | collective-permute-start | bytes 245768 | tf_op jit(solution)/shard_map/ppermute | solution.py:344
  117.1 10.2 %collective-permute-start.28 = (bf16[20,16,128]{2,1,0:T(8,128)(2,1)S(1)}, bf16[20,16,128]{2,1,0:T(8,128)(2,1)S(1)}, u32[]{:S(2)}, u32[]{:S(2)}) collective-permute-start(bf16[20,16,128]{2,1,0:T(8,128)(2,1)S(1)} %shard_map.111.refs_0_), channel_id=1, source_target_pairs={{0,2},{1,3},{2,0},{3,1},{4,6},{5,7},{6,4},{7,5},{8,10},{9,11},{10,... | collective-permute-start | bytes 245768 | tf_op jit(solution)/shard_map/ppermute | solution.py:344
  120.7 12.0 %collective-permute-start.29 = (bf16[20,16,128]{2,1,0:T(8,128)(2,1)S(1)}, bf16[20,16,128]{2,1,0:T(8,128)(2,1)S(1)}, u32[]{:S(2)}, u32[]{:S(2)}) collective-permute-start(bf16[20,16,128]{2,1,0:T(8,128)(2,1)S(1)} %shard_map.111.refs_0_), channel_id=1, source_target_pairs={{0,3},{1,2},{2,1},{3,0},{4,7},{5,6},{6,5},{7,4},{8,11},{9,10},{10,... | collective-permute-start | bytes 245768 | tf_op jit(solution)/shard_map/ppermute | solution.py:344
  120.9 11.9 %collective-permute-start.30 = (bf16[20,16,128]{2,1,0:T(8,128)(2,1)S(1)}, bf16[20,16,128]{2,1,0:T(8,128)(2,1)S(1)}, u32[]{:S(2)}, u32[]{:S(2)}) collective-permute-start(bf16[20,16,128]{2,1,0:T(8,128)(2,1)S(1)} %shard_map.111.refs_0_), channel_id=1, source_target_pairs={{0,4},{1,5},{2,6},{3,7},{4,0},{5,1},{6,2},{7,3},{8,12},{9,13},{10,... | collective-permute-start | bytes 245768 | tf_op jit(solution)/shard_map/ppermute | solution.py:344
  124.2 11.5 %collective-permute-start.31 = (bf16[20,16,128]{2,1,0:T(8,128)(2,1)S(1)}, bf16[20,16,128]{2,1,0:T(8,128)(2,1)S(1)}, u32[]{:S(2)}, u32[]{:S(2)}) collective-permute-start(bf16[20,16,128]{2,1,0:T(8,128)(2,1)S(1)} %shard_map.111.refs_0_), channel_id=1, source_target_pairs={{0,5},{1,4},{2,7},{3,6},{4,1},{5,0},{6,3},{7,2},{8,13},{9,12},{10,... | collective-permute-start | bytes 245768 | tf_op jit(solution)/shard_map/ppermute | solution.py:344
  125.0 10.7 %collective-permute-start.32 = (bf16[20,16,128]{2,1,0:T(8,128)(2,1)S(1)}, bf16[20,16,128]{2,1,0:T(8,128)(2,1)S(1)}, u32[]{:S(2)}, u32[]{:S(2)}) collective-permute-start(bf16[20,16,128]{2,1,0:T(8,128)(2,1)S(1)} %shard_map.111.refs_0_), channel_id=1, source_target_pairs={{0,6},{1,7},{2,4},{3,5},{4,2},{5,3},{6,0},{7,1},{8,14},{9,15},{10,... | collective-permute-start | bytes 245768 | tf_op jit(solution)/shard_map/ppermute | solution.py:344
  127.3 8.4 %collective-permute-start.33 = (bf16[20,16,128]{2,1,0:T(8,128)(2,1)S(1)}, bf16[20,16,128]{2,1,0:T(8,128)(2,1)S(1)}, u32[]{:S(2)}, u32[]{:S(2)}) collective-permute-start(bf16[20,16,128]{2,1,0:T(8,128)(2,1)S(1)} %shard_map.111.refs_0_), channel_id=1, source_target_pairs={{0,7},{1,6},{2,5},{3,4},{4,3},{5,2},{6,1},{7,0},{8,15},{9,14},{10,... | collective-permute-start | bytes 245768 | tf_op jit(solution)/shard_map/ppermute | solution.py:344
  132.7 5.3 %collective-permute-start.35 = (bf16[20,16,128]{2,1,0:T(8,128)(2,1)S(1)}, bf16[20,16,128]{2,1,0:T(8,128)(2,1)S(1)}, u32[]{:S(2)}, u32[]{:S(2)}) collective-permute-start(bf16[20,16,128]{2,1,0:T(8,128)(2,1)S(1)} %shard_map.111.refs_0_), channel_id=1, source_target_pairs={{0,8},{8,0},{16,24},{24,16},{1,9},{9,1},{17,25},{25,17},{2,10},{10... | collective-permute-start | bytes 245768 | tf_op jit(solution)/shard_map/ppermute | solution.py:507
  132.8 5.2 %collective-permute-start.36 = (bf16[20,16,128]{2,1,0:T(8,128)(2,1)S(1)}, bf16[20,16,128]{2,1,0:T(8,128)(2,1)S(1)}, u32[]{:S(2)}, u32[]{:S(2)}) collective-permute-start(bf16[20,16,128]{2,1,0:T(8,128)(2,1)S(1)} %collective-permute-done.34.refs_1_), channel_id=1, source_target_pairs={{0,8},{8,0},{16,24},{24,16},{1,9},{9,1},{17,25},{25,17},{2,10},{10... | collective-permute-start | bytes 245768 | tf_op jit(solution)/shard_map/ppermute | solution.py:507
  (11 other events, 11.9 us)

commit v4 on v3

--- a/solution.py
+++ b/solution.py
@@ -48,7 +48,7 @@
     return jnp.where(u > 0.0, u + 1.0, jnp.exp(jnp.minimum(u, 0.0)))
 
 
-def whole_call(kernel, out_shape, kinds, flops, moved, scratch=(), alias=None, smem=False):
+def whole_call(kernel, out_shape, kinds, flops, moved, scratch=(), alias=None, smem=False, room=20):
     return pl.pallas_call(
         kernel,
         out_shape=out_shape,
@@ -57,7 +57,7 @@
         input_output_aliases=alias or {},
         out_specs=SMEM if smem else jax.tree.map(lambda _: VMEM, out_shape),
         cost_estimate=pl.CostEstimate(flops=flops, bytes_accessed=moved, transcendentals=0),
-        compiler_params=pltpu.CompilerParams(vmem_limit_bytes=20 * 1024 * 1024),
+        compiler_params=pltpu.CompilerParams(vmem_limit_bytes=room * 1024 * 1024),
     )
 
 
@@ -243,6 +243,10 @@
                 chunk[s * heads + h] = outer[r * rows : (r + 1) * rows]
 
 
+def add_kernel(pos_ref, one_ref, two_ref, out_ref):
+    out_ref[...] = (one_ref[...].astype(F32) + two_ref[...].astype(F32)).astype(BF16)
+
+
 def sum_kernel(*refs):
     parts, keep_ref, give_ref = refs[1:-2], refs[-2], refs[-1]
     half = keep_ref.shape[0]
@@ -372,6 +376,7 @@
             0,
             2_000_000,
             scratch=[pltpu.VMEM(w_qkv.shape, BF16), pltpu.SemaphoreType.DMA((5,))],
+            room=60,
         )(place_of, w_qkv)
 
     pieces = [prep((1, 2), wide_kv), prep((0,), wide_q)]
@@ -468,7 +473,11 @@
         scratch=[pltpu.VMEM(asked.shape, F32)],
     )(pos, blocks, asked, group, *last_q)
 
-    for k in range(members - 1, 0, -1):
+    far = members - 1
+    parts[far - 1] = whole_call(
+        add_kernel, chunk, "svv", 0, 250_000
+    )(pos, parts[far - 1], xor(1, parts.pop()))
+    for k in range(far - 1, 0, -1):
         parts[k] = xor(k, parts[k])
     q_other = swap("y", q_give)
 
@@ -478,7 +487,7 @@
             jax.ShapeDtypeStruct((pairs // 2, rows, LANES), F32),
             jax.ShapeDtypeStruct((pairs // 2, rows, LANES), BF16),
         ],
-        "s" + "v" * members,
+        "s" + "v" * far,
         0,
         1_000_000,
     )(pos, *parts)
@@ -491,7 +500,8 @@
         500_000,
     )(pos, keep, got, old)
 
-    gathered = [new] + [xor(k, new) for k in range(1, members)]
+    gathered = [new] + [xor(k, new) for k in range(1, far)]
+    gathered.append(xor(1, gathered[far - 1]))
     q_other = whole_call(
         query_kernel,
         jax.ShapeDtypeStruct((count, heads * LANES), BF16),

time: 140 us -> 133 us (0.950)
  starting transfers between devices: 46.9 us -> 38 us
  Pallas kernels: 37.3 us -> 41.3 us
  local copies, waits for them, and re-layouts: 7.45 us -> 3.53 us
  waiting for transfers between devices: 46.6 us -> 48.6 us
    ppermute x14, waiting for transfers between devices: 8.76 us -> 3.33 us  [xor(): return lax.ppermute(v, ('z', 'x'), [(i, i ^ k) for i in range(members)])]
    unnamed x46 -> x28, local copies, waits for them, and re-layouts: 6.59 us -> 2.16 us
    ppermute x8, waiting for transfers between devices: 35.3 us -> 39.7 us  [rounds(): got.append(lax.ppermute(give, ('c', 'z', 'x'), step))]
    ppermute x14, starting transfers between devices: 24.3 us -> 20.2 us  [xor(): return lax.ppermute(v, ('z', 'x'), [(i, i ^ k) for i in range(members)])]
    pallas_call x2, Pallas kernels: 2.87 us -> 5.76 us  [prep(): whole_call(functools.partial(prep_kernel, kinds), jax.ShapeDtypeStruct((d...]
    ppermute x8, starting transfers between devices: 13.2 us -> 11.3 us  [rounds(): got.append(lax.ppermute(give, ('c', 'z', 'x'), step))]
    ppermute x12, waiting for transfers between devices: 2.51 us -> 4.2 us  [swap(): return lax.ppermute(v, axis, SWAP)]
    ppermute x3, starting transfers between devices: 2.14 us -> 0.6 us  [layer(): moved = lax.ppermute(every[i], ('o', 'y', 'c'), step)]
  transfers between devices with their start and end apart: 37 -> 37, of which waited for: 10 -> 11; matrix products, arithmetic and copies ran while one was open for 1% -> 1% of each run, Pallas kernels for 24% -> 26%
where the time goes in v4:
time: 133 us; the launch traced here: 132 us
  waiting for transfers between devices  48.6 us (37%)
  Pallas kernels  41.3 us (31%)
  starting transfers between devices  38 us (29%)
  local copies, waits for them, and re-layouts  3.53 us (3%)
    ppermute x8, waiting for transfers between devices, rounds(): got.append(lax.ppermute(give, ('c', 'z', 'x'), step))  39.7 us
    ppermute x14, starting transfers between devices, xor(): return lax.ppermute(v, ('z', 'x'), [(i, i ^ k) for i in range(members)])  20.2 us
    pallas_call x5, Pallas kernels, multiply(): whole_call(functools.partial(mul_kernel, slots, acc is None), jax.ShapeDt...  13.6 us
    ppermute x8, starting transfers between devices, rounds(): got.append(lax.ppermute(give, ('c', 'z', 'x'), step))  11.3 us
    ppermute x12, starting transfers between devices, swap(): return lax.ppermute(v, axis, SWAP)  5.92 us
    pallas_call x2, Pallas kernels, prep(): whole_call(functools.partial(prep_kernel, kinds), jax.ShapeDtypeStruct((d...  5.76 us
    ppermute x12, waiting for transfers between devices, swap(): return lax.ppermute(v, axis, SWAP)  4.2 us
    pallas_call x1, Pallas kernels, layer(): whole_call(functools.partial(kv_kernel, last, streams, frames, heads, siz...  4.18 us
  transfers between devices with their start and end apart: 37, of which 11 were waited for; matrix products, arithmetic and copies ran while one was open for 1% of the time, Pallas kernels for 26%

profile of v4, /device:TPU:0, one launch (start us, length us, event | category | flops | bytes accessed | tf_op | source)
XLA Modules:
  0.0 132.3 jit_solution(9435577762515931352)
XLA Ops:
  1.2 3.2 %shard_map.103.refs_0_ = bf16[280,1152]{1,0:T(8,128)(2,1)} custom-call(s32[6]{0:T(128)} %stack.27.pos_ref, bf16[280,3360]{1,0:T(8,128)(2,1)} %w_hbm.3), custom_call_target="tpu_custom_call" | custom-call | bytes 2000000 | tf_op jit(solution)/shard_map/pallas_call | solution.py:372
  4.4 3.1 %collective-permute-start.11 = (bf16[280,1152]{1,0:T(8,128)(2,1)}, bf16[280,1152]{1,0:T(8,128)(2,1)S(1)}, u32[]{:S(2)}, u32[]{:S(2)}) collective-permute-start(bf16[280,1152]{1,0:T(8,128)(2,1)} %shard_map.103.refs_0_), channel_id=1, source_target_pairs={{0,2},{1,3},{2,0},{3,1},{4,6},{5,7},{6,4},{7,5},{8,9},{9,8},{10,12... | collective-permute-start | bytes 1935368 | tf_op jit(solution)/shard_map/ppermute | solution.py:404
  7.5 8.7 %collective-permute-done.11.refs_1_.early_ref = bf16[280,1152]{1,0:T(8,128)(2,1)S(1)} collective-permute-done((bf16[280,1152]{1,0:T(8,128)(2,1)}, bf16[280,1152]{1,0:T(8,128)(2,1)S(1)}, u32[]{:S(2)}, u32[]{:S(2)}) %collective-permute-start.11) | collective-permute-done | bytes 645152 | tf_op jit(solution)/shard_map/ppermute | solution.py:404
  16.2 1.9 %collective-permute-start.13 = (bf16[280,1152]{1,0:T(8,128)(2,1)S(1)}, bf16[280,1152]{1,0:T(8,128)(2,1)S(1)}, u32[]{:S(2)}, u32[]{:S(2)}) collective-permute-start(bf16[280,1152]{1,0:T(8,128)(2,1)S(1)} %collective-permute-done.11.refs_1_.early_ref), channel_id=1, source_target_pairs={{0,1},{1,0},{2,4},{3,5},{4,2},{5,3},{6,7},{7,6},{8,10},{9,11},{10,... | collective-permute-start | bytes 1935368 | tf_op jit(solution)/shard_map/ppermute | solution.py:404
  18.9 7.8 %collective-permute-done.13.refs_1_.late_ref.early_ref = bf16[280,1152]{1,0:T(8,128)(2,1)S(1)} collective-permute-done((bf16[280,1152]{1,0:T(8,128)(2,1)S(1)}, bf16[280,1152]{1,0:T(8,128)(2,1)S(1)}, u32[]{:S(2)}, u32[]{:S(2)}) %collective-permute-start.13) | collective-permute-done | bytes 645152 | tf_op jit(solution)/shard_map/ppermute | solution.py:404
  26.7 1.4 %shard_map.106 = bf16[280,1152]{1,0:T(8,128)(2,1)} custom-call(s32[16]{0:T(128)S(1)} %concatenate.4.pos_ref.refs_0_, bf16[280,1152]{1,0:T(8,128)(2,1)S(1)} %collective-permute-done.11.refs_1_.early_ref, bf16[280,1152]{1,0:T(8,128)(2,1)S(1)} %collective-permute-done.13.refs_1_.late_ref.early_ref), custom_call_target="tpu_custom_call" | custom-call | bytes 1000000 | tf_op jit(solution)/shard_map/pallas_call | solution.py:385
  28.1 2.0 %collective-permute-start.15 = (bf16[280,1152]{1,0:T(8,128)(2,1)}, bf16[280,1152]{1,0:T(8,128)(2,1)S(1)}, u32[]{:S(2)}, u32[]{:S(2)}) collective-permute-start(bf16[280,1152]{1,0:T(8,128)(2,1)} %shard_map.106), channel_id=1, source_target_pairs={{0,2},{1,3},{2,0},{3,1},{4,6},{5,7},{6,4},{7,5},{8,9},{9,8},{10,11... | collective-permute-start | bytes 1935368 | tf_op jit(solution)/shard_map/ppermute | solution.py:404
  30.1 2.6 %shard_map.95.refs_0_ = bf16[280,640]{1,0:T(8,128)(2,1)} custom-call(s32[6]{0:T(128)} %stack.27.pos_ref, bf16[280,3360]{1,0:T(8,128)(2,1)} %w_hbm.3), custom_call_target="tpu_custom_call" | custom-call | bytes 2000000 | tf_op jit(solution)/shard_map/pallas_call | solution.py:372
  32.8 11.1 %collective-permute-done.1.refs_1_.early_ref = bf16[280,640]{1,0:T(8,128)(2,1)S(1)} collective-permute-done((bf16[280,640]{1,0:T(8,128)(2,1)}, bf16[280,640]{1,0:T(8,128)(2,1)S(1)}, u32[]{:S(2)}, u32[]{:S(2)}) %collective-permute-start.1) | collective-permute-done | bytes 358432 | tf_op jit(solution)/shard_map/ppermute | solution.py:404
  43.9 1.3 %collective-permute-start.3 = (bf16[280,640]{1,0:T(8,128)(2,1)S(1)}, bf16[280,640]{1,0:T(8,128)(2,1)S(1)}, u32[]{:S(2)}, u32[]{:S(2)}) collective-permute-start(bf16[280,640]{1,0:T(8,128)(2,1)S(1)} %collective-permute-done.1.refs_1_.early_ref), channel_id=1, source_target_pairs={{0,1},{1,0},{2,4},{3,5},{4,2},{5,3},{6,7},{7,6},{8,10},{9,11},{10,... | collective-permute-start | bytes 1075208 | tf_op jit(solution)/shard_map/ppermute | solution.py:404
  45.2 1.5 %collective-permute-start = (bf16[192,2240]{1,0:T(8,128)(2,1)S(1)}, bf16[192,2240]{1,0:T(8,128)(2,1)S(1)}, u32[]{:S(2)}, u32[]{:S(2)}) collective-permute-start(bf16[192,2240]{1,0:T(8,128)(2,1)S(1)} %bitcast.11), channel_id=1, source_target_pairs={{0,16},{16,0},{1,17},{17,1},{2,18},{18,2},{3,19},{19,3},{4,20},{20... | collective-permute-start | bytes 2580488 | tf_op jit(solution)/shard_map/ppermute | solution.py:345
  47.9 4.9 %collective-permute-done.3.refs_3_.late_ref.early_ref = bf16[280,640]{1,0:T(8,128)(2,1)S(1)} collective-permute-done((bf16[280,640]{1,0:T(8,128)(2,1)S(1)}, bf16[280,640]{1,0:T(8,128)(2,1)S(1)}, u32[]{:S(2)}, u32[]{:S(2)}) %collective-permute-start.3) | collective-permute-done | bytes 358432 | tf_op jit(solution)/shard_map/ppermute | solution.py:404
  53.4 0.9 collective-permute-start.5
  54.8 6.1 %collective-permute-done.5.refs_1_.late_ref = bf16[280,640]{1,0:T(8,128)(2,1)S(1)} collective-permute-done((bf16[280,640]{1,0:T(8,128)(2,1)S(1)}, bf16[280,640]{1,0:T(8,128)(2,1)S(1)}, u32[]{:S(2)}, u32[]{:S(2)}) %collective-permute-start.5) | collective-permute-done | bytes 358432 | tf_op jit(solution)/shard_map/ppermute | solution.py:404
  60.9 1.3 collective-permute-done.17.refs_2_
  62.1 1.3 shard_map.100
  63.5 0.9 copy-done.2
  64.4 1.3 %collective-permute-start.7 = (bf16[280,640]{1,0:T(8,128)(2,1)}, bf16[280,640]{1,0:T(8,128)(2,1)}, u32[]{:S(2)}, u32[]{:S(2)}) collective-permute-start(bf16[280,640]{1,0:T(8,128)(2,1)} %shard_map.100), channel_id=1, source_target_pairs={{0,1},{1,0},{2,3},{3,2},{4,5},{5,4},{6,7},{7,6},{8,10},{9,11},{10,... | collective-permute-start | bytes 1075208 | tf_op jit(solution)/shard_map/ppermute | solution.py:404
  65.8 0.9 shard_map.99
  66.7 1.2 copy-done.3
  67.9 1.3 shard_map.94.blocks_ref.refs_0_
  69.2 1.6 %collective-permute-start.10 = (s32[2]{0:T(128)S(1)}, s32[2]{0:T(128)S(1)}, u32[]{:S(2)}, u32[]{:S(2)}) collective-permute-start(s32[2]{0:T(128)S(1)} %copy-done.9), channel_id=1, source_target_pairs={{0,16},{16,0},{1,17},{17,1},{2,18},{18,2},{3,19},{19,3},{4,20},{20... | collective-permute-start | bytes 32 | tf_op jit(solution)/shard_map/ppermute | solution.py:345
  70.8 3.2 %shard_map.104.refs_0_ = f32[384,1152]{1,0:T(8,128)S(1)} custom-call(s32[16]{0:T(128)S(1)} %concatenate.4.pos_ref.refs_0_, bf16[8,384,280]{2,1,0:T(8,128)(2,1)S(1)} %shard_map.94.blocks_ref.refs_0_, bf16[280,1152]{1,0:T(8,128)(2,1)S(1)} %copy-done, bf16[280,1152]{1,0:T(8,128)(2,1)S(1)} %collective-permute-done.11.refs_1_.early_ref, ...), custom_call_target="tpu_custom_call" | custom-call | flops 1500000000 | bytes 5000000 | tf_op jit(solution)/shard_map/pallas_call | solution.py:430
  74.6 2.6 %shard_map.105.refs_0_ = f32[384,1152]{1,0:T(8,128)S(1)} custom-call(s32[16]{0:T(128)S(1)} %concatenate.4.pos_ref.refs_0_, bf16[8,384,280]{2,1,0:T(8,128)(2,1)S(1)} %shard_map.94.blocks_ref.refs_0_, f32[384,1152]{1,0:T(8,128)S(1)} %shard_map.104.refs_0_, ...), custom_call_target="tpu_custom_call", output_to_operand_aliasing={{}: (2, {})} | custom-call | flops 1500000000 | bytes 5000000 | tf_op jit(solution)/shard_map/pallas_call | solution.py:430
  77.8 2.6 %shard_map.107.refs_1_ = f32[384,1152]{1,0:T(8,128)S(1)} custom-call(s32[16]{0:T(128)S(1)} %concatenate.4.pos_ref.refs_0_, bf16[8,384,280]{2,1,0:T(8,128)(2,1)S(1)} %shard_map.94.blocks_ref.refs_0_, f32[384,1152]{1,0:T(8,128)S(1)} %shard_map.105.refs_0_, ...), custom_call_target="tpu_custom_call", output_to_operand_aliasing={{}: (2, {})} | custom-call | flops 1500000000 | bytes 5000000 | tf_op jit(solution)/shard_map/pallas_call | solution.py:430
  80.5 4.2 %shard_map.109 = (bf16[20,16,128]{2,1,0:T(8,128)(2,1)S(1)}, bf16[20,16,128]{2,1,0:T(8,128)(2,1)S(1)}, bf16[20,16,128]{2,1,0:T(8,128)(2,1)S(1)}, bf16[20,16,128]{...) custom-call(s32[16]{0:T(128)S(1)} %concatenate.4.pos_ref.refs_0_, ...), custom_call_target="tpu_custom_call" | custom-call | flops 1500000000 | bytes 5000000 | tf_op jit(solution)/shard_map/pallas_call | solution.py:455
  85.2 1.5 %collective-permute-start.19 = (bf16[20,16,128]{2,1,0:T(8,128)(2,1)S(1)}, bf16[20,16,128]{2,1,0:T(8,128)(2,1)S(1)}, u32[]{:S(2)}, u32[]{:S(2)}) collective-permute-start(bf16[20,16,128]{2,1,0:T(8,128)(2,1)S(1)} %get-tuple-element.25), channel_id=1, source_target_pairs={{0,1},{1,0},{2,3},{3,2},{4,5},{5,4},{6,7},{7,6},{8,9},{9,8},{10,11... | collective-permute-start | bytes 245768 | tf_op jit(solution)/shard_map/ppermute | solution.py:348
  86.7 3.2 %shard_map.96.refs_0_ = f32[384,640]{1,0:T(8,128)S(1)} custom-call(s32[16]{0:T(128)S(1)} %concatenate.4.pos_ref.refs_0_, bf16[8,384,280]{2,1,0:T(8,128)(2,1)S(1)} %shard_map.94.blocks_ref.refs_0_, bf16[280,640]{1,0:T(8,128)(2,1)S(1)} %copy-done.6, bf16[280,640]{1,0:T(8,128)(2,1)S(1)} %copy-done.8, bf16[280,640]{1,0:T(8,128)(2,1)S(1)} %collective-permute-done.2.refs_2_, ...), custom_call_target="tpu_custom_call" | custom-call | flops 1500000000 | bytes 5000000 | tf_op jit(solution)/shard_map/pallas_call | solution.py:430
  90.4 1.6 %collective-permute-start.21 = (bf16[20,16,128]{2,1,0:T(8,128)(2,1)S(1)}, bf16[20,16,128]{2,1,0:T(8,128)(2,1)S(1)}, u32[]{:S(2)}, u32[]{:S(2)}) collective-permute-start(bf16[20,16,128]{2,1,0:T(8,128)(2,1)S(1)} %get-tuple-element.27), channel_id=1, source_target_pairs={{0,3},{1,2},{2,1},{3,0},{4,7},{5,6},{6,5},{7,4},{8,11},{9,10},{10,... | collective-permute-start | bytes 245768 | tf_op jit(solution)/shard_map/ppermute | solution.py:348
  92.6 2.7 %collective-permute-start.22 = (bf16[20,16,128]{2,1,0:T(8,128)(2,1)S(1)}, bf16[20,16,128]{2,1,0:T(8,128)(2,1)S(1)}, u32[]{:S(2)}, u32[]{:S(2)}) collective-permute-start(bf16[20,16,128]{2,1,0:T(8,128)(2,1)S(1)} %get-tuple-element.28), channel_id=1, source_target_pairs={{0,4},{1,5},{2,6},{3,7},{4,0},{5,1},{6,2},{7,3},{8,12},{9,13},{10,... | collective-permute-start | bytes 245768 | tf_op jit(solution)/shard_map/ppermute | solution.py:348
  95.3 1.2 collective-permute-start.23
  96.5 3.1 %collective-permute-start.25 = (bf16[20,16,128]{2,1,0:T(8,128)(2,1)S(1)}, bf16[20,16,128]{2,1,0:T(8,128)(2,1)S(1)}, u32[]{:S(2)}, u32[]{:S(2)}) collective-permute-start(bf16[20,16,128]{2,1,0:T(8,128)(2,1)S(1)} %shard_map.110), channel_id=1, source_target_pairs={{0,6},{1,7},{2,4},{3,5},{4,2},{5,3},{6,0},{7,1},{8,14},{9,15},{10,... | collective-permute-start | bytes 245768 | tf_op jit(solution)/shard_map/ppermute | solution.py:348
  99.6 2.0 %shard_map.98.old_ref = f32[384,640]{1,0:T(8,128)S(1)} custom-call(s32[16]{0:T(128)S(1)} %concatenate.4.pos_ref.refs_0_, bf16[8,384,280]{2,1,0:T(8,128)(2,1)S(1)} %shard_map.94.blocks_ref.refs_0_, f32[384,640]{1,0:T(8,128)S(1)} %shard_map.96.refs_0_, bf16[280,640]{1,0:T(8,128)(2,1)S(1)} %copy-done.5, ...), custom_call_target="tpu_custom_call", output_to_operand_aliasing={{}: (2, {})} | custom-call | flops 1500000000 | bytes 5000000 | tf_op jit(solution)/shard_map/pallas_call | solution.py:430
  101.7 2.6 %shard_map.101 = (bf16[192,640]{1,0:T(8,128)(2,1)S(1)}, bf16[192,560]{1,0:T(8,128)(2,1)S(1)}) custom-call(s32[16]{0:T(128)S(1)} %concatenate.4.pos_ref.refs_0_, bf16[8,384,280]{2,1,0:T(8,128)(2,1)S(1)} %shard_map.94.blocks_ref.refs_0_, f32[384,640]{1,0:T(8,128)S(1)} %shard_map.98.old_ref, bf16[560,640]{1,0:T(8,128)(2,1)S(1)} %get-tuple-element.20.group_ref.refs_4_, ...), custom_call_target="tpu_custom_call" | custom-call | flops 700000000 | bytes 3000000 | tf_op jit(solution)/shard_map/pallas_call | solution.py:464
  104.9 1.2 collective-permute-done.23.refs_6_
  107.3 4.2 %collective-permute-done.26.got_ref = bf16[10,16,128]{2,1,0:T(8,128)(2,1)S(1)} collective-permute-done((bf16[10,16,128]{2,1,0:T(8,128)(2,1)S(1)}, bf16[10,16,128]{2,1,0:T(8,128)(2,1)S(1)}, u32[]{:S(2)}, u32[]{:S(2)}) %collective-permute-start.26) | collective-permute-done | bytes 40992 | tf_op jit(solution)/shard_map/ppermute | solution.py:345
  112.6 1.5 %collective-permute-start.32 = (bf16[20,16,128]{2,1,0:T(8,128)(2,1)S(1)}, bf16[20,16,128]{2,1,0:T(8,128)(2,1)S(1)}, u32[]{:S(2)}, u32[]{:S(2)}) collective-permute-start(bf16[20,16,128]{2,1,0:T(8,128)(2,1)S(1)} %shard_map.112.refs_0_), channel_id=1, source_target_pairs={{0,6},{1,7},{2,4},{3,5},{4,2},{5,3},{6,0},{7,1},{8,14},{9,15},{10,... | collective-permute-start | bytes 245768 | tf_op jit(solution)/shard_map/ppermute | solution.py:348
  114.2 1.0 collective-permute-start.27
  115.2 1.3 %collective-permute-done.34.refs_1_ = bf16[20,16,128]{2,1,0:T(8,128)(2,1)S(1)} collective-permute-done((bf16[20,16,128]{2,1,0:T(8,128)(2,1)S(1)}, bf16[20,16,128]{2,1,0:T(8,128)(2,1)S(1)}, u32[]{:S(2)}, u32[]{:S(2)}) %collective-permute-start.34) | collective-permute-done | bytes 81952 | tf_op jit(solution)/shard_map/ppermute | solution.py:517
  116.6 1.9 %collective-permute-start.29 = (bf16[20,16,128]{2,1,0:T(8,128)(2,1)S(1)}, bf16[20,16,128]{2,1,0:T(8,128)(2,1)S(1)}, u32[]{:S(2)}, u32[]{:S(2)}) collective-permute-start(bf16[20,16,128]{2,1,0:T(8,128)(2,1)S(1)} %shard_map.112.refs_0_), channel_id=1, source_target_pairs={{0,3},{1,2},{2,1},{3,0},{4,7},{5,6},{6,5},{7,4},{8,11},{9,10},{10,... | collective-permute-start | bytes 245768 | tf_op jit(solution)/shard_map/ppermute | solution.py:348
  119.3 1.3 %collective-permute-start.30 = (bf16[20,16,128]{2,1,0:T(8,128)(2,1)S(1)}, bf16[20,16,128]{2,1,0:T(8,128)(2,1)S(1)}, u32[]{:S(2)}, u32[]{:S(2)}) collective-permute-start(bf16[20,16,128]{2,1,0:T(8,128)(2,1)S(1)} %shard_map.112.refs_0_), channel_id=1, source_target_pairs={{0,4},{1,5},{2,6},{3,7},{4,0},{5,1},{6,2},{7,3},{8,12},{9,13},{10,... | collective-permute-start | bytes 245768 | tf_op jit(solution)/shard_map/ppermute | solution.py:348
  120.6 1.8 %collective-permute-start.31 = (bf16[20,16,128]{2,1,0:T(8,128)(2,1)S(1)}, bf16[20,16,128]{2,1,0:T(8,128)(2,1)S(1)}, u32[]{:S(2)}, u32[]{:S(2)}) collective-permute-start(bf16[20,16,128]{2,1,0:T(8,128)(2,1)S(1)} %shard_map.112.refs_0_), channel_id=1, source_target_pairs={{0,5},{1,4},{2,7},{3,6},{4,1},{5,0},{6,3},{7,2},{8,13},{9,12},{10,... | collective-permute-start | bytes 245768 | tf_op jit(solution)/shard_map/ppermute | solution.py:348
  122.4 1.3 collective-permute-start.33
  123.7 2.8 %shard_map.114.place_ref = s32[20]{0:T(128)S(1)} custom-call(s32[16]{0:T(128)S(1)} %concatenate.4.pos_ref.refs_0_, s32[80]{0:T(128)S(1)} %copy-done.10), custom_call_target="tpu_custom_call" | custom-call | bytes 1000 | tf_op jit(solution)/shard_map/pallas_call | solution.py:521
  126.4 0.9 shard_map.102.other_ref
  127.4 1.3 shard_map.115
  128.6 1.4 %collective-permute-done.31.refs_5_ = bf16[20,16,128]{2,1,0:T(8,128)(2,1)S(1)} collective-permute-done((bf16[20,16,128]{2,1,0:T(8,128)(2,1)S(1)}, bf16[20,16,128]{2,1,0:T(8,128)(2,1)S(1)}, u32[]{:S(2)}, u32[]{:S(2)}) %collective-permute-start.31) | collective-permute-done | bytes 81952 | tf_op jit(solution)/shard_map/ppermute | solution.py:348
  130.1 2.2 %shard_map.113 = bf16[192,1120]{1,0:T(8,128)(2,1)} custom-call(s32[16]{0:T(128)S(1)} %concatenate.4.pos_ref.refs_0_, s32[2]{0:T(128)S(1)} %copy-done.9, bf16[192,640]{1,0:T(8,128)(2,1)S(1)} %get-tuple-element.21.own_ref, bf16[192,640]{1,0:T(8,128)(2,1)S(1)} %shard_map.102.other_ref, bf16[20,16,128]{2,1,0:T(8,128)(2,1)S(1)} %shard_map.112.refs_0_, ...), custom_call_target="tpu_custom_call" | custom-call | flops 1500000000 | bytes 3000000 | tf_op jit(solution)/shard_map/pallas_call | solution.py:541
  (80 shorter events, 10.4 us)
Async XLA Ops:
  4.4 11.8 %collective-permute-start.11 = (bf16[280,1152]{1,0:T(8,128)(2,1)}, bf16[280,1152]{1,0:T(8,128)(2,1)S(1)}, u32[]{:S(2)}, u32[]{:S(2)}) collective-permute-start(bf16[280,1152]{1,0:T(8,128)(2,1)} %shard_map.103.refs_0_), channel_id=1, source_target_pairs={{0,2},{1,3},{2,0},{3,1},{4,6},{5,7},{6,4},{7,5},{8,9},{9,8},{10,12... | collective-permute-start | bytes 1935368 | tf_op jit(solution)/shard_map/ppermute | solution.py:404
  16.2 10.5 %collective-permute-start.13 = (bf16[280,1152]{1,0:T(8,128)(2,1)S(1)}, bf16[280,1152]{1,0:T(8,128)(2,1)S(1)}, u32[]{:S(2)}, u32[]{:S(2)}) collective-permute-start(bf16[280,1152]{1,0:T(8,128)(2,1)S(1)} %collective-permute-done.11.refs_1_.early_ref), channel_id=1, source_target_pairs={{0,1},{1,0},{2,4},{3,5},{4,2},{5,3},{6,7},{7,6},{8,10},{9,11},{10,... | collective-permute-start | bytes 1935368 | tf_op jit(solution)/shard_map/ppermute | solution.py:404
  18.9 26.3 %copy-start.1 = (bf16[2,4,24,2240]{3,2,1,0:T(8,128)(2,1)S(1)}, bf16[2,4,24,2240]{3,2,1,0:T(8,128)(2,1)}, u32[]{:S(2)}) copy-start(bf16[2,4,24,2240]{3,2,1,0:T(8,128)(2,1)} %param.7) | copy-start | bytes 2580484
  28.1 18.6 %collective-permute-start.15 = (bf16[280,1152]{1,0:T(8,128)(2,1)}, bf16[280,1152]{1,0:T(8,128)(2,1)S(1)}, u32[]{:S(2)}, u32[]{:S(2)}) collective-permute-start(bf16[280,1152]{1,0:T(8,128)(2,1)} %shard_map.106), channel_id=1, source_target_pairs={{0,2},{1,3},{2,0},{3,1},{4,6},{5,7},{6,4},{7,5},{8,9},{9,8},{10,11... | collective-permute-start | bytes 1935368 | tf_op jit(solution)/shard_map/ppermute | solution.py:404
  32.7 11.1 %collective-permute-start.1 = (bf16[280,640]{1,0:T(8,128)(2,1)}, bf16[280,640]{1,0:T(8,128)(2,1)S(1)}, u32[]{:S(2)}, u32[]{:S(2)}) collective-permute-start(bf16[280,640]{1,0:T(8,128)(2,1)} %shard_map.95.refs_0_), channel_id=1, source_target_pairs={{0,2},{1,3},{2,0},{3,1},{4,6},{5,7},{6,4},{7,5},{8,9},{9,8},{10,12... | collective-permute-start | bytes 1075208 | tf_op jit(solution)/shard_map/ppermute | solution.py:404
  43.9 19.6 %copy-start.7 = (bf16[280,640]{1,0:T(8,128)(2,1)}, bf16[280,640]{1,0:T(8,128)(2,1)S(1)}, u32[]{:S(2)}) copy-start(bf16[280,640]{1,0:T(8,128)(2,1)S(1)} %collective-permute-done.1.refs_1_.early_ref) | copy-start | bytes 1075204
  43.9 8.9 %collective-permute-start.3 = (bf16[280,640]{1,0:T(8,128)(2,1)S(1)}, bf16[280,640]{1,0:T(8,128)(2,1)S(1)}, u32[]{:S(2)}, u32[]{:S(2)}) collective-permute-start(bf16[280,640]{1,0:T(8,128)(2,1)S(1)} %collective-permute-done.1.refs_1_.early_ref), channel_id=1, source_target_pairs={{0,1},{1,0},{2,4},{3,5},{4,2},{5,3},{6,7},{7,6},{8,10},{9,11},{10,... | collective-permute-start | bytes 1075208 | tf_op jit(solution)/shard_map/ppermute | solution.py:404
  45.2 20.5 %copy-start.11 = (f32[2,10,14,112]{3,0,2,1:T(2,128)S(1)}, f32[2,10,14,112]{3,0,2,1:T(2,128)}, u32[]{:S(2)}) copy-start(f32[2,10,14,112]{3,0,2,1:T(2,128)} %param.9) | copy-start | bytes 376324
  45.2 20.6 %copy-start.12 = (f32[2,10,112]{2,0,1:T(2,128)S(1)}, f32[2,10,112]{2,0,1:T(2,128)}, u32[]{:S(2)}) copy-start(f32[2,10,112]{2,0,1:T(2,128)} %param.10) | copy-start | bytes 26884
  45.2 18.3 %collective-permute-start = (bf16[192,2240]{1,0:T(8,128)(2,1)S(1)}, bf16[192,2240]{1,0:T(8,128)(2,1)S(1)}, u32[]{:S(2)}, u32[]{:S(2)}) collective-permute-start(bf16[192,2240]{1,0:T(8,128)(2,1)S(1)} %bitcast.11), channel_id=1, source_target_pairs={{0,16},{16,0},{1,17},{17,1},{2,18},{18,2},{3,19},{19,3},{4,20},{20... | collective-permute-start | bytes 2580488 | tf_op jit(solution)/shard_map/ppermute | solution.py:345
  47.3 14.8 %collective-permute-start.17 = (bf16[280,1152]{1,0:T(8,128)(2,1)S(1)}, bf16[280,1152]{1,0:T(8,128)(2,1)}, u32[]{:S(2)}, u32[]{:S(2)}) collective-permute-start(bf16[280,1152]{1,0:T(8,128)(2,1)S(1)} %shard_map.108), channel_id=1, source_target_pairs={{0,1},{1,0},{2,3},{3,2},{4,5},{5,4},{6,7},{7,6},{8,10},{9,11},{10,... | collective-permute-start | bytes 1935368 | tf_op jit(solution)/shard_map/ppermute | solution.py:404
  53.4 7.5 %collective-permute-start.5 = (bf16[280,640]{1,0:T(8,128)(2,1)S(1)}, bf16[280,640]{1,0:T(8,128)(2,1)S(1)}, u32[]{:S(2)}, u32[]{:S(2)}) collective-permute-start(bf16[280,640]{1,0:T(8,128)(2,1)S(1)} %shard_map.97), channel_id=1, source_target_pairs={{0,2},{1,3},{2,0},{3,1},{4,6},{5,7},{6,4},{7,5},{8,9},{9,8},{10,11... | collective-permute-start | bytes 1075208 | tf_op jit(solution)/shard_map/ppermute | solution.py:404
  54.3 14.9 %collective-permute-start.12 = (bf16[280,1152]{1,0:T(8,128)(2,1)S(1)}, bf16[280,1152]{1,0:T(8,128)(2,1)}, u32[]{:S(2)}, u32[]{:S(2)}) collective-permute-start(bf16[280,1152]{1,0:T(8,128)(2,1)S(1)} %collective-permute-done.11.refs_1_.early_ref), channel_id=1, source_target_pairs={{0,8},{8,0},{1,9},{9,1},{2,10},{10,2},{3,11},{11,3},{4,12},{12,4},... | collective-permute-start | bytes 1935368 | tf_op jit(solution)/shard_map/ppermute | solution.py:345
  54.3 19.8 %collective-permute-start.14 = (bf16[280,1152]{1,0:T(8,128)(2,1)S(1)}, bf16[280,1152]{1,0:T(8,128)(2,1)}, u32[]{:S(2)}, u32[]{:S(2)}) collective-permute-start(bf16[280,1152]{1,0:T(8,128)(2,1)S(1)} %collective-permute-done.13.refs_1_.late_ref.early_ref), channel_id=1, source_target_pairs={{0,8},{8,0},{1,9},{9,1},{2,10},{10,2},{3,11},{11,3},{4,12},{12,4},... | collective-permute-start | bytes 1935368 | tf_op jit(solution)/shard_map/ppermute | solution.py:345
  60.9 2.6 %copy-start.4 = (bf16[280,640]{1,0:T(8,128)(2,1)}, bf16[280,640]{1,0:T(8,128)(2,1)S(1)}, u32[]{:S(2)}) copy-start(bf16[280,640]{1,0:T(8,128)(2,1)S(1)} %collective-permute-done.5.refs_1_.late_ref) | copy-start | bytes 1075204
  60.9 16.5 %collective-permute-start.16 = (bf16[280,1152]{1,0:T(8,128)(2,1)S(1)}, bf16[280,1152]{1,0:T(8,128)(2,1)}, u32[]{:S(2)}, u32[]{:S(2)}) collective-permute-start(bf16[280,1152]{1,0:T(8,128)(2,1)S(1)} %collective-permute-done.15.refs_1_.late_ref), channel_id=1, source_target_pairs={{0,8},{8,0},{1,9},{9,1},{2,10},{10,2},{3,11},{11,3},{4,12},{12,4},... | collective-permute-start | bytes 1935368 | tf_op jit(solution)/shard_map/ppermute | solution.py:345
  62.1 18.3 %collective-permute-start.18 = (bf16[280,1152]{1,0:T(8,128)(2,1)}, bf16[280,1152]{1,0:T(8,128)(2,1)}, u32[]{:S(2)}, u32[]{:S(2)}) collective-permute-start(bf16[280,1152]{1,0:T(8,128)(2,1)} %collective-permute-done.17.refs_2_), channel_id=1, source_target_pairs={{0,8},{8,0},{1,9},{9,1},{2,10},{10,2},{3,11},{11,3},{4,12},{12,4},... | collective-permute-start | bytes 1935368 | tf_op jit(solution)/shard_map/ppermute | solution.py:345
  64.4 12.8 %collective-permute-start.7 = (bf16[280,640]{1,0:T(8,128)(2,1)}, bf16[280,640]{1,0:T(8,128)(2,1)}, u32[]{:S(2)}, u32[]{:S(2)}) collective-permute-start(bf16[280,640]{1,0:T(8,128)(2,1)} %shard_map.100), channel_id=1, source_target_pairs={{0,1},{1,0},{2,3},{3,2},{4,5},{5,4},{6,7},{7,6},{8,10},{9,11},{10,... | collective-permute-start | bytes 1075208 | tf_op jit(solution)/shard_map/ppermute | solution.py:404
  67.9 1.3 %copy-start.9 = (s32[2]{0:T(128)S(1)}, s32[2]{0:T(128)}, u32[]{:S(2)}) copy-start(s32[2]{0:T(128)} %near_ref.3) | copy-start | bytes 28
  67.9 2.9 %copy-start = (bf16[280,1152]{1,0:T(8,128)(2,1)S(1)}, bf16[280,1152]{1,0:T(8,128)(2,1)}, u32[]{:S(2)}) copy-start(bf16[280,1152]{1,0:T(8,128)(2,1)} %shard_map.103.refs_0_) | copy-start | bytes 1935364
  69.2 4.8 %copy-start.8 = (bf16[280,640]{1,0:T(8,128)(2,1)S(1)}, bf16[280,640]{1,0:T(8,128)(2,1)}, u32[]{:S(2)}) copy-start(bf16[280,640]{1,0:T(8,128)(2,1)} %copy-done.7) | copy-start | bytes 1075204
  69.2 4.8 %collective-permute-start.10 = (s32[2]{0:T(128)S(1)}, s32[2]{0:T(128)S(1)}, u32[]{:S(2)}, u32[]{:S(2)}) collective-permute-start(s32[2]{0:T(128)S(1)} %copy-done.9), channel_id=1, source_target_pairs={{0,16},{16,0},{1,17},{17,1},{2,18},{18,2},{3,19},{19,3},{4,20},{20... | collective-permute-start | bytes 32 | tf_op jit(solution)/shard_map/ppermute | solution.py:345
  74.0 3.2 %copy-start.5 = (bf16[280,640]{1,0:T(8,128)(2,1)S(1)}, bf16[280,640]{1,0:T(8,128)(2,1)}, u32[]{:S(2)}) copy-start(bf16[280,640]{1,0:T(8,128)(2,1)} %copy-done.4) | copy-start | bytes 1075204
  74.0 11.2 %collective-permute-start.2 = (bf16[280,640]{1,0:T(8,128)(2,1)S(1)}, bf16[280,640]{1,0:T(8,128)(2,1)S(1)}, u32[]{:S(2)}, u32[]{:S(2)}) collective-permute-start(bf16[280,640]{1,0:T(8,128)(2,1)S(1)} %copy-done.8), channel_id=1, source_target_pairs={{0,8},{8,0},{1,9},{9,1},{2,10},{10,2},{3,11},{11,3},{4,12},{12,4},... | collective-permute-start | bytes 1075208 | tf_op jit(solution)/shard_map/ppermute | solution.py:345
  74.1 12.6 %collective-permute-start.4 = (bf16[280,640]{1,0:T(8,128)(2,1)S(1)}, bf16[280,640]{1,0:T(8,128)(2,1)S(1)}, u32[]{:S(2)}, u32[]{:S(2)}) collective-permute-start(bf16[280,640]{1,0:T(8,128)(2,1)S(1)} %collective-permute-done.3.refs_3_.late_ref.early_ref), channel_id=1, source_target_pairs={{0,8},{8,0},{1,9},{9,1},{2,10},{10,2},{3,11},{11,3},{4,12},{12,4},... | collective-permute-start | bytes 1075208 | tf_op jit(solution)/shard_map/ppermute | solution.py:345
  77.2 15.3 %collective-permute-start.6 = (bf16[280,640]{1,0:T(8,128)(2,1)S(1)}, bf16[280,640]{1,0:T(8,128)(2,1)S(1)}, u32[]{:S(2)}, u32[]{:S(2)}) collective-permute-start(bf16[280,640]{1,0:T(8,128)(2,1)S(1)} %copy-done.5), channel_id=1, source_target_pairs={{0,8},{8,0},{1,9},{9,1},{2,10},{10,2},{3,11},{11,3},{4,12},{12,4},... | collective-permute-start | bytes 1075208 | tf_op jit(solution)/shard_map/ppermute | solution.py:345
  77.4 17.9 %collective-permute-start.8 = (bf16[280,640]{1,0:T(8,128)(2,1)}, bf16[280,640]{1,0:T(8,128)(2,1)S(1)}, u32[]{:S(2)}, u32[]{:S(2)}) collective-permute-start(bf16[280,640]{1,0:T(8,128)(2,1)} %collective-permute-done.7.refs_0_), channel_id=1, source_target_pairs={{0,8},{8,0},{1,9},{9,1},{2,10},{10,2},{3,11},{11,3},{4,12},{12,4},... | collective-permute-start | bytes 1075208 | tf_op jit(solution)/shard_map/ppermute | solution.py:345
  80.4 6.3 %copy-start.6 = (bf16[280,640]{1,0:T(8,128)(2,1)S(1)}, bf16[280,640]{1,0:T(8,128)(2,1)}, u32[]{:S(2)}) copy-start(bf16[280,640]{1,0:T(8,128)(2,1)} %shard_map.95.refs_0_) | copy-start | bytes 1075204
  84.6 5.7 %collective-permute-start.24 = (bf16[20,16,128]{2,1,0:T(8,128)(2,1)S(1)}, bf16[20,16,128]{2,1,0:T(8,128)(2,1)S(1)}, u32[]{:S(2)}, u32[]{:S(2)}) collective-permute-start(bf16[20,16,128]{2,1,0:T(8,128)(2,1)S(1)} %get-tuple-element.31), channel_id=1, source_target_pairs={{0,1},{1,0},{2,3},{3,2},{4,5},{5,4},{6,7},{7,6},{8,9},{9,8},{10,11... | collective-permute-start | bytes 245768 | tf_op jit(solution)/shard_map/ppermute | solution.py:348
  85.2 11.3 %collective-permute-start.19 = (bf16[20,16,128]{2,1,0:T(8,128)(2,1)S(1)}, bf16[20,16,128]{2,1,0:T(8,128)(2,1)S(1)}, u32[]{:S(2)}, u32[]{:S(2)}) collective-permute-start(bf16[20,16,128]{2,1,0:T(8,128)(2,1)S(1)} %get-tuple-element.25), channel_id=1, source_target_pairs={{0,1},{1,0},{2,3},{3,2},{4,5},{5,4},{6,7},{7,6},{8,9},{9,8},{10,11... | collective-permute-start | bytes 245768 | tf_op jit(solution)/shard_map/ppermute | solution.py:348
  89.9 14.3 %collective-permute-start.20 = (bf16[20,16,128]{2,1,0:T(8,128)(2,1)S(1)}, bf16[20,16,128]{2,1,0:T(8,128)(2,1)S(1)}, u32[]{:S(2)}, u32[]{:S(2)}) collective-permute-start(bf16[20,16,128]{2,1,0:T(8,128)(2,1)S(1)} %get-tuple-element.26), channel_id=1, source_target_pairs={{0,2},{1,3},{2,0},{3,1},{4,6},{5,7},{6,4},{7,5},{8,10},{9,11},{10,... | collective-permute-start | bytes 245768 | tf_op jit(solution)/shard_map/ppermute | solution.py:348
  90.4 14.5 %collective-permute-start.21 = (bf16[20,16,128]{2,1,0:T(8,128)(2,1)S(1)}, bf16[20,16,128]{2,1,0:T(8,128)(2,1)S(1)}, u32[]{:S(2)}, u32[]{:S(2)}) collective-permute-start(bf16[20,16,128]{2,1,0:T(8,128)(2,1)S(1)} %get-tuple-element.27), channel_id=1, source_target_pairs={{0,3},{1,2},{2,1},{3,0},{4,7},{5,6},{6,5},{7,4},{8,11},{9,10},{10,... | collective-permute-start | bytes 245768 | tf_op jit(solution)/shard_map/ppermute | solution.py:348
  92.6 12.3 %collective-permute-start.22 = (bf16[20,16,128]{2,1,0:T(8,128)(2,1)S(1)}, bf16[20,16,128]{2,1,0:T(8,128)(2,1)S(1)}, u32[]{:S(2)}, u32[]{:S(2)}) collective-permute-start(bf16[20,16,128]{2,1,0:T(8,128)(2,1)S(1)} %get-tuple-element.28), channel_id=1, source_target_pairs={{0,4},{1,5},{2,6},{3,7},{4,0},{5,1},{6,2},{7,3},{8,12},{9,13},{10,... | collective-permute-start | bytes 245768 | tf_op jit(solution)/shard_map/ppermute | solution.py:348
  95.3 10.7 %collective-permute-start.23 = (bf16[20,16,128]{2,1,0:T(8,128)(2,1)S(1)}, bf16[20,16,128]{2,1,0:T(8,128)(2,1)S(1)}, u32[]{:S(2)}, u32[]{:S(2)}) collective-permute-start(bf16[20,16,128]{2,1,0:T(8,128)(2,1)S(1)} %get-tuple-element.29), channel_id=1, source_target_pairs={{0,5},{1,4},{2,7},{3,6},{4,1},{5,0},{6,3},{7,2},{8,13},{9,12},{10,... | collective-permute-start | bytes 245768 | tf_op jit(solution)/shard_map/ppermute | solution.py:348
  96.5 9.5 %collective-permute-start.25 = (bf16[20,16,128]{2,1,0:T(8,128)(2,1)S(1)}, bf16[20,16,128]{2,1,0:T(8,128)(2,1)S(1)}, u32[]{:S(2)}, u32[]{:S(2)}) collective-permute-start(bf16[20,16,128]{2,1,0:T(8,128)(2,1)S(1)} %shard_map.110), channel_id=1, source_target_pairs={{0,6},{1,7},{2,4},{3,5},{4,2},{5,3},{6,0},{7,1},{8,14},{9,15},{10,... | collective-permute-start | bytes 245768 | tf_op jit(solution)/shard_map/ppermute | solution.py:348
  101.7 22.0 %copy-start.10 = (s32[80]{0:T(128)S(1)}, s32[80]{0:T(128)}, u32[]{:S(2)}) copy-start(s32[80]{0:T(128)} %new_ref.1) | copy-start | bytes 964
  104.3 12.2 %collective-permute-start.9 = (bf16[192,560]{1,0:T(8,128)(2,1)S(1)}, bf16[192,560]{1,0:T(8,128)(2,1)S(1)}, u32[]{:S(2)}, u32[]{:S(2)}) collective-permute-start(bf16[192,560]{1,0:T(8,128)(2,1)S(1)} %get-tuple-element.22), channel_id=1, source_target_pairs={{0,16},{16,0},{1,17},{17,1},{2,18},{18,2},{3,19},{19,3},{4,20},{20... | collective-permute-start | bytes 645128 | tf_op jit(solution)/shard_map/ppermute | solution.py:345
  106.7 4.8 %collective-permute-start.26 = (bf16[10,16,128]{2,1,0:T(8,128)(2,1)S(1)}, bf16[10,16,128]{2,1,0:T(8,128)(2,1)S(1)}, u32[]{:S(2)}, u32[]{:S(2)}) collective-permute-start(bf16[10,16,128]{2,1,0:T(8,128)(2,1)S(1)} %get-tuple-element.33), channel_id=1, source_target_pairs={{0,16},{16,0},{1,17},{17,1},{2,18},{18,2},{3,19},{19,3},{4,20},{20... | collective-permute-start | bytes 122888 | tf_op jit(solution)/shard_map/ppermute | solution.py:345
  112.0 4.5 %collective-permute-start.34 = (bf16[20,16,128]{2,1,0:T(8,128)(2,1)S(1)}, bf16[20,16,128]{2,1,0:T(8,128)(2,1)S(1)}, u32[]{:S(2)}, u32[]{:S(2)}) collective-permute-start(bf16[20,16,128]{2,1,0:T(8,128)(2,1)S(1)} %shard_map.112.refs_0_), channel_id=1, source_target_pairs={{0,16},{8,24},{16,0},{24,8},{1,17},{9,25},{17,1},{25,9},{2,18},{10... | collective-permute-start | bytes 245768 | tf_op jit(solution)/shard_map/ppermute | solution.py:517
  112.6 4.0 %collective-permute-start.35 = (bf16[20,16,128]{2,1,0:T(8,128)(2,1)S(1)}, bf16[20,16,128]{2,1,0:T(8,128)(2,1)S(1)}, u32[]{:S(2)}, u32[]{:S(2)}) collective-permute-start(bf16[20,16,128]{2,1,0:T(8,128)(2,1)S(1)} %shard_map.112.refs_0_), channel_id=1, source_target_pairs={{0,8},{8,0},{16,24},{24,16},{1,9},{9,1},{17,25},{25,17},{2,10},{10... | collective-permute-start | bytes 245768 | tf_op jit(solution)/shard_map/ppermute | solution.py:517
  112.6 6.7 %collective-permute-start.32 = (bf16[20,16,128]{2,1,0:T(8,128)(2,1)S(1)}, bf16[20,16,128]{2,1,0:T(8,128)(2,1)S(1)}, u32[]{:S(2)}, u32[]{:S(2)}) collective-permute-start(bf16[20,16,128]{2,1,0:T(8,128)(2,1)S(1)} %shard_map.112.refs_0_), channel_id=1, source_target_pairs={{0,6},{1,7},{2,4},{3,5},{4,2},{5,3},{6,0},{7,1},{8,14},{9,15},{10,... | collective-permute-start | bytes 245768 | tf_op jit(solution)/shard_map/ppermute | solution.py:348
  114.2 6.4 %collective-permute-start.27 = (bf16[20,16,128]{2,1,0:T(8,128)(2,1)S(1)}, bf16[20,16,128]{2,1,0:T(8,128)(2,1)S(1)}, u32[]{:S(2)}, u32[]{:S(2)}) collective-permute-start(bf16[20,16,128]{2,1,0:T(8,128)(2,1)S(1)} %shard_map.112.refs_0_), channel_id=1, source_target_pairs={{0,1},{1,0},{2,3},{3,2},{4,5},{5,4},{6,7},{7,6},{8,9},{9,8},{10,11... | collective-permute-start | bytes 245768 | tf_op jit(solution)/shard_map/ppermute | solution.py:348
  116.5 5.9 %collective-permute-start.36 = (bf16[20,16,128]{2,1,0:T(8,128)(2,1)S(1)}, bf16[20,16,128]{2,1,0:T(8,128)(2,1)S(1)}, u32[]{:S(2)}, u32[]{:S(2)}) collective-permute-start(bf16[20,16,128]{2,1,0:T(8,128)(2,1)S(1)} %collective-permute-done.34.refs_1_), channel_id=1, source_target_pairs={{0,8},{8,0},{16,24},{24,16},{1,9},{9,1},{17,25},{25,17},{2,10},{10... | collective-permute-start | bytes 245768 | tf_op jit(solution)/shard_map/ppermute | solution.py:517
  116.5 12.1 %collective-permute-start.28 = (bf16[20,16,128]{2,1,0:T(8,128)(2,1)S(1)}, bf16[20,16,128]{2,1,0:T(8,128)(2,1)S(1)}, u32[]{:S(2)}, u32[]{:S(2)}) collective-permute-start(bf16[20,16,128]{2,1,0:T(8,128)(2,1)S(1)} %shard_map.112.refs_0_), channel_id=1, source_target_pairs={{0,2},{1,3},{2,0},{3,1},{4,6},{5,7},{6,4},{7,5},{8,10},{9,11},{10,... | collective-permute-start | bytes 245768 | tf_op jit(solution)/shard_map/ppermute | solution.py:348
  116.6 12.0 %collective-permute-start.29 = (bf16[20,16,128]{2,1,0:T(8,128)(2,1)S(1)}, bf16[20,16,128]{2,1,0:T(8,128)(2,1)S(1)}, u32[]{:S(2)}, u32[]{:S(2)}) collective-permute-start(bf16[20,16,128]{2,1,0:T(8,128)(2,1)S(1)} %shard_map.112.refs_0_), channel_id=1, source_target_pairs={{0,3},{1,2},{2,1},{3,0},{4,7},{5,6},{6,5},{7,4},{8,11},{9,10},{10,... | collective-permute-start | bytes 245768 | tf_op jit(solution)/shard_map/ppermute | solution.py:348
  119.3 9.4 %collective-permute-start.30 = (bf16[20,16,128]{2,1,0:T(8,128)(2,1)S(1)}, bf16[20,16,128]{2,1,0:T(8,128)(2,1)S(1)}, u32[]{:S(2)}, u32[]{:S(2)}) collective-permute-start(bf16[20,16,128]{2,1,0:T(8,128)(2,1)S(1)} %shard_map.112.refs_0_), channel_id=1, source_target_pairs={{0,4},{1,5},{2,6},{3,7},{4,0},{5,1},{6,2},{7,3},{8,12},{9,13},{10,... | collective-permute-start | bytes 245768 | tf_op jit(solution)/shard_map/ppermute | solution.py:348
  120.6 9.5 %collective-permute-start.31 = (bf16[20,16,128]{2,1,0:T(8,128)(2,1)S(1)}, bf16[20,16,128]{2,1,0:T(8,128)(2,1)S(1)}, u32[]{:S(2)}, u32[]{:S(2)}) collective-permute-start(bf16[20,16,128]{2,1,0:T(8,128)(2,1)S(1)} %shard_map.112.refs_0_), channel_id=1, source_target_pairs={{0,5},{1,4},{2,7},{3,6},{4,1},{5,0},{6,3},{7,2},{8,13},{9,12},{10,... | collective-permute-start | bytes 245768 | tf_op jit(solution)/shard_map/ppermute | solution.py:348
  122.4 7.7 %collective-permute-start.33 = (bf16[20,16,128]{2,1,0:T(8,128)(2,1)S(1)}, bf16[20,16,128]{2,1,0:T(8,128)(2,1)S(1)}, u32[]{:S(2)}, u32[]{:S(2)}) collective-permute-start(bf16[20,16,128]{2,1,0:T(8,128)(2,1)S(1)} %collective-permute-done.32.refs_6_), channel_id=1, source_target_pairs={{0,1},{1,0},{2,3},{3,2},{4,5},{5,4},{6,7},{7,6},{8,9},{9,8},{10,11... | collective-permute-start | bytes 245768 | tf_op jit(solution)/shard_map/ppermute | solution.py:348
  (2 other events, 2.1 us)

commit v5 on v4

--- a/solution.py
+++ b/solution.py
@@ -85,7 +85,7 @@
         copy.wait()
         for turn in range(2):
 
-            @pl.when(pos_ref[3] == turn)
+            @pl.when(pos_ref[0] == turn)
             def _():
                 for j, kind in enumerate(kinds):
                     start = (2 * kind + turn) * width - low
@@ -163,14 +163,10 @@
     return total
 
 
-def column_step(wide):
-    return next(step for step in (384, 256, LANES) if wide % step == 0)
-
-
 def mul_kernel(slots, fresh, pos_ref, blocks_ref, *refs):
     acc_ref = refs[-1]
     given = refs[:-1] if fresh else refs[1:-1]
-    step = column_step(acc_ref.shape[1])
+    step = acc_ref.shape[1]
 
     @pl.loop(0, acc_ref.shape[1] // step)
     def _(t):
@@ -181,7 +177,7 @@
 
 def ask_kernel(slots, width, pos_ref, blocks_ref, old_ref, group_ref, *refs):
     given, (mine_ref, give_ref, acc_ref) = refs[:-3], refs[-3:]
-    step = column_step(acc_ref.shape[1])
+    step = acc_ref.shape[1]
 
     @pl.loop(0, acc_ref.shape[1] // step)
     def _(t):
@@ -203,7 +199,7 @@
     given, refs = refs[:count], refs[count:]
     group_ref, plain_ref = refs[:2]
     chunks, acc_ref = refs[2:-1], refs[-1]
-    step = column_step(acc_ref.shape[1])
+    step = acc_ref.shape[1]
 
     @pl.loop(0, acc_ref.shape[1] // step)
     def _(t):
@@ -376,8 +372,7 @@
             0,
             2_000_000,
             scratch=[pltpu.VMEM(w_qkv.shape, BF16), pltpu.SemaphoreType.DMA((5,))],
-            room=60,
-        )(place_of, w_qkv)
+        )(y.reshape(1), pltpu.with_memory_space_constraint(w_qkv, pltpu.HBM))
 
     pieces = [prep((1, 2), wide_kv), prep((0,), wide_q)]
 

time: 133 us -> 127 us (0.955)
  Pallas kernels: 41.3 us -> 32.7 us
    pallas_call x5, Pallas kernels: 13.6 us -> 10.6 us  [multiply(): whole_call(functools.partial(mul_kernel, slots, acc is None), jax.ShapeDt...]
    pallas_call x2, Pallas kernels: 5.76 us -> 2.85 us  [prep(): whole_call(functools.partial(prep_kernel, kinds), jax.ShapeDtypeStruct((d...]
    ppermute x14, waiting for transfers between devices: 3.33 us -> 5.79 us  [xor(): return lax.ppermute(v, ('z', 'x'), [(i, i ^ k) for i in range(members)])]
    unnamed x28 -> x30, local copies, waits for them, and re-layouts: 2.16 us -> 3.34 us
  transfers between devices with their start and end apart: 37 -> 37, of which waited for: 11 -> 12; matrix products, arithmetic and copies ran while one was open for 1% -> 1% of each run, Pallas kernels for 26% -> 22%
where the time goes in v5:
time: 127 us
  waiting for transfers between devices  49.9 us (39%)
  starting transfers between devices  39.3 us (31%)
  Pallas kernels  32.7 us (26%)
  local copies, waits for them, and re-layouts  4.12 us (3%)
    ppermute x8, waiting for transfers between devices, rounds(): got.append(lax.ppermute(give, ('c', 'z', 'x'), step))  40.3 us
    ppermute x14, starting transfers between devices, xor(): return lax.ppermute(v, ('z', 'x'), [(i, i ^ k) for i in range(members)])  20.5 us
    ppermute x8, starting transfers between devices, rounds(): got.append(lax.ppermute(give, ('c', 'z', 'x'), step))  11.6 us
    pallas_call x5, Pallas kernels, multiply(): whole_call(functools.partial(mul_kernel, slots, acc is None), jax.ShapeDt...  10.6 us
    ppermute x12, starting transfers between devices, swap(): return lax.ppermute(v, axis, SWAP)  6.44 us
    ppermute x14, waiting for transfers between devices, xor(): return lax.ppermute(v, ('z', 'x'), [(i, i ^ k) for i in range(members)])  5.79 us
    pallas_call x1, Pallas kernels, layer(): whole_call(functools.partial(kv_kernel, last, streams, frames, heads, siz...  3.7 us
    unnamed x30, local copies, waits for them, and re-layouts  3.34 us
  transfers between devices with their start and end apart: 37, of which 12 were waited for; matrix products, arithmetic and copies ran while one was open for 1% of the time, Pallas kernels for 22%

profile of v5, /device:TPU:0, one launch (start us, length us, event | category | flops | bytes accessed | tf_op | source)
XLA Modules:
  0.0 127.1 jit_solution(14714485083851432134)
XLA Ops:
  0.6 1.6 %shard_map.103.refs_0_ = bf16[280,1152]{1,0:T(8,128)(2,1)S(1)} custom-call(s32[1]{0:T(128)} %bitcast.3.pos_ref, bf16[280,3360]{1,0:T(8,128)(2,1)} %w_hbm.3), custom_call_target="tpu_custom_call" | custom-call | bytes 2000000 | tf_op jit(solution)/shard_map/pallas_call | solution.py:368
  2.3 3.1 %collective-permute-start.11 = (bf16[280,1152]{1,0:T(8,128)(2,1)S(1)}, bf16[280,1152]{1,0:T(8,128)(2,1)S(1)}, u32[]{:S(2)}, u32[]{:S(2)}) collective-permute-start(bf16[280,1152]{1,0:T(8,128)(2,1)S(1)} %shard_map.103.refs_0_), channel_id=1, source_target_pairs={{0,2},{1,3},{2,0},{3,1},{4,6},{5,7},{6,4},{7,5},{8,9},{9,8},{10,12... | collective-permute-start | bytes 1935368 | tf_op jit(solution)/shard_map/ppermute | solution.py:399
  5.4 8.5 %collective-permute-done.11.refs_1_.early_ref = bf16[280,1152]{1,0:T(8,128)(2,1)S(1)} collective-permute-done((bf16[280,1152]{1,0:T(8,128)(2,1)S(1)}, bf16[280,1152]{1,0:T(8,128)(2,1)S(1)}, u32[]{:S(2)}, u32[]{:S(2)}) %collective-permute-start.11) | collective-permute-done | bytes 645152 | tf_op jit(solution)/shard_map/ppermute | solution.py:399
  13.9 1.9 %collective-permute-start.13 = (bf16[280,1152]{1,0:T(8,128)(2,1)S(1)}, bf16[280,1152]{1,0:T(8,128)(2,1)S(1)}, u32[]{:S(2)}, u32[]{:S(2)}) collective-permute-start(bf16[280,1152]{1,0:T(8,128)(2,1)S(1)} %collective-permute-done.11.refs_1_.early_ref), channel_id=1, source_target_pairs={{0,1},{1,0},{2,4},{3,5},{4,2},{5,3},{6,7},{7,6},{8,10},{9,11},{10,... | collective-permute-start | bytes 1935368 | tf_op jit(solution)/shard_map/ppermute | solution.py:399
  16.6 7.8 %collective-permute-done.13.refs_1_.late_ref.early_ref = bf16[280,1152]{1,0:T(8,128)(2,1)S(1)} collective-permute-done((bf16[280,1152]{1,0:T(8,128)(2,1)S(1)}, bf16[280,1152]{1,0:T(8,128)(2,1)S(1)}, u32[]{:S(2)}, u32[]{:S(2)}) %collective-permute-start.13) | collective-permute-done | bytes 645152 | tf_op jit(solution)/shard_map/ppermute | solution.py:399
  24.9 2.1 %collective-permute-start.15 = (bf16[280,1152]{1,0:T(8,128)(2,1)S(1)}, bf16[280,1152]{1,0:T(8,128)(2,1)S(1)}, u32[]{:S(2)}, u32[]{:S(2)}) collective-permute-start(bf16[280,1152]{1,0:T(8,128)(2,1)S(1)} %shard_map.106), channel_id=1, source_target_pairs={{0,2},{1,3},{2,0},{3,1},{4,6},{5,7},{6,4},{7,5},{8,9},{9,8},{10,11... | collective-permute-start | bytes 1935368 | tf_op jit(solution)/shard_map/ppermute | solution.py:399
  27.0 1.2 shard_map.95.refs_0_
  28.3 12.1 %collective-permute-done.1.refs_1_.early_ref = bf16[280,640]{1,0:T(8,128)(2,1)S(1)} collective-permute-done((bf16[280,640]{1,0:T(8,128)(2,1)S(1)}, bf16[280,640]{1,0:T(8,128)(2,1)S(1)}, u32[]{:S(2)}, u32[]{:S(2)}) %collective-permute-start.1) | collective-permute-done | bytes 358432 | tf_op jit(solution)/shard_map/ppermute | solution.py:399
  40.4 1.3 %collective-permute-start.3 = (bf16[280,640]{1,0:T(8,128)(2,1)S(1)}, bf16[280,640]{1,0:T(8,128)(2,1)S(1)}, u32[]{:S(2)}, u32[]{:S(2)}) collective-permute-start(bf16[280,640]{1,0:T(8,128)(2,1)S(1)} %collective-permute-done.1.refs_1_.early_ref), channel_id=1, source_target_pairs={{0,1},{1,0},{2,4},{3,5},{4,2},{5,3},{6,7},{7,6},{8,10},{9,11},{10,... | collective-permute-start | bytes 1075208 | tf_op jit(solution)/shard_map/ppermute | solution.py:399
  41.8 1.5 %collective-permute-start = (bf16[192,2240]{1,0:T(8,128)(2,1)S(1)}, bf16[192,2240]{1,0:T(8,128)(2,1)S(1)}, u32[]{:S(2)}, u32[]{:S(2)}) collective-permute-start(bf16[192,2240]{1,0:T(8,128)(2,1)S(1)} %bitcast.11), channel_id=1, source_target_pairs={{0,16},{16,0},{1,17},{17,1},{2,18},{18,2},{3,19},{19,3},{4,20},{20... | collective-permute-start | bytes 2580488 | tf_op jit(solution)/shard_map/ppermute | solution.py:341
  44.5 4.8 %collective-permute-done.3.refs_3_.late_ref.early_ref = bf16[280,640]{1,0:T(8,128)(2,1)S(1)} collective-permute-done((bf16[280,640]{1,0:T(8,128)(2,1)S(1)}, bf16[280,640]{1,0:T(8,128)(2,1)S(1)}, u32[]{:S(2)}, u32[]{:S(2)}) %collective-permute-start.3) | collective-permute-done | bytes 358432 | tf_op jit(solution)/shard_map/ppermute | solution.py:399
  49.9 1.1 collective-permute-start.5
  51.5 5.8 %collective-permute-done.5.refs_1_.late_ref = bf16[280,640]{1,0:T(8,128)(2,1)S(1)} collective-permute-done((bf16[280,640]{1,0:T(8,128)(2,1)S(1)}, bf16[280,640]{1,0:T(8,128)(2,1)S(1)}, u32[]{:S(2)}, u32[]{:S(2)}) %collective-permute-start.5) | collective-permute-done | bytes 358432 | tf_op jit(solution)/shard_map/ppermute | solution.py:399
  57.3 1.4 %collective-permute-done.17.refs_2_ = bf16[280,1152]{1,0:T(8,128)(2,1)} collective-permute-done((bf16[280,1152]{1,0:T(8,128)(2,1)S(1)}, bf16[280,1152]{1,0:T(8,128)(2,1)}, u32[]{:S(2)}, u32[]{:S(2)}) %collective-permute-start.17) | collective-permute-done | bytes 645152 | tf_op jit(solution)/shard_map/ppermute | solution.py:399
  58.7 1.3 %shard_map.100 = bf16[280,640]{1,0:T(8,128)(2,1)} custom-call(s32[16]{0:T(128)S(1)} %concatenate.3.pos_ref.refs_0_, bf16[280,640]{1,0:T(8,128)(2,1)S(1)} %collective-permute-done.3.refs_3_.late_ref.early_ref, bf16[280,640]{1,0:T(8,128)(2,1)S(1)} %collective-permute-done.5.refs_1_.late_ref), custom_call_target="tpu_custom_call" | custom-call | bytes 1000000 | tf_op jit(solution)/shard_map/pallas_call | solution.py:380
  60.0 0.9 copy-done.2
  61.0 1.3 %collective-permute-start.7 = (bf16[280,640]{1,0:T(8,128)(2,1)}, bf16[280,640]{1,0:T(8,128)(2,1)S(1)}, u32[]{:S(2)}, u32[]{:S(2)}) collective-permute-start(bf16[280,640]{1,0:T(8,128)(2,1)} %shard_map.100), channel_id=1, source_target_pairs={{0,1},{1,0},{2,3},{3,2},{4,5},{5,4},{6,7},{7,6},{8,10},{9,11},{10,... | collective-permute-start | bytes 1075208 | tf_op jit(solution)/shard_map/ppermute | solution.py:399
  62.4 0.9 shard_map.99
  63.3 1.2 copy-done.1
  64.5 1.2 copy-done.3
  65.6 1.3 %shard_map.94.blocks_ref.refs_0_ = bf16[8,384,280]{2,1,0:T(8,128)(2,1)S(1)} custom-call(s32[16]{0:T(128)S(1)} %concatenate.3.pos_ref.refs_0_, bf16[192,2240]{1,0:T(8,128)(2,1)S(1)} %bitcast.12, bf16[192,2240]{1,0:T(8,128)(2,1)S(1)} %copy-done.3), custom_call_target="tpu_custom_call" | custom-call | bytes 4000000 | tf_op jit(solution)/shard_map/pallas_call | solution.py:418
  67.0 1.6 %collective-permute-start.10 = (s32[2]{0:T(128)S(1)}, s32[2]{0:T(128)S(1)}, u32[]{:S(2)}, u32[]{:S(2)}) collective-permute-start(s32[2]{0:T(128)S(1)} %copy-done.10), channel_id=1, source_target_pairs={{0,16},{16,0},{1,17},{17,1},{2,18},{18,2},{3,19},{19,3},{4,20},{20... | collective-permute-start | bytes 32 | tf_op jit(solution)/shard_map/ppermute | solution.py:341
  68.6 2.7 %shard_map.104.refs_0_ = f32[384,1152]{1,0:T(8,128)S(1)} custom-call(s32[16]{0:T(128)S(1)} %concatenate.3.pos_ref.refs_0_, bf16[8,384,280]{2,1,0:T(8,128)(2,1)S(1)} %shard_map.94.blocks_ref.refs_0_, bf16[280,1152]{1,0:T(8,128)(2,1)S(1)} %shard_map.103.refs_0_, bf16[280,1152]{1,0:T(8,128)(2,1)S(1)} %collective-permute-done.11.refs_1_.early_ref, ...), custom_call_target="tpu_custom_call" | custom-call | flops 1500000000 | bytes 5000000 | tf_op jit(solution)/shard_map/pallas_call | solution.py:425
  71.9 2.3 %shard_map.105.refs_0_ = f32[384,1152]{1,0:T(8,128)S(1)} custom-call(s32[16]{0:T(128)S(1)} %concatenate.3.pos_ref.refs_0_, bf16[8,384,280]{2,1,0:T(8,128)(2,1)S(1)} %shard_map.94.blocks_ref.refs_0_, f32[384,1152]{1,0:T(8,128)S(1)} %shard_map.104.refs_0_, ...), custom_call_target="tpu_custom_call", output_to_operand_aliasing={{}: (2, {})} | custom-call | flops 1500000000 | bytes 5000000 | tf_op jit(solution)/shard_map/pallas_call | solution.py:425
  74.8 2.3 %shard_map.107.refs_1_ = f32[384,1152]{1,0:T(8,128)S(1)} custom-call(s32[16]{0:T(128)S(1)} %concatenate.3.pos_ref.refs_0_, bf16[8,384,280]{2,1,0:T(8,128)(2,1)S(1)} %shard_map.94.blocks_ref.refs_0_, f32[384,1152]{1,0:T(8,128)S(1)} %shard_map.105.refs_0_, ...), custom_call_target="tpu_custom_call", output_to_operand_aliasing={{}: (2, {})} | custom-call | flops 1500000000 | bytes 5000000 | tf_op jit(solution)/shard_map/pallas_call | solution.py:425
  77.1 3.7 %shard_map.109 = (bf16[20,16,128]{2,1,0:T(8,128)(2,1)S(1)}, bf16[20,16,128]{2,1,0:T(8,128)(2,1)S(1)}, bf16[20,16,128]{2,1,0:T(8,128)(2,1)S(1)}, bf16[20,16,128]{...) custom-call(s32[16]{0:T(128)S(1)} %concatenate.3.pos_ref.refs_0_, ...), custom_call_target="tpu_custom_call" | custom-call | flops 1500000000 | bytes 5000000 | tf_op jit(solution)/shard_map/pallas_call | solution.py:450
  81.4 1.5 %collective-permute-start.19 = (bf16[20,16,128]{2,1,0:T(8,128)(2,1)S(1)}, bf16[20,16,128]{2,1,0:T(8,128)(2,1)S(1)}, u32[]{:S(2)}, u32[]{:S(2)}) collective-permute-start(bf16[20,16,128]{2,1,0:T(8,128)(2,1)S(1)} %get-tuple-element.25), channel_id=1, source_target_pairs={{0,1},{1,0},{2,3},{3,2},{4,5},{5,4},{6,7},{7,6},{8,9},{9,8},{10,11... | collective-permute-start | bytes 245768 | tf_op jit(solution)/shard_map/ppermute | solution.py:344
  82.9 2.1 %shard_map.96.refs_0_ = f32[384,640]{1,0:T(8,128)S(1)} custom-call(s32[16]{0:T(128)S(1)} %concatenate.3.pos_ref.refs_0_, bf16[8,384,280]{2,1,0:T(8,128)(2,1)S(1)} %shard_map.94.blocks_ref.refs_0_, bf16[280,640]{1,0:T(8,128)(2,1)S(1)} %copy-done.7, bf16[280,640]{1,0:T(8,128)(2,1)S(1)} %copy-done.9, bf16[280,640]{1,0:T(8,128)(2,1)S(1)} %collective-permute-done.2.refs_2_, ...), custom_call_target="tpu_custom_call" | custom-call | flops 1500000000 | bytes 5000000 | tf_op jit(solution)/shard_map/pallas_call | solution.py:425
  86.2 1.0 collective-permute-start.21
  87.8 2.7 %collective-permute-start.22 = (bf16[20,16,128]{2,1,0:T(8,128)(2,1)S(1)}, bf16[20,16,128]{2,1,0:T(8,128)(2,1)S(1)}, u32[]{:S(2)}, u32[]{:S(2)}) collective-permute-start(bf16[20,16,128]{2,1,0:T(8,128)(2,1)S(1)} %get-tuple-element.28), channel_id=1, source_target_pairs={{0,4},{1,5},{2,6},{3,7},{4,0},{5,1},{6,2},{7,3},{8,12},{9,13},{10,... | collective-permute-start | bytes 245768 | tf_op jit(solution)/shard_map/ppermute | solution.py:344
  90.5 1.1 collective-permute-start.23
  91.6 3.2 %collective-permute-start.25 = (bf16[20,16,128]{2,1,0:T(8,128)(2,1)S(1)}, bf16[20,16,128]{2,1,0:T(8,128)(2,1)S(1)}, u32[]{:S(2)}, u32[]{:S(2)}) collective-permute-start(bf16[20,16,128]{2,1,0:T(8,128)(2,1)S(1)} %shard_map.110), channel_id=1, source_target_pairs={{0,6},{1,7},{2,4},{3,5},{4,2},{5,3},{6,0},{7,1},{8,14},{9,15},{10,... | collective-permute-start | bytes 245768 | tf_op jit(solution)/shard_map/ppermute | solution.py:344
  94.8 1.3 %shard_map.98.old_ref = f32[384,640]{1,0:T(8,128)S(1)} custom-call(s32[16]{0:T(128)S(1)} %concatenate.3.pos_ref.refs_0_, bf16[8,384,280]{2,1,0:T(8,128)(2,1)S(1)} %shard_map.94.blocks_ref.refs_0_, f32[384,640]{1,0:T(8,128)S(1)} %shard_map.96.refs_0_, bf16[280,640]{1,0:T(8,128)(2,1)S(1)} %copy-done.5, ...), custom_call_target="tpu_custom_call", output_to_operand_aliasing={{}: (2, {})} | custom-call | flops 1500000000 | bytes 5000000 | tf_op jit(solution)/shard_map/pallas_call | solution.py:425
  96.1 1.3 %shard_map.101 = (bf16[192,640]{1,0:T(8,128)(2,1)S(1)}, bf16[192,560]{1,0:T(8,128)(2,1)S(1)}) custom-call(s32[16]{0:T(128)S(1)} %concatenate.3.pos_ref.refs_0_, bf16[8,384,280]{2,1,0:T(8,128)(2,1)S(1)} %shard_map.94.blocks_ref.refs_0_, f32[384,640]{1,0:T(8,128)S(1)} %shard_map.98.old_ref, bf16[560,640]{1,0:T(8,128)(2,1)S(1)} %get-tuple-element.20.group_ref.refs_4_, ...), custom_call_target="tpu_custom_call" | custom-call | flops 700000000 | bytes 3000000 | tf_op jit(solution)/shard_map/pallas_call | solution.py:459
  98.3 2.8 %collective-permute-done.23.refs_6_ = bf16[20,16,128]{2,1,0:T(8,128)(2,1)S(1)} collective-permute-done((bf16[20,16,128]{2,1,0:T(8,128)(2,1)S(1)}, bf16[20,16,128]{2,1,0:T(8,128)(2,1)S(1)}, u32[]{:S(2)}, u32[]{:S(2)}) %collective-permute-start.23) | collective-permute-done | bytes 81952 | tf_op jit(solution)/shard_map/ppermute | solution.py:344
  101.7 0.9 collective-permute-start.26
  102.6 3.2 %collective-permute-done.26.got_ref = bf16[10,16,128]{2,1,0:T(8,128)(2,1)S(1)} collective-permute-done((bf16[10,16,128]{2,1,0:T(8,128)(2,1)S(1)}, bf16[10,16,128]{2,1,0:T(8,128)(2,1)S(1)}, u32[]{:S(2)}, u32[]{:S(2)}) %collective-permute-start.26) | collective-permute-done | bytes 40992 | tf_op jit(solution)/shard_map/ppermute | solution.py:341
  107.2 2.4 %collective-permute-start.32 = (bf16[20,16,128]{2,1,0:T(8,128)(2,1)S(1)}, bf16[20,16,128]{2,1,0:T(8,128)(2,1)S(1)}, u32[]{:S(2)}, u32[]{:S(2)}) collective-permute-start(bf16[20,16,128]{2,1,0:T(8,128)(2,1)S(1)} %shard_map.112.refs_0_), channel_id=1, source_target_pairs={{0,6},{1,7},{2,4},{3,5},{4,2},{5,3},{6,0},{7,1},{8,14},{9,15},{10,... | collective-permute-start | bytes 245768 | tf_op jit(solution)/shard_map/ppermute | solution.py:344
  110.9 0.9 collective-permute-start.28
  111.8 1.4 %collective-permute-start.29 = (bf16[20,16,128]{2,1,0:T(8,128)(2,1)S(1)}, bf16[20,16,128]{2,1,0:T(8,128)(2,1)S(1)}, u32[]{:S(2)}, u32[]{:S(2)}) collective-permute-start(bf16[20,16,128]{2,1,0:T(8,128)(2,1)S(1)} %shard_map.112.refs_0_), channel_id=1, source_target_pairs={{0,3},{1,2},{2,1},{3,0},{4,7},{5,6},{6,5},{7,4},{8,11},{9,10},{10,... | collective-permute-start | bytes 245768 | tf_op jit(solution)/shard_map/ppermute | solution.py:344
  114.0 1.8 %collective-permute-start.30 = (bf16[20,16,128]{2,1,0:T(8,128)(2,1)S(1)}, bf16[20,16,128]{2,1,0:T(8,128)(2,1)S(1)}, u32[]{:S(2)}, u32[]{:S(2)}) collective-permute-start(bf16[20,16,128]{2,1,0:T(8,128)(2,1)S(1)} %shard_map.112.refs_0_), channel_id=1, source_target_pairs={{0,4},{1,5},{2,6},{3,7},{4,0},{5,1},{6,2},{7,3},{8,12},{9,13},{10,... | collective-permute-start | bytes 245768 | tf_op jit(solution)/shard_map/ppermute | solution.py:344
  115.8 1.0 collective-permute-start.31
  116.7 1.6 %collective-permute-start.33 = (bf16[20,16,128]{2,1,0:T(8,128)(2,1)S(1)}, bf16[20,16,128]{2,1,0:T(8,128)(2,1)S(1)}, u32[]{:S(2)}, u32[]{:S(2)}) collective-permute-start(bf16[20,16,128]{2,1,0:T(8,128)(2,1)S(1)} %collective-permute-done.32.refs_6_), channel_id=1, source_target_pairs={{0,1},{1,0},{2,3},{3,2},{4,5},{5,4},{6,7},{7,6},{8,9},{9,8},{10,11... | collective-permute-start | bytes 245768 | tf_op jit(solution)/shard_map/ppermute | solution.py:344
  118.4 2.8 %shard_map.114.place_ref = s32[20]{0:T(128)S(1)} custom-call(s32[16]{0:T(128)S(1)} %concatenate.3.pos_ref.refs_0_, s32[80]{0:T(128)S(1)} %copy-done.11), custom_call_target="tpu_custom_call" | custom-call | bytes 1000 | tf_op jit(solution)/shard_map/pallas_call | solution.py:516
  121.2 0.9 shard_map.102.other_ref
  122.1 1.3 shard_map.115
  123.3 1.5 %collective-permute-done.31.refs_5_ = bf16[20,16,128]{2,1,0:T(8,128)(2,1)S(1)} collective-permute-done((bf16[20,16,128]{2,1,0:T(8,128)(2,1)S(1)}, bf16[20,16,128]{2,1,0:T(8,128)(2,1)S(1)}, u32[]{:S(2)}, u32[]{:S(2)}) %collective-permute-start.31) | collective-permute-done | bytes 81952 | tf_op jit(solution)/shard_map/ppermute | solution.py:344
  124.8 2.2 %shard_map.113 = bf16[192,1120]{1,0:T(8,128)(2,1)} custom-call(s32[16]{0:T(128)S(1)} %concatenate.3.pos_ref.refs_0_, s32[2]{0:T(128)S(1)} %copy-done.10, bf16[192,640]{1,0:T(8,128)(2,1)S(1)} %get-tuple-element.21.own_ref, bf16[192,640]{1,0:T(8,128)(2,1)S(1)} %shard_map.102.other_ref, bf16[20,16,128]{2,1,0:T(8,128)(2,1)S(1)} %shard_map.112.refs_0_, ...), custom_call_target="tpu_custom_call" | custom-call | flops 1500000000 | bytes 3000000 | tf_op jit(solution)/shard_map/pallas_call | solution.py:536
  (81 shorter events, 12.3 us)
Async XLA Ops:
  2.3 11.6 %collective-permute-start.11 = (bf16[280,1152]{1,0:T(8,128)(2,1)S(1)}, bf16[280,1152]{1,0:T(8,128)(2,1)S(1)}, u32[]{:S(2)}, u32[]{:S(2)}) collective-permute-start(bf16[280,1152]{1,0:T(8,128)(2,1)S(1)} %shard_map.103.refs_0_), channel_id=1, source_target_pairs={{0,2},{1,3},{2,0},{3,1},{4,6},{5,7},{6,4},{7,5},{8,9},{9,8},{10,12... | collective-permute-start | bytes 1935368 | tf_op jit(solution)/shard_map/ppermute | solution.py:399
  13.9 10.5 %collective-permute-start.13 = (bf16[280,1152]{1,0:T(8,128)(2,1)S(1)}, bf16[280,1152]{1,0:T(8,128)(2,1)S(1)}, u32[]{:S(2)}, u32[]{:S(2)}) collective-permute-start(bf16[280,1152]{1,0:T(8,128)(2,1)S(1)} %collective-permute-done.11.refs_1_.early_ref), channel_id=1, source_target_pairs={{0,1},{1,0},{2,4},{3,5},{4,2},{5,3},{6,7},{7,6},{8,10},{9,11},{10,... | collective-permute-start | bytes 1935368 | tf_op jit(solution)/shard_map/ppermute | solution.py:399
  16.6 25.2 %copy-start = (bf16[2,4,24,2240]{3,2,1,0:T(8,128)(2,1)S(1)}, bf16[2,4,24,2240]{3,2,1,0:T(8,128)(2,1)}, u32[]{:S(2)}) copy-start(bf16[2,4,24,2240]{3,2,1,0:T(8,128)(2,1)} %param.7) | copy-start | bytes 2580484
  24.9 18.4 %collective-permute-start.15 = (bf16[280,1152]{1,0:T(8,128)(2,1)S(1)}, bf16[280,1152]{1,0:T(8,128)(2,1)S(1)}, u32[]{:S(2)}, u32[]{:S(2)}) collective-permute-start(bf16[280,1152]{1,0:T(8,128)(2,1)S(1)} %shard_map.106), channel_id=1, source_target_pairs={{0,2},{1,3},{2,0},{3,1},{4,6},{5,7},{6,4},{7,5},{8,9},{9,8},{10,11... | collective-permute-start | bytes 1935368 | tf_op jit(solution)/shard_map/ppermute | solution.py:399
  28.2 16.3 %copy-start.6 = (bf16[280,640]{1,0:T(8,128)(2,1)}, bf16[280,640]{1,0:T(8,128)(2,1)S(1)}, u32[]{:S(2)}) copy-start(bf16[280,640]{1,0:T(8,128)(2,1)S(1)} %shard_map.95.refs_0_) | copy-start | bytes 1075204
  28.2 12.2 %collective-permute-start.1 = (bf16[280,640]{1,0:T(8,128)(2,1)S(1)}, bf16[280,640]{1,0:T(8,128)(2,1)S(1)}, u32[]{:S(2)}, u32[]{:S(2)}) collective-permute-start(bf16[280,640]{1,0:T(8,128)(2,1)S(1)} %shard_map.95.refs_0_), channel_id=1, source_target_pairs={{0,2},{1,3},{2,0},{3,1},{4,6},{5,7},{6,4},{7,5},{8,9},{9,8},{10,12... | collective-permute-start | bytes 1075208 | tf_op jit(solution)/shard_map/ppermute | solution.py:399
  40.4 19.6 %copy-start.8 = (bf16[280,640]{1,0:T(8,128)(2,1)}, bf16[280,640]{1,0:T(8,128)(2,1)S(1)}, u32[]{:S(2)}) copy-start(bf16[280,640]{1,0:T(8,128)(2,1)S(1)} %collective-permute-done.1.refs_1_.early_ref) | copy-start | bytes 1075204
  40.4 8.8 %collective-permute-start.3 = (bf16[280,640]{1,0:T(8,128)(2,1)S(1)}, bf16[280,640]{1,0:T(8,128)(2,1)S(1)}, u32[]{:S(2)}, u32[]{:S(2)}) collective-permute-start(bf16[280,640]{1,0:T(8,128)(2,1)S(1)} %collective-permute-done.1.refs_1_.early_ref), channel_id=1, source_target_pairs={{0,1},{1,0},{2,4},{3,5},{4,2},{5,3},{6,7},{7,6},{8,10},{9,11},{10,... | collective-permute-start | bytes 1075208 | tf_op jit(solution)/shard_map/ppermute | solution.py:399
  41.8 20.5 %copy-start.12 = (f32[2,10,14,112]{3,0,2,1:T(2,128)S(1)}, f32[2,10,14,112]{3,0,2,1:T(2,128)}, u32[]{:S(2)}) copy-start(f32[2,10,14,112]{3,0,2,1:T(2,128)} %param.9) | copy-start | bytes 376324
  41.8 20.6 %copy-start.13 = (f32[2,10,112]{2,0,1:T(2,128)S(1)}, f32[2,10,112]{2,0,1:T(2,128)}, u32[]{:S(2)}) copy-start(f32[2,10,112]{2,0,1:T(2,128)} %param.10) | copy-start | bytes 26884
  41.8 18.2 %collective-permute-start = (bf16[192,2240]{1,0:T(8,128)(2,1)S(1)}, bf16[192,2240]{1,0:T(8,128)(2,1)S(1)}, u32[]{:S(2)}, u32[]{:S(2)}) collective-permute-start(bf16[192,2240]{1,0:T(8,128)(2,1)S(1)} %bitcast.11), channel_id=1, source_target_pairs={{0,16},{16,0},{1,17},{17,1},{2,18},{18,2},{3,19},{19,3},{4,20},{20... | collective-permute-start | bytes 2580488 | tf_op jit(solution)/shard_map/ppermute | solution.py:341
  43.9 14.8 %collective-permute-start.17 = (bf16[280,1152]{1,0:T(8,128)(2,1)S(1)}, bf16[280,1152]{1,0:T(8,128)(2,1)}, u32[]{:S(2)}, u32[]{:S(2)}) collective-permute-start(bf16[280,1152]{1,0:T(8,128)(2,1)S(1)} %shard_map.108), channel_id=1, source_target_pairs={{0,1},{1,0},{2,3},{3,2},{4,5},{5,4},{6,7},{7,6},{8,10},{9,11},{10,... | collective-permute-start | bytes 1935368 | tf_op jit(solution)/shard_map/ppermute | solution.py:399
  49.9 7.5 %collective-permute-start.5 = (bf16[280,640]{1,0:T(8,128)(2,1)S(1)}, bf16[280,640]{1,0:T(8,128)(2,1)S(1)}, u32[]{:S(2)}, u32[]{:S(2)}) collective-permute-start(bf16[280,640]{1,0:T(8,128)(2,1)S(1)} %shard_map.97), channel_id=1, source_target_pairs={{0,2},{1,3},{2,0},{3,1},{4,6},{5,7},{6,4},{7,5},{8,9},{9,8},{10,11... | collective-permute-start | bytes 1075208 | tf_op jit(solution)/shard_map/ppermute | solution.py:399
  51.0 16.0 %collective-permute-start.12 = (bf16[280,1152]{1,0:T(8,128)(2,1)S(1)}, bf16[280,1152]{1,0:T(8,128)(2,1)}, u32[]{:S(2)}, u32[]{:S(2)}) collective-permute-start(bf16[280,1152]{1,0:T(8,128)(2,1)S(1)} %collective-permute-done.11.refs_1_.early_ref), channel_id=1, source_target_pairs={{0,8},{8,0},{1,9},{9,1},{2,10},{10,2},{3,11},{11,3},{4,12},{12,4},... | collective-permute-start | bytes 1935368 | tf_op jit(solution)/shard_map/ppermute | solution.py:341
  51.0 20.4 %collective-permute-start.14 = (bf16[280,1152]{1,0:T(8,128)(2,1)S(1)}, bf16[280,1152]{1,0:T(8,128)(2,1)}, u32[]{:S(2)}, u32[]{:S(2)}) collective-permute-start(bf16[280,1152]{1,0:T(8,128)(2,1)S(1)} %collective-permute-done.13.refs_1_.late_ref.early_ref), channel_id=1, source_target_pairs={{0,8},{8,0},{1,9},{9,1},{2,10},{10,2},{3,11},{11,3},{4,12},{12,4},... | collective-permute-start | bytes 1935368 | tf_op jit(solution)/shard_map/ppermute | solution.py:341
  57.3 2.7 %copy-start.4 = (bf16[280,640]{1,0:T(8,128)(2,1)}, bf16[280,640]{1,0:T(8,128)(2,1)S(1)}, u32[]{:S(2)}) copy-start(bf16[280,640]{1,0:T(8,128)(2,1)S(1)} %collective-permute-done.5.refs_1_.late_ref) | copy-start | bytes 1075204
  57.3 17.0 %collective-permute-start.16 = (bf16[280,1152]{1,0:T(8,128)(2,1)S(1)}, bf16[280,1152]{1,0:T(8,128)(2,1)}, u32[]{:S(2)}, u32[]{:S(2)}) collective-permute-start(bf16[280,1152]{1,0:T(8,128)(2,1)S(1)} %collective-permute-done.15.refs_1_.late_ref), channel_id=1, source_target_pairs={{0,8},{8,0},{1,9},{9,1},{2,10},{10,2},{3,11},{11,3},{4,12},{12,4},... | collective-permute-start | bytes 1935368 | tf_op jit(solution)/shard_map/ppermute | solution.py:341
  58.7 18.4 %collective-permute-start.18 = (bf16[280,1152]{1,0:T(8,128)(2,1)}, bf16[280,1152]{1,0:T(8,128)(2,1)}, u32[]{:S(2)}, u32[]{:S(2)}) collective-permute-start(bf16[280,1152]{1,0:T(8,128)(2,1)} %collective-permute-done.17.refs_2_), channel_id=1, source_target_pairs={{0,8},{8,0},{1,9},{9,1},{2,10},{10,2},{3,11},{11,3},{4,12},{12,4},... | collective-permute-start | bytes 1935368 | tf_op jit(solution)/shard_map/ppermute | solution.py:341
  61.0 13.2 %collective-permute-start.7 = (bf16[280,640]{1,0:T(8,128)(2,1)}, bf16[280,640]{1,0:T(8,128)(2,1)S(1)}, u32[]{:S(2)}, u32[]{:S(2)}) collective-permute-start(bf16[280,640]{1,0:T(8,128)(2,1)} %shard_map.100), channel_id=1, source_target_pairs={{0,1},{1,0},{2,3},{3,2},{4,5},{5,4},{6,7},{7,6},{8,10},{9,11},{10,... | collective-permute-start | bytes 1075208 | tf_op jit(solution)/shard_map/ppermute | solution.py:399
  65.6 1.3 %copy-start.10 = (s32[2]{0:T(128)S(1)}, s32[2]{0:T(128)}, u32[]{:S(2)}) copy-start(s32[2]{0:T(128)} %near_ref.3) | copy-start | bytes 28
  67.0 4.3 %copy-start.9 = (bf16[280,640]{1,0:T(8,128)(2,1)S(1)}, bf16[280,640]{1,0:T(8,128)(2,1)}, u32[]{:S(2)}) copy-start(bf16[280,640]{1,0:T(8,128)(2,1)} %copy-done.8) | copy-start | bytes 1075204
  67.0 4.3 %collective-permute-start.10 = (s32[2]{0:T(128)S(1)}, s32[2]{0:T(128)S(1)}, u32[]{:S(2)}, u32[]{:S(2)}) collective-permute-start(s32[2]{0:T(128)S(1)} %copy-done.10), channel_id=1, source_target_pairs={{0,16},{16,0},{1,17},{17,1},{2,18},{18,2},{3,19},{19,3},{4,20},{20... | collective-permute-start | bytes 32 | tf_op jit(solution)/shard_map/ppermute | solution.py:341
  71.3 2.9 %copy-start.5 = (bf16[280,640]{1,0:T(8,128)(2,1)S(1)}, bf16[280,640]{1,0:T(8,128)(2,1)}, u32[]{:S(2)}) copy-start(bf16[280,640]{1,0:T(8,128)(2,1)} %copy-done.4) | copy-start | bytes 1075204
  71.3 10.1 %collective-permute-start.2 = (bf16[280,640]{1,0:T(8,128)(2,1)S(1)}, bf16[280,640]{1,0:T(8,128)(2,1)S(1)}, u32[]{:S(2)}, u32[]{:S(2)}) collective-permute-start(bf16[280,640]{1,0:T(8,128)(2,1)S(1)} %copy-done.9), channel_id=1, source_target_pairs={{0,8},{8,0},{1,9},{9,1},{2,10},{10,2},{3,11},{11,3},{4,12},{12,4},... | collective-permute-start | bytes 1075208 | tf_op jit(solution)/shard_map/ppermute | solution.py:341
  71.4 11.5 %collective-permute-start.4 = (bf16[280,640]{1,0:T(8,128)(2,1)S(1)}, bf16[280,640]{1,0:T(8,128)(2,1)S(1)}, u32[]{:S(2)}, u32[]{:S(2)}) collective-permute-start(bf16[280,640]{1,0:T(8,128)(2,1)S(1)} %collective-permute-done.3.refs_3_.late_ref.early_ref), channel_id=1, source_target_pairs={{0,8},{8,0},{1,9},{9,1},{2,10},{10,2},{3,11},{11,3},{4,12},{12,4},... | collective-permute-start | bytes 1075208 | tf_op jit(solution)/shard_map/ppermute | solution.py:341
  74.2 13.6 %collective-permute-start.6 = (bf16[280,640]{1,0:T(8,128)(2,1)S(1)}, bf16[280,640]{1,0:T(8,128)(2,1)S(1)}, u32[]{:S(2)}, u32[]{:S(2)}) collective-permute-start(bf16[280,640]{1,0:T(8,128)(2,1)S(1)} %copy-done.5), channel_id=1, source_target_pairs={{0,8},{8,0},{1,9},{9,1},{2,10},{10,2},{3,11},{11,3},{4,12},{12,4},... | collective-permute-start | bytes 1075208 | tf_op jit(solution)/shard_map/ppermute | solution.py:341
  74.3 16.1 %collective-permute-start.8 = (bf16[280,640]{1,0:T(8,128)(2,1)S(1)}, bf16[280,640]{1,0:T(8,128)(2,1)S(1)}, u32[]{:S(2)}, u32[]{:S(2)}) collective-permute-start(bf16[280,640]{1,0:T(8,128)(2,1)S(1)} %collective-permute-done.7.refs_0_), channel_id=1, source_target_pairs={{0,8},{8,0},{1,9},{9,1},{2,10},{10,2},{3,11},{11,3},{4,12},{12,4},... | collective-permute-start | bytes 1075208 | tf_op jit(solution)/shard_map/ppermute | solution.py:341
  77.1 5.8 %copy-start.7 = (bf16[280,640]{1,0:T(8,128)(2,1)S(1)}, bf16[280,640]{1,0:T(8,128)(2,1)}, u32[]{:S(2)}) copy-start(bf16[280,640]{1,0:T(8,128)(2,1)} %copy-done.6) | copy-start | bytes 1075204
  80.8 5.4 %collective-permute-start.24 = (bf16[20,16,128]{2,1,0:T(8,128)(2,1)S(1)}, bf16[20,16,128]{2,1,0:T(8,128)(2,1)S(1)}, u32[]{:S(2)}, u32[]{:S(2)}) collective-permute-start(bf16[20,16,128]{2,1,0:T(8,128)(2,1)S(1)} %get-tuple-element.31), channel_id=1, source_target_pairs={{0,1},{1,0},{2,3},{3,2},{4,5},{5,4},{6,7},{7,6},{8,9},{9,8},{10,11... | collective-permute-start | bytes 245768 | tf_op jit(solution)/shard_map/ppermute | solution.py:344
  81.4 10.2 %collective-permute-start.19 = (bf16[20,16,128]{2,1,0:T(8,128)(2,1)S(1)}, bf16[20,16,128]{2,1,0:T(8,128)(2,1)S(1)}, u32[]{:S(2)}, u32[]{:S(2)}) collective-permute-start(bf16[20,16,128]{2,1,0:T(8,128)(2,1)S(1)} %get-tuple-element.25), channel_id=1, source_target_pairs={{0,1},{1,0},{2,3},{3,2},{4,5},{5,4},{6,7},{7,6},{8,9},{9,8},{10,11... | collective-permute-start | bytes 245768 | tf_op jit(solution)/shard_map/ppermute | solution.py:344
  85.0 12.4 %collective-permute-start.20 = (bf16[20,16,128]{2,1,0:T(8,128)(2,1)S(1)}, bf16[20,16,128]{2,1,0:T(8,128)(2,1)S(1)}, u32[]{:S(2)}, u32[]{:S(2)}) collective-permute-start(bf16[20,16,128]{2,1,0:T(8,128)(2,1)S(1)} %get-tuple-element.26), channel_id=1, source_target_pairs={{0,2},{1,3},{2,0},{3,1},{4,6},{5,7},{6,4},{7,5},{8,10},{9,11},{10,... | collective-permute-start | bytes 245768 | tf_op jit(solution)/shard_map/ppermute | solution.py:344
  86.2 12.1 %collective-permute-start.21 = (bf16[20,16,128]{2,1,0:T(8,128)(2,1)S(1)}, bf16[20,16,128]{2,1,0:T(8,128)(2,1)S(1)}, u32[]{:S(2)}, u32[]{:S(2)}) collective-permute-start(bf16[20,16,128]{2,1,0:T(8,128)(2,1)S(1)} %get-tuple-element.27), channel_id=1, source_target_pairs={{0,3},{1,2},{2,1},{3,0},{4,7},{5,6},{6,5},{7,4},{8,11},{9,10},{10,... | collective-permute-start | bytes 245768 | tf_op jit(solution)/shard_map/ppermute | solution.py:344
  87.8 10.5 %collective-permute-start.22 = (bf16[20,16,128]{2,1,0:T(8,128)(2,1)S(1)}, bf16[20,16,128]{2,1,0:T(8,128)(2,1)S(1)}, u32[]{:S(2)}, u32[]{:S(2)}) collective-permute-start(bf16[20,16,128]{2,1,0:T(8,128)(2,1)S(1)} %get-tuple-element.28), channel_id=1, source_target_pairs={{0,4},{1,5},{2,6},{3,7},{4,0},{5,1},{6,2},{7,3},{8,12},{9,13},{10,... | collective-permute-start | bytes 245768 | tf_op jit(solution)/shard_map/ppermute | solution.py:344
  90.5 10.6 %collective-permute-start.23 = (bf16[20,16,128]{2,1,0:T(8,128)(2,1)S(1)}, bf16[20,16,128]{2,1,0:T(8,128)(2,1)S(1)}, u32[]{:S(2)}, u32[]{:S(2)}) collective-permute-start(bf16[20,16,128]{2,1,0:T(8,128)(2,1)S(1)} %get-tuple-element.29), channel_id=1, source_target_pairs={{0,5},{1,4},{2,7},{3,6},{4,1},{5,0},{6,3},{7,2},{8,13},{9,12},{10,... | collective-permute-start | bytes 245768 | tf_op jit(solution)/shard_map/ppermute | solution.py:344
  91.6 9.5 %collective-permute-start.25 = (bf16[20,16,128]{2,1,0:T(8,128)(2,1)S(1)}, bf16[20,16,128]{2,1,0:T(8,128)(2,1)S(1)}, u32[]{:S(2)}, u32[]{:S(2)}) collective-permute-start(bf16[20,16,128]{2,1,0:T(8,128)(2,1)S(1)} %shard_map.110), channel_id=1, source_target_pairs={{0,6},{1,7},{2,4},{3,5},{4,2},{5,3},{6,0},{7,1},{8,14},{9,15},{10,... | collective-permute-start | bytes 245768 | tf_op jit(solution)/shard_map/ppermute | solution.py:344
  96.1 22.3 %copy-start.11 = (s32[80]{0:T(128)S(1)}, s32[80]{0:T(128)}, u32[]{:S(2)}) copy-start(s32[80]{0:T(128)} %new_ref.1) | copy-start | bytes 964
  97.4 13.4 %collective-permute-start.9 = (bf16[192,560]{1,0:T(8,128)(2,1)S(1)}, bf16[192,560]{1,0:T(8,128)(2,1)S(1)}, u32[]{:S(2)}, u32[]{:S(2)}) collective-permute-start(bf16[192,560]{1,0:T(8,128)(2,1)S(1)} %get-tuple-element.22), channel_id=1, source_target_pairs={{0,16},{16,0},{1,17},{17,1},{2,18},{18,2},{3,19},{19,3},{4,20},{20... | collective-permute-start | bytes 645128 | tf_op jit(solution)/shard_map/ppermute | solution.py:341
  101.7 4.1 %collective-permute-start.26 = (bf16[10,16,128]{2,1,0:T(8,128)(2,1)S(1)}, bf16[10,16,128]{2,1,0:T(8,128)(2,1)S(1)}, u32[]{:S(2)}, u32[]{:S(2)}) collective-permute-start(bf16[10,16,128]{2,1,0:T(8,128)(2,1)S(1)} %get-tuple-element.33), channel_id=1, source_target_pairs={{0,16},{16,0},{1,17},{17,1},{2,18},{18,2},{3,19},{19,3},{4,20},{20... | collective-permute-start | bytes 122888 | tf_op jit(solution)/shard_map/ppermute | solution.py:341
  106.4 4.5 %collective-permute-start.34 = (bf16[20,16,128]{2,1,0:T(8,128)(2,1)S(1)}, bf16[20,16,128]{2,1,0:T(8,128)(2,1)S(1)}, u32[]{:S(2)}, u32[]{:S(2)}) collective-permute-start(bf16[20,16,128]{2,1,0:T(8,128)(2,1)S(1)} %shard_map.112.refs_0_), channel_id=1, source_target_pairs={{0,16},{8,24},{16,0},{24,8},{1,17},{9,25},{17,1},{25,9},{2,18},{10... | collective-permute-start | bytes 245768 | tf_op jit(solution)/shard_map/ppermute | solution.py:512
  107.2 4.6 %collective-permute-start.35 = (bf16[20,16,128]{2,1,0:T(8,128)(2,1)S(1)}, bf16[20,16,128]{2,1,0:T(8,128)(2,1)S(1)}, u32[]{:S(2)}, u32[]{:S(2)}) collective-permute-start(bf16[20,16,128]{2,1,0:T(8,128)(2,1)S(1)} %shard_map.112.refs_0_), channel_id=1, source_target_pairs={{0,8},{8,0},{16,24},{24,16},{1,9},{9,1},{17,25},{25,17},{2,10},{10... | collective-permute-start | bytes 245768 | tf_op jit(solution)/shard_map/ppermute | solution.py:512
  107.2 6.8 %collective-permute-start.32 = (bf16[20,16,128]{2,1,0:T(8,128)(2,1)S(1)}, bf16[20,16,128]{2,1,0:T(8,128)(2,1)S(1)}, u32[]{:S(2)}, u32[]{:S(2)}) collective-permute-start(bf16[20,16,128]{2,1,0:T(8,128)(2,1)S(1)} %shard_map.112.refs_0_), channel_id=1, source_target_pairs={{0,6},{1,7},{2,4},{3,5},{4,2},{5,3},{6,0},{7,1},{8,14},{9,15},{10,... | collective-permute-start | bytes 245768 | tf_op jit(solution)/shard_map/ppermute | solution.py:344
  109.6 6.2 %collective-permute-start.27 = (bf16[20,16,128]{2,1,0:T(8,128)(2,1)S(1)}, bf16[20,16,128]{2,1,0:T(8,128)(2,1)S(1)}, u32[]{:S(2)}, u32[]{:S(2)}) collective-permute-start(bf16[20,16,128]{2,1,0:T(8,128)(2,1)S(1)} %shard_map.112.refs_0_), channel_id=1, source_target_pairs={{0,1},{1,0},{2,3},{3,2},{4,5},{5,4},{6,7},{7,6},{8,9},{9,8},{10,11... | collective-permute-start | bytes 245768 | tf_op jit(solution)/shard_map/ppermute | solution.py:344
  110.9 5.9 %collective-permute-start.36 = (bf16[20,16,128]{2,1,0:T(8,128)(2,1)S(1)}, bf16[20,16,128]{2,1,0:T(8,128)(2,1)S(1)}, u32[]{:S(2)}, u32[]{:S(2)}) collective-permute-start(bf16[20,16,128]{2,1,0:T(8,128)(2,1)S(1)} %collective-permute-done.34.refs_1_), channel_id=1, source_target_pairs={{0,8},{8,0},{16,24},{24,16},{1,9},{9,1},{17,25},{25,17},{2,10},{10... | collective-permute-start | bytes 245768 | tf_op jit(solution)/shard_map/ppermute | solution.py:512
  110.9 12.5 %collective-permute-start.28 = (bf16[20,16,128]{2,1,0:T(8,128)(2,1)S(1)}, bf16[20,16,128]{2,1,0:T(8,128)(2,1)S(1)}, u32[]{:S(2)}, u32[]{:S(2)}) collective-permute-start(bf16[20,16,128]{2,1,0:T(8,128)(2,1)S(1)} %shard_map.112.refs_0_), channel_id=1, source_target_pairs={{0,2},{1,3},{2,0},{3,1},{4,6},{5,7},{6,4},{7,5},{8,10},{9,11},{10,... | collective-permute-start | bytes 245768 | tf_op jit(solution)/shard_map/ppermute | solution.py:344
  111.8 11.5 %collective-permute-start.29 = (bf16[20,16,128]{2,1,0:T(8,128)(2,1)S(1)}, bf16[20,16,128]{2,1,0:T(8,128)(2,1)S(1)}, u32[]{:S(2)}, u32[]{:S(2)}) collective-permute-start(bf16[20,16,128]{2,1,0:T(8,128)(2,1)S(1)} %shard_map.112.refs_0_), channel_id=1, source_target_pairs={{0,3},{1,2},{2,1},{3,0},{4,7},{5,6},{6,5},{7,4},{8,11},{9,10},{10,... | collective-permute-start | bytes 245768 | tf_op jit(solution)/shard_map/ppermute | solution.py:344
  114.0 9.4 %collective-permute-start.30 = (bf16[20,16,128]{2,1,0:T(8,128)(2,1)S(1)}, bf16[20,16,128]{2,1,0:T(8,128)(2,1)S(1)}, u32[]{:S(2)}, u32[]{:S(2)}) collective-permute-start(bf16[20,16,128]{2,1,0:T(8,128)(2,1)S(1)} %shard_map.112.refs_0_), channel_id=1, source_target_pairs={{0,4},{1,5},{2,6},{3,7},{4,0},{5,1},{6,2},{7,3},{8,12},{9,13},{10,... | collective-permute-start | bytes 245768 | tf_op jit(solution)/shard_map/ppermute | solution.py:344
  115.8 9.1 %collective-permute-start.31 = (bf16[20,16,128]{2,1,0:T(8,128)(2,1)S(1)}, bf16[20,16,128]{2,1,0:T(8,128)(2,1)S(1)}, u32[]{:S(2)}, u32[]{:S(2)}) collective-permute-start(bf16[20,16,128]{2,1,0:T(8,128)(2,1)S(1)} %shard_map.112.refs_0_), channel_id=1, source_target_pairs={{0,5},{1,4},{2,7},{3,6},{4,1},{5,0},{6,3},{7,2},{8,13},{9,12},{10,... | collective-permute-start | bytes 245768 | tf_op jit(solution)/shard_map/ppermute | solution.py:344
  116.7 8.1 %collective-permute-start.33 = (bf16[20,16,128]{2,1,0:T(8,128)(2,1)S(1)}, bf16[20,16,128]{2,1,0:T(8,128)(2,1)S(1)}, u32[]{:S(2)}, u32[]{:S(2)}) collective-permute-start(bf16[20,16,128]{2,1,0:T(8,128)(2,1)S(1)} %collective-permute-done.32.refs_6_), channel_id=1, source_target_pairs={{0,1},{1,0},{2,3},{3,2},{4,5},{5,4},{6,7},{7,6},{8,9},{9,8},{10,11... | collective-permute-start | bytes 245768 | tf_op jit(solution)/shard_map/ppermute | solution.py:344
  (3 other events, 3.3 us)

commit v6 on v5

--- a/solution.py
+++ b/solution.py
@@ -61,26 +61,25 @@
     )
 
 
-def prep_kernel(kinds, pos_ref, w_hbm, out_ref, w_ref, sems):
-    depth, total = w_hbm.shape
+def prep_kernel(kinds, first, last, pos_ref, w_hbm, out_ref, w_ref, sems):
+    total = w_hbm.shape[1]
     width = total // 6
-    cuts = sems.shape[0]
-    edges = [depth * i // cuts // 8 * 8 for i in range(cuts)] + [depth]
-    spans = list(zip(edges, edges[1:]))
-    low = min(kinds) * 2 * width // LANES * LANES
     high = min(-(-(max(kinds) + 1) * 2 * width // LANES) * LANES, total)
+    mid = (last - first) // 32 * 16
+    spans = [(0, mid), (mid, last - first)]
     copies = []
     for i, (lo, hi) in enumerate(spans):
         if high == total:
-            low, source, target = 0, w_hbm.at[lo:hi], w_ref.at[lo:hi]
+            source, target = w_hbm.at[first + lo : first + hi], w_ref.at[lo:hi]
         else:
-            source, target = w_hbm.at[lo:hi, low:high], w_ref.at[lo:hi, : high - low]
+            source = w_hbm.at[first + lo : first + hi, :high]
+            target = w_ref.at[lo:hi, :high]
         copies.append(pltpu.make_async_copy(source, target, sems.at[i]))
     for copy in copies:
         copy.start()
     used = len(kinds) * width
     if used < out_ref.shape[1]:
-        out_ref[:, used:] = jnp.zeros((depth, out_ref.shape[1] - used), BF16)
+        out_ref[:, used:] = jnp.zeros((last - first, out_ref.shape[1] - used), BF16)
     for copy, (lo, hi) in zip(copies, spans):
         copy.wait()
         for turn in range(2):
@@ -88,7 +87,7 @@
             @pl.when(pos_ref[0] == turn)
             def _():
                 for j, kind in enumerate(kinds):
-                    start = (2 * kind + turn) * width - low
+                    start = (2 * kind + turn) * width
                     out_ref[lo:hi, j * width : (j + 1) * width] = w_ref[
                         lo:hi, start : start + width
                     ]
@@ -137,33 +136,41 @@
         old_ref[u, rows - 1 :, :size] = ksum[u : u + 1]
 
 
-def block_kernel(pos_ref, own_ref, other_ref, out_ref):
-    members, both, _ = out_ref.shape
+def block_kernel(pos_ref, own_ref, other_ref, lead_ref, tail_ref):
+    members, both, half = lead_ref.shape
     count = both // 2
     depth = own_ref.shape[1] // members
     for b in range(members):
-        out_ref[b, :count, :depth] = own_ref[:, b * depth : (b + 1) * depth]
-        out_ref[b, count:, :depth] = other_ref[:, b * depth : (b + 1) * depth]
-
-
-def add_products(slots, pos_ref, blocks_ref, refs, tile):
-    terms = []
+        for span, ref in ((slice(0, count), own_ref), (slice(count, both), other_ref)):
+            lead_ref[b, span] = ref[:, b * depth : b * depth + half]
+            tail_ref[b, span] = ref[:, b * depth + half : (b + 1) * depth]
+
+
+def add_products(slots, split, pos_ref, lead_ref, tail_ref, refs, tile):
+    half = lead_ref.shape[2]
+
+    def rows(i, *at):
+        if split:
+            return refs[2 * i][*at, :, tile], refs[2 * i + 1][*at, :, tile]
+        return refs[i][*at, :half, tile], refs[i][*at, half:, tile]
+
     if slots == ("core",):
         first = pos_ref[2] == 0
-        weight = jnp.where(first, refs[0][:, tile], refs[1][:, tile])
-        terms = [(jnp.where(first, pos_ref[14], pos_ref[15]), weight)]
+        weights = [jnp.where(first, a, b) for a, b in zip(rows(0), rows(1))]
+        terms = [(jnp.where(first, pos_ref[14], pos_ref[15]), weights)]
     elif slots == ("all",):
-        terms = [(b, refs[0][b, :, tile]) for b in range(refs[0].shape[0])]
+        terms = [(b, rows(0, b)) for b in range(refs[0].shape[0])]
     else:
-        terms = [(pos_ref[slot], ref[:, tile]) for slot, ref in zip(slots, refs)]
+        terms = [(pos_ref[slot], rows(i)) for i, slot in enumerate(slots)]
     total = None
-    for index, weight in terms:
-        term = jnp.dot(blocks_ref[index], weight, preferred_element_type=F32)
-        total = term if total is None else total + term
+    for index, (lead, tail) in terms:
+        for lhs, weight in ((lead_ref, lead), (tail_ref, tail)):
+            term = jnp.dot(lhs[index], weight, preferred_element_type=F32)
+            total = term if total is None else total + term
     return total
 
 
-def mul_kernel(slots, fresh, pos_ref, blocks_ref, *refs):
+def mul_kernel(slots, split, fresh, pos_ref, lead_ref, tail_ref, *refs):
     acc_ref = refs[-1]
     given = refs[:-1] if fresh else refs[1:-1]
     step = acc_ref.shape[1]
@@ -171,11 +178,11 @@
     @pl.loop(0, acc_ref.shape[1] // step)
     def _(t):
         tile = pl.ds(pl.multiple_of(t * step, step), step)
-        term = add_products(slots, pos_ref, blocks_ref, given, tile)
+        term = add_products(slots, split, pos_ref, lead_ref, tail_ref, given, tile)
         acc_ref[:, tile] = term if fresh else refs[0][:, tile] + term
 
 
-def ask_kernel(slots, width, pos_ref, blocks_ref, old_ref, group_ref, *refs):
+def ask_kernel(slots, width, pos_ref, lead_ref, tail_ref, old_ref, group_ref, *refs):
     given, (mine_ref, give_ref, acc_ref) = refs[:-3], refs[-3:]
     step = acc_ref.shape[1]
 
@@ -183,7 +190,7 @@
     def _(t):
         tile = pl.ds(pl.multiple_of(t * step, step), step)
         acc_ref[:, tile] = old_ref[:, tile] + add_products(
-            slots, pos_ref, blocks_ref, given, tile
+            slots, False, pos_ref, lead_ref, tail_ref, given, tile
         )
 
     count = acc_ref.shape[0] // 2
@@ -194,8 +201,8 @@
 
 
 def kv_kernel(slots, streams, frames, heads, size, rows, pos_ref, near_ref, far_ref, *refs):
-    blocks_ref, old_ref, refs = refs[0], refs[1], refs[2:]
-    count = 2 if slots == ("core",) else 1
+    lead_ref, tail_ref, old_ref, refs = refs[0], refs[1], refs[2], refs[3:]
+    count = 4 if slots == ("core",) else 2
     given, refs = refs[:count], refs[count:]
     group_ref, plain_ref = refs[:2]
     chunks, acc_ref = refs[2:-1], refs[-1]
@@ -205,7 +212,7 @@
     def _(t):
         tile = pl.ds(pl.multiple_of(t * step, step), step)
         acc_ref[:, tile] = old_ref[:, tile] + add_products(
-            slots, pos_ref, blocks_ref, given, tile
+            slots, True, pos_ref, lead_ref, tail_ref, given, tile
         )
 
     width = heads * size
@@ -297,13 +304,15 @@
 def place_kernel(units, pos_ref, new_ref, place_ref):
     me = pos_ref[5]
 
-    @pl.loop(0, new_ref.shape[0])
-    def _(g):
-        spot = new_ref[g]
-
-        @pl.when(spot // units == me)
-        def _():
-            place_ref[spot % units] = ((g // units) ^ me) * units + g % units
+    @pl.loop(0, new_ref.shape[0] // units)
+    def _(owner):
+        first = (owner ^ me) * units
+        for local in range(units):
+            spot = new_ref[owner * units + local] - me * units
+
+            @pl.when((spot >= 0) & (spot < units))
+            def _():
+                place_ref[spot] = first + local
 
 
 def pick_kernel(share, size, rows, spots, place_ref, *refs):
@@ -364,17 +373,24 @@
     wide_kv = -(-2 * width // LANES) * LANES
     wide_q = -(-width // LANES) * LANES
 
-    def prep(kinds, wide):
+    half = -(-depth // 32) * 16
+
+    def prep(kinds, wide, first, last):
         return whole_call(
-            functools.partial(prep_kernel, kinds),
-            jax.ShapeDtypeStruct((depth, wide), BF16),
+            functools.partial(prep_kernel, kinds, first, last),
+            jax.ShapeDtypeStruct((last - first, wide), BF16),
             "sh",
             0,
             2_000_000,
-            scratch=[pltpu.VMEM(w_qkv.shape, BF16), pltpu.SemaphoreType.DMA((5,))],
+            scratch=[
+                pltpu.VMEM((last - first, w_qkv.shape[1]), BF16),
+                pltpu.SemaphoreType.DMA((2,)),
+            ],
         )(y.reshape(1), pltpu.with_memory_space_constraint(w_qkv, pltpu.HBM))
 
-    pieces = [prep((1, 2), wide_kv), prep((0,), wide_q)]
+    leads = prep((1, 2), wide_kv, 0, half)
+    tails = prep((1, 2), wide_kv, half, depth)
+    wholes = prep((0,), wide_q, 0, depth)
 
     def choose(core, early, late):
         return whole_call(
@@ -415,46 +431,57 @@
         0,
         2_000_000,
     )(pos, state_in.reshape(units, share, size), ksum_in.reshape(units, size))
-    blocks = whole_call(
-        block_kernel, jax.ShapeDtypeStruct((members, 2 * count, depth), BF16), "svv", 0, 4_000_000
+    lead_blocks, tail_blocks = whole_call(
+        block_kernel,
+        [
+            jax.ShapeDtypeStruct((members, 2 * count, rows_of), BF16)
+            for rows_of in (half, depth - half)
+        ],
+        "svv",
+        0,
+        4_000_000,
     )(pos, own_tokens, other_tokens)
 
-    def multiply(slots, acc, *given):
+    def multiply(slots, split, acc, *given):
         first = [] if acc is None else [acc]
         wide = given[0].shape[-1]
         return whole_call(
-            functools.partial(mul_kernel, slots, acc is None),
+            functools.partial(mul_kernel, slots, split, acc is None),
             jax.ShapeDtypeStruct((2 * count, wide), F32),
-            "sv" + "v" * (len(first) + len(given)),
+            "svv" + "v" * (len(first) + len(given)),
             1_500_000_000,
             5_000_000,
-            alias={2: 0} if first else None,
-        )(pos, blocks, *first, *given)
+            alias={3: 0} if first else None,
+        )(pos, lead_blocks, tail_blocks, *first, *given)
 
     if fast:
-        kvs, qs = rounds(pieces[0]), rounds(pieces[1])
-        acc = multiply((7, 8, 9), None, pieces[0], *kvs[0])
-        acc = multiply((10, 11), acc, *kvs[1])
-        acc = multiply((12, 13), acc, *kvs[2])
+        kvs = [
+            (a, e, a_there, e_there)
+            for (a, a_there), (e, e_there) in zip(rounds(leads), rounds(tails))
+        ]
+        qs = rounds(wholes)
+        acc = multiply((7, 8, 9), True, None, leads, tails, *kvs[0])
+        acc = multiply((10, 11), True, acc, *kvs[1])
+        acc = multiply((12, 13), True, acc, *kvs[2])
+        asked = multiply((7, 8, 9, 10, 11), False, None, wholes, *qs[0], *qs[1])
+        asked = multiply((12, 13), False, asked, *qs[2])
         last, last_kv, last_q = ("core",), kvs[3], qs[3]
-        asked = multiply((7, 8, 9, 10, 11), None, pieces[1], *qs[0], *qs[1])
-        asked = multiply((12, 13), asked, *qs[2])
     else:
-        last, last_kv, last_q = ("all",), *(
-            (lax.all_gather(piece, ("z", "x"), axis=0, tiled=False),) for piece in pieces
-        )
-        acc, asked = (jnp.zeros((2 * count, piece.shape[1]), F32) for piece in pieces)
+        last = ("all",)
+        whole_kv = [lax.all_gather(v, ("z", "x"), axis=0, tiled=False) for v in (leads, tails)]
+        last_kv, last_q = whole_kv, [lax.all_gather(wholes, ("z", "x"), axis=0, tiled=False)]
+        acc, asked = (jnp.zeros((2 * count, wide), F32) for wide in (wide_kv, wide_q))
 
     pairs = 2 * streams * heads
     chunk = jax.ShapeDtypeStruct((pairs, rows, LANES), BF16)
     parts = whole_call(
         functools.partial(kv_kernel, last, streams, frames, heads, size, rows),
         [chunk] * members,
-        "sss" + "v" * (4 + len(last_kv)),
+        "sss" + "v" * (5 + len(last_kv)),
         1_500_000_000,
         5_000_000,
         scratch=[pltpu.VMEM(acc.shape, F32)],
-    )(pos, frames_live, far_live, blocks, acc, *last_kv, group, plain)
+    )(pos, frames_live, far_live, lead_blocks, tail_blocks, acc, *last_kv, group, plain)
     parts = list(parts)
     q, q_give = whole_call(
         functools.partial(ask_kernel, last, width),
@@ -462,11 +489,11 @@
             jax.ShapeDtypeStruct((count, heads * LANES), BF16),
             jax.ShapeDtypeStruct((count, width), BF16),
         ],
-        "svvv" + "v" * len(last_q),
+        "svvvv" + "v" * len(last_q),
         700_000_000,
         3_000_000,
         scratch=[pltpu.VMEM(asked.shape, F32)],
-    )(pos, blocks, asked, group, *last_q)
+    )(pos, lead_blocks, tail_blocks, asked, group, *last_q)
 
     far = members - 1
     parts[far - 1] = whole_call(

time: 127 us -> 119 us (0.937)
  waiting for transfers between devices: 49.9 us -> 30.8 us
  starting transfers between devices: 39.3 us -> 47.8 us
  Pallas kernels: 32.7 us -> 36 us
    ppermute x8 -> x12, waiting for transfers between devices: 40.3 us -> 14.9 us  [rounds(): got.append(lax.ppermute(give, ('c', 'z', 'x'), step))]
    ppermute x12 -> x16, waiting for transfers between devices: 3.24 us -> 8.15 us  [swap(): return lax.ppermute(v, axis, SWAP)]
    ppermute x8 -> x12, starting transfers between devices: 11.6 us -> 15.6 us  [rounds(): got.append(lax.ppermute(give, ('c', 'z', 'x'), step))]
    ppermute x12 -> x16, starting transfers between devices: 6.44 us -> 9.84 us  [swap(): return lax.ppermute(v, axis, SWAP)]
    pallas_call x4 -> x6, Pallas kernels: 3.08 us -> 5.52 us  [choose(): whole_call(functools.partial(choose_kernel, core), jax.ShapeDtypeStruct(e...]
    ppermute x14, waiting for transfers between devices: 5.79 us -> 7.72 us  [xor(): return lax.ppermute(v, ('z', 'x'), [(i, i ^ k) for i in range(members)])]
    pallas_call x8 -> x9, Pallas kernels: 14.8 us -> 16.6 us  [the longest x5 10.6 us: multiply(): whole_call(functools.partial(mul_kernel, slots, split, acc is None), jax....]
    pallas_call x1, Pallas kernels: 2.77 us -> 1.34 us  [layer(): whole_call(functools.partial(place_kernel, units), jax.ShapeDtypeStruct((...]
  transfers between devices with their start and end apart: 37 -> 45, of which waited for: 12 -> 11; matrix products, arithmetic and copies ran while one was open for 1% -> 1% of each run, Pallas kernels for 22% -> 27%
where the time goes in v6:
time: 119 us
  starting transfers between devices  47.8 us (40%)
  Pallas kernels  36 us (30%)
  waiting for transfers between devices  30.8 us (26%)
  local copies, waits for them, and re-layouts  3.18 us (3%)
    ppermute x14, starting transfers between devices, xor(): return lax.ppermute(v, ('z', 'x'), [(i, i ^ k) for i in range(members)])  20.7 us
    ppermute x12, starting transfers between devices, rounds(): got.append(lax.ppermute(give, ('c', 'z', 'x'), step))  15.6 us
    ppermute x12, waiting for transfers between devices, rounds(): got.append(lax.ppermute(give, ('c', 'z', 'x'), step))  14.9 us
    pallas_call x5, Pallas kernels, multiply(): whole_call(functools.partial(mul_kernel, slots, split, acc is None), jax....  10.6 us
    ppermute x16, starting transfers between devices, swap(): return lax.ppermute(v, axis, SWAP)  9.84 us
    ppermute x16, waiting for transfers between devices, swap(): return lax.ppermute(v, axis, SWAP)  8.15 us
    ppermute x14, waiting for transfers between devices, xor(): return lax.ppermute(v, ('z', 'x'), [(i, i ^ k) for i in range(members)])  7.72 us
    pallas_call x6, Pallas kernels, choose(): whole_call(functools.partial(choose_kernel, core), jax.ShapeDtypeStruct(e...  5.52 us
  transfers between devices with their start and end apart: 45, of which 11 were waited for; matrix products, arithmetic and copies ran while one was open for 1% of the time, Pallas kernels for 27%

profile of v6, /device:TPU:0, one launch (start us, length us, event | category | flops | bytes accessed | tf_op | source)
XLA Modules:
  0.0 118.8 jit_solution(7746326425171100066)
XLA Ops:
  0.6 1.3 %shard_map.104.refs_1_ = bf16[136,1152]{1,0:T(8,128)(2,1)S(1)} custom-call(s32[1]{0:T(128)} %bitcast.3.pos_ref, bf16[280,3360]{1,0:T(8,128)(2,1)} %w_hbm.5), custom_call_target="tpu_custom_call" | custom-call | bytes 2000000 | tf_op jit(solution)/shard_map/pallas_call | solution.py:379
  2.0 3.1 %collective-permute-start.12 = (bf16[136,1152]{1,0:T(8,128)(2,1)S(1)}, bf16[136,1152]{1,0:T(8,128)(2,1)S(1)}, u32[]{:S(2)}, u32[]{:S(2)}) collective-permute-start(bf16[136,1152]{1,0:T(8,128)(2,1)S(1)} %shard_map.104.refs_1_), channel_id=1, source_target_pairs={{0,2},{1,3},{2,0},{3,1},{4,6},{5,7},{6,4},{7,5},{8,9},{9,8},{10,12... | collective-permute-start | bytes 940040 | tf_op jit(solution)/shard_map/ppermute | solution.py:415
  6.3 1.3 %shard_map.103.refs_0_ = bf16[144,1152]{1,0:T(8,128)(2,1)S(1)} custom-call(s32[1]{0:T(128)} %bitcast.3.pos_ref, bf16[280,3360]{1,0:T(8,128)(2,1)} %w_hbm.5), custom_call_target="tpu_custom_call" | custom-call | bytes 2000000 | tf_op jit(solution)/shard_map/pallas_call | solution.py:379
  7.6 2.1 %collective-permute-start.11 = (bf16[144,1152]{1,0:T(8,128)(2,1)S(1)}, bf16[144,1152]{1,0:T(8,128)(2,1)S(1)}, u32[]{:S(2)}, u32[]{:S(2)}) collective-permute-start(bf16[144,1152]{1,0:T(8,128)(2,1)S(1)} %shard_map.103.refs_0_), channel_id=1, source_target_pairs={{0,2},{1,3},{2,0},{3,1},{4,6},{5,7},{6,4},{7,5},{8,9},{9,8},{10,12... | collective-permute-start | bytes 995336 | tf_op jit(solution)/shard_map/ppermute | solution.py:415
  9.7 1.6 %collective-permute-start = (bf16[192,2240]{1,0:T(8,128)(2,1)}, bf16[192,2240]{1,0:T(8,128)(2,1)}, u32[]{:S(2)}, u32[]{:S(2)}) collective-permute-start(bf16[192,2240]{1,0:T(8,128)(2,1)} %bitcast.7.own_ref), channel_id=1, source_target_pairs={{0,16},{16,0},{1,17},{17,1},{2,18},{18,2},{3,19},{19,3},{4,20},{20... | collective-permute-start | bytes 2580488 | tf_op jit(solution)/shard_map/ppermute | solution.py:350
  11.4 1.5 %collective-permute-start.16 = (bf16[136,1152]{1,0:T(8,128)(2,1)S(1)}, bf16[136,1152]{1,0:T(8,128)(2,1)S(1)}, u32[]{:S(2)}, u32[]{:S(2)}) collective-permute-start(bf16[136,1152]{1,0:T(8,128)(2,1)S(1)} %collective-permute-done.12.refs_3_.early_ref), channel_id=1, source_target_pairs={{0,1},{1,0},{2,4},{3,5},{4,2},{5,3},{6,7},{7,6},{8,10},{9,11},{10,... | collective-permute-start | bytes 940040 | tf_op jit(solution)/shard_map/ppermute | solution.py:415
  12.9 7.9 %collective-permute-done.11.refs_2_.early_ref = bf16[144,1152]{1,0:T(8,128)(2,1)S(1)} collective-permute-done((bf16[144,1152]{1,0:T(8,128)(2,1)S(1)}, bf16[144,1152]{1,0:T(8,128)(2,1)S(1)}, u32[]{:S(2)}, u32[]{:S(2)}) %collective-permute-start.11) | collective-permute-done | bytes 331808 | tf_op jit(solution)/shard_map/ppermute | solution.py:415
  20.7 1.9 %collective-permute-start.15 = (bf16[144,1152]{1,0:T(8,128)(2,1)S(1)}, bf16[144,1152]{1,0:T(8,128)(2,1)S(1)}, u32[]{:S(2)}, u32[]{:S(2)}) collective-permute-start(bf16[144,1152]{1,0:T(8,128)(2,1)S(1)} %collective-permute-done.11.refs_2_.early_ref), channel_id=1, source_target_pairs={{0,1},{1,0},{2,4},{3,5},{4,2},{5,3},{6,7},{7,6},{8,10},{9,11},{10,... | collective-permute-start | bytes 995336 | tf_op jit(solution)/shard_map/ppermute | solution.py:415
  22.8 2.0 %collective-permute-start.10 = (s32[2]{0:T(128)S(1)}, s32[2]{0:T(128)S(1)}, u32[]{:S(2)}, u32[]{:S(2)}) collective-permute-start(s32[2]{0:T(128)S(1)} %copy-done.7), channel_id=1, source_target_pairs={{0,16},{16,0},{1,17},{17,1},{2,18},{18,2},{3,19},{19,3},{4,20},{20... | collective-permute-start | bytes 32 | tf_op jit(solution)/shard_map/ppermute | solution.py:350
  24.7 5.8 %collective-permute-done.10.far_ref = s32[2]{0:T(128)S(1)} collective-permute-done((s32[2]{0:T(128)S(1)}, s32[2]{0:T(128)S(1)}, u32[]{:S(2)}, u32[]{:S(2)}) %collective-permute-start.10) | collective-permute-done | bytes 40 | tf_op jit(solution)/shard_map/ppermute | solution.py:350
  32.4 1.7 %collective-permute-start.20 = (bf16[136,1152]{1,0:T(8,128)(2,1)S(1)}, bf16[136,1152]{1,0:T(8,128)(2,1)}, u32[]{:S(2)}, u32[]{:S(2)}) collective-permute-start(bf16[136,1152]{1,0:T(8,128)(2,1)S(1)} %shard_map.108), channel_id=1, source_target_pairs={{0,2},{1,3},{2,0},{3,1},{4,6},{5,7},{6,4},{7,5},{8,9},{9,8},{10,11... | collective-permute-start | bytes 940040 | tf_op jit(solution)/shard_map/ppermute | solution.py:415
  35.8 1.7 %collective-permute-start.5 = (bf16[280,640]{1,0:T(8,128)(2,1)S(1)}, bf16[280,640]{1,0:T(8,128)(2,1)S(1)}, u32[]{:S(2)}, u32[]{:S(2)}) collective-permute-start(bf16[280,640]{1,0:T(8,128)(2,1)S(1)} %shard_map.97), channel_id=1, source_target_pairs={{0,2},{1,3},{2,0},{3,1},{4,6},{5,7},{6,4},{7,5},{8,9},{9,8},{10,11... | collective-permute-start | bytes 1075208 | tf_op jit(solution)/shard_map/ppermute | solution.py:415
  37.5 2.0 %collective-permute-done.20.refs_2_.late_ref = bf16[136,1152]{1,0:T(8,128)(2,1)} collective-permute-done((bf16[136,1152]{1,0:T(8,128)(2,1)S(1)}, bf16[136,1152]{1,0:T(8,128)(2,1)}, u32[]{:S(2)}, u32[]{:S(2)}) %collective-permute-start.20) | collective-permute-done | bytes 313376 | tf_op jit(solution)/shard_map/ppermute | solution.py:415
  40.5 2.4 %collective-permute-done.19.refs_1_.late_ref = bf16[144,1152]{1,0:T(8,128)(2,1)S(1)} collective-permute-done((bf16[144,1152]{1,0:T(8,128)(2,1)S(1)}, bf16[144,1152]{1,0:T(8,128)(2,1)S(1)}, u32[]{:S(2)}, u32[]{:S(2)}) %collective-permute-start.19) | collective-permute-done | bytes 331808 | tf_op jit(solution)/shard_map/ppermute | solution.py:415
  42.9 1.1 collective-permute-start.24
  44.1 1.3 %shard_map.110 = bf16[144,1152]{1,0:T(8,128)(2,1)} custom-call(s32[16]{0:T(128)S(1)} %concatenate.3.pos_ref.refs_0_, bf16[144,1152]{1,0:T(8,128)(2,1)S(1)} %collective-permute-done.15.refs_1_.late_ref.early_ref, bf16[144,1152]{1,0:T(8,128)(2,1)S(1)} %collective-permute-done.19.refs_1_.late_ref), custom_call_target="tpu_custom_call" | custom-call | bytes 1000000 | tf_op jit(solution)/shard_map/pallas_call | solution.py:396
  46.3 2.6 %collective-permute-done.5.refs_1_.late_ref = bf16[280,640]{1,0:T(8,128)(2,1)S(1)} collective-permute-done((bf16[280,640]{1,0:T(8,128)(2,1)S(1)}, bf16[280,640]{1,0:T(8,128)(2,1)S(1)}, u32[]{:S(2)}, u32[]{:S(2)}) %collective-permute-start.5) | collective-permute-done | bytes 358432 | tf_op jit(solution)/shard_map/ppermute | solution.py:415
  48.9 1.5 %shard_map.100 = bf16[280,640]{1,0:T(8,128)(2,1)} custom-call(s32[16]{0:T(128)S(1)} %concatenate.3.pos_ref.refs_0_, bf16[280,640]{1,0:T(8,128)(2,1)S(1)} %collective-permute-done.3.refs_3_.late_ref.early_ref, bf16[280,640]{1,0:T(8,128)(2,1)S(1)} %collective-permute-done.5.refs_1_.late_ref), custom_call_target="tpu_custom_call" | custom-call | bytes 1000000 | tf_op jit(solution)/shard_map/pallas_call | solution.py:396
  55.6 2.3 %shard_map.94 = (bf16[8,384,144]{2,1,0:T(8,128)(2,1)S(1)}, bf16[8,384,136]{2,1,0:T(8,128)(2,1)S(1)}) custom-call(s32[16]{0:T(128)S(1)} %concatenate.3.pos_ref.refs_0_, bf16[192,2240]{1,0:T(8,128)(2,1)} %bitcast.7.own_ref, bf16[192,2240]{1,0:T(8,128)(2,1)} %collective-permute-done.other_ref), custom_call_target="tpu_custom_call" | custom-call | bytes 4000000 | tf_op jit(solution)/shard_map/pallas_call | solution.py:434
  58.0 2.8 %shard_map.105.refs_0_ = f32[384,1152]{1,0:T(8,128)S(1)} custom-call(s32[16]{0:T(128)S(1)} %concatenate.3.pos_ref.refs_0_, bf16[8,384,144]{2,1,0:T(8,128)(2,1)S(1)} %get-tuple-element.22.lead_ref.refs_0_, bf16[8,384,136]{2,1,0:T(8,128)(2,1)S(1)} %get-tuple-element.23.tail_ref.refs_1_, bf16[144,1152]{1,0:T(8,128)(2,1)S(1)} %shard_map.103.refs_0_, ...), custom_call_target="tpu_custom_call" | custom-call | flops 1500000000 | bytes 5000000 | tf_op jit(solution)/shard_map/pallas_call | solution.py:448
  61.5 1.8 %shard_map.106.refs_0_ = f32[384,1152]{1,0:T(8,128)S(1)} custom-call(s32[16]{0:T(128)S(1)} %concatenate.3.pos_ref.refs_0_, bf16[8,384,144]{2,1,0:T(8,128)(2,1)S(1)} %get-tuple-element.22.lead_ref.refs_0_, bf16[8,384,136]{2,1,0:T(8,128)(2,1)S(1)} %get-tuple-element.23.tail_ref.refs_1_, ...), custom_call_target="tpu_custom_call", output_to_operand_aliasing={{}: (3, {})} | custom-call | flops 1500000000 | bytes 5000000 | tf_op jit(solution)/shard_map/pallas_call | solution.py:448
  63.9 2.4 %shard_map.109.refs_2_ = f32[384,1152]{1,0:T(8,128)S(1)} custom-call(s32[16]{0:T(128)S(1)} %concatenate.3.pos_ref.refs_0_, bf16[8,384,144]{2,1,0:T(8,128)(2,1)S(1)} %get-tuple-element.22.lead_ref.refs_0_, bf16[8,384,136]{2,1,0:T(8,128)(2,1)S(1)} %get-tuple-element.23.tail_ref.refs_1_, ...), custom_call_target="tpu_custom_call", output_to_operand_aliasing={{}: (3, {})} | custom-call | flops 1500000000 | bytes 5000000 | tf_op jit(solution)/shard_map/pallas_call | solution.py:448
  66.3 3.7 %shard_map.112 = (bf16[20,16,128]{2,1,0:T(8,128)(2,1)S(1)}, bf16[20,16,128]{2,1,0:T(8,128)(2,1)S(1)}, bf16[20,16,128]{2,1,0:T(8,128)(2,1)S(1)}, bf16[20,16,128]{...) custom-call(s32[16]{0:T(128)S(1)} %concatenate.3.pos_ref.refs_0_, ...), custom_call_target="tpu_custom_call" | custom-call | flops 1500000000 | bytes 5000000 | tf_op jit(solution)/shard_map/pallas_call | solution.py:477
  70.0 1.6 %collective-permute-start.32 = (bf16[20,16,128]{2,1,0:T(8,128)(2,1)S(1)}, bf16[20,16,128]{2,1,0:T(8,128)(2,1)S(1)}, u32[]{:S(2)}, u32[]{:S(2)}) collective-permute-start(bf16[20,16,128]{2,1,0:T(8,128)(2,1)S(1)} %get-tuple-element.35), channel_id=1, source_target_pairs={{0,1},{1,0},{2,3},{3,2},{4,5},{5,4},{6,7},{7,6},{8,9},{9,8},{10,11... | collective-permute-start | bytes 245768 | tf_op jit(solution)/shard_map/ppermute | solution.py:353
  72.1 2.2 %shard_map.96.refs_0_ = f32[384,640]{1,0:T(8,128)S(1)} custom-call(s32[16]{0:T(128)S(1)} %concatenate.3.pos_ref.refs_0_, bf16[8,384,144]{2,1,0:T(8,128)(2,1)S(1)} %get-tuple-element.22.lead_ref.refs_0_, bf16[8,384,136]{2,1,0:T(8,128)(2,1)S(1)} %get-tuple-element.23.tail_ref.refs_1_, bf16[280,640]{1,0:T(8,128)(2,1)S(1)} %shard_map.95.refs_0_, ...), custom_call_target="tpu_custom_call" | custom-call | flops 1500000000 | bytes 5000000 | tf_op jit(solution)/shard_map/pallas_call | solution.py:448
  74.3 1.8 %collective-permute-start.28 = (bf16[20,16,128]{2,1,0:T(8,128)(2,1)S(1)}, bf16[20,16,128]{2,1,0:T(8,128)(2,1)S(1)}, u32[]{:S(2)}, u32[]{:S(2)}) collective-permute-start(bf16[20,16,128]{2,1,0:T(8,128)(2,1)S(1)} %get-tuple-element.30), channel_id=1, source_target_pairs={{0,2},{1,3},{2,0},{3,1},{4,6},{5,7},{6,4},{7,5},{8,10},{9,11},{10,... | collective-permute-start | bytes 245768 | tf_op jit(solution)/shard_map/ppermute | solution.py:353
  76.1 1.3 %collective-permute-start.29 = (bf16[20,16,128]{2,1,0:T(8,128)(2,1)S(1)}, bf16[20,16,128]{2,1,0:T(8,128)(2,1)S(1)}, u32[]{:S(2)}, u32[]{:S(2)}) collective-permute-start(bf16[20,16,128]{2,1,0:T(8,128)(2,1)S(1)} %get-tuple-element.31), channel_id=1, source_target_pairs={{0,3},{1,2},{2,1},{3,0},{4,7},{5,6},{6,5},{7,4},{8,11},{9,10},{10,... | collective-permute-start | bytes 245768 | tf_op jit(solution)/shard_map/ppermute | solution.py:353
  77.9 2.3 %collective-permute-start.30 = (bf16[20,16,128]{2,1,0:T(8,128)(2,1)S(1)}, bf16[20,16,128]{2,1,0:T(8,128)(2,1)S(1)}, u32[]{:S(2)}, u32[]{:S(2)}) collective-permute-start(bf16[20,16,128]{2,1,0:T(8,128)(2,1)S(1)} %get-tuple-element.32), channel_id=1, source_target_pairs={{0,4},{1,5},{2,6},{3,7},{4,0},{5,1},{6,2},{7,3},{8,12},{9,13},{10,... | collective-permute-start | bytes 245768 | tf_op jit(solution)/shard_map/ppermute | solution.py:353
  80.2 1.3 %collective-permute-start.31 = (bf16[20,16,128]{2,1,0:T(8,128)(2,1)S(1)}, bf16[20,16,128]{2,1,0:T(8,128)(2,1)S(1)}, u32[]{:S(2)}, u32[]{:S(2)}) collective-permute-start(bf16[20,16,128]{2,1,0:T(8,128)(2,1)S(1)} %get-tuple-element.33), channel_id=1, source_target_pairs={{0,5},{1,4},{2,7},{3,6},{4,1},{5,0},{6,3},{7,2},{8,13},{9,12},{10,... | collective-permute-start | bytes 245768 | tf_op jit(solution)/shard_map/ppermute | solution.py:353
  81.5 2.3 %collective-permute-start.33 = (bf16[20,16,128]{2,1,0:T(8,128)(2,1)S(1)}, bf16[20,16,128]{2,1,0:T(8,128)(2,1)S(1)}, u32[]{:S(2)}, u32[]{:S(2)}) collective-permute-start(bf16[20,16,128]{2,1,0:T(8,128)(2,1)S(1)} %shard_map.113), channel_id=1, source_target_pairs={{0,6},{1,7},{2,4},{3,5},{4,2},{5,3},{6,0},{7,1},{8,14},{9,15},{10,... | collective-permute-start | bytes 245768 | tf_op jit(solution)/shard_map/ppermute | solution.py:353
  83.8 1.3 %shard_map.98.old_ref = f32[384,640]{1,0:T(8,128)S(1)} custom-call(s32[16]{0:T(128)S(1)} %concatenate.3.pos_ref.refs_0_, bf16[8,384,144]{2,1,0:T(8,128)(2,1)S(1)} %get-tuple-element.22.lead_ref.refs_0_, bf16[8,384,136]{2,1,0:T(8,128)(2,1)S(1)} %get-tuple-element.23.tail_ref.refs_1_, ...), custom_call_target="tpu_custom_call", output_to_operand_aliasing={{}: (3, {})} | custom-call | flops 1500000000 | bytes 5000000 | tf_op jit(solution)/shard_map/pallas_call | solution.py:448
  85.2 1.8 %shard_map.101 = (bf16[192,640]{1,0:T(8,128)(2,1)S(1)}, bf16[192,560]{1,0:T(8,128)(2,1)S(1)}) custom-call(s32[16]{0:T(128)S(1)} %concatenate.3.pos_ref.refs_0_, bf16[8,384,144]{2,1,0:T(8,128)(2,1)S(1)} %get-tuple-element.22.lead_ref.refs_0_, bf16[8,384,136]{2,1,0:T(8,128)(2,1)S(1)} %get-tuple-element.23.tail_ref.refs_1_, f32[384,640]{1,0:T(8,128)S(1)} %shard_map.98.old_ref, ...), custom_call_target="tpu_custom_call" | custom-call | flops 700000000 | bytes 3000000 | tf_op jit(solution)/shard_map/pallas_call | solution.py:486
  86.9 1.7 %collective-permute-start.9 = (bf16[192,560]{1,0:T(8,128)(2,1)S(1)}, bf16[192,560]{1,0:T(8,128)(2,1)S(1)}, u32[]{:S(2)}, u32[]{:S(2)}) collective-permute-start(bf16[192,560]{1,0:T(8,128)(2,1)S(1)} %get-tuple-element.26), channel_id=1, source_target_pairs={{0,16},{16,0},{1,17},{17,1},{2,18},{18,2},{3,19},{19,3},{4,20},{20... | collective-permute-start | bytes 645128 | tf_op jit(solution)/shard_map/ppermute | solution.py:350
  88.7 2.2 %collective-permute-done.31.refs_6_ = bf16[20,16,128]{2,1,0:T(8,128)(2,1)S(1)} collective-permute-done((bf16[20,16,128]{2,1,0:T(8,128)(2,1)S(1)}, bf16[20,16,128]{2,1,0:T(8,128)(2,1)S(1)}, u32[]{:S(2)}, u32[]{:S(2)}) %collective-permute-start.31) | collective-permute-done | bytes 81952 | tf_op jit(solution)/shard_map/ppermute | solution.py:353
  91.6 1.7 %collective-permute-start.34 = (bf16[10,16,128]{2,1,0:T(8,128)(2,1)S(1)}, bf16[10,16,128]{2,1,0:T(8,128)(2,1)S(1)}, u32[]{:S(2)}, u32[]{:S(2)}) collective-permute-start(bf16[10,16,128]{2,1,0:T(8,128)(2,1)S(1)} %get-tuple-element.37), channel_id=1, source_target_pairs={{0,16},{16,0},{1,17},{17,1},{2,18},{18,2},{3,19},{19,3},{4,20},{20... | collective-permute-start | bytes 122888 | tf_op jit(solution)/shard_map/ppermute | solution.py:350
  93.3 2.4 %collective-permute-done.34.got_ref = bf16[10,16,128]{2,1,0:T(8,128)(2,1)S(1)} collective-permute-done((bf16[10,16,128]{2,1,0:T(8,128)(2,1)S(1)}, bf16[10,16,128]{2,1,0:T(8,128)(2,1)S(1)}, u32[]{:S(2)}, u32[]{:S(2)}) %collective-permute-start.34) | collective-permute-done | bytes 40992 | tf_op jit(solution)/shard_map/ppermute | solution.py:350
  96.2 1.7 %collective-permute-start.42 = (bf16[20,16,128]{2,1,0:T(8,128)(2,1)S(1)}, bf16[20,16,128]{2,1,0:T(8,128)(2,1)S(1)}, u32[]{:S(2)}, u32[]{:S(2)}) collective-permute-start(bf16[20,16,128]{2,1,0:T(8,128)(2,1)S(1)} %shard_map.115.refs_0_), channel_id=1, source_target_pairs={{0,16},{8,24},{16,0},{24,8},{1,17},{9,25},{17,1},{25,9},{2,18},{10... | collective-permute-start | bytes 245768 | tf_op jit(solution)/shard_map/ppermute | solution.py:539
  97.9 2.0 %collective-permute-start.40 = (bf16[20,16,128]{2,1,0:T(8,128)(2,1)S(1)}, bf16[20,16,128]{2,1,0:T(8,128)(2,1)S(1)}, u32[]{:S(2)}, u32[]{:S(2)}) collective-permute-start(bf16[20,16,128]{2,1,0:T(8,128)(2,1)S(1)} %shard_map.115.refs_0_), channel_id=1, source_target_pairs={{0,6},{1,7},{2,4},{3,5},{4,2},{5,3},{6,0},{7,1},{8,14},{9,15},{10,... | collective-permute-start | bytes 245768 | tf_op jit(solution)/shard_map/ppermute | solution.py:353
  99.9 1.3 %collective-permute-start.35 = (bf16[20,16,128]{2,1,0:T(8,128)(2,1)S(1)}, bf16[20,16,128]{2,1,0:T(8,128)(2,1)S(1)}, u32[]{:S(2)}, u32[]{:S(2)}) collective-permute-start(bf16[20,16,128]{2,1,0:T(8,128)(2,1)S(1)} %shard_map.115.refs_0_), channel_id=1, source_target_pairs={{0,1},{1,0},{2,3},{3,2},{4,5},{5,4},{6,7},{7,6},{8,9},{9,8},{10,11... | collective-permute-start | bytes 245768 | tf_op jit(solution)/shard_map/ppermute | solution.py:353
  102.0 2.8 %collective-permute-done.40.refs_6_ = bf16[20,16,128]{2,1,0:T(8,128)(2,1)S(1)} collective-permute-done((bf16[20,16,128]{2,1,0:T(8,128)(2,1)S(1)}, bf16[20,16,128]{2,1,0:T(8,128)(2,1)S(1)}, u32[]{:S(2)}, u32[]{:S(2)}) %collective-permute-start.40) | collective-permute-done | bytes 81952 | tf_op jit(solution)/shard_map/ppermute | solution.py:353
  104.7 1.3 %collective-permute-start.37 = (bf16[20,16,128]{2,1,0:T(8,128)(2,1)S(1)}, bf16[20,16,128]{2,1,0:T(8,128)(2,1)S(1)}, u32[]{:S(2)}, u32[]{:S(2)}) collective-permute-start(bf16[20,16,128]{2,1,0:T(8,128)(2,1)S(1)} %shard_map.115.refs_0_), channel_id=1, source_target_pairs={{0,3},{1,2},{2,1},{3,0},{4,7},{5,6},{6,5},{7,4},{8,11},{9,10},{10,... | collective-permute-start | bytes 245768 | tf_op jit(solution)/shard_map/ppermute | solution.py:353
  106.0 2.2 %collective-permute-start.38 = (bf16[20,16,128]{2,1,0:T(8,128)(2,1)S(1)}, bf16[20,16,128]{2,1,0:T(8,128)(2,1)S(1)}, u32[]{:S(2)}, u32[]{:S(2)}) collective-permute-start(bf16[20,16,128]{2,1,0:T(8,128)(2,1)S(1)} %shard_map.115.refs_0_), channel_id=1, source_target_pairs={{0,4},{1,5},{2,6},{3,7},{4,0},{5,1},{6,2},{7,3},{8,12},{9,13},{10,... | collective-permute-start | bytes 245768 | tf_op jit(solution)/shard_map/ppermute | solution.py:353
  108.2 1.4 %collective-permute-start.39 = (bf16[20,16,128]{2,1,0:T(8,128)(2,1)S(1)}, bf16[20,16,128]{2,1,0:T(8,128)(2,1)S(1)}, u32[]{:S(2)}, u32[]{:S(2)}) collective-permute-start(bf16[20,16,128]{2,1,0:T(8,128)(2,1)S(1)} %shard_map.115.refs_0_), channel_id=1, source_target_pairs={{0,5},{1,4},{2,7},{3,6},{4,1},{5,0},{6,3},{7,2},{8,13},{9,12},{10,... | collective-permute-start | bytes 245768 | tf_op jit(solution)/shard_map/ppermute | solution.py:353
  110.4 1.3 %shard_map.117.place_ref = s32[20]{0:T(128)S(1)} custom-call(s32[16]{0:T(128)S(1)} %concatenate.3.pos_ref.refs_0_, s32[80]{0:T(128)S(1)} %copy-done.8), custom_call_target="tpu_custom_call" | custom-call | bytes 1000 | tf_op jit(solution)/shard_map/pallas_call | solution.py:543
  112.7 1.3 %shard_map.118 = (f32[20,14,112]{2,1,0:T(8,128)}, f32[20,112]{1,0:T(8,128)}) custom-call(s32[20]{0:T(128)S(1)} %shard_map.117.place_ref, bf16[20,16,128]{2,1,0:T(8,128)(2,1)S(1)} %shard_map.115.refs_0_, bf16[20,16,128]{2,1,0:T(8,128)(2,1)S(1)} %collective-permute-done.42.refs_1_, bf16[20,16,128]{2,1,0:T(8,128)(2,1)S(1)} %collective-permute-done.43.refs_2_, ...), custom_call_target="tpu_custom_call" | custom-call | flops 1000000 | bytes 800000 | tf_op jit(solution)/shard_map/pallas_call | solution.py:551
  113.9 1.2 collective-permute-done.38.refs_4_
  115.1 1.5 %collective-permute-done.39.refs_5_ = bf16[20,16,128]{2,1,0:T(8,128)(2,1)S(1)} collective-permute-done((bf16[20,16,128]{2,1,0:T(8,128)(2,1)S(1)}, bf16[20,16,128]{2,1,0:T(8,128)(2,1)S(1)}, u32[]{:S(2)}, u32[]{:S(2)}) %collective-permute-start.39) | collective-permute-done | bytes 81952 | tf_op jit(solution)/shard_map/ppermute | solution.py:353
  116.6 2.2 %shard_map.116 = bf16[192,1120]{1,0:T(8,128)(2,1)} custom-call(s32[16]{0:T(128)S(1)} %concatenate.3.pos_ref.refs_0_, s32[2]{0:T(128)S(1)} %copy-done.7, bf16[192,640]{1,0:T(8,128)(2,1)S(1)} %get-tuple-element.25.own_ref, bf16[192,640]{1,0:T(8,128)(2,1)S(1)} %shard_map.102.other_ref, bf16[20,16,128]{2,1,0:T(8,128)(2,1)S(1)} %shard_map.115.refs_0_, ...), custom_call_target="tpu_custom_call" | custom-call | flops 1500000000 | bytes 3000000 | tf_op jit(solution)/shard_map/pallas_call | solution.py:563
  (94 shorter events, 18.0 us)
Async XLA Ops:
  2.0 20.8 %copy-start.7 = (s32[2]{0:T(128)S(1)}, s32[2]{0:T(128)}, u32[]{:S(2)}) copy-start(s32[2]{0:T(128)} %near_ref.3) | copy-start | bytes 28
  2.0 9.4 %collective-permute-start.12 = (bf16[136,1152]{1,0:T(8,128)(2,1)S(1)}, bf16[136,1152]{1,0:T(8,128)(2,1)S(1)}, u32[]{:S(2)}, u32[]{:S(2)}) collective-permute-start(bf16[136,1152]{1,0:T(8,128)(2,1)S(1)} %shard_map.104.refs_1_), channel_id=1, source_target_pairs={{0,2},{1,3},{2,0},{3,1},{4,6},{5,7},{6,4},{7,5},{8,9},{9,8},{10,12... | collective-permute-start | bytes 940040 | tf_op jit(solution)/shard_map/ppermute | solution.py:415
  6.2 16.5 %collective-permute-start.1 = (bf16[280,640]{1,0:T(8,128)(2,1)S(1)}, bf16[280,640]{1,0:T(8,128)(2,1)S(1)}, u32[]{:S(2)}, u32[]{:S(2)}) collective-permute-start(bf16[280,640]{1,0:T(8,128)(2,1)S(1)} %shard_map.95.refs_0_), channel_id=1, source_target_pairs={{0,2},{1,3},{2,0},{3,1},{4,6},{5,7},{6,4},{7,5},{8,9},{9,8},{10,12... | collective-permute-start | bytes 1075208 | tf_op jit(solution)/shard_map/ppermute | solution.py:415
  7.6 13.1 %collective-permute-start.11 = (bf16[144,1152]{1,0:T(8,128)(2,1)S(1)}, bf16[144,1152]{1,0:T(8,128)(2,1)S(1)}, u32[]{:S(2)}, u32[]{:S(2)}) collective-permute-start(bf16[144,1152]{1,0:T(8,128)(2,1)S(1)} %shard_map.103.refs_0_), channel_id=1, source_target_pairs={{0,2},{1,3},{2,0},{3,1},{4,6},{5,7},{6,4},{7,5},{8,9},{9,8},{10,12... | collective-permute-start | bytes 995336 | tf_op jit(solution)/shard_map/ppermute | solution.py:415
  9.7 35.6 %collective-permute-start = (bf16[192,2240]{1,0:T(8,128)(2,1)}, bf16[192,2240]{1,0:T(8,128)(2,1)}, u32[]{:S(2)}, u32[]{:S(2)}) collective-permute-start(bf16[192,2240]{1,0:T(8,128)(2,1)} %bitcast.7.own_ref), channel_id=1, source_target_pairs={{0,16},{16,0},{1,17},{17,1},{2,18},{18,2},{3,19},{19,3},{4,20},{20... | collective-permute-start | bytes 2580488 | tf_op jit(solution)/shard_map/ppermute | solution.py:350
  11.4 24.4 %copy-start = (bf16[136,1152]{1,0:T(8,128)(2,1)}, bf16[136,1152]{1,0:T(8,128)(2,1)S(1)}, u32[]{:S(2)}) copy-start(bf16[136,1152]{1,0:T(8,128)(2,1)S(1)} %collective-permute-done.12.refs_3_.early_ref) | copy-start | bytes 940036
  11.4 19.1 %collective-permute-start.16 = (bf16[136,1152]{1,0:T(8,128)(2,1)S(1)}, bf16[136,1152]{1,0:T(8,128)(2,1)S(1)}, u32[]{:S(2)}, u32[]{:S(2)}) collective-permute-start(bf16[136,1152]{1,0:T(8,128)(2,1)S(1)} %collective-permute-done.12.refs_3_.early_ref), channel_id=1, source_target_pairs={{0,1},{1,0},{2,4},{3,5},{4,2},{5,3},{6,7},{7,6},{8,10},{9,11},{10,... | collective-permute-start | bytes 940040 | tf_op jit(solution)/shard_map/ppermute | solution.py:415
  20.7 11.6 %collective-permute-start.15 = (bf16[144,1152]{1,0:T(8,128)(2,1)S(1)}, bf16[144,1152]{1,0:T(8,128)(2,1)S(1)}, u32[]{:S(2)}, u32[]{:S(2)}) collective-permute-start(bf16[144,1152]{1,0:T(8,128)(2,1)S(1)} %collective-permute-done.11.refs_2_.early_ref), channel_id=1, source_target_pairs={{0,1},{1,0},{2,4},{3,5},{4,2},{5,3},{6,7},{7,6},{8,10},{9,11},{10,... | collective-permute-start | bytes 995336 | tf_op jit(solution)/shard_map/ppermute | solution.py:415
  22.7 12.0 %collective-permute-start.3 = (bf16[280,640]{1,0:T(8,128)(2,1)S(1)}, bf16[280,640]{1,0:T(8,128)(2,1)S(1)}, u32[]{:S(2)}, u32[]{:S(2)}) collective-permute-start(bf16[280,640]{1,0:T(8,128)(2,1)S(1)} %collective-permute-done.1.refs_1_.early_ref), channel_id=1, source_target_pairs={{0,1},{1,0},{2,4},{3,5},{4,2},{5,3},{6,7},{7,6},{8,10},{9,11},{10,... | collective-permute-start | bytes 1075208 | tf_op jit(solution)/shard_map/ppermute | solution.py:415
  22.8 7.7 %collective-permute-start.10 = (s32[2]{0:T(128)S(1)}, s32[2]{0:T(128)S(1)}, u32[]{:S(2)}, u32[]{:S(2)}) collective-permute-start(s32[2]{0:T(128)S(1)} %copy-done.7), channel_id=1, source_target_pairs={{0,16},{16,0},{1,17},{17,1},{2,18},{18,2},{3,19},{19,3},{4,20},{20... | collective-permute-start | bytes 32 | tf_op jit(solution)/shard_map/ppermute | solution.py:350
  30.5 5.3 %collective-permute-start.14 = (bf16[136,1152]{1,0:T(8,128)(2,1)S(1)}, bf16[136,1152]{1,0:T(8,128)(2,1)}, u32[]{:S(2)}, u32[]{:S(2)}) collective-permute-start(bf16[136,1152]{1,0:T(8,128)(2,1)S(1)} %collective-permute-done.12.refs_3_.early_ref), channel_id=1, source_target_pairs={{0,8},{8,0},{1,9},{9,1},{2,10},{10,2},{3,11},{11,3},{4,12},{12,4},... | collective-permute-start | bytes 940040 | tf_op jit(solution)/shard_map/ppermute | solution.py:350
  30.5 7.0 %collective-permute-start.13 = (bf16[144,1152]{1,0:T(8,128)(2,1)S(1)}, bf16[144,1152]{1,0:T(8,128)(2,1)}, u32[]{:S(2)}, u32[]{:S(2)}) collective-permute-start(bf16[144,1152]{1,0:T(8,128)(2,1)S(1)} %collective-permute-done.11.refs_2_.early_ref), channel_id=1, source_target_pairs={{0,8},{8,0},{1,9},{9,1},{2,10},{10,2},{3,11},{11,3},{4,12},{12,4},... | collective-permute-start | bytes 995336 | tf_op jit(solution)/shard_map/ppermute | solution.py:350
  32.4 7.1 %collective-permute-start.20 = (bf16[136,1152]{1,0:T(8,128)(2,1)S(1)}, bf16[136,1152]{1,0:T(8,128)(2,1)}, u32[]{:S(2)}, u32[]{:S(2)}) collective-permute-start(bf16[136,1152]{1,0:T(8,128)(2,1)S(1)} %shard_map.108), channel_id=1, source_target_pairs={{0,2},{1,3},{2,0},{3,1},{4,6},{5,7},{6,4},{7,5},{8,9},{9,8},{10,11... | collective-permute-start | bytes 940040 | tf_op jit(solution)/shard_map/ppermute | solution.py:415
  34.7 8.2 %collective-permute-start.19 = (bf16[144,1152]{1,0:T(8,128)(2,1)S(1)}, bf16[144,1152]{1,0:T(8,128)(2,1)S(1)}, u32[]{:S(2)}, u32[]{:S(2)}) collective-permute-start(bf16[144,1152]{1,0:T(8,128)(2,1)S(1)} %shard_map.107), channel_id=1, source_target_pairs={{0,2},{1,3},{2,0},{3,1},{4,6},{5,7},{6,4},{7,5},{8,9},{9,8},{10,11... | collective-permute-start | bytes 995336 | tf_op jit(solution)/shard_map/ppermute | solution.py:415
  35.8 13.1 %collective-permute-start.5 = (bf16[280,640]{1,0:T(8,128)(2,1)S(1)}, bf16[280,640]{1,0:T(8,128)(2,1)S(1)}, u32[]{:S(2)}, u32[]{:S(2)}) collective-permute-start(bf16[280,640]{1,0:T(8,128)(2,1)S(1)} %shard_map.97), channel_id=1, source_target_pairs={{0,2},{1,3},{2,0},{3,1},{4,6},{5,7},{6,4},{7,5},{8,9},{9,8},{10,11... | collective-permute-start | bytes 1075208 | tf_op jit(solution)/shard_map/ppermute | solution.py:415
  37.5 8.8 %collective-permute-start.18 = (bf16[136,1152]{1,0:T(8,128)(2,1)S(1)}, bf16[136,1152]{1,0:T(8,128)(2,1)S(1)}, u32[]{:S(2)}, u32[]{:S(2)}) collective-permute-start(bf16[136,1152]{1,0:T(8,128)(2,1)S(1)} %collective-permute-done.16.refs_2_.late_ref.early_ref), channel_id=1, source_target_pairs={{0,8},{8,0},{1,9},{9,1},{2,10},{10,2},{3,11},{11,3},{4,12},{12,4},... | collective-permute-start | bytes 940040 | tf_op jit(solution)/shard_map/ppermute | solution.py:350
  39.5 10.9 %collective-permute-start.17 = (bf16[144,1152]{1,0:T(8,128)(2,1)S(1)}, bf16[144,1152]{1,0:T(8,128)(2,1)S(1)}, u32[]{:S(2)}, u32[]{:S(2)}) collective-permute-start(bf16[144,1152]{1,0:T(8,128)(2,1)S(1)} %collective-permute-done.15.refs_1_.late_ref.early_ref), channel_id=1, source_target_pairs={{0,8},{8,0},{1,9},{9,1},{2,10},{10,2},{3,11},{11,3},{4,12},{12,4},... | collective-permute-start | bytes 995336 | tf_op jit(solution)/shard_map/ppermute | solution.py:350
  42.9 9.0 %collective-permute-start.24 = (bf16[136,1152]{1,0:T(8,128)(2,1)S(1)}, bf16[136,1152]{1,0:T(8,128)(2,1)}, u32[]{:S(2)}, u32[]{:S(2)}) collective-permute-start(bf16[136,1152]{1,0:T(8,128)(2,1)S(1)} %shard_map.111), channel_id=1, source_target_pairs={{0,1},{1,0},{2,3},{3,2},{4,5},{5,4},{6,7},{7,6},{8,10},{9,11},{10,... | collective-permute-start | bytes 940040 | tf_op jit(solution)/shard_map/ppermute | solution.py:415
  45.4 12.5 %collective-permute-start.23 = (bf16[144,1152]{1,0:T(8,128)(2,1)}, bf16[144,1152]{1,0:T(8,128)(2,1)}, u32[]{:S(2)}, u32[]{:S(2)}) collective-permute-start(bf16[144,1152]{1,0:T(8,128)(2,1)} %shard_map.110), channel_id=1, source_target_pairs={{0,1},{1,0},{2,3},{3,2},{4,5},{5,4},{6,7},{7,6},{8,10},{9,11},{10,... | collective-permute-start | bytes 995336 | tf_op jit(solution)/shard_map/ppermute | solution.py:415
  46.3 15.2 %collective-permute-start.21 = (bf16[144,1152]{1,0:T(8,128)(2,1)S(1)}, bf16[144,1152]{1,0:T(8,128)(2,1)}, u32[]{:S(2)}, u32[]{:S(2)}) collective-permute-start(bf16[144,1152]{1,0:T(8,128)(2,1)S(1)} %collective-permute-done.19.refs_1_.late_ref), channel_id=1, source_target_pairs={{0,8},{8,0},{1,9},{9,1},{2,10},{10,2},{3,11},{11,3},{4,12},{12,4},... | collective-permute-start | bytes 995336 | tf_op jit(solution)/shard_map/ppermute | solution.py:350
  48.9 12.0 %collective-permute-start.22 = (bf16[136,1152]{1,0:T(8,128)(2,1)}, bf16[136,1152]{1,0:T(8,128)(2,1)}, u32[]{:S(2)}, u32[]{:S(2)}) collective-permute-start(bf16[136,1152]{1,0:T(8,128)(2,1)} %collective-permute-done.20.refs_2_.late_ref), channel_id=1, source_target_pairs={{0,8},{8,0},{1,9},{9,1},{2,10},{10,2},{3,11},{11,3},{4,12},{12,4},... | collective-permute-start | bytes 940040 | tf_op jit(solution)/shard_map/ppermute | solution.py:350
  51.1 12.2 %collective-permute-start.7 = (bf16[280,640]{1,0:T(8,128)(2,1)}, bf16[280,640]{1,0:T(8,128)(2,1)}, u32[]{:S(2)}, u32[]{:S(2)}) collective-permute-start(bf16[280,640]{1,0:T(8,128)(2,1)} %shard_map.100), channel_id=1, source_target_pairs={{0,1},{1,0},{2,3},{3,2},{4,5},{5,4},{6,7},{7,6},{8,10},{9,11},{10,... | collective-permute-start | bytes 1075208 | tf_op jit(solution)/shard_map/ppermute | solution.py:415
  51.9 11.8 %collective-permute-start.26 = (bf16[136,1152]{1,0:T(8,128)(2,1)}, bf16[136,1152]{1,0:T(8,128)(2,1)}, u32[]{:S(2)}, u32[]{:S(2)}) collective-permute-start(bf16[136,1152]{1,0:T(8,128)(2,1)} %collective-permute-done.24.refs_4_), channel_id=1, source_target_pairs={{0,8},{8,0},{1,9},{9,1},{2,10},{10,2},{3,11},{11,3},{4,12},{12,4},... | collective-permute-start | bytes 940040 | tf_op jit(solution)/shard_map/ppermute | solution.py:350
  57.9 8.4 %collective-permute-start.25 = (bf16[144,1152]{1,0:T(8,128)(2,1)}, bf16[144,1152]{1,0:T(8,128)(2,1)S(1)}, u32[]{:S(2)}, u32[]{:S(2)}) collective-permute-start(bf16[144,1152]{1,0:T(8,128)(2,1)} %collective-permute-done.23.refs_3_), channel_id=1, source_target_pairs={{0,8},{8,0},{1,9},{9,1},{2,10},{10,2},{3,11},{11,3},{4,12},{12,4},... | collective-permute-start | bytes 995336 | tf_op jit(solution)/shard_map/ppermute | solution.py:350
  60.9 10.7 %collective-permute-start.2 = (bf16[280,640]{1,0:T(8,128)(2,1)S(1)}, bf16[280,640]{1,0:T(8,128)(2,1)S(1)}, u32[]{:S(2)}, u32[]{:S(2)}) collective-permute-start(bf16[280,640]{1,0:T(8,128)(2,1)S(1)} %collective-permute-done.1.refs_1_.early_ref), channel_id=1, source_target_pairs={{0,8},{8,0},{1,9},{9,1},{2,10},{10,2},{3,11},{11,3},{4,12},{12,4},... | collective-permute-start | bytes 1075208 | tf_op jit(solution)/shard_map/ppermute | solution.py:350
  61.4 10.7 %collective-permute-start.4 = (bf16[280,640]{1,0:T(8,128)(2,1)S(1)}, bf16[280,640]{1,0:T(8,128)(2,1)S(1)}, u32[]{:S(2)}, u32[]{:S(2)}) collective-permute-start(bf16[280,640]{1,0:T(8,128)(2,1)S(1)} %collective-permute-done.3.refs_3_.late_ref.early_ref), channel_id=1, source_target_pairs={{0,8},{8,0},{1,9},{9,1},{2,10},{10,2},{3,11},{11,3},{4,12},{12,4},... | collective-permute-start | bytes 1075208 | tf_op jit(solution)/shard_map/ppermute | solution.py:350
  63.3 14.6 %collective-permute-start.6 = (bf16[280,640]{1,0:T(8,128)(2,1)S(1)}, bf16[280,640]{1,0:T(8,128)(2,1)S(1)}, u32[]{:S(2)}, u32[]{:S(2)}) collective-permute-start(bf16[280,640]{1,0:T(8,128)(2,1)S(1)} %collective-permute-done.5.refs_1_.late_ref), channel_id=1, source_target_pairs={{0,8},{8,0},{1,9},{9,1},{2,10},{10,2},{3,11},{11,3},{4,12},{12,4},... | collective-permute-start | bytes 1075208 | tf_op jit(solution)/shard_map/ppermute | solution.py:350
  63.8 17.7 %collective-permute-start.8 = (bf16[280,640]{1,0:T(8,128)(2,1)}, bf16[280,640]{1,0:T(8,128)(2,1)S(1)}, u32[]{:S(2)}, u32[]{:S(2)}) collective-permute-start(bf16[280,640]{1,0:T(8,128)(2,1)} %collective-permute-done.7.refs_0_), channel_id=1, source_target_pairs={{0,8},{8,0},{1,9},{9,1},{2,10},{10,2},{3,11},{11,3},{4,12},{12,4},... | collective-permute-start | bytes 1075208 | tf_op jit(solution)/shard_map/ppermute | solution.py:350
  70.0 6.1 %collective-permute-start.32 = (bf16[20,16,128]{2,1,0:T(8,128)(2,1)S(1)}, bf16[20,16,128]{2,1,0:T(8,128)(2,1)S(1)}, u32[]{:S(2)}, u32[]{:S(2)}) collective-permute-start(bf16[20,16,128]{2,1,0:T(8,128)(2,1)S(1)} %get-tuple-element.35), channel_id=1, source_target_pairs={{0,1},{1,0},{2,3},{3,2},{4,5},{5,4},{6,7},{7,6},{8,9},{9,8},{10,11... | collective-permute-start | bytes 245768 | tf_op jit(solution)/shard_map/ppermute | solution.py:353
  71.5 8.6 %collective-permute-start.27 = (bf16[20,16,128]{2,1,0:T(8,128)(2,1)S(1)}, bf16[20,16,128]{2,1,0:T(8,128)(2,1)S(1)}, u32[]{:S(2)}, u32[]{:S(2)}) collective-permute-start(bf16[20,16,128]{2,1,0:T(8,128)(2,1)S(1)} %get-tuple-element.29), channel_id=1, source_target_pairs={{0,1},{1,0},{2,3},{3,2},{4,5},{5,4},{6,7},{7,6},{8,9},{9,8},{10,11... | collective-permute-start | bytes 245768 | tf_op jit(solution)/shard_map/ppermute | solution.py:353
  74.3 12.6 %collective-permute-start.28 = (bf16[20,16,128]{2,1,0:T(8,128)(2,1)S(1)}, bf16[20,16,128]{2,1,0:T(8,128)(2,1)S(1)}, u32[]{:S(2)}, u32[]{:S(2)}) collective-permute-start(bf16[20,16,128]{2,1,0:T(8,128)(2,1)S(1)} %get-tuple-element.30), channel_id=1, source_target_pairs={{0,2},{1,3},{2,0},{3,1},{4,6},{5,7},{6,4},{7,5},{8,10},{9,11},{10,... | collective-permute-start | bytes 245768 | tf_op jit(solution)/shard_map/ppermute | solution.py:353
  76.1 12.6 %collective-permute-start.29 = (bf16[20,16,128]{2,1,0:T(8,128)(2,1)S(1)}, bf16[20,16,128]{2,1,0:T(8,128)(2,1)S(1)}, u32[]{:S(2)}, u32[]{:S(2)}) collective-permute-start(bf16[20,16,128]{2,1,0:T(8,128)(2,1)S(1)} %get-tuple-element.31), channel_id=1, source_target_pairs={{0,3},{1,2},{2,1},{3,0},{4,7},{5,6},{6,5},{7,4},{8,11},{9,10},{10,... | collective-permute-start | bytes 245768 | tf_op jit(solution)/shard_map/ppermute | solution.py:353
  77.9 10.8 %collective-permute-start.30 = (bf16[20,16,128]{2,1,0:T(8,128)(2,1)S(1)}, bf16[20,16,128]{2,1,0:T(8,128)(2,1)S(1)}, u32[]{:S(2)}, u32[]{:S(2)}) collective-permute-start(bf16[20,16,128]{2,1,0:T(8,128)(2,1)S(1)} %get-tuple-element.32), channel_id=1, source_target_pairs={{0,4},{1,5},{2,6},{3,7},{4,0},{5,1},{6,2},{7,3},{8,12},{9,13},{10,... | collective-permute-start | bytes 245768 | tf_op jit(solution)/shard_map/ppermute | solution.py:353
  80.2 10.8 %collective-permute-start.31 = (bf16[20,16,128]{2,1,0:T(8,128)(2,1)S(1)}, bf16[20,16,128]{2,1,0:T(8,128)(2,1)S(1)}, u32[]{:S(2)}, u32[]{:S(2)}) collective-permute-start(bf16[20,16,128]{2,1,0:T(8,128)(2,1)S(1)} %get-tuple-element.33), channel_id=1, source_target_pairs={{0,5},{1,4},{2,7},{3,6},{4,1},{5,0},{6,3},{7,2},{8,13},{9,12},{10,... | collective-permute-start | bytes 245768 | tf_op jit(solution)/shard_map/ppermute | solution.py:353
  81.5 9.4 %collective-permute-start.33 = (bf16[20,16,128]{2,1,0:T(8,128)(2,1)S(1)}, bf16[20,16,128]{2,1,0:T(8,128)(2,1)S(1)}, u32[]{:S(2)}, u32[]{:S(2)}) collective-permute-start(bf16[20,16,128]{2,1,0:T(8,128)(2,1)S(1)} %shard_map.113), channel_id=1, source_target_pairs={{0,6},{1,7},{2,4},{3,5},{4,2},{5,3},{6,0},{7,1},{8,14},{9,15},{10,... | collective-permute-start | bytes 245768 | tf_op jit(solution)/shard_map/ppermute | solution.py:353
  85.1 25.2 %copy-start.8 = (s32[80]{0:T(128)S(1)}, s32[80]{0:T(128)}, u32[]{:S(2)}) copy-start(s32[80]{0:T(128)} %new_ref.1) | copy-start | bytes 964
  86.9 21.2 %collective-permute-start.9 = (bf16[192,560]{1,0:T(8,128)(2,1)S(1)}, bf16[192,560]{1,0:T(8,128)(2,1)S(1)}, u32[]{:S(2)}, u32[]{:S(2)}) collective-permute-start(bf16[192,560]{1,0:T(8,128)(2,1)S(1)} %get-tuple-element.26), channel_id=1, source_target_pairs={{0,16},{16,0},{1,17},{17,1},{2,18},{18,2},{3,19},{19,3},{4,20},{20... | collective-permute-start | bytes 645128 | tf_op jit(solution)/shard_map/ppermute | solution.py:350
  91.6 4.1 %collective-permute-start.34 = (bf16[10,16,128]{2,1,0:T(8,128)(2,1)S(1)}, bf16[10,16,128]{2,1,0:T(8,128)(2,1)S(1)}, u32[]{:S(2)}, u32[]{:S(2)}) collective-permute-start(bf16[10,16,128]{2,1,0:T(8,128)(2,1)S(1)} %get-tuple-element.37), channel_id=1, source_target_pairs={{0,16},{16,0},{1,17},{17,1},{2,18},{18,2},{3,19},{19,3},{4,20},{20... | collective-permute-start | bytes 122888 | tf_op jit(solution)/shard_map/ppermute | solution.py:350
  96.2 5.0 %collective-permute-start.42 = (bf16[20,16,128]{2,1,0:T(8,128)(2,1)S(1)}, bf16[20,16,128]{2,1,0:T(8,128)(2,1)S(1)}, u32[]{:S(2)}, u32[]{:S(2)}) collective-permute-start(bf16[20,16,128]{2,1,0:T(8,128)(2,1)S(1)} %shard_map.115.refs_0_), channel_id=1, source_target_pairs={{0,16},{8,24},{16,0},{24,8},{1,17},{9,25},{17,1},{25,9},{2,18},{10... | collective-permute-start | bytes 245768 | tf_op jit(solution)/shard_map/ppermute | solution.py:539
  97.9 3.3 %collective-permute-start.43 = (bf16[20,16,128]{2,1,0:T(8,128)(2,1)S(1)}, bf16[20,16,128]{2,1,0:T(8,128)(2,1)S(1)}, u32[]{:S(2)}, u32[]{:S(2)}) collective-permute-start(bf16[20,16,128]{2,1,0:T(8,128)(2,1)S(1)} %shard_map.115.refs_0_), channel_id=1, source_target_pairs={{0,8},{8,0},{16,24},{24,16},{1,9},{9,1},{17,25},{25,17},{2,10},{10... | collective-permute-start | bytes 245768 | tf_op jit(solution)/shard_map/ppermute | solution.py:539
  97.9 6.8 %collective-permute-start.40 = (bf16[20,16,128]{2,1,0:T(8,128)(2,1)S(1)}, bf16[20,16,128]{2,1,0:T(8,128)(2,1)S(1)}, u32[]{:S(2)}, u32[]{:S(2)}) collective-permute-start(bf16[20,16,128]{2,1,0:T(8,128)(2,1)S(1)} %shard_map.115.refs_0_), channel_id=1, source_target_pairs={{0,6},{1,7},{2,4},{3,5},{4,2},{5,3},{6,0},{7,1},{8,14},{9,15},{10,... | collective-permute-start | bytes 245768 | tf_op jit(solution)/shard_map/ppermute | solution.py:353
  99.9 6.1 %collective-permute-start.35 = (bf16[20,16,128]{2,1,0:T(8,128)(2,1)S(1)}, bf16[20,16,128]{2,1,0:T(8,128)(2,1)S(1)}, u32[]{:S(2)}, u32[]{:S(2)}) collective-permute-start(bf16[20,16,128]{2,1,0:T(8,128)(2,1)S(1)} %shard_map.115.refs_0_), channel_id=1, source_target_pairs={{0,1},{1,0},{2,3},{3,2},{4,5},{5,4},{6,7},{7,6},{8,9},{9,8},{10,11... | collective-permute-start | bytes 245768 | tf_op jit(solution)/shard_map/ppermute | solution.py:353
  101.2 8.4 %collective-permute-start.44 = (bf16[20,16,128]{2,1,0:T(8,128)(2,1)S(1)}, bf16[20,16,128]{2,1,0:T(8,128)(2,1)S(1)}, u32[]{:S(2)}, u32[]{:S(2)}) collective-permute-start(bf16[20,16,128]{2,1,0:T(8,128)(2,1)S(1)} %collective-permute-done.42.refs_1_), channel_id=1, source_target_pairs={{0,8},{8,0},{16,24},{24,16},{1,9},{9,1},{17,25},{25,17},{2,10},{10... | collective-permute-start | bytes 245768 | tf_op jit(solution)/shard_map/ppermute | solution.py:539
  101.2 12.7 %collective-permute-start.36 = (bf16[20,16,128]{2,1,0:T(8,128)(2,1)S(1)}, bf16[20,16,128]{2,1,0:T(8,128)(2,1)S(1)}, u32[]{:S(2)}, u32[]{:S(2)}) collective-permute-start(bf16[20,16,128]{2,1,0:T(8,128)(2,1)S(1)} %shard_map.115.refs_0_), channel_id=1, source_target_pairs={{0,2},{1,3},{2,0},{3,1},{4,6},{5,7},{6,4},{7,5},{8,10},{9,11},{10,... | collective-permute-start | bytes 245768 | tf_op jit(solution)/shard_map/ppermute | solution.py:353
  104.7 9.2 %collective-permute-start.37 = (bf16[20,16,128]{2,1,0:T(8,128)(2,1)S(1)}, bf16[20,16,128]{2,1,0:T(8,128)(2,1)S(1)}, u32[]{:S(2)}, u32[]{:S(2)}) collective-permute-start(bf16[20,16,128]{2,1,0:T(8,128)(2,1)S(1)} %shard_map.115.refs_0_), channel_id=1, source_target_pairs={{0,3},{1,2},{2,1},{3,0},{4,7},{5,6},{6,5},{7,4},{8,11},{9,10},{10,... | collective-permute-start | bytes 245768 | tf_op jit(solution)/shard_map/ppermute | solution.py:353
  106.0 9.1 %collective-permute-start.38 = (bf16[20,16,128]{2,1,0:T(8,128)(2,1)S(1)}, bf16[20,16,128]{2,1,0:T(8,128)(2,1)S(1)}, u32[]{:S(2)}, u32[]{:S(2)}) collective-permute-start(bf16[20,16,128]{2,1,0:T(8,128)(2,1)S(1)} %shard_map.115.refs_0_), channel_id=1, source_target_pairs={{0,4},{1,5},{2,6},{3,7},{4,0},{5,1},{6,2},{7,3},{8,12},{9,13},{10,... | collective-permute-start | bytes 245768 | tf_op jit(solution)/shard_map/ppermute | solution.py:353
  108.2 8.4 %collective-permute-start.39 = (bf16[20,16,128]{2,1,0:T(8,128)(2,1)S(1)}, bf16[20,16,128]{2,1,0:T(8,128)(2,1)S(1)}, u32[]{:S(2)}, u32[]{:S(2)}) collective-permute-start(bf16[20,16,128]{2,1,0:T(8,128)(2,1)S(1)} %shard_map.115.refs_0_), channel_id=1, source_target_pairs={{0,5},{1,4},{2,7},{3,6},{4,1},{5,0},{6,3},{7,2},{8,13},{9,12},{10,... | collective-permute-start | bytes 245768 | tf_op jit(solution)/shard_map/ppermute | solution.py:353
  109.6 7.0 %collective-permute-start.41 = (bf16[20,16,128]{2,1,0:T(8,128)(2,1)S(1)}, bf16[20,16,128]{2,1,0:T(8,128)(2,1)S(1)}, u32[]{:S(2)}, u32[]{:S(2)}) collective-permute-start(bf16[20,16,128]{2,1,0:T(8,128)(2,1)S(1)} %collective-permute-done.40.refs_6_), channel_id=1, source_target_pairs={{0,1},{1,0},{2,3},{3,2},{4,5},{5,4},{6,7},{7,6},{8,9},{9,8},{10,11... | collective-permute-start | bytes 245768 | tf_op jit(solution)/shard_map/ppermute | solution.py:353
  (8 other events, 52.3 us)
